TPU v7x, 32 devices: a whole 2x2x4 slice. The times are simulated.
32 devices in a mesh: rep: 4 (over z), fsdp: 8 (over y, x, core).
Axes of the slice: x: 2, y: 2, z: 4, core: 2. Of those that a mesh axis runs over, the one named last changes fastest.
Arguments:
- hidden_in: bfloat16 [4, 1024, 2048], P('rep', 'fsdp'), may hold values from -6 to 6
- segments: int32 [4, 1024], P('rep', 'fsdp'), may hold values from 0 to 7, never falling along the last dimension, each value on 1 to 768 neighbouring positions
- routes: int32 [4, 1024, 8], P('rep', 'fsdp'), may hold values from 0 to 15, all different within a row; in each aligned block of 128 rows (0 to 127, 128 to 255, ..., all dimensions but the last counted through in order) at most 96 rows name the same one
- doc_sets: int32 [4, 8], P('rep'), may hold values from 0 to 7, each once within a row
- cotangent: bfloat16 [4, 1024, 2048], P('rep', 'fsdp'), may hold values from -6 to 6
- w_qkv: bfloat16 [3, 2048, 2048], P(None, 'fsdp'), may hold values from -0.125 to 0.125
- w_out: bfloat16 [2048, 2048], P('fsdp'), may hold values from -0.5 to 0.5
- gain_attn: bfloat16 [2048], P('fsdp'), may hold values from 0.25 to 1.75
- gain_moe: bfloat16 [2048], P('fsdp'), may hold values from 0.25 to 1.75
- router: bfloat16 [2048, 16], P('fsdp'), may hold values from -0.0625 to 0.0625
- w_gate: bfloat16 [16, 2048, 1024], P('fsdp'), may hold values from -0.125 to 0.125
- w_up: bfloat16 [16, 2048, 1024], P('fsdp'), may hold values from -0.125 to 0.125
- w_down: bfloat16 [16, 1024, 2048], P('fsdp'), may hold values from -0.75 to 0.75
- a_attn: bfloat16 [4, 2048, 128], P(None, 'fsdp'), may hold values from -0.125 to 0.125
- b_attn: bfloat16 [4, 2048, 128], P(None, 'fsdp'), may hold values from -0.75 to 0.75
- exp_a_in: bfloat16 [16, 2, 2048, 128], P('fsdp'), may hold values from -0.125 to 0.125
- exp_b_in: bfloat16 [16, 2, 128, 1024], P('fsdp'), may hold values from -0.75 to 0.75
- exp_a_down: bfloat16 [16, 1024, 128], P('fsdp'), may hold values from -0.1875 to 0.1875
- exp_b_down: bfloat16 [16, 128, 2048], P('fsdp'), may hold values from -0.75 to 0.75
Outputs:
- layer_out: bfloat16 [4, 1024, 2048], P('rep', 'fsdp')
- grad_in: bfloat16 [4, 1024, 2048], P('rep', 'fsdp')
- grad_a_attn: float32 [4, 2048, 128], P(None, 'fsdp')
- grad_b_attn: float32 [4, 2048, 128], P(None, 'fsdp')
- grad_exp_a_in: float32 [16, 2, 2048, 128], P('fsdp')
- grad_exp_b_in: float32 [16, 2, 128, 1024], P('fsdp')
- grad_exp_a_down: float32 [16, 1024, 128], P('fsdp')
- grad_exp_b_down: float32 [16, 128, 2048], P('fsdp')
Inputs may be any that keep to these rules, and one draw needn't show every extreme that they name: `segments`: a sequence's document numbers never fall; each of the 8 documents is present and at most 768 tokens long, and one of them is exactly that long. `routes`: each token names 8 different experts; among the tokens of one device at most 96 name the same expert, and in every draw some expert is named by exactly 96 tokens of one device. `doc_sets`: the documents of a sequence take the 8 adapter sets in some order.
All inputs are finite; a program needn't handle non-finite values.
Results may differ from a plain program's by a relative error of at most 0.035.
Values may be sent and summed in bfloat16 or wider, within the bound.
No kernel may reach another device: no remote copies, remote signals or barrier semaphores. Data moves between devices by JAX's collectives and lax.ppermute only.
A program may use at most 384 MiB of HBM per device.

v0:
```python
import math

import jax
import jax.numpy as jnp
from jax import lax
from jax.sharding import PartitionSpec as P

HD = 128
TOP = 8
R = 16
SETS = 8
SR = 128


EPSILON = 1e-05
MASKED = -1e30


def rms_scale(values):
    return values * lax.rsqrt(jnp.mean(values * values, axis=-1, keepdims=True) + EPSILON)


def norm_back(values, gain_row, upstream_grad):
    result, pull_back = jax.vjp(lambda inner_rows: rms_scale(inner_rows) * gain_row, values)
    return pull_back(upstream_grad)[0]


def rope_tables(positions, head_size):
    half_size = head_size // 2
    inv_freq = jnp.exp(
        jnp.arange(half_size, dtype=jnp.float32) * (-2.0 * math.log(10000.0) / head_size)
    )
    angles = positions.astype(jnp.float32)[:, None] * inv_freq[None, :]
    return (jnp.cos(angles), jnp.sin(angles))


def rotate(values, cosine, sine_table):
    half_size = values.shape[-1] // 2
    front_half = values[..., :half_size]
    back_half = values[..., half_size:]
    cos_rows = cosine[:, None, :]
    sin_rows = sine_table[:, None, :]
    return jnp.concatenate(
        [
            front_half * cos_rows - back_half * sin_rows,
            back_half * cos_rows + front_half * sin_rows,
        ],
        axis=-1,
    )


def shards(
    hidden_in,
    segments,
    routes,
    doc_sets,
    cotangent,
    w_qkv,
    w_out,
    gain_attn,
    gain_moe,
    router,
    w_gate,
    w_up,
    w_down,
    a_attn,
    b_attn,
    exp_a_in,
    exp_b_in,
    exp_a_down,
    exp_b_down,
):
    shard_count = lax.axis_size("fsdp")
    shard_index = lax.axis_index("fsdp")
    tok_rows = hidden_in.shape[1]
    model_width = hidden_in.shape[2]
    head_count = model_width // HD
    local_experts = w_gate.shape[0]
    experts_all = local_experts * shard_count
    capacity = max(2, 3 * tok_rows * TOP // (2 * experts_all))
    score_scale = HD ** (-0.5)
    (
        attention_weight_full,
        output_weight_full,
        adapter_down_weight,
        adapter_up_weight,
        first_norm_gain_full,
        second_norm_gain_full,
        router_weight_full,
    ) = (
        lax.all_gather(w_qkv, "fsdp", axis=1, tiled=True),
        lax.all_gather(w_out, "fsdp", axis=0, tiled=True),
        lax.all_gather(a_attn, "fsdp", axis=1, tiled=True),
        lax.all_gather(b_attn, "fsdp", axis=1, tiled=True),
        lax.all_gather(gain_attn, "fsdp", axis=0, tiled=True),
        lax.all_gather(gain_moe, "fsdp", axis=0, tiled=True),
        lax.all_gather(router, "fsdp", axis=0, tiled=True),
    )
    gain_one = first_norm_gain_full.astype(jnp.float32)
    gain_two = second_norm_gain_full.astype(jnp.float32)
    seg_local = segments[0]
    set_token = jnp.sum(
        jnp.where(seg_local[:, None] == jnp.arange(SETS)[None, :], doc_sets[0][None, :], 0), axis=1
    )
    document_set_mask = (set_token[:, None] == (jnp.arange(SR) // R)[None, :]).astype(jnp.float32)
    mask_half = document_set_mask.astype(jnp.bfloat16)
    hidden_f = hidden_in[0].astype(jnp.float32)
    first_normed_rows = (rms_scale(hidden_f) * gain_one).astype(jnp.bfloat16)
    attention_rank_branch = (
        jnp.einsum(
            "xj,zje->zxe",
            first_normed_rows,
            adapter_down_weight[:3],
            preferred_element_type=jnp.float32,
        )
        * document_set_mask[None]
    ).astype(jnp.bfloat16)
    projected = jnp.einsum(
        "td,pde->pte", first_normed_rows, attention_weight_full, preferred_element_type=jnp.float32
    ) + jnp.einsum(
        "nzv,nwv->nzw",
        attention_rank_branch,
        adapter_up_weight[:3],
        preferred_element_type=jnp.float32,
    )
    positions = shard_index * tok_rows + jnp.arange(tok_rows)
    cosine, sine_table = rope_tables(positions, HD)
    queries = rotate(projected[0].reshape(tok_rows, head_count, HD), cosine, sine_table).astype(
        jnp.bfloat16
    )
    keys_own = (
        rotate(projected[1].reshape(tok_rows, head_count, HD), cosine, sine_table)
        .astype(jnp.bfloat16)
        .reshape(tok_rows, model_width)
    )
    values_own = projected[2].astype(jnp.bfloat16)
    seg_own = seg_local.astype(jnp.bfloat16)
    run_max = jnp.full((head_count, tok_rows), MASKED, jnp.float32)
    key_piece = lax.all_gather(keys_own, "fsdp", axis=0, tiled=True)
    value_piece = lax.all_gather(values_own, "fsdp", axis=0, tiled=True)
    seg_piece = lax.all_gather(seg_own, "fsdp", axis=0, tiled=True)
    piece_rows = key_piece.shape[0]
    scores = (
        jnp.einsum(
            "qhd,khd->hqk",
            queries,
            key_piece.reshape(piece_rows, head_count, HD),
            preferred_element_type=jnp.float32,
        )
        * score_scale
    )
    same_doc = seg_local[:, None] == seg_piece.astype(jnp.int32)[None, :]
    scores = jnp.where(same_doc[None], scores, MASKED)
    new_max = jnp.maximum(run_max, jnp.max(scores, axis=2))
    exp_scores = jnp.exp(scores - new_max[:, :, None])
    new_sum = jnp.sum(exp_scores, axis=2)
    new_acc = jnp.einsum(
        "hqk,khd->qhd",
        exp_scores.astype(jnp.bfloat16),
        value_piece.reshape(piece_rows, head_count, HD),
        preferred_element_type=jnp.float32,
    )
    folded = (new_max, new_sum, new_acc)
    run_max, run_sum, run_acc = folded
    log_sum = run_max + jnp.log(run_sum)
    attended = run_acc / jnp.transpose(run_sum)[:, :, None]
    attention_rounded_rows = attended.reshape(tok_rows, model_width).astype(jnp.bfloat16)
    output_rank_branch = (
        jnp.dot(attention_rounded_rows, adapter_down_weight[3], preferred_element_type=jnp.float32)
        * document_set_mask
    ).astype(jnp.bfloat16)
    resid_one = hidden_f + (
        jnp.dot(attention_rounded_rows, output_weight_full, preferred_element_type=jnp.float32)
        + jnp.einsum(
            "nd,gd->ng",
            output_rank_branch,
            adapter_up_weight[3],
            preferred_element_type=jnp.float32,
        )
    )
    normed_two = (rms_scale(resid_one) * gain_two).astype(jnp.bfloat16)
    logits = jnp.dot(normed_two, router_weight_full, preferred_element_type=jnp.float32)
    my_routes = routes[0]
    gate_weights = jax.nn.softmax(jnp.take_along_axis(logits, my_routes, axis=1), axis=-1)
    flat_routes = my_routes.reshape(-1)
    one_hot = (flat_routes[:, None] == jnp.arange(experts_all)[None, :]).astype(jnp.int32)
    slot_index = jnp.sum((jnp.cumsum(one_hot, axis=0) - 1) * one_hot, axis=1)
    token_index = jnp.arange(tok_rows * TOP) // TOP
    send_rows = (
        jnp.zeros((experts_all, capacity, model_width), jnp.bfloat16)
        .at[flat_routes, slot_index]
        .set(normed_two[token_index])
    )
    send_sets = (
        jnp.zeros((experts_all, capacity), jnp.bfloat16)
        .at[flat_routes, slot_index]
        .set(set_token[token_index].astype(jnp.bfloat16))
    )
    rows_got = lax.all_to_all(
        send_rows.reshape(shard_count, local_experts, capacity, model_width),
        "fsdp",
        split_axis=0,
        concat_axis=0,
        tiled=True,
    )
    sets_got = lax.all_to_all(
        send_sets.reshape(shard_count, local_experts, capacity),
        "fsdp",
        split_axis=0,
        concat_axis=0,
        tiled=True,
    )
    slot_mask = (sets_got.astype(jnp.int32)[..., None] == jnp.arange(SR) // R).astype(jnp.float32)
    low_in = (
        jnp.einsum("necd,eids->necis", rows_got, exp_a_in, preferred_element_type=jnp.float32)
        * slot_mask[:, :, :, None, :]
    ).astype(jnp.bfloat16)
    gate_h = jnp.einsum(
        "necd,edf->necf", rows_got, w_gate, preferred_element_type=jnp.float32
    ) + jnp.einsum(
        "necs,esf->necf", low_in[:, :, :, 0], exp_b_in[:, 0], preferred_element_type=jnp.float32
    )
    up_h = jnp.einsum(
        "necd,edf->necf", rows_got, w_up, preferred_element_type=jnp.float32
    ) + jnp.einsum(
        "necs,esf->necf", low_in[:, :, :, 1], exp_b_in[:, 1], preferred_element_type=jnp.float32
    )
    activation = (jax.nn.silu(gate_h) * up_h).astype(jnp.bfloat16)
    low_down = (
        jnp.einsum("necf,efs->necs", activation, exp_a_down, preferred_element_type=jnp.float32)
        * slot_mask
    ).astype(jnp.bfloat16)
    expert_out = (
        jnp.einsum("necf,efd->necd", activation, w_down, preferred_element_type=jnp.float32)
        + jnp.einsum("necs,esd->necd", low_down, exp_b_down, preferred_element_type=jnp.float32)
    ).astype(jnp.bfloat16)
    expert_out, rows_got, slot_mask, low_in, gate_h, up_h, activation, low_down = (
        expert_out,
        rows_got,
        slot_mask,
        low_in,
        gate_h,
        up_h,
        activation,
        low_down,
    )
    returned = lax.all_to_all(expert_out, "fsdp", split_axis=0, concat_axis=0, tiled=True)
    route_out = (
        returned.reshape(experts_all, capacity, model_width)[flat_routes, slot_index]
        .reshape(tok_rows, TOP, model_width)
        .astype(jnp.float32)
    )
    layer_value = resid_one + jnp.sum(gate_weights[:, :, None] * route_out, axis=1)
    (
        attention_weight_full,
        output_weight_full,
        adapter_down_weight,
        adapter_up_weight,
        first_norm_gain_full,
        second_norm_gain_full,
        router_weight_full,
    ) = (
        lax.all_gather(w_qkv, "fsdp", axis=1, tiled=True),
        lax.all_gather(w_out, "fsdp", axis=0, tiled=True),
        lax.all_gather(a_attn, "fsdp", axis=1, tiled=True),
        lax.all_gather(b_attn, "fsdp", axis=1, tiled=True),
        lax.all_gather(gain_attn, "fsdp", axis=0, tiled=True),
        lax.all_gather(gain_moe, "fsdp", axis=0, tiled=True),
        lax.all_gather(router, "fsdp", axis=0, tiled=True),
    )
    gain_one = first_norm_gain_full.astype(jnp.float32)
    gain_two = second_norm_gain_full.astype(jnp.float32)
    upstream = cotangent[0].astype(jnp.float32)
    d_route = (gate_weights[:, :, None] * upstream[:, None, :]).astype(jnp.bfloat16)
    d_gates = jnp.sum(upstream[:, None, :] * route_out, axis=2)
    d_chosen = gate_weights * (d_gates - jnp.sum(gate_weights * d_gates, axis=1, keepdims=True))
    d_logits = jnp.sum(
        jnp.where(
            my_routes[:, :, None] == jnp.arange(experts_all)[None, None, :],
            d_chosen[:, :, None],
            0.0,
        ),
        axis=1,
    ).astype(jnp.bfloat16)
    send_grads = (
        jnp.zeros((experts_all, capacity, model_width), jnp.bfloat16)
        .at[flat_routes, slot_index]
        .set(d_route.reshape(tok_rows * TOP, model_width))
    )
    grads_got = lax.all_to_all(
        send_grads.reshape(shard_count, local_experts, capacity, model_width),
        "fsdp",
        split_axis=0,
        concat_axis=0,
        tiled=True,
    )
    slot_half = slot_mask.astype(jnp.bfloat16)
    d_low_down = (
        jnp.einsum(
            "necd,esd->necs", grads_got, exp_b_down, preferred_element_type=jnp.float32
        ).astype(jnp.bfloat16)
        * slot_half
    )
    d_activation = jnp.einsum(
        "necd,efd->necf", grads_got, w_down, preferred_element_type=jnp.float32
    ) + jnp.einsum("necs,efs->necf", d_low_down, exp_a_down, preferred_element_type=jnp.float32)
    silu_value, silu_pull = jax.vjp(
        lambda gate_in, up_in: jax.nn.silu(gate_in) * up_in, gate_h, up_h
    )
    d_gate_h, d_up_h = silu_pull(d_activation)
    d_gate_h = d_gate_h.astype(jnp.bfloat16)
    d_up_h = d_up_h.astype(jnp.bfloat16)
    d_both = jnp.stack([d_gate_h, d_up_h], axis=3)
    d_low_in = (
        jnp.einsum(
            "necif,eisf->necis", d_both, exp_b_in, preferred_element_type=jnp.float32
        ).astype(jnp.bfloat16)
        * slot_half[:, :, :, None, :]
    )
    d_rows = (
        jnp.einsum("necf,edf->necd", d_gate_h, w_gate, preferred_element_type=jnp.float32)
        + jnp.einsum("necf,edf->necd", d_up_h, w_up, preferred_element_type=jnp.float32)
        + jnp.einsum("necis,eids->necd", d_low_in, exp_a_in, preferred_element_type=jnp.float32)
    )
    returned_grads = lax.all_to_all(
        d_rows.astype(jnp.bfloat16), "fsdp", split_axis=0, concat_axis=0, tiled=True
    )
    g_exp_b_down = jnp.einsum(
        "necs,necd->esd", low_down, grads_got, preferred_element_type=jnp.float32
    )
    g_exp_a_down = jnp.einsum(
        "necf,necs->efs", activation, d_low_down, preferred_element_type=jnp.float32
    )
    g_exp_b_in = jnp.einsum("necis,necif->eisf", low_in, d_both, preferred_element_type=jnp.float32)
    g_exp_a_in = jnp.einsum(
        "necd,necis->eids", rows_got, d_low_in, preferred_element_type=jnp.float32
    )
    d_normed_two = jnp.sum(
        returned_grads.reshape(experts_all, capacity, model_width)[flat_routes, slot_index]
        .reshape(tok_rows, TOP, model_width)
        .astype(jnp.float32),
        axis=1,
    ) + jnp.einsum("te,de->td", d_logits, router_weight_full, preferred_element_type=jnp.float32)
    d_resid_one = upstream + norm_back(resid_one, gain_two, d_normed_two)
    branch_gradient = d_resid_one.astype(jnp.bfloat16)
    output_adapter_gradient = (
        jnp.dot(branch_gradient, adapter_up_weight[3], preferred_element_type=jnp.float32).astype(
            jnp.bfloat16
        )
        * mask_half
    )
    d_att = (
        jnp.einsum(
            "te,de->td", branch_gradient, output_weight_full, preferred_element_type=jnp.float32
        )
        + jnp.einsum(
            "cr,ar->ca",
            output_adapter_gradient,
            adapter_down_weight[3],
            preferred_element_type=jnp.float32,
        )
    ).astype(jnp.bfloat16)
    output_up_gradient = jnp.einsum(
        "ts,te->es", output_rank_branch, branch_gradient, preferred_element_type=jnp.float32
    )
    output_down_gradient = jnp.einsum(
        "td,ts->ds",
        attention_rounded_rows,
        output_adapter_gradient,
        preferred_element_type=jnp.float32,
    )
    d_att_heads = d_att.reshape(tok_rows, head_count, HD)
    delta_rows = jnp.transpose(jnp.sum(d_att_heads.astype(jnp.float32) * attended, axis=2))
    key_piece = lax.all_gather(keys_own, "fsdp", axis=0, tiled=True)
    value_piece = lax.all_gather(values_own, "fsdp", axis=0, tiled=True)
    seg_piece = lax.all_gather(seg_own, "fsdp", axis=0, tiled=True)
    piece_rows = key_piece.shape[0]
    key_heads = key_piece.reshape(piece_rows, head_count, HD)
    value_heads = value_piece.reshape(piece_rows, head_count, HD)
    scores = (
        jnp.einsum("qhd,khd->hqk", queries, key_heads, preferred_element_type=jnp.float32)
        * score_scale
    )
    same_doc = seg_local[:, None] == seg_piece.astype(jnp.int32)[None, :]
    scores = jnp.where(same_doc[None], scores, MASKED)
    soft_probs = jnp.exp(scores - log_sum[:, :, None])
    d_probs = jnp.einsum(
        "qhd,khd->hqk", d_att_heads, value_heads, preferred_element_type=jnp.float32
    )
    d_scores = (soft_probs * (d_probs - delta_rows[:, :, None])).astype(jnp.bfloat16)
    soft_probs, d_scores = (soft_probs, d_scores)
    d_query_part = jnp.einsum(
        "hqk,khd->qhd", d_scores, key_heads, preferred_element_type=jnp.float32
    )
    d_key_part = jnp.einsum(
        "hqk,qhd->khd", d_scores, queries, preferred_element_type=jnp.float32
    ).reshape(piece_rows, model_width)
    d_value_part = jnp.einsum(
        "hqk,qhd->khd",
        soft_probs.astype(jnp.bfloat16),
        d_att_heads,
        preferred_element_type=jnp.float32,
    ).reshape(piece_rows, model_width)
    back_state = (d_query_part, d_key_part, d_value_part)
    d_query, d_keys_all, d_values_all = back_state
    d_keys_mine, d_values_mine = (
        lax.psum_scatter(
            d_keys_all.astype(jnp.bfloat16), "fsdp", scatter_dimension=0, tiled=True
        ).astype(jnp.float32),
        lax.psum_scatter(
            d_values_all.astype(jnp.bfloat16), "fsdp", scatter_dimension=0, tiled=True
        ).astype(jnp.float32),
    )
    d_query_pre = (
        rotate(d_query * score_scale, cosine, -sine_table)
        .reshape(tok_rows, model_width)
        .astype(jnp.bfloat16)
    )
    d_key_pre = (
        rotate((d_keys_mine * score_scale).reshape(tok_rows, head_count, HD), cosine, -sine_table)
        .reshape(tok_rows, model_width)
        .astype(jnp.bfloat16)
    )
    projected_gradient = jnp.stack([d_query_pre, d_key_pre, d_values_mine.astype(jnp.bfloat16)])
    projection_adapter_gradient = (
        jnp.einsum(
            "jah,jho->jao",
            projected_gradient,
            adapter_up_weight[:3],
            preferred_element_type=jnp.float32,
        ).astype(jnp.bfloat16)
        * mask_half[None]
    )
    d_normed_one = jnp.einsum(
        "pte,pde->td", projected_gradient, attention_weight_full, preferred_element_type=jnp.float32
    ) + jnp.einsum(
        "czn,cvn->zv",
        projection_adapter_gradient,
        adapter_down_weight[:3],
        preferred_element_type=jnp.float32,
    )
    attention_up_gradient = jnp.einsum(
        "pts,pte->pes",
        attention_rank_branch,
        projected_gradient,
        preferred_element_type=jnp.float32,
    )
    attention_down_gradient = jnp.einsum(
        "td,pts->pds",
        first_normed_rows,
        projection_adapter_gradient,
        preferred_element_type=jnp.float32,
    )
    d_hidden = d_resid_one + norm_back(hidden_f, gain_one, d_normed_one)
    adapter_down_gradient = jnp.concatenate(
        [attention_down_gradient, output_down_gradient[None]], axis=0
    )
    adapter_up_gradient = jnp.concatenate([attention_up_gradient, output_up_gradient[None]], axis=0)
    part_down, part_up = (
        lax.psum_scatter(
            adapter_down_gradient.astype(jnp.bfloat16), "fsdp", scatter_dimension=1, tiled=True
        ).astype(jnp.float32),
        lax.psum_scatter(
            adapter_up_gradient.astype(jnp.bfloat16), "fsdp", scatter_dimension=1, tiled=True
        ).astype(jnp.float32),
    )
    summed = (
        lax.psum(part_down.astype(jnp.bfloat16), "rep").astype(jnp.float32),
        lax.psum(part_up.astype(jnp.bfloat16), "rep").astype(jnp.float32),
        lax.psum(g_exp_a_in.astype(jnp.bfloat16), "rep").astype(jnp.float32),
        lax.psum(g_exp_b_in.astype(jnp.bfloat16), "rep").astype(jnp.float32),
        lax.psum(g_exp_a_down.astype(jnp.bfloat16), "rep").astype(jnp.float32),
        lax.psum(g_exp_b_down.astype(jnp.bfloat16), "rep").astype(jnp.float32),
    )
    return (
        layer_value.astype(jnp.bfloat16)[None],
        d_hidden.astype(jnp.bfloat16)[None],
        summed[0],
        summed[1],
        summed[2],
        summed[3],
        summed[4],
        summed[5],
    )


def solution(mesh):
    return jax.shard_map(
        shards,
        mesh=mesh,
        in_specs=(
            P("rep", "fsdp", None),
            P("rep", "fsdp"),
            P("rep", "fsdp", None),
            P("rep", None),
            P("rep", "fsdp", None),
            P(None, "fsdp", None),
            P("fsdp", None),
            P("fsdp"),
            P("fsdp"),
            P("fsdp", None),
            P("fsdp", None, None),
            P("fsdp", None, None),
            P("fsdp", None, None),
            P(None, "fsdp", None),
            P(None, "fsdp", None),
            P("fsdp", None, None, None),
            P("fsdp", None, None, None),
            P("fsdp", None, None),
            P("fsdp", None, None),
        ),
        out_specs=(
            P("rep", "fsdp", None),
            P("rep", "fsdp", None),
            P(None, "fsdp", None),
            P(None, "fsdp", None),
            P("fsdp", None, None, None),
            P("fsdp", None, None, None),
            P("fsdp", None, None),
            P("fsdp", None, None),
        ),
        check_vma=False,
    )
```

profile of v0, /device:TPU:0, one launch (start us, length us, event | category | flops | bytes accessed | tf_op | source)
XLA Modules:
  0.0 1259.2 jit_solution(7164601508888039294)
XLA Ops:
  10.1 10.3 all-gather.1
  23.3 17.3 %all-gather.13.cloned.1.call-done = bf16[4,2048,128]{2,1,0:T(8,128)(2,1)} async-done(((bf16[4,256,128]{2,1,0:T(8,128)(2,1)}), bf16[4,2048,128]{2,1,0:T(8,128)(2,1)}) %all-gather.13.cloned.1.call-update) | async-done | bytes 2097168 | tf_op jit(solution)/shard_map/all_gather | solution.py:93
  42.6 125.2 %all-gather.11.cloned.1.call-done = bf16[3,2048,2048]{2,1,0:T(8,128)(2,1)} async-done(((bf16[3,256,2048]{2,1,0:T(8,128)(2,1)}), bf16[3,2048,2048]{2,1,0:T(8,128)(2,1)}) %all-gather.11.cloned.1.call-update) | async-done | bytes 25165840 | tf_op jit(solution)/shard_map/all_gather | solution.py:91
  167.8 13.4 %fusion.209 = f32[128,3,2048]{2,0,1:T(8,128)} fusion(bf16[3,2048,2048]{2,1,0:T(8,128)(2,1)} %all-gather.11.cloned.1.call-done, bf16[1,128,2048]{2,1,0:T(8,128)(2,1)S(1)} %copy-done.5, f32[2048]{0:T(1024)S(1)} %bitcast.378, f32[128]{0:T(128)S(1)} %fusion.194), kind=kOutput, calls=%fused_computation.284 | convolution fusion | flops 3222274048 | bytes 28844544 | tf_op jit(solution)/shard_map/td,pde->pte/dot_general | solution.py:118
  181.2 16.5 %all-gather.15.cloned.1.call-done = bf16[4,2048,128]{2,1,0:T(8,128)(2,1)} async-done(((bf16[4,256,128]{2,1,0:T(8,128)(2,1)}), bf16[4,2048,128]{2,1,0:T(8,128)(2,1)}) %all-gather.15.cloned.1.call-update) | async-done | bytes 2097168 | tf_op jit(solution)/shard_map/all_gather | solution.py:94
  237.4 9.2 all-gather.2
  246.6 8.8 all-gather.3
  261.3 18.5 %all-gather.17.cloned.1.call-done = bf16[1024,2048]{0,1:T(8,128)(2,1)} async-done(((bf16[128,2048]{0,1:T(8,128)(2,1)}), bf16[1024,2048]{0,1:T(8,128)(2,1)}) %all-gather.17.cloned.1.call-update) | async-done | bytes 4194320 | tf_op jit(solution)/shard_map/all_gather | solution.py:139
  296.5 39.4 %all-gather.19.cloned.1.call-done = bf16[2048,2048]{1,0:T(8,128)(2,1)} async-done(((bf16[256,2048]{1,0:T(8,128)(2,1)}), bf16[2048,2048]{1,0:T(8,128)(2,1)}) %all-gather.19.cloned.1.call-update) | async-done | bytes 8388624 | tf_op jit(solution)/shard_map/all_gather | solution.py:92
  343.3 24.2 %scatter_custom_fusion = bf16[1536,2048]{1,0:T(8,128)(2,1)} fusion(s32[1024]{0:T(1024)S(1)} %get-tuple-element.112, bf16[128,2048]{1,0:T(8,128)(2,1)S(1)} %multiply_convert_fusion.1, s32[1024]{0:T(1024)S(1)} %get-tuple-element.111, bf16[]{:T(256)} %constant.97.clone.1), kind=kCustom, calls=%fused_computation.75 | custom fusion | bytes 6291458
  372.6 74.5 %all_gather.49 = bf16[2048,16]{0,1:T(8,128)(2,1)S(1)} all-gather(bf16[256,16]{0,1:T(8,128)(2,1)S(1)} %copy-done.59), channel_id=1, replica_groups=mesh['rep'=4,'fsdp'=8] {'fsdp'}, dimensions={0}, use_global_device_ids=true | all-gather | bytes 73728 | tf_op jit(solution)/shard_map/all_gather | solution.py:97
  457.8 10.6 scatter_custom_fusion.2
  486.5 58.5 %all-to-all-done.3 = bf16[8,2,96,2048]{3,2,1,0:T(8,128)(2,1)} async-done(((bf16[8,2,96,2048]{3,2,1,0:T(8,128)(2,1)}), bf16[8,2,96,2048]{3,2,1,0:T(8,128)(2,1)}, u32[]{:S(2)}, u32[]{:S(2)}) %all-to-all-start.3) | async-done | bytes 6291488 | tf_op jit(solution)/shard_map/all_to_all | solution.py:290
  554.0 13.0 %fusion.5 = f32[2,8,96,1024]{3,2,1,0:T(8,128)} fusion(bf16[2,2048,1024]{2,1,0:T(8,128)(2,1)} %param.30, bf16[8,2,96,2048]{3,2,1,0:T(8,128)(2,1)} %all-to-all-done), kind=kOutput, calls=%fused_computation.19 | convolution fusion | flops 6442450944 | bytes 20971520 | tf_op jit(solution)/shard_map/necd,edf->necf/dot_general | solution.py:223
  567.0 10.5 fusion.9
  577.5 22.9 %fusion.26 = (bf16[8,2,96,1024]{3,2,0,1:T(8,128)(2,1)}, bf16[8,2,96,1024]{3,2,0,1:T(8,128)(2,1)}, bf16[8,2,96,1024]{3,2,0,1:T(8,128)(2,1)}) fusion(f32[2,8,96,1024]{3,2,1,0:T(8,128)} %fusion.174, f32[2,8,96,1024]{3,2,1,0:T(8,128)} %fusion.9, f32[2,8,96,1024]{3,2,1,0:T(8,128)} %fusion.170, f32[2,8,96,1024]{3,2,1,0:T(8,128)} %fusion.5, ...), kind=kOutput, calls=%fused_computation.48 | convolution fusion | flops 6472335360 | bytes 55574528 | tf_op jit(solution)/shard_map/necd,efd->necf/dot_general | solution.py:304
  603.3 13.6 %fusion.13 = f32[2,8,96,2048]{3,2,1,0:T(8,128)} fusion(bf16[8,2,96,1024]{3,2,0,1:T(8,128)(2,1)} %get-tuple-element.66, bf16[2,1024,2048]{2,1,0:T(8,128)(2,1)} %param.31), kind=kOutput, calls=%fused_computation.27 | convolution fusion | flops 6442450944 | bytes 24117248 | tf_op jit(solution)/shard_map/necf,efd->necd/dot_general | solution.py:234
  636.4 13.7 %fusion.3 = f32[2,8,96,2048]{3,2,1,0:T(8,128)} fusion(bf16[8,2,96,1024]{3,2,0,1:T(8,128)(2,1)} %get-tuple-element.64, bf16[2,2048,1024]{2,1,0:T(8,128)(2,1)} %param.30), kind=kOutput, calls=%fused_computation.17 | convolution fusion | flops 6442450944 | bytes 24117248 | tf_op jit(solution)/shard_map/necf,edf->necd/dot_general | solution.py:322
  650.2 11.7 fusion.7
  661.9 12.2 fusion.23
  680.7 22.5 %all-to-all-done.2 = bf16[8,2,96,2048]{3,2,1,0:T(8,128)(2,1)} async-done(((bf16[8,2,96,2048]{3,2,1,0:T(8,128)(2,1)}), bf16[8,2,96,2048]{3,2,1,0:T(8,128)(2,1)}, u32[]{:S(2)}, u32[]{:S(2)}) %all-to-all-start.2) | async-done | bytes 6291488 | tf_op jit(solution)/shard_map/all_to_all | solution.py:247
  708.2 25.5 %gather_fusion.1 = bf16[1024,2048]{1,0:T(8,128)(2,1)} fusion(bf16[16,96,2048]{2,1,0:T(8,128)(2,1)} %bitcast.51, s32[1024]{0:T(1024)S(1)} %bitcast.352), kind=kCustom, calls=%fused_computation.2 | custom fusion | bytes 8396800 | tf_op jit(solution)/shard_map/gather | solution.py:249
  739.9 39.7 %all-to-all-done.4 = bf16[8,2,96,2048]{3,2,1,0:T(8,128)(2,1)} async-done(((bf16[8,2,96,2048]{3,2,1,0:T(8,128)(2,1)}), bf16[8,2,96,2048]{3,2,1,0:T(8,128)(2,1)}, u32[]{:S(2)}, u32[]{:S(2)}) %all-to-all-start.4) | async-done | bytes 6291488 | tf_op jit(solution)/shard_map/all_to_all | solution.py:325
  779.6 26.0 %gather_fusion.2 = bf16[1024,2048]{1,0:T(8,128)(2,1)} fusion(bf16[16,96,2048]{2,1,0:T(8,128)(2,1)} %bitcast.75, s32[1024]{0:T(1024)S(1)} %bitcast.353), kind=kCustom, calls=%fused_computation.3 | custom fusion | bytes 8396800 | tf_op jit(solution)/shard_map/gather | solution.py:339
  825.8 9.2 multiply_convert_fusion
  847.2 8.3 fusion.78
  869.1 28.6 %reduce-scatter.13.cloned.1.call-done = bf16[128,2048]{1,0:T(8,128)(2,1)} async-done(((bf16[1024,2048]{1,0:T(8,128)(2,1)}), bf16[128,2048]{1,0:T(8,128)(2,1)}) %reduce-scatter.13.cloned.1.call-update) | async-done | bytes 524304
  922.3 30.5 %reduce-scatter.7.cloned.1.call-done = bf16[128,2048]{1,0:T(8,128)(2,1)} async-done(((bf16[1024,2048]{1,0:T(8,128)(2,1)}), bf16[128,2048]{1,0:T(8,128)(2,1)}) %reduce-scatter.7.cloned.1.call-update) | async-done | bytes 524304 | tf_op jit(solution)/shard_map/reduce_scatter | solution.py:410
  982.5 16.3 %reduce-scatter.11.cloned.1.call-done = bf16[4,256,128]{2,1,0:T(8,128)(2,1)} async-done(((bf16[4,2048,128]{2,1,0:T(8,128)(2,1)}), bf16[4,256,128]{2,1,0:T(8,128)(2,1)}) %reduce-scatter.11.cloned.1.call-update) | async-done | bytes 262160 | tf_op jit(solution)/shard_map/reduce_scatter | solution.py:463
  998.8 45.3 %reduce-scatter.9.cloned.1.call-done = bf16[4,256,128]{1,2,0:T(8,128)(2,1)} async-done(((bf16[4,2048,128]{1,2,0:T(8,128)(2,1)}), bf16[4,256,128]{1,2,0:T(8,128)(2,1)}) %reduce-scatter.9.cloned.1.call-update) | async-done | bytes 262160 | tf_op jit(solution)/shard_map/reduce_scatter | solution.py:460
  1047.1 15.0 %fusion.157 = (f32[128]{0:T(128)S(1)}, f32[128,2048]{1,0:T(8,128)}) fusion(bf16[1,128,2048]{2,1,0:T(8,128)(2,1)} %param.19, f32[2048]{0:T(1024)S(1)} %bitcast.380, f32[128,2048]{1,0:T(8,128)} %convolution_bitcast_fusion.1, bf16[3,2048,2048]{2,1,0:T(8,128)(2,1)} %all-gather.11.cloned.1.call-done, bf16[1,128,2048]{2,1,0:T(8,128)(2,1)} %bitcast.376, ...), kind=kOutput, calls=%fused_computation.164 | convolution fusion | flops 3224109056 | bytes 29368832 | tf_op jit(solution)/shard_map/pte,pde->td/dot_general | solution.py:434
  1064.6 173.6 %all-reduce.3.cloned.1.call-done = (bf16[4,256,128]{1,2,0:T(8,128)(2,1)}, bf16[2,2,2048,128]{2,3,1,0:T(8,128)(2,1)}, bf16[4,256,128]{2,1,0:T(8,128)(2,1)}, bf16[...) async-done(((bf16[4,256,128]{1,2,0:T(8,128)(2,1)}, bf16[2,2,2048,128]{2,3,1,0:T(8,128)(2,1)}, ...) | async-done | bytes 5242896 | tf_op jit(solution)/shard_map/psum | solution.py:468
  (319 shorter events, 279.4 us)
Async XLA Ops:
  7.2 467.2 %copy-start = (bf16[2,2,2048,128]{3,2,1,0:T(8,128)(2,1)S(1)}, bf16[2,2,2048,128]{3,2,1,0:T(8,128)(2,1)}, u32[]{:S(2)}) copy-start(bf16[2,2,2048,128]{3,2,1,0:T(8,128)(2,1)} %param.34) | copy-start | bytes 6291460
  7.2 160.6 %copy-start.5 = (bf16[1,128,2048]{2,1,0:T(8,128)(2,1)S(1)}, bf16[1,128,2048]{2,1,0:T(8,128)(2,1)}, u32[]{:S(2)}) copy-start(bf16[1,128,2048]{2,1,0:T(8,128)(2,1)} %param.19) | copy-start | bytes 1572868
  7.2 33.4 %all-gather.13.cloned.1.call-start = ((), (), s32[]{:S(2)}) async-start(), calls=%async_computation.10 | async-start | bytes 2359296 | tf_op jit(solution)/shard_map/all_gather | solution.py:93
  7.9 159.9 %all-gather.11.cloned.1.call-start = ((), (), s32[]{:S(2)}) async-start(), calls=%async_computation.9 | async-start | bytes 28311552 | tf_op jit(solution)/shard_map/all_gather | solution.py:91
  8.7 189.0 %all-gather.15.cloned.1.call-start = ((), (), s32[]{:S(2)}) async-start(), calls=%async_computation.11 | async-start | bytes 2359296 | tf_op jit(solution)/shard_map/all_gather | solution.py:94
  9.4 246.2 %all-gather.21.cloned.1.call-start = ((), (), s32[]{:S(2)}) async-start(), calls=%async_computation.17 | async-start | bytes 4718592 | tf_op jit(solution)/shard_map/all_gather | solution.py:140
  20.5 160.7 %copy-start.42 = (f32[8,1,256]{2,1,0:T(1,128)}, f32[8,1,256]{2,1,0:T(1,128)S(1)}, u32[]{:S(2)}) copy-start(f32[8,1,256]{2,1,0:T(1,128)S(1)} %convert_element_type.369) | copy-start | bytes 24580
  21.3 273.6 %copy-start.1 = (s32[128]{0:T(128)}, s32[128]{0:T(128)S(1)}, u32[]{:S(2)}) copy-start(s32[128]{0:T(128)S(1)} %select_reduce_fusion.1) | copy-start | bytes 1540
  22.6 158.6 %copy-start.57 = (f32[128]{0:T(128)}, f32[128]{0:T(128)S(1)}, u32[]{:S(2)}) copy-start(f32[128]{0:T(128)S(1)} %fusion.194) | copy-start | bytes 1540
  42.6 155.0 %copy-start.47 = (bf16[3,128,128]{2,1,0:T(8,128)(2,1)}, bf16[3,128,128]{2,1,0:T(8,128)(2,1)S(1)}, u32[]{:S(2)}) copy-start(bf16[3,128,128]{2,1,0:T(8,128)(2,1)S(1)} %fusion.146) | copy-start | bytes 294916
  203.2 76.6 %all-gather.17.cloned.1.call-start = ((), (), s32[]{:S(2)}) async-start(), calls=%async_computation.12 | async-start | bytes 4718592 | tf_op jit(solution)/shard_map/all_gather | solution.py:139
  209.2 70.6 %copy-start.14 = (bf16[128,16,64]{2,0,1:T(8,128)(2,1)}, bf16[128,16,64]{2,0,1:T(8,128)(2,1)S(1)}, u32[]{:S(2)}) copy-start(bf16[128,16,64]{2,0,1:T(8,128)(2,1)S(1)} %get-tuple-element.71) | copy-start | bytes 786436
  212.4 123.6 %all-gather.19.cloned.1.call-start = ((), (), s32[]{:S(2)}) async-start(), calls=%async_computation.13 | async-start | bytes 9437184 | tf_op jit(solution)/shard_map/all_gather | solution.py:92
  234.0 133.5 %all-to-all-start.1 = ((bf16[8,2,96]{2,1,0:T(2,128)(2,1)}), bf16[8,2,96]{2,1,0:T(2,128)(2,1)S(1)}, u32[]{:S(2)}, u32[]{:S(2)}) async-start(bf16[8,2,96]{2,1,0:T(2,128)(2,1)} %reshape.598), calls=%async_computation.1 | async-start | bytes 8192 | tf_op jit(solution)/shard_map/all_to_all | solution.py:206
  255.4 86.8 %copy-start.49 = (f32[8,1,256]{2,1,0:T(1,128)}, f32[8,1,256]{2,1,0:T(1,128)S(1)}, u32[]{:S(2)}) copy-start(f32[8,1,256]{2,1,0:T(1,128)S(1)} %convert_element_type.371) | copy-start | bytes 24580
  294.9 45.7 %copy-start.19 = (bf16[128,16,128]{0,2,1:T(8,128)(2,1)}, bf16[128,16,128]{0,2,1:T(8,128)(2,1)S(1)}, u32[]{:S(2)}) copy-start(bf16[128,16,128]{0,2,1:T(8,128)(2,1)S(1)} %get-tuple-element.101) | copy-start | bytes 1572868
  296.5 44.1 %copy-start.45 = (bf16[128,128]{1,0:T(8,128)(2,1)}, bf16[128,128]{1,0:T(8,128)(2,1)S(1)}, u32[]{:S(2)}) copy-start(bf16[128,128]{1,0:T(8,128)(2,1)S(1)} %fusion.149) | copy-start | bytes 98308
  367.6 100.8 %all-to-all-start = ((bf16[8,2,96,2048]{3,2,1,0:T(8,128)(2,1)}), bf16[8,2,96,2048]{3,2,1,0:T(8,128)(2,1)}, u32[]{:S(2)}, u32[]{:S(2)}) async-start(bf16[8,2,96,2048]{3,2,1,0:T(8,128)(2,1)} %bitcast.354), calls=%async_computation | async-start | bytes 12582912 | tf_op jit(solution)/shard_map/all_to_all | solution.py:199
  468.4 76.6 %all-to-all-start.3 = ((bf16[8,2,96,2048]{3,2,1,0:T(8,128)(2,1)}), bf16[8,2,96,2048]{3,2,1,0:T(8,128)(2,1)}, u32[]{:S(2)}, u32[]{:S(2)}) async-start(bf16[8,2,96,2048]{3,2,1,0:T(8,128)(2,1)} %bitcast.355), calls=%async_computation.3 | async-start | bytes 12582912 | tf_op jit(solution)/shard_map/all_to_all | solution.py:290
  479.1 65.9 %copy-start.26 = (bf16[2,128,2048]{2,1,0:T(8,128)(2,1)S(1)}, bf16[2,128,2048]{2,1,0:T(8,128)(2,1)}, u32[]{:S(2)}) copy-start(bf16[2,128,2048]{2,1,0:T(8,128)(2,1)} %param.37) | copy-start | bytes 3145732
  626.5 76.7 %all-to-all-start.2 = ((bf16[8,2,96,2048]{3,2,1,0:T(8,128)(2,1)}), bf16[8,2,96,2048]{3,2,1,0:T(8,128)(2,1)}, u32[]{:S(2)}, u32[]{:S(2)}) async-start(bf16[8,2,96,2048]{3,2,1,0:T(8,128)(2,1)} %copy.262), calls=%async_computation.2 | async-start | bytes 12582912 | tf_op jit(solution)/shard_map/all_to_all | solution.py:247
  703.2 76.4 %all-to-all-start.4 = ((bf16[8,2,96,2048]{3,2,1,0:T(8,128)(2,1)}), bf16[8,2,96,2048]{3,2,1,0:T(8,128)(2,1)}, u32[]{:S(2)}, u32[]{:S(2)}) async-start(bf16[8,2,96,2048]{3,2,1,0:T(8,128)(2,1)} %copy.267), calls=%async_computation.4 | async-start | bytes 12582912 | tf_op jit(solution)/shard_map/all_to_all | solution.py:325
  708.0 189.8 %reduce-scatter.13.cloned.1.call-start = ((), (), s32[]{:S(2)}) async-start(), calls=%async_computation.18 | async-start | bytes 4718592
  779.6 31.3 %copy-start.50 = (f32[8,1,256]{2,1,0:T(1,128)S(1)}, f32[8,1,256]{2,1,0:T(1,128)}, u32[]{:S(2)}) copy-start(f32[8,1,256]{2,1,0:T(1,128)} %copy-done.49) | copy-start | bytes 24580
  847.1 105.7 %reduce-scatter.7.cloned.1.call-start = ((), (), s32[]{:S(2)}) async-start(), calls=%async_computation.14 | async-start | bytes 4718592 | tf_op jit(solution)/shard_map/reduce_scatter | solution.py:410
  862.2 136.6 %reduce-scatter.11.cloned.1.call-start = ((), (), s32[]{:S(2)}) async-start(), calls=%async_computation.16 | async-start | bytes 2359296 | tf_op jit(solution)/shard_map/reduce_scatter | solution.py:463
  869.1 37.6 %copy-start.35 = (f32[128,64]{1,0:T(8,128)S(1)}, f32[128,64]{1,0:T(8,128)}, u32[]{:S(2)}) copy-start(f32[128,64]{1,0:T(8,128)} %copy-done.34) | copy-start | bytes 98308
  869.1 37.6 %copy-start.44 = (f32[128,64]{1,0:T(8,128)S(1)}, f32[128,64]{1,0:T(8,128)}, u32[]{:S(2)}) copy-start(f32[128,64]{1,0:T(8,128)} %get-tuple-element.94) | copy-start | bytes 98308
  906.7 46.1 %copy-start.48 = (bf16[3,128,128]{2,1,0:T(8,128)(2,1)S(1)}, bf16[3,128,128]{2,1,0:T(8,128)(2,1)}, u32[]{:S(2)}) copy-start(bf16[3,128,128]{2,1,0:T(8,128)(2,1)} %copy-done.47) | copy-start | bytes 294916
  957.4 86.7 %reduce-scatter.9.cloned.1.call-start = ((), (), s32[]{:S(2)}) async-start(), calls=%async_computation.15 | async-start | bytes 2359296 | tf_op jit(solution)/shard_map/reduce_scatter | solution.py:460
  964.3 273.9 %all-reduce.3.cloned.1.call-start = ((), (), s32[]{:S(2)}) async-start(), calls=%async_computation.19 | async-start | bytes 10485760 | tf_op jit(solution)/shard_map/psum | solution.py:468
  976.2 67.9 %copy-start.40 = (bf16[3,128,128]{2,1,0:T(8,128)(2,1)S(1)}, bf16[3,128,128]{2,1,0:T(8,128)(2,1)}, u32[]{:S(2)}) copy-start(bf16[3,128,128]{2,1,0:T(8,128)(2,1)} %copy-done.39) | copy-start | bytes 294916
  (60 other events, 747.7 us)
Sparse Core Ops, SparseCore 0:
  9.9 30.5 all-gather.12
  42.5 125.3 all-gather.10
  169.7 27.8 all-gather.14
  203.3 36.7 all-gather.20
  242.3 37.4 all-gather.16
  281.6 54.3 all-gather.18
  847.2 50.4 reduce-scatter.12
  901.5 51.2 reduce-scatter.6
  957.5 41.2 reduce-scatter.10
  1002.8 41.2 reduce-scatter.8
  1047.5 190.6 all-reduce.2
where the time goes:
time: 1270 us; the launch traced here: 1260 us
  waiting for transfers between devices  634 us (50%)
  matrix products  250 us (20%)
  local copies, waits for them, and re-layouts  168 us (13%)
  blocking collectives  103 us (8%)
  other arithmetic  65.3 us (5%)
  starting transfers between devices  23.8 us (2%)
  between operations  15.3 us (1%)
    psum x1, waiting for transfers between devices, shards(): lax.psum(part_down.astype(jnp.bfloat16), 'rep').astype(jnp.float32)  174 us
    all_gather x1, waiting for transfers between devices, shards(): lax.all_gather(w_qkv, 'fsdp', axis=1, tiled=True)  125 us
    all_gather x1, blocking collectives, shards(): lax.all_gather(router, 'fsdp', axis=0, tiled=True)  74.5 us
    unnamed x167, local copies, waits for them, and re-layouts  69 us
    all_to_all x1, waiting for transfers between devices, shards(): lax.all_to_all(send_grads.reshape(shard_count, local_experts, capacity, m...  58.5 us
    reduce_scatter x1, waiting for transfers between devices, shards(): lax.psum_scatter(adapter_down_gradient.astype(jnp.bfloat16), 'fsdp', scat...  45.3 us
    all_to_all x1, waiting for transfers between devices, shards(): lax.all_to_all(d_rows.astype(jnp.bfloat16), 'fsdp', split_axis=0, concat_...  39.7 us
    all_gather x1, waiting for transfers between devices, shards(): lax.all_gather(w_out, 'fsdp', axis=0, tiled=True)  39.4 us
  transfers between devices with their start and end apart: 16, of which 13 were waited for; matrix products, arithmetic and copies ran while one was open for 24% of the time, Pallas kernels for 0%

commit v1 on v0

--- a/solution.py
+++ b/solution.py
@@ -49,7 +49,7 @@
     )
 
 
-def shards(
+def gathered_layer(
     hidden_in,
     segments,
     routes,
@@ -484,7 +484,331 @@
     )
 
 
+EVERY = 8
+
+
+def swap(values, bits):
+    return lax.ppermute(values, "fsdp", [(i, i ^ bits) for i in range(EVERY)])
+
+
+def gather_relative(values):
+    half = values.shape[0] // 2
+    side, over = swap(values, 2), swap(values, 4)
+    far = jnp.concatenate([swap(side[:half], 4), swap(over[half:], 2)], axis=0)
+    mine = [values, side, over, far]
+    other = [swap(block, 1) for block in mine]
+    return [mine[0], other[0], mine[1], other[1], mine[2], other[2], mine[3], other[3]]
+
+
+def add_half(left, right):
+    return (left.astype(jnp.float32) + right.astype(jnp.float32)).astype(jnp.bfloat16)
+
+
+def scatter_relative(blocks):
+    got = [swap(blocks[j], 1) for j in (7, 3, 5, 1)]
+    far = add_half(blocks[6], got[0])
+    half = far.shape[0] // 2
+    far_side, far_over = swap(far[:half], 2), swap(far[half:], 4)
+    side = blocks[2].astype(jnp.float32) + got[1].astype(jnp.float32)
+    over = blocks[4].astype(jnp.float32) + got[2].astype(jnp.float32)
+    side = jnp.concatenate([side[:half], side[half:] + far_over.astype(jnp.float32)], axis=0)
+    over = jnp.concatenate([over[:half] + far_side.astype(jnp.float32), over[half:]], axis=0)
+    side, over = swap(side.astype(jnp.bfloat16), 2), swap(over.astype(jnp.bfloat16), 4)
+    return (
+        blocks[0].astype(jnp.float32)
+        + got[3].astype(jnp.float32)
+        + side.astype(jnp.float32)
+        + over.astype(jnp.float32)
+    )
+
+
+def exchange_relative(blocks):
+    return [blocks[0]] + [swap(blocks[j], j) for j in range(1, EVERY)]
+
+
+def rep_swap(values, bits):
+    return lax.ppermute(values, "rep", [(i, i ^ bits) for i in range(4)])
+
+
+def pick(pair, index):
+    return lax.dynamic_index_in_dim(pair, index, 0, keepdims=False)
+
+
+def joined(own, other, index):
+    return jnp.where(index == 0, jnp.stack([own, other]), jnp.stack([other, own]))
+
+
+def sum_rep(values):
+    where = lax.axis_index("rep")
+    low_bit, high_bit = where % 2, where // 2
+    rows, columns = values.shape
+    halves = values.reshape(2, rows // 2, columns)
+    half = add_half(pick(halves, low_bit), rep_swap(pick(halves, 1 - low_bit), 1))
+    parts = half.reshape(2, rows // 4, columns)
+    part = add_half(pick(parts, high_bit), rep_swap(pick(parts, 1 - high_bit), 2))
+    half = joined(part, rep_swap(part, 2), high_bit).reshape(rows // 2, columns)
+    return joined(half, rep_swap(half, 1), low_bit).reshape(rows, columns)
+
+
+def dot32(left, right):
+    return jnp.dot(left, right, preferred_element_type=jnp.float32)
+
+
+def dot_nt(left, right):
+    return lax.dot_general(left, right, (((1,), (1,)), ((), ())), preferred_element_type=jnp.float32)
+
+
+def dot_tn(left, right):
+    return lax.dot_general(left, right, (((0,), (0,)), ((), ())), preferred_element_type=jnp.float32)
+
+
+def in_order(blocks, me):
+    rows = blocks[0].shape[0]
+    whole = jnp.zeros((rows * EVERY, blocks[0].shape[1]), blocks[0].dtype)
+    for j, block in enumerate(blocks):
+        whole = lax.dynamic_update_slice(whole, block, ((me ^ j) * rows, 0))
+    return whole
+
+
+def block_of(values, index, rows):
+    return lax.dynamic_slice_in_dim(values, index * rows, rows, axis=0)
+
+
+def after(value, gate):
+    return lax.optimization_barrier((value, gate))[0]
+
+
+def set_masks(seg, doc_sets):
+    set_token = jnp.sum(
+        jnp.where(seg[:, None] == jnp.arange(SETS)[None, :], doc_sets[0][None, :], 0), axis=1
+    )
+    return (set_token[:, None] == (jnp.arange(SR) // R)[None, :]).astype(jnp.float32)
+
+
+def split_layer(
+    hidden_in,
+    segments,
+    routes,
+    doc_sets,
+    cotangent,
+    w_qkv,
+    w_out,
+    gain_attn,
+    gain_moe,
+    router,
+    w_gate,
+    w_up,
+    w_down,
+    a_attn,
+    b_attn,
+    exp_a_in,
+    exp_b_in,
+    exp_a_down,
+    exp_b_down,
+):
+    bf16, f32 = jnp.bfloat16, jnp.float32
+    me = lax.axis_index("fsdp")
+    rows = hidden_in.shape[1]
+    width = hidden_in.shape[2]
+    wide = width // EVERY
+    heads = wide // HD
+    experts_all = w_gate.shape[0] * EVERY
+    score_scale = HD ** (-0.5)
+    tokens = rows * EVERY
+    meta = jnp.concatenate([routes[0], segments[0][:, None]], axis=1).astype(bf16)
+    meta = jnp.pad(meta, ((0, 0), (0, 128 - meta.shape[1])))
+    hidden_blocks = gather_relative(jnp.concatenate([hidden_in[0], meta], axis=1))
+    w_own = lax.all_to_all(
+        w_qkv.reshape(3, wide, EVERY, wide).transpose(2, 0, 1, 3),
+        "fsdp",
+        split_axis=0,
+        concat_axis=0,
+        tiled=True,
+    )
+    w_own = w_own.transpose(1, 0, 2, 3).reshape(3, width, wide)
+    small = jnp.concatenate(
+        [a_attn[0], a_attn[1], a_attn[2], a_attn[3], b_attn[3], router, gain_attn[:, None], gain_moe[:, None]],
+        axis=1,
+    )
+    small = jnp.pad(small, ((0, 0), (0, 768 - small.shape[1])))
+    small_blocks = gather_relative(small)
+    small_all = in_order(small_blocks, me)
+    a_qkv, b_out = small_all[:, : 3 * SR], small_all[:, 4 * SR : 5 * SR]
+    router_all = small_all[:, 5 * SR : 5 * SR + experts_all]
+    gain_one = small_all[:, 5 * SR + experts_all].astype(f32)
+    gain_two = small_all[:, 5 * SR + experts_all + 1].astype(f32)
+    a_out = jnp.concatenate([block[:, 3 * SR : 4 * SR] for block in small_blocks], axis=0)
+    hidden_ext = jnp.concatenate(hidden_blocks, axis=0)
+    hidden_f = hidden_ext[:, :width].astype(f32)
+    routes_all = hidden_ext[:, width : width + TOP].astype(jnp.int32)
+    seg_all = hidden_ext[:, width + TOP].astype(jnp.int32)
+    mask = set_masks(seg_all, doc_sets)
+    mask_own = set_masks(segments[0], doc_sets)
+    mask_half, mask_own_half = mask.astype(bf16), mask_own.astype(bf16)
+    normed_one = (rms_scale(hidden_f) * gain_one).astype(bf16)
+    w_out_rel = jnp.concatenate(gather_relative(after(w_out, normed_one)), axis=0)
+    low_qkv = (
+        dot32(normed_one, a_qkv).reshape(tokens, 3, SR) * mask[:, None, :]
+    ).astype(bf16)
+    proj = [dot32(normed_one, w_own[i]) + dot_nt(low_qkv[:, i], b_attn[i]) for i in range(3)]
+    order = me ^ jnp.arange(EVERY)
+    positions = (order[:, None] * rows + jnp.arange(rows)[None, :]).reshape(-1)
+    cosine, sine_table = rope_tables(positions, HD)
+    queries = rotate(proj[0].reshape(tokens, heads, HD), cosine, sine_table).astype(bf16)
+    keys = rotate(proj[1].reshape(tokens, heads, HD), cosine, sine_table).astype(bf16)
+    values = proj[2].reshape(tokens, heads, HD).astype(bf16)
+    same_doc = (seg_all[:, None] == seg_all[None, :])[None]
+    scores = jnp.einsum("qhd,khd->hqk", queries, keys, preferred_element_type=f32) * score_scale
+    scores = jnp.where(same_doc, scores, MASKED)
+    top_score = jnp.max(scores, axis=2)
+    exp_scores = jnp.exp(scores - top_score[:, :, None])
+    score_sum = jnp.sum(exp_scores, axis=2)
+    log_sum = top_score + jnp.log(score_sum)
+    attended = jnp.einsum(
+        "hqk,khd->qhd", exp_scores.astype(bf16), values, preferred_element_type=f32
+    ) / jnp.transpose(score_sum)[:, :, None]
+    att_half = attended.reshape(tokens, wide).astype(bf16)
+    att_own = jnp.concatenate(
+        exchange_relative([att_half[j * rows : (j + 1) * rows] for j in range(EVERY)]), axis=1
+    )
+    low_out = (dot32(att_own, a_out) * mask_own).astype(bf16)
+    resid_one = hidden_in[0].astype(f32) + (dot32(att_own, w_out_rel) + dot_nt(low_out, b_out))
+    normed_own = (rms_scale(resid_one) * gain_two).astype(bf16)
+    normed_two = jnp.concatenate(gather_relative(normed_own), axis=0)
+    cot_all = jnp.concatenate(gather_relative(after(cotangent[0], normed_two)), axis=0)
+    logits = dot32(normed_two, router_all)
+    ids = jnp.arange(experts_all)
+    named = jnp.any(routes_all[:, :, None] == ids[None, None, :], axis=1)
+    gates = jax.nn.softmax(jnp.where(named, logits, -jnp.inf), axis=-1)
+    own_gates = lax.dynamic_slice_in_dim(gates, me * 2, 2, axis=1)
+    out_sum, row_sum, gate_cols, grads = 0.0, 0.0, 0.0, []
+    cot_f = cot_all.astype(f32)
+    for k in range(2):
+        gate = own_gates[:, k : k + 1]
+        a_in = jnp.concatenate([exp_a_in[k, 0], exp_a_in[k, 1]], axis=1)
+        low_in = (dot32(normed_two, a_in).reshape(tokens, 2, SR) * mask[:, None, :]).astype(bf16)
+        gate_h = dot32(normed_two, w_gate[k]) + dot32(low_in[:, 0], exp_b_in[k, 0])
+        up_h = dot32(normed_two, w_up[k]) + dot32(low_in[:, 1], exp_b_in[k, 1])
+        activation = (jax.nn.silu(gate_h) * up_h).astype(bf16)
+        low_down = (dot32(activation, exp_a_down[k]) * mask).astype(bf16)
+        expert_out = (
+            (dot32(activation, w_down[k]) + dot32(low_down, exp_b_down[k])).astype(bf16).astype(f32)
+        )
+        out_sum = out_sum + gate * expert_out
+        d_gate = jnp.sum(cot_f * expert_out, axis=1, keepdims=True)
+        high = d_gate.astype(bf16)
+        gate_cols = (
+            gate_cols
+            + jnp.where(jnp.arange(128)[None, :] == 2 * me + k, high.astype(f32), 0.0)
+            + jnp.where(jnp.arange(128)[None, :] == 2 * me + k + experts_all, d_gate - high.astype(f32), 0.0)
+        )
+        d_out = (gate * cot_f).astype(bf16)
+        d_low_down = dot_nt(d_out, exp_b_down[k]).astype(bf16) * mask_half
+        d_act = dot_nt(d_out, w_down[k]) + dot_nt(d_low_down, exp_a_down[k])
+        _, pull = jax.vjp(lambda a, b: jax.nn.silu(a) * b, gate_h, up_h)
+        d_gate_h, d_up_h = pull(d_act)
+        d_gate_h, d_up_h = d_gate_h.astype(bf16), d_up_h.astype(bf16)
+        d_low_in = [
+            dot_nt(d_gate_h, exp_b_in[k, 0]).astype(bf16) * mask_half,
+            dot_nt(d_up_h, exp_b_in[k, 1]).astype(bf16) * mask_half,
+        ]
+        d_low_both = jnp.concatenate(d_low_in, axis=1)
+        d_row = dot_nt(d_gate_h, w_gate[k]) + dot_nt(d_up_h, w_up[k]) + dot_nt(d_low_both, a_in)
+        row_sum = row_sum + d_row.astype(bf16).astype(f32)
+        g_a_in = dot_tn(d_low_both, normed_two).reshape(2, SR, width)
+        g_b_in = jnp.stack([dot_tn(low_in[:, 0], d_gate_h), dot_tn(low_in[:, 1], d_up_h)])
+        g_a_down = dot_tn(d_low_down, activation)
+        g_b_down = dot_tn(low_down, d_out)
+        packed = jnp.concatenate(
+            [
+                g_a_in.reshape(2 * SR, width),
+                g_b_down,
+                g_b_in.reshape(SR, width),
+                g_a_down.reshape(SR // 2, width),
+            ],
+            axis=0,
+        ).astype(bf16)
+        grads.append(sum_rep(packed).astype(f32))
+    out_ext = jnp.concatenate([out_sum, gate_cols], axis=1).astype(bf16)
+    blocks = [out_ext[j * rows : (j + 1) * rows] for j in range(EVERY)]
+    out_got = scatter_relative(blocks)
+    layer_out = resid_one + out_got[:, :width]
+    d_gates = out_got[:, width : width + experts_all] + out_got[:, width + experts_all : width + 2 * experts_all]
+    gates_own_tok = gates[:rows]
+    d_chosen = gates_own_tok * (d_gates - jnp.sum(gates_own_tok * d_gates, axis=1, keepdims=True))
+    d_logits = d_chosen.astype(bf16)
+    row_half = row_sum.astype(bf16)
+    d_normed_two = scatter_relative(
+        [row_half[j * rows : (j + 1) * rows] for j in range(EVERY)]
+    ) + dot_nt(d_logits, router_all)
+    upstream = cotangent[0].astype(f32)
+    d_resid = upstream + norm_back(resid_one, gain_two, d_normed_two)
+    d_branch = d_resid.astype(bf16)
+    d_low_out = dot32(d_branch, b_out).astype(bf16) * mask_own_half
+    d_att_own = (dot_nt(d_branch, w_out_rel) + dot_nt(d_low_out, a_out)).astype(bf16)
+    d_att = jnp.concatenate(
+        exchange_relative([d_att_own[:, j * wide : (j + 1) * wide] for j in range(EVERY)]), axis=0
+    ).reshape(tokens, heads, HD)
+    g_b_out = dot_tn(d_branch, low_out)
+    g_a_out = dot_tn(att_own, d_low_out)
+    delta = jnp.transpose(jnp.sum(d_att.astype(f32) * attended, axis=2))
+    scores = jnp.einsum("qhd,khd->hqk", queries, keys, preferred_element_type=f32) * score_scale
+    scores = jnp.where(same_doc, scores, MASKED)
+    probs = jnp.exp(scores - log_sum[:, :, None])
+    d_probs = jnp.einsum("qhd,khd->hqk", d_att, values, preferred_element_type=f32)
+    d_scores = (probs * (d_probs - delta[:, :, None])).astype(bf16)
+    d_queries = jnp.einsum("hqk,khd->qhd", d_scores, keys, preferred_element_type=f32)
+    d_keys = jnp.einsum("hqk,qhd->khd", d_scores, queries, preferred_element_type=f32)
+    d_values = jnp.einsum("hqk,qhd->khd", probs.astype(bf16), d_att, preferred_element_type=f32)
+    d_proj = [
+        rotate(d_queries * score_scale, cosine, -sine_table).reshape(tokens, wide).astype(bf16),
+        rotate(d_keys * score_scale, cosine, -sine_table).reshape(tokens, wide).astype(bf16),
+        d_values.reshape(tokens, wide).astype(bf16),
+    ]
+    d_low = jnp.concatenate(
+        [dot32(d_proj[i], b_attn[i]).astype(bf16) * mask_half for i in range(3)], axis=1
+    )
+    d_normed = dot_nt(d_low, a_qkv)
+    for i in range(3):
+        d_normed = d_normed + dot_nt(d_proj[i], w_own[i])
+    d_normed = d_normed.astype(bf16)
+    d_normed_own = scatter_relative([d_normed[j * rows : (j + 1) * rows] for j in range(EVERY)])
+    grad_in = d_resid + norm_back(hidden_in[0].astype(f32), gain_one, d_normed_own)
+    g_a_qkv = dot_tn(normed_one, d_low)
+    g_b_qkv = [dot_tn(d_proj[i], low_qkv[:, i]) for i in range(3)]
+    sums = []
+    for j in range(EVERY):
+        sums.append(
+            jnp.concatenate(
+                [
+                    block_of(g_a_qkv, me ^ j, wide),
+                    g_a_out[j * wide : (j + 1) * wide],
+                    block_of(g_b_out, me ^ j, wide),
+                ],
+                axis=1,
+            ).astype(bf16)
+        )
+    g_sum = jnp.concatenate([scatter_relative(sums)] + g_b_qkv, axis=1)
+    g_sum = sum_rep(g_sum.astype(bf16)).astype(f32)
+    cut = [g_sum[:, i * SR : (i + 1) * SR] for i in range(8)]
+    grad_a = jnp.stack([cut[0], cut[1], cut[2], cut[3]])
+    grad_b = jnp.stack([cut[5], cut[6], cut[7], cut[4]])
+    at = [2 * SR, 3 * SR, 4 * SR]
+    return (
+        layer_out.astype(bf16)[None],
+        grad_in.astype(bf16)[None],
+        grad_a,
+        grad_b,
+        jnp.stack([g[: at[0]].reshape(2, SR, width).transpose(0, 2, 1) for g in grads]),
+        jnp.stack([g[at[1] : at[2]].reshape(2, SR, w_gate.shape[2]) for g in grads]),
+        jnp.stack([g[at[2] :].reshape(SR, w_gate.shape[2]).T for g in grads]),
+        jnp.stack([g[at[0] : at[1]] for g in grads]),
+    )
+
+
 def solution(mesh):
+    shape = dict(mesh.shape)
+    shards = split_layer if shape == {"rep": 4, "fsdp": EVERY} else gathered_layer
     return jax.shard_map(
         shards,
         mesh=mesh,

time: 1270 us -> 852 us (0.67)
  waiting for transfers between devices: 634 us -> 214 us
  blocking collectives: 103 us -> 0 us
  starting transfers between devices: 23.8 us -> 83.9 us
  other arithmetic: 65.3 us -> 89.1 us
  local copies, waits for them, and re-layouts: 168 us -> 189 us
    all_gather x6 -> x0, waiting for transfers between devices: 217 us -> none  [the longest x1 125 us: shards(): lax.all_gather(w_qkv, 'fsdp', axis=1, tiled=True)]
    ppermute x0 -> x98, waiting for transfers between devices: none -> 214 us  [the longest x86 159 us: swap(): return lax.ppermute(values, 'fsdp', [(i, i ^ bits) for i in range(EVERY)])]
    psum x1 -> x0, waiting for transfers between devices: 174 us -> none  [shards(): lax.psum(part_down.astype(jnp.bfloat16), 'rep').astype(jnp.float32)]
    all_to_all x5 -> x1, waiting for transfers between devices: 121 us -> 0.01 us  [split_layer(): lax.all_to_all(w_qkv.reshape(3, wide, EVERY, wide).transpose(2, 0, 1, 3),...]
    all_gather x4 -> x0, blocking collectives: 103 us -> none  [the longest x1 74.5 us: shards(): lax.all_gather(router, 'fsdp', axis=0, tiled=True)]
    reduce_scatter x3 -> x0, waiting for transfers between devices: 92.1 us -> none  [the longest x1 45.3 us: shards(): lax.psum_scatter(adapter_down_gradient.astype(jnp.bfloat16), 'fsdp', scat...]
    ppermute x0 -> x98, starting transfers between devices: none -> 79.3 us  [the longest x86 56.5 us: swap(): return lax.ppermute(values, 'fsdp', [(i, i ^ bits) for i in range(EVERY)])]
    gather x7 -> x0, local copies, waits for them, and re-layouts: 65.4 us -> none  [the longest x1 26 us: shards(): returned_grads.reshape(experts_all, capacity, model_width)]
  transfers between devices with their start and end apart: 16 -> 99, of which waited for: 13 -> 37; matrix products, arithmetic and copies ran while one was open for 24% -> 44% of each run, Pallas kernels for 0% -> 0%
where the time goes in v1:
time: 852 us; the launch traced here: 837 us
  matrix products  258 us (30%)
  waiting for transfers between devices  214 us (25%)
  local copies, waits for them, and re-layouts  189 us (22%)
  other arithmetic  89.1 us (10%)
  starting transfers between devices  83.9 us (10%)
    ppermute x86, waiting for transfers between devices, swap(): return lax.ppermute(values, 'fsdp', [(i, i ^ bits) for i in range(EVERY)])  159 us
    dot_general x27, matrix products, dot_nt(): lax.dot_general(left, right, (((1,), (1,)), ((), ())), preferred_element_...  117 us
    dot_general x27, matrix products, dot32(): return jnp.dot(left, right, preferred_element_type=jnp.float32)  89 us
    unnamed x377, local copies, waits for them, and re-layouts  62.8 us
    ppermute x86, starting transfers between devices, swap(): return lax.ppermute(values, 'fsdp', [(i, i ^ bits) for i in range(EVERY)])  56.5 us
    ppermute x12, waiting for transfers between devices, rep_swap(): return lax.ppermute(values, 'rep', [(i, i ^ bits) for i in range(4)])  54.9 us
    dot_general x16, matrix products, dot_tn(): lax.dot_general(left, right, (((0,), (0,)), ((), ())), preferred_element_...  29.5 us
    ppermute x12, starting transfers between devices, rep_swap(): return lax.ppermute(values, 'rep', [(i, i ^ bits) for i in range(4)])  22.8 us
  transfers between devices with their start and end apart: 99, of which 37 were waited for; matrix products, arithmetic and copies ran while one was open for 44% of the time, Pallas kernels for 0%

profile of v1, /device:TPU:0, one launch (start us, length us, event | category | flops | bytes accessed | tf_op | source)
XLA Modules:
  0.0 837.5 jit_solution(3720765066492531667)
XLA Ops:
  47.0 20.3 %collective-permute-done.13 = bf16[128,768]{1,0:T(8,128)(2,1)} collective-permute-done((bf16[128,768]{1,0:T(8,128)(2,1)}, bf16[128,768]{1,0:T(8,128)(2,1)}, u32[]{:S(2)}, u32[]{:S(2)}) %collective-permute-start.13) | collective-permute-done | bytes 196640 | tf_op jit(solution)/shard_map/ppermute | solution.py:491
  89.0 7.8 concatenate.165
  115.7 13.3 %collective-permute-done.26 = bf16[256,2048]{1,0:T(8,128)(2,1)} collective-permute-done((bf16[256,2048]{1,0:T(8,128)(2,1)S(1)}, bf16[256,2048]{1,0:T(8,128)(2,1)}, u32[]{:S(2)}, u32[]{:S(2)}) %collective-permute-start.26) | collective-permute-done | bytes 1048608 | tf_op jit(solution)/shard_map/ppermute | solution.py:491
  219.0 6.4 multiply_reduce_fusion.2
  231.6 9.5 %collective-permute-done.34 = bf16[128,2048]{0,1:T(8,128)(2,1)S(1)} collective-permute-done((bf16[128,2048]{0,1:T(8,128)(2,1)S(1)}, bf16[128,2048]{0,1:T(8,128)(2,1)S(1)}, u32[]{:S(2)}, u32[]{:S(2)}) %collective-permute-start.34) | collective-permute-done | bytes 524320 | tf_op jit(solution)/shard_map/ppermute | solution.py:491
  247.6 8.3 collective-permute-done.37
  260.8 7.5 concatenate.175
  279.4 6.4 fusion.92
  285.8 6.1 fusion.86
  291.9 6.1 fusion.89
  302.9 6.2 fusion.83
  318.6 7.4 concatenate.179
  331.1 10.7 %multiply_convert_fusion.2 = (bf16[1024,1024]{1,0:T(8,128)(2,1)S(1)}, bf16[1024,1024]{1,0:T(8,128)(2,1)}, bf16[1024,1024]{1,0:T(8,128)(2,1)S(1)}) fusion(f32[1024,1024]{1,0:T(8,128)} %fusion.83, f32[1024,1024]{1,0:T(8,128)S(1)} %copy-done.52, f32[1024,1024]{1,0:T(8,128)S(1)} %fusion.203, bf16[2,1024,2048]{2,1,0:T(8,128)(2,1)} %param.31, ...), kind=kOutput, calls=%fused_computation.72 | convolution fusion | flops 4319084544 | bytes 27267072 | tf_op jit(solution)/shard_map/dot_general | solution.py:558
  353.0 13.0 %multiply_convert_fusion.1 = (bf16[1024,1024]{1,0:T(8,128)(2,1)}, bf16[1024,1024]{1,0:T(8,128)(2,1)}, bf16[1024,1024]{1,0:T(8,128)(2,1)S(1)}) fusion(f32[1024,1024]{1,0:T(8,128)} %fusion.89, f32[1024,1024]{1,0:T(8,128)} %fusion.92, f32[1024,1024]{1,0:T(8,128)} %fusion.194, bf16[2,1024,2048]{2,1,0:T(8,128)(2,1)} %param.31, ...), kind=kOutput, calls=%fused_computation.71 | convolution fusion | flops 4319084544 | bytes 27267072 | tf_op jit(solution)/shard_map/dot_general | solution.py:558
  373.4 6.8 fusion.27
  380.3 6.7 fusion.23
  387.0 9.1 %fusion.21 = f32[1024,2048]{0,1:T(8,128)} fusion(bf16[1024,1024]{1,0:T(8,128)(2,1)S(1)} %get-tuple-element.37, bf16[2,1024,2048]{2,1,0:T(8,128)(2,1)} %param.31), kind=kOutput, calls=%fused_computation.49 | convolution fusion | flops 4294967296 | bytes 14680064 | tf_op jit(solution)/shard_map/dot_general | solution.py:554
  396.2 6.8 fusion.39
  403.0 7.0 fusion.35
  410.0 9.0 %fusion.33 = f32[1024,2048]{0,1:T(8,128)} fusion(bf16[1024,1024]{1,0:T(8,128)(2,1)S(1)} %get-tuple-element.34, bf16[2,1024,2048]{2,1,0:T(8,128)(2,1)} %param.31), kind=kOutput, calls=%fused_computation.61 | convolution fusion | flops 4294967296 | bytes 14680064 | tf_op jit(solution)/shard_map/dot_general | solution.py:554
  447.6 6.9 add_convert_fusion.1
  488.3 10.9 %collective-permute-done.61 = bf16[64,2048]{0,1:T(8,128)(2,1)S(1)} collective-permute-done((bf16[64,2048]{0,1:T(8,128)(2,1)}, bf16[64,2048]{0,1:T(8,128)(2,1)S(1)}, u32[]{:S(2)}, u32[]{:S(2)}) %collective-permute-start.61) | collective-permute-done | bytes 262176 | tf_op jit(solution)/shard_map/ppermute | solution.py:491
  529.2 7.1 collective-permute-done.51
  556.6 6.5 fusion.74
  589.7 7.0 fusion.114
  652.0 10.2 %add_convert_fusion = bf16[1024,2048]{0,1:T(8,128)(2,1)S(1)} fusion(f32[1024,2048]{0,1:T(8,128)} %fusion.303, f32[1024,2048]{0,1:T(8,128)} %fusion.302, f32[1024,2048]{0,1:T(8,128)} %fusion.301, bf16[2048,768]{0,1:T(8,128)(2,1)} %constant_dynamic-update-slice_fusion.35, bf16[1024,128]{0,1:T(8,128)(2,1)S(1)} %copy-done.113, ...), kind=kOutput, calls=%fused_computation.24 | convolution fusion | flops 1621360640 | bytes 31719424 | tf_op jit(solution)/shard_map/dot_general | solution.py:558
  687.4 11.3 %collective-permute-done.73 = bf16[64,2048]{0,1:T(8,128)(2,1)S(1)} collective-permute-done((bf16[64,2048]{0,1:T(8,128)(2,1)S(1)}, bf16[64,2048]{0,1:T(8,128)(2,1)S(1)}, u32[]{:S(2)}, u32[]{:S(2)}) %collective-permute-start.73) | collective-permute-done | bytes 262176 | tf_op jit(solution)/shard_map/ppermute | solution.py:491
  700.2 10.3 %collective-permute-done.76 = bf16[64,2048]{0,1:T(8,128)(2,1)S(1)} collective-permute-done((bf16[64,2048]{0,1:T(8,128)(2,1)S(1)}, bf16[64,2048]{0,1:T(8,128)(2,1)S(1)}, u32[]{:S(2)}, u32[]{:S(2)}) %collective-permute-start.76) | collective-permute-done | bytes 262176 | tf_op jit(solution)/shard_map/ppermute | solution.py:491
  722.7 6.8 collective-permute-done.86
  732.1 6.1 collective-permute-done.96
  740.0 17.8 %collective-permute-done.87 = bf16[64,1024]{1,0:T(8,128)(2,1)S(1)} collective-permute-done((bf16[64,1024]{1,0:T(8,128)(2,1)S(1)}, bf16[64,1024]{1,0:T(8,128)(2,1)S(1)}, u32[]{:S(2)}, u32[]{:S(2)}) %collective-permute-start.87) | collective-permute-done | bytes 131104 | tf_op jit(solution)/shard_map/ppermute | solution.py:530
  764.3 20.9 %collective-permute-done.88 = bf16[64,1024]{1,0:T(8,128)(2,1)S(1)} collective-permute-done((bf16[64,1024]{1,0:T(8,128)(2,1)S(1)}, bf16[64,1024]{1,0:T(8,128)(2,1)S(1)}, u32[]{:S(2)}, u32[]{:S(2)}) %collective-permute-start.88) | collective-permute-done | bytes 131104 | tf_op jit(solution)/shard_map/ppermute | solution.py:530
  (836 shorter events, 537.2 us)
Async XLA Ops:
  8.7 29.5 %collective-permute-start.8 = (bf16[256,768]{1,0:T(8,128)(2,1)S(1)}, bf16[256,768]{1,0:T(8,128)(2,1)}, u32[]{:S(2)}, u32[]{:S(2)}) collective-permute-start(bf16[256,768]{1,0:T(8,128)(2,1)S(1)} %pad.9), channel_id=1, source_target_pairs={{0,1},{1,0},{2,3},{3,2},{4,5},{5,4},{6,7},{7,6},{8,9},{9,8},{10,11... | collective-permute-start | bytes 1179656 | tf_op jit(solution)/shard_map/ppermute | solution.py:491
  12.3 30.0 %collective-permute-start.3 = (bf16[128,2176]{0,1:T(8,128)(2,1)}, bf16[128,2176]{0,1:T(8,128)(2,1)}, u32[]{:S(2)}, u32[]{:S(2)}) collective-permute-start(bf16[128,2176]{0,1:T(8,128)(2,1)} %pad_maximum_fusion.15), channel_id=1, source_target_pairs={{0,4},{1,5},{2,6},{3,7},{4,0},{5,1},{6,2},{7,3},{8,12},{9,13},{10,... | collective-permute-start | bytes 1671176 | tf_op jit(solution)/shard_map/ppermute | solution.py:491
  12.8 32.1 %collective-permute-start.1 = (bf16[128,2176]{0,1:T(8,128)(2,1)}, bf16[128,2176]{0,1:T(8,128)(2,1)}, u32[]{:S(2)}, u32[]{:S(2)}) collective-permute-start(bf16[128,2176]{0,1:T(8,128)(2,1)} %pad_maximum_fusion.15), channel_id=1, source_target_pairs={{0,2},{1,3},{2,0},{3,1},{4,6},{5,7},{6,4},{7,5},{8,10},{9,11},{10,... | collective-permute-start | bytes 1671176 | tf_op jit(solution)/shard_map/ppermute | solution.py:491
  21.5 117.0 %all-to-all-start = ((bf16[8,3,256,256]{2,3,1,0:T(8,128)(2,1)}), bf16[8,3,256,256]{2,3,1,0:T(8,128)(2,1)}, u32[]{:S(2)}, u32[]{:S(2)}) async-start(bf16[8,3,256,256]{2,3,1,0:T(8,128)(2,1)} %copy.355), calls=%async_computation | async-start | bytes 6291456 | tf_op jit(solution)/shard_map/all_to_all | solution.py:621
  34.0 36.3 %collective-permute-start.14 = (bf16[128,768]{1,0:T(8,128)(2,1)}, bf16[128,768]{1,0:T(8,128)(2,1)}, u32[]{:S(2)}, u32[]{:S(2)}) collective-permute-start(bf16[128,768]{1,0:T(8,128)(2,1)} %slice.736), channel_id=1, source_target_pairs={{0,2},{1,3},{2,0},{3,1},{4,6},{5,7},{6,4},{7,5},{8,10},{9,11},{10,... | collective-permute-start | bytes 589832 | tf_op jit(solution)/shard_map/ppermute | solution.py:491
  36.6 30.6 %collective-permute-start.13 = (bf16[128,768]{1,0:T(8,128)(2,1)}, bf16[128,768]{1,0:T(8,128)(2,1)}, u32[]{:S(2)}, u32[]{:S(2)}) collective-permute-start(bf16[128,768]{1,0:T(8,128)(2,1)} %slice.735), channel_id=1, source_target_pairs={{0,4},{1,5},{2,6},{3,7},{4,0},{5,1},{6,2},{7,3},{8,12},{9,13},{10,... | collective-permute-start | bytes 589832 | tf_op jit(solution)/shard_map/ppermute | solution.py:491
  38.2 35.7 %collective-permute-start.10 = (bf16[256,768]{1,0:T(8,128)(2,1)S(1)}, bf16[256,768]{1,0:T(8,128)(2,1)}, u32[]{:S(2)}, u32[]{:S(2)}) collective-permute-start(bf16[256,768]{1,0:T(8,128)(2,1)S(1)} %collective-permute-done.9), channel_id=1, source_target_pairs={{0,1},{1,0},{2,3},{3,2},{4,5},{5,4},{6,7},{7,6},{8,9},{9,8},{10,11... | collective-permute-start | bytes 1179656 | tf_op jit(solution)/shard_map/ppermute | solution.py:491
  42.3 46.7 %collective-permute-start = (bf16[128,2176]{0,1:T(8,128)(2,1)}, bf16[128,2176]{0,1:T(8,128)(2,1)}, u32[]{:S(2)}, u32[]{:S(2)}) collective-permute-start(bf16[128,2176]{0,1:T(8,128)(2,1)} %pad_maximum_fusion.15), channel_id=1, source_target_pairs={{0,1},{1,0},{2,3},{3,2},{4,5},{5,4},{6,7},{7,6},{8,9},{9,8},{10,11... | collective-permute-start | bytes 1671176 | tf_op jit(solution)/shard_map/ppermute | solution.py:491
  44.9 29.9 %collective-permute-start.12 = (bf16[256,768]{1,0:T(8,128)(2,1)S(1)}, bf16[256,768]{1,0:T(8,128)(2,1)}, u32[]{:S(2)}, u32[]{:S(2)}) collective-permute-start(bf16[256,768]{1,0:T(8,128)(2,1)S(1)} %collective-permute-done.11), channel_id=1, source_target_pairs={{0,1},{1,0},{2,3},{3,2},{4,5},{5,4},{6,7},{7,6},{8,9},{9,8},{10,11... | collective-permute-start | bytes 1179656 | tf_op jit(solution)/shard_map/ppermute | solution.py:491
  105.3 29.8 %collective-permute-start.23 = (bf16[256,2048]{1,0:T(8,128)(2,1)S(1)}, bf16[256,2048]{1,0:T(8,128)(2,1)S(1)}, u32[]{:S(2)}, u32[]{:S(2)}) collective-permute-start(bf16[256,2048]{1,0:T(8,128)(2,1)S(1)} %copy-done.98), channel_id=1, source_target_pairs={{0,1},{1,0},{2,3},{3,2},{4,5},{5,4},{6,7},{7,6},{8,9},{9,8},{10,11... | collective-permute-start | bytes 3145736 | tf_op jit(solution)/shard_map/ppermute | solution.py:491
  131.0 74.8 %collective-permute-start.29 = (bf16[128,2048]{1,0:T(8,128)(2,1)}, bf16[128,2048]{1,0:T(8,128)(2,1)}, u32[]{:S(2)}, u32[]{:S(2)}) collective-permute-start(bf16[128,2048]{1,0:T(8,128)(2,1)} %slice.759), channel_id=1, source_target_pairs={{0,2},{1,3},{2,0},{3,1},{4,6},{5,7},{6,4},{7,5},{8,10},{9,11},{10,... | collective-permute-start | bytes 1572872 | tf_op jit(solution)/shard_map/ppermute | solution.py:491
  133.4 72.3 %collective-permute-start.28 = (bf16[128,2048]{1,0:T(8,128)(2,1)}, bf16[128,2048]{1,0:T(8,128)(2,1)}, u32[]{:S(2)}, u32[]{:S(2)}) collective-permute-start(bf16[128,2048]{1,0:T(8,128)(2,1)} %slice.758), channel_id=1, source_target_pairs={{0,4},{1,5},{2,6},{3,7},{4,0},{5,1},{6,2},{7,3},{8,12},{9,13},{10,... | collective-permute-start | bytes 1572872 | tf_op jit(solution)/shard_map/ppermute | solution.py:491
  134.6 77.2 %collective-permute-start.27 = (bf16[256,2048]{1,0:T(8,128)(2,1)}, bf16[256,2048]{1,0:T(8,128)(2,1)}, u32[]{:S(2)}, u32[]{:S(2)}) collective-permute-start(bf16[256,2048]{1,0:T(8,128)(2,1)} %collective-permute-done.26), channel_id=1, source_target_pairs={{0,1},{1,0},{2,3},{3,2},{4,5},{5,4},{6,7},{7,6},{8,9},{9,8},{10,11... | collective-permute-start | bytes 3145736 | tf_op jit(solution)/shard_map/ppermute | solution.py:491
  134.6 72.6 %collective-permute-start.25 = (bf16[256,2048]{1,0:T(8,128)(2,1)}, bf16[256,2048]{1,0:T(8,128)(2,1)}, u32[]{:S(2)}, u32[]{:S(2)}) collective-permute-start(bf16[256,2048]{1,0:T(8,128)(2,1)} %collective-permute-done.24), channel_id=1, source_target_pairs={{0,1},{1,0},{2,3},{3,2},{4,5},{5,4},{6,7},{7,6},{8,9},{9,8},{10,11... | collective-permute-start | bytes 3145736 | tf_op jit(solution)/shard_map/ppermute | solution.py:491
  268.2 31.5 %collective-permute-start.42 = (bf16[128,2048]{0,1:T(8,128)(2,1)S(1)}, bf16[128,2048]{0,1:T(8,128)(2,1)}, u32[]{:S(2)}, u32[]{:S(2)}) collective-permute-start(bf16[128,2048]{0,1:T(8,128)(2,1)S(1)} %bitcast.447), channel_id=1, source_target_pairs={{0,4},{1,5},{2,6},{3,7},{4,0},{5,1},{6,2},{7,3},{8,12},{9,13},{10,... | collective-permute-start | bytes 1572872 | tf_op jit(solution)/shard_map/ppermute | solution.py:491
  269.3 32.7 %collective-permute-start.40 = (bf16[128,2048]{0,1:T(8,128)(2,1)S(1)}, bf16[128,2048]{0,1:T(8,128)(2,1)}, u32[]{:S(2)}, u32[]{:S(2)}) collective-permute-start(bf16[128,2048]{0,1:T(8,128)(2,1)S(1)} %bitcast.448), channel_id=1, source_target_pairs={{0,2},{1,3},{2,0},{3,1},{4,6},{5,7},{6,4},{7,5},{8,10},{9,11},{10,... | collective-permute-start | bytes 1572872 | tf_op jit(solution)/shard_map/ppermute | solution.py:491
  270.4 47.8 %collective-permute-start.39 = (bf16[128,2048]{0,1:T(8,128)(2,1)S(1)}, bf16[128,2048]{0,1:T(8,128)(2,1)}, u32[]{:S(2)}, u32[]{:S(2)}) collective-permute-start(bf16[128,2048]{0,1:T(8,128)(2,1)S(1)} %bitcast.449), channel_id=1, source_target_pairs={{0,1},{1,0},{2,3},{3,2},{4,5},{5,4},{6,7},{7,6},{8,9},{9,8},{10,11... | collective-permute-start | bytes 1572872 | tf_op jit(solution)/shard_map/ppermute | solution.py:491
  426.7 93.6 %collective-permute-start.90 = (bf16[288,2048]{1,0:T(8,128)(2,1)}, bf16[288,2048]{1,0:T(8,128)(2,1)}, u32[]{:S(2)}, u32[]{:S(2)}) collective-permute-start(bf16[288,2048]{1,0:T(8,128)(2,1)} %dynamic-slice_bitcast_fusion.1), channel_id=1, source_target_pairs={{0,8},{8,0},{16,24},{24,16},{1,9},{9,1},{17,25},{25,17},{2,10},{10... | collective-permute-start | bytes 3538952 | tf_op jit(solution)/shard_map/ppermute | solution.py:530
  439.1 84.4 %collective-permute-start.94 = (bf16[288,2048]{1,0:T(8,128)(2,1)}, bf16[288,2048]{1,0:T(8,128)(2,1)}, u32[]{:S(2)}, u32[]{:S(2)}) collective-permute-start(bf16[288,2048]{1,0:T(8,128)(2,1)} %dynamic-slice_bitcast_fusion), channel_id=1, source_target_pairs={{0,8},{8,0},{16,24},{24,16},{1,9},{9,1},{17,25},{25,17},{2,10},{10... | collective-permute-start | bytes 3538952 | tf_op jit(solution)/shard_map/ppermute | solution.py:530
  470.4 73.3 %collective-permute-start.55 = (bf16[128,2048]{0,1:T(8,128)(2,1)}, bf16[128,2048]{0,1:T(8,128)(2,1)}, u32[]{:S(2)}, u32[]{:S(2)}) collective-permute-start(bf16[128,2048]{0,1:T(8,128)(2,1)} %get-tuple-element.57), channel_id=1, source_target_pairs={{0,1},{1,0},{2,3},{3,2},{4,5},{5,4},{6,7},{7,6},{8,9},{9,8},{10,11... | collective-permute-start | bytes 1572872 | tf_op jit(solution)/shard_map/ppermute | solution.py:491
  470.8 57.2 %collective-permute-start.47 = (bf16[128,2176]{0,1:T(8,128)(2,1)}, bf16[128,2176]{0,1:T(8,128)(2,1)}, u32[]{:S(2)}, u32[]{:S(2)}) collective-permute-start(bf16[128,2176]{0,1:T(8,128)(2,1)} %get-tuple-element.43), channel_id=1, source_target_pairs={{0,1},{1,0},{2,3},{3,2},{4,5},{5,4},{6,7},{7,6},{8,9},{9,8},{10,11... | collective-permute-start | bytes 1671176 | tf_op jit(solution)/shard_map/ppermute | solution.py:491
  513.7 30.0 %collective-permute-start.59 = (bf16[128,2048]{0,1:T(8,128)(2,1)}, bf16[128,2048]{0,1:T(8,128)(2,1)}, u32[]{:S(2)}, u32[]{:S(2)}) collective-permute-start(bf16[128,2048]{0,1:T(8,128)(2,1)} %pad_maximum_fusion.25), channel_id=1, source_target_pairs={{0,2},{1,3},{2,0},{3,1},{4,6},{5,7},{6,4},{7,5},{8,10},{9,11},{10,... | collective-permute-start | bytes 1572872 | tf_op jit(solution)/shard_map/ppermute | solution.py:491
  536.3 127.1 %collective-permute-start.91 = (bf16[144,2048]{1,0:T(8,128)(2,1)}, bf16[144,2048]{1,0:T(8,128)(2,1)}, u32[]{:S(2)}, u32[]{:S(2)}) collective-permute-start(bf16[144,2048]{1,0:T(8,128)(2,1)} %dynamic-slice_bitcast_fusion.3), channel_id=1, source_target_pairs={{0,16},{8,24},{16,0},{24,8},{1,17},{9,25},{17,1},{25,9},{2,18},{10... | collective-permute-start | bytes 1769480 | tf_op jit(solution)/shard_map/ppermute | solution.py:530
  539.1 127.3 %collective-permute-start.95 = (bf16[144,2048]{1,0:T(8,128)(2,1)}, bf16[144,2048]{1,0:T(8,128)(2,1)}, u32[]{:S(2)}, u32[]{:S(2)}) collective-permute-start(bf16[144,2048]{1,0:T(8,128)(2,1)} %dynamic-slice_bitcast_fusion.2), channel_id=1, source_target_pairs={{0,16},{8,24},{16,0},{24,8},{1,17},{9,25},{17,1},{25,9},{2,18},{10... | collective-permute-start | bytes 1769480 | tf_op jit(solution)/shard_map/ppermute | solution.py:530
  650.4 62.3 %collective-permute-start.78 = (bf16[256,640]{0,1:T(8,128)(2,1)}, bf16[256,640]{0,1:T(8,128)(2,1)}, u32[]{:S(2)}, u32[]{:S(2)}) collective-permute-start(bf16[256,640]{0,1:T(8,128)(2,1)} %pad_maximum_fusion.38), channel_id=1, source_target_pairs={{0,1},{1,0},{2,3},{3,2},{4,5},{5,4},{6,7},{7,6},{8,9},{9,8},{10,11... | collective-permute-start | bytes 983048 | tf_op jit(solution)/shard_map/ppermute | solution.py:491
  676.2 86.0 %collective-permute-start.70 = (bf16[128,2048]{0,1:T(8,128)(2,1)}, bf16[128,2048]{0,1:T(8,128)(2,1)}, u32[]{:S(2)}, u32[]{:S(2)}) collective-permute-start(bf16[128,2048]{0,1:T(8,128)(2,1)} %get-tuple-element.50), channel_id=1, source_target_pairs={{0,1},{1,0},{2,3},{3,2},{4,5},{5,4},{6,7},{7,6},{8,9},{9,8},{10,11... | collective-permute-start | bytes 1572872 | tf_op jit(solution)/shard_map/ppermute | solution.py:491
  676.3 43.4 %collective-permute-start.92 = (bf16[144,2048]{1,0:T(8,128)(2,1)}, bf16[144,2048]{1,0:T(8,128)(2,1)}, u32[]{:S(2)}, u32[]{:S(2)}) collective-permute-start(bf16[144,2048]{1,0:T(8,128)(2,1)} %fusion.126), channel_id=1, source_target_pairs={{0,16},{8,24},{16,0},{24,8},{1,17},{9,25},{17,1},{25,9},{2,18},{10... | collective-permute-start | bytes 1769480 | tf_op jit(solution)/shard_map/ppermute | solution.py:530
  680.2 32.8 %collective-permute-start.82 = (bf16[256,640]{0,1:T(8,128)(2,1)S(1)}, bf16[256,640]{0,1:T(8,128)(2,1)S(1)}, u32[]{:S(2)}, u32[]{:S(2)}) collective-permute-start(bf16[256,640]{0,1:T(8,128)(2,1)S(1)} %pad_maximum_fusion.41), channel_id=1, source_target_pairs={{0,2},{1,3},{2,0},{3,1},{4,6},{5,7},{6,4},{7,5},{8,10},{9,11},{10,... | collective-permute-start | bytes 983048 | tf_op jit(solution)/shard_map/ppermute | solution.py:491
  713.0 49.4 %collective-permute-start.74 = (bf16[128,2048]{0,1:T(8,128)(2,1)}, bf16[128,2048]{0,1:T(8,128)(2,1)}, u32[]{:S(2)}, u32[]{:S(2)}) collective-permute-start(bf16[128,2048]{0,1:T(8,128)(2,1)} %pad_maximum_fusion.27), channel_id=1, source_target_pairs={{0,2},{1,3},{2,0},{3,1},{4,6},{5,7},{6,4},{7,5},{8,10},{9,11},{10,... | collective-permute-start | bytes 1572872 | tf_op jit(solution)/shard_map/ppermute | solution.py:491
  719.8 42.6 %collective-permute-start.77 = (bf16[128,2048]{0,1:T(8,128)(2,1)S(1)}, bf16[128,2048]{0,1:T(8,128)(2,1)S(1)}, u32[]{:S(2)}, u32[]{:S(2)}) collective-permute-start(bf16[128,2048]{0,1:T(8,128)(2,1)S(1)} %pad_maximum_fusion.28), channel_id=1, source_target_pairs={{0,4},{1,5},{2,6},{3,7},{4,0},{5,1},{6,2},{7,3},{8,12},{9,13},{10,... | collective-permute-start | bytes 1572872 | tf_op jit(solution)/shard_map/ppermute | solution.py:491
  729.5 73.0 %collective-permute-start.93 = (bf16[288,2048]{1,0:T(8,128)(2,1)S(1)}, bf16[288,2048]{1,0:T(8,128)(2,1)}, u32[]{:S(2)}, u32[]{:S(2)}) collective-permute-start(bf16[288,2048]{1,0:T(8,128)(2,1)S(1)} %bitcast.439), channel_id=1, source_target_pairs={{0,8},{8,0},{16,24},{24,16},{1,9},{9,1},{17,25},{25,17},{2,10},{10... | collective-permute-start | bytes 3538952 | tf_op jit(solution)/shard_map/ppermute | solution.py:530
  757.9 50.3 %collective-permute-start.97 = (bf16[288,2048]{1,0:T(8,128)(2,1)S(1)}, bf16[288,2048]{1,0:T(8,128)(2,1)}, u32[]{:S(2)}, u32[]{:S(2)}) collective-permute-start(bf16[288,2048]{1,0:T(8,128)(2,1)S(1)} %bitcast.441), channel_id=1, source_target_pairs={{0,8},{8,0},{16,24},{24,16},{1,9},{9,1},{17,25},{25,17},{2,10},{10... | collective-permute-start | bytes 3538952 | tf_op jit(solution)/shard_map/ppermute | solution.py:530
  (240 other events, 3013.8 us)

commit v2 on v0

--- a/solution.py
+++ b/solution.py
@@ -1,8 +1,11 @@
+import functools
 import math
 
 import jax
 import jax.numpy as jnp
 from jax import lax
+from jax.experimental import pallas as pl
+from jax.experimental.pallas import tpu as pltpu
 from jax.sharding import PartitionSpec as P
 
 HD = 128
@@ -49,7 +52,7 @@
     )
 
 
-def shards(
+def gathered_layer(
     hidden_in,
     segments,
     routes,
@@ -484,7 +487,882 @@
     )
 
 
+EVERY = 8
+TILE = 256
+CUT = 512
+VMEM_BYTES = 64000000
+
+
+def mm(left, right):
+    return jnp.dot(left, right, preferred_element_type=jnp.float32)
+
+
+def mm_nt(left, right):
+    return lax.dot_general(left, right, (((1,), (1,)), ((), ())), preferred_element_type=jnp.float32)
+
+
+def whole():
+    return pl.BlockSpec(memory_space=pltpu.VMEM)
+
+
+def in_place():
+    return pl.BlockSpec(memory_space=pl.ANY)
+
+
+def scalars():
+    return pl.BlockSpec(memory_space=pltpu.SMEM)
+
+
+def params():
+    return pltpu.CompilerParams(vmem_limit_bytes=VMEM_BYTES)
+
+
+def cost(flops, moved):
+    return pl.CostEstimate(flops=flops, bytes_accessed=moved, transcendentals=0)
+
+
+def shape_of(shape, dtype=jnp.bfloat16):
+    return jax.ShapeDtypeStruct(shape, dtype)
+
+
+def swap(values, bits):
+    return lax.ppermute(values, "fsdp", [(i, i ^ bits) for i in range(EVERY)])
+
+
+def gather_relative(values):
+    half = values.shape[0] // 2
+    side, over = swap(values, 2), swap(values, 4)
+    far = jnp.concatenate([swap(side[:half], 4), swap(over[half:], 2)], axis=0)
+    mine = [values, side, over, far]
+    other = [swap(block, 1) for block in mine]
+    return [mine[0], other[0], mine[1], other[1], mine[2], other[2], mine[3], other[3]]
+
+
+def add_half(left, right):
+    return (left.astype(jnp.float32) + right.astype(jnp.float32)).astype(jnp.bfloat16)
+
+
+def scatter_relative(even, odd):
+    rows = even.shape[0] // 4
+    half = rows // 2
+    got = swap(odd, 1)
+
+    def pair(start):
+        return add_half(even[start : start + half], got[start : start + half])
+
+    far_side = swap(pair(3 * rows), 2)
+    far_over = swap(pair(3 * rows + half), 4)
+    side_top = swap(pair(rows), 2)
+    over_low = swap(pair(2 * rows + half), 4)
+    side_low = swap(add_half(pair(rows + half), far_over), 2)
+    over_top = swap(add_half(pair(2 * rows), far_side), 4)
+    return even, got, side_top, side_low, over_top, over_low
+
+
+def sum_pieces(even, got, side_top, side_low, over_top, over_low):
+    f32 = jnp.float32
+    top = side_top.astype(f32) + over_top.astype(f32)
+    low = side_low.astype(f32) + over_low.astype(f32)
+    return even.astype(f32) + got.astype(f32) + jnp.concatenate([top, low], axis=0)
+
+
+def piece_specs(rows, columns, at=0):
+    return [pl.BlockSpec((rows, columns), lambda i: (0, at))] * 2 + [
+        pl.BlockSpec((rows // 2, columns), lambda i: (0, at))
+    ] * 4
+
+
+def rep_swap(values, bits):
+    return lax.ppermute(values, "rep", [(i, i ^ bits) for i in range(4)])
+
+
+def pick(pair, index):
+    return lax.dynamic_index_in_dim(pair, index, 0, keepdims=False)
+
+
+def joined(own, other, index):
+    return jnp.where(index == 0, jnp.stack([own, other]), jnp.stack([other, own]))
+
+
+def sum_rep(values):
+    where = lax.axis_index("rep")
+    low_bit, high_bit = where % 2, where // 2
+    rows, columns = values.shape
+    halves = values.reshape(2, rows // 2, columns)
+    half = add_half(pick(halves, low_bit), rep_swap(pick(halves, 1 - low_bit), 1))
+    parts = half.reshape(2, rows // 4, columns)
+    part = add_half(pick(parts, high_bit), rep_swap(pick(parts, 1 - high_bit), 2))
+    half = joined(part, rep_swap(part, 2), high_bit).reshape(rows // 2, columns)
+    return joined(half, rep_swap(half, 1), low_bit).reshape(rows, columns)
+
+
+def sum_rep_short(values):
+    values = add_half(values, rep_swap(values, 1))
+    return add_half(values, rep_swap(values, 2))
+
+
+def turn(values, cosine, signed_sine):
+    return values * cosine + pltpu.roll(values, HD // 2, 1) * signed_sine
+
+
+def project_kernel(
+    rows, width, wide,
+    me_ref, gain_ref, mask_ref, cos_ref, sin_ref, up_ref, *refs,
+):
+    f32, bf16 = jnp.float32, jnp.bfloat16
+    hidden_hbm, w_hbm, small_hbm = refs[:EVERY], refs[EVERY : 2 * EVERY], refs[2 * EVERY : 3 * EVERY]
+    q_ref, k_ref, v_ref, normed_ref, low_ref, hidden, weight, down, sems = refs[3 * EVERY :]
+    me = me_ref[0]
+    copies = []
+    for j in range(EVERY):
+        at = pl.multiple_of((me ^ j) * wide, wide)
+        copies.append(
+            [
+                pltpu.make_async_copy(hidden_hbm[j], hidden.at[j * rows : (j + 1) * rows], sems.at[j, 0]),
+                pltpu.make_async_copy(
+                    small_hbm[j].at[:, 0 : 3 * SR], down.at[pl.ds(at, wide), :], sems.at[j, 1]
+                ),
+            ]
+            + [
+                pltpu.make_async_copy(
+                    w_hbm[j].at[i], weight.at[pl.ds(at, wide), i * wide : (i + 1) * wide], sems.at[j, 2 + i]
+                )
+                for i in range(3)
+            ]
+        )
+    for group in copies:
+        for item in group:
+            item.start()
+    for group in copies:
+        for item in group:
+            item.wait()
+    gain = gain_ref[...]
+
+    def chunk(c, _):
+        at = pl.ds(pl.multiple_of(c * TILE, TILE), TILE)
+        values = hidden[at, :].astype(f32)
+        scale = lax.rsqrt(jnp.mean(values * values, axis=1, keepdims=True) + EPSILON)
+        normed = (values * scale * gain).astype(bf16)
+        normed_ref[at, :] = normed
+        mask = mask_ref[at, :]
+        low = (mm(normed, down[...]) * jnp.concatenate([mask] * 3, axis=1)).astype(bf16)
+        low_ref[at, :] = low
+        cosine, sine = cos_ref[at, :], sin_ref[at, :]
+        for i, ref in enumerate((q_ref, k_ref, v_ref)):
+            proj = mm(normed, weight[:, i * wide : (i + 1) * wide]) + mm_nt(
+                low[:, i * SR : (i + 1) * SR], up_ref[i]
+            )
+            for h in range(wide // HD):
+                part = proj[:, h * HD : (h + 1) * HD]
+                ref[at, h * HD : (h + 1) * HD] = (turn(part, cosine, sine) if i < 2 else part).astype(bf16)
+        return 0
+
+    lax.fori_loop(0, EVERY * rows // TILE, chunk, 0)
+
+
+def project(me, gain, mask, cosine, sine, up, hidden_blocks, w_blocks, small_blocks):
+    rows, width = hidden_blocks[0].shape
+    wide = width // EVERY
+    tokens = rows * EVERY
+    return pl.pallas_call(
+        functools.partial(project_kernel, rows, width, wide),
+        in_specs=[scalars()] + [whole()] * 5 + [in_place()] * (3 * EVERY),
+        out_specs=[whole()] * 5,
+        out_shape=[shape_of((tokens, wide))] * 3 + [shape_of((tokens, width)), shape_of((tokens, 3 * SR))],
+        scratch_shapes=[
+            pltpu.VMEM((tokens, width), jnp.bfloat16),
+            pltpu.VMEM((width, 3 * wide), jnp.bfloat16),
+            pltpu.VMEM((width, 3 * SR), jnp.bfloat16),
+            pltpu.SemaphoreType.DMA((EVERY, 5)),
+        ],
+        compiler_params=params(),
+        cost_estimate=cost(2 * tokens * width * 3 * (wide + SR), 16 << 20),
+        name="project",
+    )(me, gain, mask, cosine, sine, up, *hidden_blocks, *w_blocks, *small_blocks)
+
+
+def attend_kernel(rows, q_ref, k_ref, v_ref, col_ref, row_ref, att_ref, lse_ref, *outs):
+    f32, bf16 = jnp.float32, jnp.bfloat16
+    scale = HD ** (-0.5)
+    seg_row = row_ref[0:1, :]
+    for h in range(q_ref.shape[1] // HD):
+        lanes = slice(h * HD, (h + 1) * HD)
+        for c in range(q_ref.shape[0] // TILE):
+            at = slice(c * TILE, (c + 1) * TILE)
+            scores = mm_nt(q_ref[at, lanes], k_ref[:, lanes]) * scale
+            scores = jnp.where(col_ref[at, 0:1] == seg_row, scores, MASKED)
+            top = jnp.max(scores, axis=1, keepdims=True)
+            weights = jnp.exp(scores - top)
+            total = jnp.sum(weights, axis=1, keepdims=True)
+            att = mm(weights.astype(bf16), v_ref[:, lanes]) / total
+            att_ref[at, lanes] = att
+            log_sum = jnp.broadcast_to(top + jnp.log(total), (TILE, HD))
+            lse_ref[h : h + 1, at] = log_sum.T[0:1, :]
+            for part in range(TILE // rows):
+                outs[c * (TILE // rows) + part][:, lanes] = att[part * rows : (part + 1) * rows].astype(bf16)
+
+
+def attend(rows, queries, keys, values, seg_col, seg_row):
+    tokens, wide = queries.shape
+    return pl.pallas_call(
+        functools.partial(attend_kernel, rows),
+        in_specs=[whole()] * 5,
+        out_specs=[whole()] * (2 + EVERY),
+        out_shape=[shape_of((tokens, wide), jnp.float32), shape_of((8, tokens), jnp.float32)]
+        + [shape_of((rows, wide))] * EVERY,
+        compiler_params=params(),
+        cost_estimate=cost(4 * tokens * tokens * wide, 4 << 20),
+        name="attend",
+    )(queries, keys, values, seg_col, seg_row)
+
+
+def mix_kernel(
+    wide,
+    me_ref, hidden_ref, gain_ref, mask_ref, router_ref, named_ref, *refs,
+):
+    f32, bf16 = jnp.float32, jnp.bfloat16
+    att_ref, w_hbm, small_hbm = refs[:EVERY], refs[EVERY : 2 * EVERY], refs[2 * EVERY : 3 * EVERY]
+    resid_ref, normed_ref, low_ref, gates_ref, weight, down, up, sems = refs[3 * EVERY :]
+    me = me_ref[0]
+    width = hidden_ref.shape[1]
+    copies = []
+    for j in range(EVERY):
+        at = pl.multiple_of((me ^ j) * wide, wide)
+        here = slice(j * wide, (j + 1) * wide)
+        copies.append(
+            [
+                pltpu.make_async_copy(small_hbm[j].at[:, 3 * SR : 4 * SR], down.at[here, :], sems.at[j, 0]),
+                pltpu.make_async_copy(
+                    small_hbm[j].at[:, 4 * SR : 5 * SR], up.at[pl.ds(at, wide), :], sems.at[j, 1]
+                ),
+                pltpu.make_async_copy(w_hbm[j], weight.at[here, :], sems.at[j, 2]),
+            ]
+        )
+    for part in range(3):
+        for group in copies:
+            group[part].start()
+    for part in range(2):
+        for group in copies:
+            group[part].wait()
+    att = jnp.concatenate([ref[...] for ref in att_ref], axis=1)
+    low = (mm(att, down[...]) * mask_ref[...]).astype(bf16)
+    low_ref[...] = low
+    total = mm_nt(low, up[...])
+    for j in range(EVERY):
+        copies[j][2].wait()
+        total = total + mm(att_ref[j][...], weight[j * wide : (j + 1) * wide, :])
+    resid = hidden_ref[...].astype(f32) + total
+    resid_ref[...] = resid
+    scale = lax.rsqrt(jnp.mean(resid * resid, axis=1, keepdims=True) + EPSILON)
+    normed = (resid * scale * gain_ref[...]).astype(bf16)
+    normed_ref[:, 0:width] = normed
+    logits = jnp.where(named_ref[...] > 0.5, mm(normed, router_ref[...]), MASKED)
+    share = jnp.exp(logits - jnp.max(logits, axis=1, keepdims=True)) * named_ref[...]
+    gates = share / jnp.sum(share, axis=1, keepdims=True)
+    gates_ref[...] = gates
+    high = gates.astype(bf16).astype(f32)
+    normed_ref[:, width : width + 128] = (high + pltpu.roll(gates - high, 64, 1)).astype(bf16)
+
+
+def mix(me, hidden, gain, mask, router, named, att_blocks, w_blocks, small_blocks):
+    rows, width = hidden.shape
+    wide = width // EVERY
+    f32 = jnp.float32
+    return pl.pallas_call(
+        functools.partial(mix_kernel, wide),
+        in_specs=[scalars()] + [whole()] * 5 + [whole()] * EVERY + [in_place()] * (2 * EVERY),
+        out_specs=[whole()] * 4,
+        out_shape=[shape_of((rows, width), f32), shape_of((rows, width + 128)), shape_of((rows, SR)),
+                   shape_of((rows, 128), f32)],
+        scratch_shapes=[
+            pltpu.VMEM((width, width), jnp.bfloat16),
+            pltpu.VMEM((width, SR), jnp.bfloat16),
+            pltpu.VMEM((width, SR), jnp.bfloat16),
+            pltpu.SemaphoreType.DMA((EVERY, 3)),
+        ],
+        compiler_params=params(),
+        cost_estimate=cost(2 * rows * width * width, 10 << 20),
+        name="mix",
+    )(me, hidden, gain, mask, router, named, *att_blocks, *w_blocks, *small_blocks)
+
+
+def expert_kernel(k, first, width, hidden, blocks, mask_ref, pick_ref, *refs):
+    f32, bf16 = jnp.float32, jnp.bfloat16
+    rows_hbm, cot_hbm, refs = refs[:blocks], refs[blocks : 2 * blocks], refs[2 * blocks :]
+    if not first:
+        prev_out, prev_row, refs = refs[:2], refs[2:4], refs[4:]
+    (
+        w_gate_hbm, w_up_hbm, w_down_hbm, a_in_hbm, b_in_hbm, a_down_hbm, b_down_hbm,
+        out_even, out_odd, row_even, row_odd, grad_ref,
+        rows_s, cot_s, w_in, w_down, silu_s, slope_s,
+        g_a_in, g_b_down, g_b_in, g_a_down, sems, block_sems,
+    ) = refs
+    out_refs, row_refs = (out_even, out_odd), (row_even, row_odd)
+    step = pl.program_id(0)
+    part = TILE // 2
+    low_at, thin_at = 2 * hidden, width
+    chunks = hidden // CUT
+    early, late, given = [], [], []
+
+    def copy(source, target, group):
+        group.append(pltpu.make_async_copy(source, target, sems.at[len(early) + len(late)]))
+
+    copy(a_in_hbm.at[k, 0], w_in.at[0:width, low_at : low_at + SR], early)
+    copy(a_in_hbm.at[k, 1], w_in.at[0:width, low_at + SR : low_at + 2 * SR], early)
+    copy(b_in_hbm.at[k, 0], w_in.at[width : width + SR, 0:hidden], early)
+    copy(b_in_hbm.at[k, 1], w_in.at[width : width + SR, hidden:low_at], early)
+    for j in range(chunks):
+        at = slice(j * CUT, (j + 1) * CUT)
+        copy(w_gate_hbm.at[k, :, at], w_in.at[0:width, at], early)
+        copy(w_up_hbm.at[k, :, at], w_in.at[0:width, hidden + j * CUT : hidden + (j + 1) * CUT], early)
+    copy(a_down_hbm.at[k], w_down.at[0:hidden, thin_at : thin_at + SR], late)
+    copy(b_down_hbm.at[k], w_down.at[hidden : hidden + SR, 0:width], late)
+    copy(w_down_hbm.at[k], w_down.at[0:hidden, 0:width], late)
+    for j in range(blocks):
+        at = slice(j * part, (j + 1) * part)
+        given.append(pltpu.make_async_copy(rows_hbm[j], rows_s.at[at, :], block_sems.at[j, 0]))
+        given.append(pltpu.make_async_copy(cot_hbm[j], cot_s.at[at, :], block_sems.at[j, 1]))
+
+    def wait_for(group, when=0):
+        @pl.when(step == when)
+        def _():
+            for item in group:
+                item.wait()
+
+    @pl.when(step == 0)
+    def _():
+        for item in given[0:4] + early + late + given[4:]:
+            item.start()
+        g_a_in[...] = jnp.zeros_like(g_a_in)
+        g_b_down[...] = jnp.zeros_like(g_b_down)
+        g_b_in[...] = jnp.zeros_like(g_b_in)
+        g_a_down[...] = jnp.zeros_like(g_a_down)
+
+    for i in range(blocks // 2):
+        wait_for(given[4 * i : 4 * i + 4], i)
+    wait_for(early[:2])
+    at_rows = pl.ds(pl.multiple_of(step * TILE, TILE), TILE)
+    mask = mask_ref[...]
+    mask_two = jnp.concatenate([mask, mask], axis=1)
+    rows = rows_s[at_rows, 0:width]
+    gate = jnp.sum(rows_s[at_rows, width:].astype(f32) * pick_ref[0:1, :], axis=1, keepdims=True)
+    low_in = (mm(rows, w_in[0:width, low_at:]) * mask_two).astype(bf16)
+    rows_gate = jnp.concatenate([rows, low_in[:, :SR]], axis=1)
+    rows_up = jnp.concatenate([rows, low_in[:, SR:]], axis=1)
+    wait_for(early[2:4])
+    act_parts = []
+    for j in range(chunks):
+        wait_for(early[4 + 2 * j : 6 + 2 * j])
+        at = slice(j * CUT, (j + 1) * CUT)
+        gate_h = mm(rows_gate, w_in[:, at])
+        up_h = mm(rows_up, w_in[:, hidden + j * CUT : hidden + (j + 1) * CUT])
+        share = 1.0 / (1.0 + jnp.exp(-gate_h))
+        silu = gate_h * share
+        silu_s[:, at] = silu
+        slope_s[:, at] = up_h * (share * (1.0 + gate_h * (1.0 - share)))
+        act_parts.append((silu * up_h).astype(bf16))
+    act = jnp.concatenate(act_parts, axis=1)
+    wait_for(late)
+
+    low_down = (mm(act, w_down[0:hidden, thin_at:]) * mask).astype(bf16)
+    act_low = jnp.concatenate([act, low_down], axis=1)
+    d_gate = jnp.zeros((TILE, 1), f32)
+    d_out_parts = []
+    for j in range(width // CUT):
+        at = slice(j * CUT, (j + 1) * CUT)
+        out = mm(act_low, w_down[:, at]).astype(bf16).astype(f32)
+        cot = cot_s[at_rows, at].astype(f32)
+        d_out_parts.append((gate * cot).astype(bf16))
+        weighted = gate * out
+        for i in range(2):
+            value = weighted[i * part : (i + 1) * part]
+            if not first:
+                value = value + prev_out[i][:, at].astype(f32)
+            out_refs[i][:, at] = value.astype(bf16)
+        d_gate = d_gate + jnp.sum(cot * out, axis=1, keepdims=True)
+    high = d_gate.astype(bf16).astype(f32)
+    extra = high * pick_ref[1:2, :] + (d_gate - high) * pick_ref[2:3, :]
+    for i in range(2):
+        value = extra[i * part : (i + 1) * part]
+        if not first:
+            value = value + prev_out[i][:, width:].astype(f32)
+        out_refs[i][:, width:] = value.astype(bf16)
+
+    mask_half = mask.astype(bf16)
+    d_out = jnp.concatenate(d_out_parts, axis=1)
+    d_low_down = mm_nt(d_out, w_down[hidden:, 0:width]).astype(bf16) * mask_half
+    d_out_low = jnp.concatenate([d_out, d_low_down], axis=1)
+    d_gate_parts, d_up_parts = [], []
+    for j in range(chunks):
+        at = slice(j * CUT, (j + 1) * CUT)
+        d_act = mm_nt(d_out_low, w_down[at, :])
+        d_gate_parts.append((d_act * slope_s[:, at]).astype(bf16))
+        d_up_parts.append((d_act * silu_s[:, at]).astype(bf16))
+    d_gate_h = jnp.concatenate(d_gate_parts, axis=1)
+    d_up_h = jnp.concatenate(d_up_parts, axis=1)
+    d_low_gate = mm_nt(d_gate_h, w_in[width:, 0:hidden]).astype(bf16) * mask_half
+    d_low_up = mm_nt(d_up_h, w_in[width:, hidden:low_at]).astype(bf16) * mask_half
+    d_low_in = jnp.concatenate([d_low_gate, d_low_up], axis=1)
+    d_all = jnp.concatenate([d_gate_h, d_up_h, d_low_in], axis=1)
+    d_low_in_t, low_down_t, low_in_t, d_low_down_t = d_low_in.T, low_down.T, low_in.T, d_low_down.T
+    for j in range(width // CUT):
+        at = slice(j * CUT, (j + 1) * CUT)
+        d_row = mm_nt(d_all, w_in[at, :]).astype(bf16)
+        for i in range(2):
+            value = d_row[i * part : (i + 1) * part]
+            if not first:
+                value = (value.astype(f32) + prev_row[i][:, at].astype(f32)).astype(bf16)
+            row_refs[i][:, at] = value
+        g_a_in[:, at] += mm(d_low_in_t, rows[:, at])
+        g_b_down[:, at] += mm(low_down_t, d_out[:, at])
+    for j in range(chunks):
+        at = slice(j * CUT, (j + 1) * CUT)
+        g_b_in[0, :, at] += mm(low_in_t[:SR], d_gate_h[:, at])
+        g_b_in[1, :, at] += mm(low_in_t[SR:], d_up_h[:, at])
+        g_a_down[:, at] += mm(d_low_down_t, act[:, at])
+
+    @pl.when(step == pl.num_programs(0) - 1)
+    def _():
+        grad_ref[0 : 2 * SR, :] = g_a_in[...].astype(bf16)
+        grad_ref[2 * SR : 3 * SR, :] = g_b_down[...].astype(bf16)
+        grad_ref[3 * SR : 4 * SR, 0:hidden] = g_b_in[0].astype(bf16)
+        grad_ref[3 * SR : 4 * SR, hidden:] = g_b_in[1].astype(bf16)
+        grad_ref[4 * SR : 4 * SR + SR // 2, 0:hidden] = g_a_down[: SR // 2].astype(bf16)
+        grad_ref[4 * SR : 4 * SR + SR // 2, hidden:] = g_a_down[SR // 2 :].astype(bf16)
+
+
+def expert_pass(k, rows, cot, mask, picks, prev, weights):
+    f32, bf16 = jnp.float32, jnp.bfloat16
+    blocks = len(rows)
+    part, width = cot[0].shape
+    hidden = weights[0].shape[2]
+    tokens = blocks * part
+    by_tile = lambda size, columns: pl.BlockSpec((size, columns), lambda i: (i, 0))
+    in_specs = [by_tile(TILE, SR), pl.BlockSpec((8, 128), lambda i: (0, 0))] + [in_place()] * (2 * blocks)
+    operands = [mask, picks, *rows, *cot]
+    if prev is not None:
+        in_specs += [by_tile(part, width + 128)] * 2 + [by_tile(part, width)] * 2
+        operands += list(prev)
+    in_specs += [in_place()] * 7
+    flops = 2 * tokens * (6 * width * hidden + 9 * SR * (width + hidden))
+    return pl.pallas_call(
+        functools.partial(expert_kernel, k, prev is None, width, hidden, blocks),
+        grid=(tokens // TILE,),
+        in_specs=in_specs,
+        out_specs=[by_tile(part, width + 128)] * 2
+        + [by_tile(part, width)] * 2
+        + [pl.BlockSpec((4 * SR + SR // 2, width), lambda i: (0, 0))],
+        out_shape=[shape_of((tokens // 2, width + 128))] * 2
+        + [shape_of((tokens // 2, width))] * 2
+        + [shape_of((4 * SR + SR // 2, width))],
+        scratch_shapes=[
+            pltpu.VMEM((tokens, width + 128), bf16),
+            pltpu.VMEM((tokens, width), bf16),
+            pltpu.VMEM((width + SR, 2 * hidden + 2 * SR), bf16),
+            pltpu.VMEM((hidden + SR, width + SR), bf16),
+            pltpu.VMEM((TILE, hidden), f32),
+            pltpu.VMEM((TILE, hidden), f32),
+            pltpu.VMEM((2 * SR, width), f32),
+            pltpu.VMEM((SR, width), f32),
+            pltpu.VMEM((2, SR, hidden), f32),
+            pltpu.VMEM((SR, hidden), f32),
+            pltpu.SemaphoreType.DMA((7 + 2 * (hidden // CUT),)),
+            pltpu.SemaphoreType.DMA((blocks, 2)),
+        ],
+        compiler_params=params(),
+        cost_estimate=cost(flops, 40 << 20),
+        name="expert",
+    )(*operands, *weights)
+
+
+def norm_grad(values, gain_row, upstream_grad):
+    scale = lax.rsqrt(jnp.mean(values * values, axis=1, keepdims=True) + EPSILON)
+    inner = gain_row * upstream_grad
+    mean = jnp.mean(values * inner, axis=1, keepdims=True)
+    return scale * inner - values * (scale * scale * scale * mean)
+
+
+def unmix_kernel(
+    wide,
+    me_ref, resid_ref, cot_ref, gain_ref, mask_ref, router_ref, gates_ref, low_ref, *refs,
+):
+    f32, bf16 = jnp.float32, jnp.bfloat16
+    row_pieces, out_pieces, extra_pieces, refs = refs[:6], refs[6:12], refs[12:18], refs[18:]
+    att_ref, w_hbm, small_hbm = refs[:EVERY], refs[EVERY : 2 * EVERY], refs[2 * EVERY : 3 * EVERY]
+    layer_ref, resid_grad_ref, grad_ref, *refs = refs[3 * EVERY :]
+    att_grads, (weight, down, up, up_grad, sems) = refs[:EVERY], refs[EVERY:]
+    me = me_ref[0]
+    width = resid_ref.shape[1]
+    copies = []
+    for j in range(EVERY):
+        at = pl.multiple_of((me ^ j) * wide, wide)
+        here = slice(j * wide, (j + 1) * wide)
+        copies.append(
+            [
+                pltpu.make_async_copy(
+                    small_hbm[j].at[:, 4 * SR : 5 * SR], up.at[pl.ds(at, wide), :], sems.at[j, 1]
+                ),
+                pltpu.make_async_copy(small_hbm[j].at[:, 3 * SR : 4 * SR], down.at[here, :], sems.at[j, 0]),
+                pltpu.make_async_copy(w_hbm[j], weight.at[here, :], sems.at[j, 2]),
+            ]
+        )
+    for which in range(3):
+        for group in copies:
+            group[which].start()
+    resid = resid_ref[...]
+    layer_ref[...] = (resid + sum_pieces(*[ref[...] for ref in out_pieces])).astype(bf16)
+    extra = sum_pieces(*[ref[...] for ref in extra_pieces])
+    gates = gates_ref[...]
+    d_gates = extra + pltpu.roll(extra, 64, 1)
+    d_chosen = gates * (d_gates - jnp.sum(gates * d_gates, axis=1, keepdims=True))
+    d_normed = sum_pieces(*[ref[...] for ref in row_pieces]) + mm_nt(d_chosen.astype(bf16), router_ref[...])
+    d_resid = cot_ref[...].astype(f32) + norm_grad(resid, gain_ref[...], d_normed)
+    resid_grad_ref[...] = d_resid
+    branch = d_resid.astype(bf16)
+    for group in copies:
+        group[0].wait()
+    d_low = (mm(branch, up[...]).astype(bf16).astype(f32) * mask_ref[...]).astype(bf16)
+    low_t, d_low_t = low_ref[...].T, d_low.T
+    up_grad[...] = mm(low_t, branch).astype(bf16)
+    for group in copies:
+        group[1].wait()
+    for j in range(EVERY):
+        here = slice(j * wide, (j + 1) * wide)
+        copies[j][2].wait()
+        att_grads[j][...] = (mm_nt(branch, weight[here, :]) + mm_nt(d_low, down[here, :])).astype(bf16)
+        at = pl.multiple_of((me ^ j) * wide, wide)
+        grad_ref[j * 2 * SR : j * 2 * SR + SR, :] = mm(d_low_t, att_ref[j][...]).astype(bf16)
+        grad_ref[j * 2 * SR + SR : (j + 1) * 2 * SR, :] = up_grad[:, pl.ds(at, wide)]
+
+
+def unmix(me, resid, cot, gain, mask, router, gates, low, row_pieces, out_pieces, att_blocks, w_blocks, small_blocks):
+    rows, width = resid.shape
+    wide = width // EVERY
+    return pl.pallas_call(
+        functools.partial(unmix_kernel, wide),
+        grid=(1,),
+        in_specs=[scalars()]
+        + [whole()] * 7
+        + piece_specs(rows, width)
+        + piece_specs(rows, width)
+        + piece_specs(rows, 128, width // 128)
+        + [whole()] * EVERY
+        + [in_place()] * (2 * EVERY),
+        out_specs=[whole()] * (3 + EVERY),
+        out_shape=[
+            shape_of((rows, width)),
+            shape_of((rows, width), jnp.float32),
+            shape_of((EVERY * 2 * SR, wide)),
+        ]
+        + [shape_of((rows, wide))] * EVERY,
+        scratch_shapes=[
+            pltpu.VMEM((width, width), jnp.bfloat16),
+            pltpu.VMEM((width, SR), jnp.bfloat16),
+            pltpu.VMEM((width, SR), jnp.bfloat16),
+            pltpu.VMEM((SR, width), jnp.bfloat16),
+            pltpu.SemaphoreType.DMA((EVERY, 3)),
+        ],
+        compiler_params=params(),
+        cost_estimate=cost(2 * rows * width * width, 14 << 20),
+        name="unmix",
+    )(me, resid, cot, gain, mask, router, gates, low, *row_pieces, *out_pieces, *out_pieces,
+      *att_blocks, *w_blocks, *small_blocks)
+
+
+def attend_back_kernel(
+    rows, wide,
+    me_ref, q_ref, k_ref, v_ref, att_ref, lse_ref, col_ref, row_ref, cos_ref, sin_ref, low_ref, mask_ref, up_ref,
+    *refs,
+):
+    f32, bf16 = jnp.float32, jnp.bfloat16
+    d_att_blocks, refs = refs[:EVERY], refs[EVERY:]
+    normed_hbm, small_hbm, refs = refs[0], refs[1 : 1 + EVERY], refs[1 + EVERY :]
+    d_proj_ref, d_low_ref, down_grad_ref, up_grad_ref, d_att, normed, down, sems = refs
+    tokens = q_ref.shape[0]
+    scale = HD ** (-0.5)
+    me = me_ref[0]
+    bring = pltpu.make_async_copy(normed_hbm, normed, sems.at[0])
+    bring.start()
+    for j in range(EVERY):
+        d_att[j * rows : (j + 1) * rows, :] = d_att_blocks[j][...]
+    seg_row = row_ref[0:1, :]
+    for h in range(wide // HD):
+        lanes = slice(h * HD, (h + 1) * HD)
+        delta = jnp.sum(d_att[:, lanes].astype(f32) * att_ref[:, lanes], axis=1, keepdims=True)
+        delta = jnp.broadcast_to(delta, (tokens, HD)).T[0:1, :]
+        log_sum = lse_ref[h : h + 1, :]
+        d_query = jnp.zeros((tokens, HD), f32)
+        for c in range(tokens // TILE):
+            at = slice(c * TILE, (c + 1) * TILE)
+            scores = mm_nt(k_ref[at, lanes], q_ref[:, lanes]) * scale
+            same = col_ref[at, 0:1] == seg_row
+            probs = jnp.where(same, jnp.exp(jnp.where(same, scores - log_sum, 0.0)), 0.0)
+            d_probs = mm_nt(v_ref[at, lanes], d_att[:, lanes])
+            d_scores = (probs * (d_probs - delta)).astype(bf16)
+            d_value = mm(probs.astype(bf16), d_att[:, lanes])
+            d_key = mm(d_scores, q_ref[:, lanes])
+            d_query = d_query + mm(d_scores.T, k_ref[at, lanes])
+            d_proj_ref[at, wide + h * HD : wide + (h + 1) * HD] = turn(
+                d_key * scale, cos_ref[at, :], -sin_ref[at, :]
+            ).astype(bf16)
+            d_proj_ref[at, 2 * wide + h * HD : 2 * wide + (h + 1) * HD] = d_value.astype(bf16)
+        d_proj_ref[:, lanes] = turn(d_query * scale, cos_ref[...], -sin_ref[...]).astype(bf16)
+    for i in range(3):
+        part = d_proj_ref[:, i * wide : (i + 1) * wide]
+        d_low = (mm(part, up_ref[i]).astype(bf16).astype(f32) * mask_ref[...]).astype(bf16)
+        d_low_ref[:, i * SR : (i + 1) * SR] = d_low
+        up_grad_ref[i * SR : (i + 1) * SR, :] = mm(low_ref[:, i * SR : (i + 1) * SR].T, part).astype(bf16)
+    d_low_t = d_low_ref[...].T
+    bring.wait()
+    for j in range(EVERY):
+        at = pl.multiple_of((me ^ j) * wide, wide)
+        down_grad_ref[j * 3 * SR : (j + 1) * 3 * SR, :] = mm(d_low_t, normed[:, pl.ds(at, wide)]).astype(bf16)
+
+
+def attend_back(rows, me, q, k, v, att, lse, seg_col, seg_row, cosine, sine, low, mask, up, d_att_blocks, normed, small):
+    tokens, wide = q.shape
+    width = wide * EVERY
+    return pl.pallas_call(
+        functools.partial(attend_back_kernel, rows, wide),
+        in_specs=[scalars()] + [whole()] * 12 + [whole()] * EVERY + [in_place()] * (1 + EVERY),
+        out_specs=[whole()] * 4,
+        out_shape=[
+            shape_of((tokens, 3 * wide)),
+            shape_of((tokens, 3 * SR)),
+            shape_of((EVERY * 3 * SR, wide)),
+            shape_of((3 * SR, wide)),
+        ],
+        scratch_shapes=[
+            pltpu.VMEM((tokens, wide), jnp.bfloat16),
+            pltpu.VMEM((tokens, width), jnp.bfloat16),
+            pltpu.VMEM((16, 128), jnp.bfloat16),
+            pltpu.SemaphoreType.DMA((2,)),
+        ],
+        compiler_params=params(),
+        cost_estimate=cost(10 * tokens * tokens * wide, 10 << 20),
+        name="attend_back",
+    )(me, q, k, v, att, lse, seg_col, seg_row, cosine, sine, low, mask, up, *d_att_blocks, normed, *small)
+
+
+def unproject_kernel(rows, wide, me_ref, proj_ref, low_ref, *refs):
+    bf16 = jnp.bfloat16
+    w_hbm, small_hbm, (even_ref, odd_ref, weight, sems) = refs[:EVERY], refs[EVERY : 2 * EVERY], refs[2 * EVERY :]
+    me = me_ref[0]
+    copies = []
+    for j in range(EVERY):
+        at = pl.multiple_of((me ^ j) * wide, wide)
+        for i in range(3):
+            copies.append(
+                pltpu.make_async_copy(
+                    w_hbm[j].at[i], weight.at[pl.ds(at, wide), i * wide : (i + 1) * wide], sems.at[j, i]
+                )
+            )
+        copies.append(
+            pltpu.make_async_copy(
+                small_hbm[j].at[:, 0 : 3 * SR],
+                weight.at[pl.ds(at, wide), 3 * wide : 3 * wide + 3 * SR],
+                sems.at[j, 3],
+            )
+        )
+    for item in copies:
+        item.start()
+    for item in copies:
+        item.wait()
+
+    def chunk(c, _):
+        at = pl.ds(pl.multiple_of(c * TILE, TILE), TILE)
+        here = pl.ds(pl.multiple_of(c * rows, rows), rows)
+        both = jnp.concatenate([proj_ref[at, :], low_ref[at, :]], axis=1)
+        for j in range(EVERY * wide // CUT):
+            lanes = slice(j * CUT, (j + 1) * CUT)
+            value = mm_nt(both, weight[lanes, :]).astype(bf16)
+            even_ref[here, lanes] = value[:rows]
+            odd_ref[here, lanes] = value[rows:]
+        return 0
+
+    lax.fori_loop(0, EVERY * rows // TILE, chunk, 0)
+
+
+def unproject(rows, me, d_proj, d_low, w_blocks, small_blocks):
+    tokens = d_proj.shape[0]
+    wide = d_proj.shape[1] // 3
+    width = wide * EVERY
+    return pl.pallas_call(
+        functools.partial(unproject_kernel, rows, wide),
+        in_specs=[scalars()] + [whole()] * 2 + [in_place()] * (2 * EVERY),
+        out_specs=[whole()] * 2,
+        out_shape=[shape_of((tokens // 2, width))] * 2,
+        scratch_shapes=[
+            pltpu.VMEM((width, 3 * wide + 3 * SR), jnp.bfloat16),
+            pltpu.SemaphoreType.DMA((EVERY, 4)),
+        ],
+        compiler_params=params(),
+        cost_estimate=cost(2 * tokens * width * 3 * (wide + SR), 12 << 20),
+        name="unproject",
+    )(me, d_proj, d_low, *w_blocks, *small_blocks)
+
+
+def finish_kernel(hidden_ref, gain_ref, resid_grad_ref, *refs):
+    pieces, out_ref = refs[:6], refs[6]
+    d_normed = sum_pieces(*[ref[...] for ref in pieces])
+    back = norm_grad(hidden_ref[...].astype(jnp.float32), gain_ref[...], d_normed)
+    out_ref[...] = (resid_grad_ref[...] + back).astype(jnp.bfloat16)
+
+
+def finish(hidden, gain, resid_grad, pieces):
+    rows, width = hidden.shape
+    return pl.pallas_call(
+        finish_kernel,
+        grid=(1,),
+        in_specs=[whole()] * 3 + piece_specs(rows, width),
+        out_specs=whole(),
+        out_shape=shape_of((rows, width)),
+        compiler_params=params(),
+        cost_estimate=cost(20 * rows * width, 6 << 20),
+        name="finish",
+    )(hidden, gain, resid_grad, *pieces)
+
+
+def set_masks(seg, doc_sets):
+    set_token = jnp.sum(
+        jnp.where(seg[:, None] == jnp.arange(SETS)[None, :], doc_sets[0][None, :], 0), axis=1
+    )
+    return (set_token[:, None] == (jnp.arange(SR) // R)[None, :]).astype(jnp.float32)
+
+
+def after(value, gate):
+    return lax.optimization_barrier((value, gate))[0]
+
+
+def split_layer(
+    hidden_in,
+    segments,
+    routes,
+    doc_sets,
+    cotangent,
+    w_qkv,
+    w_out,
+    gain_attn,
+    gain_moe,
+    router,
+    w_gate,
+    w_up,
+    w_down,
+    a_attn,
+    b_attn,
+    exp_a_in,
+    exp_b_in,
+    exp_a_down,
+    exp_b_down,
+):
+    bf16, f32 = jnp.bfloat16, jnp.float32
+    index = lax.axis_index("fsdp")
+    me = index.astype(jnp.int32).reshape(1)
+    hidden, upstream = hidden_in[0], cotangent[0]
+    rows, width = hidden.shape
+    wide = width // EVERY
+    experts_all = w_gate.shape[0] * EVERY
+    order = index ^ jnp.arange(EVERY)
+
+    thin = jnp.concatenate([gain_attn, gain_moe, router.reshape(-1)])
+    thin = lax.all_to_all(
+        jnp.broadcast_to(thin[None], (EVERY, thin.shape[0])), "fsdp", split_axis=0, concat_axis=0, tiled=True
+    )
+    gain_one = thin[:, :wide].reshape(1, width).astype(f32)
+    gain_two = thin[:, wide : 2 * wide].reshape(1, width).astype(f32)
+    router_all = thin[:, 2 * wide :].reshape(width, experts_all)
+    router_all = jnp.pad(router_all, ((0, 0), (0, 128 - experts_all)))
+    seg_own = segments[0].astype(bf16)
+    seg_blocks = [seg_own] + [swap(seg_own, j) for j in range(1, EVERY)]
+    seg_all = jnp.concatenate(seg_blocks).astype(jnp.int32)
+    mask = set_masks(seg_all, doc_sets)
+    mask_own = mask[:rows]
+    seg_row = jnp.broadcast_to(seg_all.astype(f32)[None, :], (8, rows * EVERY))
+    seg_col = jnp.broadcast_to(seg_all.astype(f32)[:, None], (rows * EVERY, 128))
+    positions = (order[:, None] * rows + jnp.arange(rows)[None, :]).reshape(-1)
+    cosine, sine = rope_tables(positions, HD)
+    cosine, sine = jnp.concatenate([cosine, cosine], axis=1), jnp.concatenate([-sine, sine], axis=1)
+    lanes = jnp.arange(128)
+    named = jnp.any(routes[0][:, :, None] == lanes[None, None, :], axis=1).astype(f32)
+
+    hidden_blocks = gather_relative(hidden)
+    w_blocks = [
+        lax.dynamic_slice_in_dim(w_qkv, order[j] * wide, wide, axis=2) for j in range(EVERY)
+    ]
+    w_blocks = [w_blocks[0]] + [swap(w_blocks[j], j) for j in range(1, EVERY)]
+    small = jnp.concatenate([a_attn[0], a_attn[1], a_attn[2], a_attn[3], b_attn[3]], axis=1)
+    small_blocks = gather_relative(small)
+
+    queries, keys, values, normed_one, low_qkv = project(
+        me, gain_one, mask, cosine, sine, b_attn, hidden_blocks, w_blocks, small_blocks
+    )
+    out_blocks = gather_relative(after(w_out, (hidden_blocks[6], w_blocks[7], w_blocks[6])))
+    att, lse, *att_blocks = attend(rows, queries, keys, values, seg_col, seg_row)
+    att_blocks = [att_blocks[0]] + [swap(att_blocks[j], j) for j in range(1, EVERY)]
+    resid_one, normed_own, low_out, gates_own = mix(
+        me, hidden, gain_two, mask_own, router_all, named, att_blocks, out_blocks, small_blocks
+    )
+    cot_blocks = gather_relative(after(upstream, out_blocks[6]))
+    normed_blocks = gather_relative(normed_own)
+
+    weights = (w_gate, w_up, w_down, exp_a_in, exp_b_in, exp_a_down, exp_b_down)
+    state, sums = None, []
+    for k in range(w_gate.shape[0]):
+        high = (lanes == 2 * index + k).astype(f32)
+        low = (lanes == 2 * index + k + 64).astype(f32)
+        picks = jnp.stack([high + low, high, low] + [jnp.zeros_like(high)] * 5)
+        *state, grads = expert_pass(k, normed_blocks, cot_blocks, mask, picks, state, weights)
+        sums.append(sum_rep(grads).astype(f32))
+    out_even, out_odd, row_even, row_odd = state
+    row_pieces = scatter_relative(row_even, row_odd)
+    out_pieces = scatter_relative(out_even, out_odd)
+    layer_out, d_resid, out_grads, *d_att_blocks = unmix(
+        me, resid_one, upstream, gain_two, mask_own, router_all, gates_own, low_out,
+        row_pieces, out_pieces, att_blocks, out_blocks, small_blocks,
+    )
+    d_att_blocks = [d_att_blocks[0]] + [swap(d_att_blocks[j], j) for j in range(1, EVERY)]
+    out_grads = out_grads.reshape(EVERY, 2 * SR, wide)
+    d_proj, d_low, down_grads, up_grads = attend_back(
+        rows, me, queries, keys, values, att, lse, seg_col, seg_row, cosine, sine, low_qkv, mask, b_attn,
+        d_att_blocks, normed_one, small_blocks,
+    )
+    even, odd = unproject(rows, me, d_proj, d_low, w_blocks, small_blocks)
+    pieces = scatter_relative(even, odd)
+    grad_in = finish(hidden, gain_one, d_resid, pieces)
+
+    def by_parity(values):
+        pairs = values.reshape(4, 2, values.shape[0] // EVERY, wide)
+        return pairs[:, 0].reshape(-1, wide), pairs[:, 1].reshape(-1, wide)
+
+    def own_sum(values):
+        size = values.shape[0] // EVERY
+        even, got, *rest = scatter_relative(*by_parity(values))
+        return sum_pieces(even[:size], got[:size], *rest).astype(bf16)
+
+    out_sum = own_sum(out_grads.reshape(-1, wide))
+    early = sum_rep_short(jnp.concatenate([out_sum, up_grads], axis=0))
+    late = sum_rep_short(own_sum(down_grads))
+    early, late = early.astype(f32).T, late.astype(f32).T
+    cut = lambda values, i: values[:, i * SR : (i + 1) * SR]
+    grad_a = jnp.stack([cut(late, 0), cut(late, 1), cut(late, 2), cut(early, 0)])
+    grad_b = jnp.stack([cut(early, 2), cut(early, 3), cut(early, 4), cut(early, 1)])
+    at = [2 * SR, 3 * SR, 4 * SR]
+    half = w_gate.shape[2]
+    return (
+        layer_out[None],
+        grad_in[None],
+        grad_a,
+        grad_b,
+        jnp.stack([g[: at[0]].reshape(2, SR, width).transpose(0, 2, 1) for g in sums]),
+        jnp.stack([jnp.stack([g[at[1] : at[2], :half], g[at[1] : at[2], half:]]) for g in sums]),
+        jnp.stack([jnp.concatenate([g[at[2] :, :half], g[at[2] :, half:]]).T for g in sums]),
+        jnp.stack([g[at[0] : at[1]] for g in sums]),
+    )
+
+
 def solution(mesh):
+    shape = dict(mesh.shape)
+    shards = split_layer if shape == {"rep": 4, "fsdp": EVERY} else gathered_layer
     return jax.shard_map(
         shards,
         mesh=mesh,

time: 1270 us -> 659 us (0.52)
  waiting for transfers between devices: 634 us -> 268 us
  matrix products: 250 us -> 0 us
  Pallas kernels: 0 us -> 175 us
  local copies, waits for them, and re-layouts: 168 us -> 56.8 us
  blocking collectives: 103 us -> 0 us
  starting transfers between devices: 23.8 us -> 96.5 us
  other arithmetic: 65.3 us -> 46.3 us
    ppermute x0 -> x115, waiting for transfers between devices: none -> 268 us  [the longest x103 169 us: swap(): return lax.ppermute(values, 'fsdp', [(i, i ^ bits) for i in range(EVERY)])]
    dot_general x43 -> x0, matrix products: 250 us -> none  [the longest x1 22.9 us: shards(): jnp.einsum('necd,efd->necf', grads_got, w_down, preferred_element_type=jn...]
    all_gather x6 -> x0, waiting for transfers between devices: 217 us -> none  [the longest x1 125 us: shards(): lax.all_gather(w_qkv, 'fsdp', axis=1, tiled=True)]
    pallas_call x0 -> x9, Pallas kernels: none -> 175 us  [the longest x2 103 us: expert_pass(): pl.pallas_call(functools.partial(expert_kernel, k, prev is None, width, h...]
    psum x1 -> x0, waiting for transfers between devices: 174 us -> none  [shards(): lax.psum(part_down.astype(jnp.bfloat16), 'rep').astype(jnp.float32)]
    all_to_all x5 -> x1, waiting for transfers between devices: 121 us -> 0.01 us  [split_layer(): lax.all_to_all(jnp.broadcast_to(thin[None], (EVERY, thin.shape[0])), 'fsd...]
    all_gather x4 -> x0, blocking collectives: 103 us -> none  [the longest x1 74.5 us: shards(): lax.all_gather(router, 'fsdp', axis=0, tiled=True)]
    ppermute x0 -> x115, starting transfers between devices: none -> 93.2 us  [the longest x103 78.9 us: swap(): return lax.ppermute(values, 'fsdp', [(i, i ^ bits) for i in range(EVERY)])]
  transfers between devices with their start and end apart: 16 -> 116, of which waited for: 13 -> 48; matrix products, arithmetic and copies ran while one was open for 24% -> 14% of each run, Pallas kernels for 0% -> 11%
where the time goes in v2:
time: 659 us; the launch traced here: 650 us
  waiting for transfers between devices  268 us (41%)
  Pallas kernels  175 us (27%)
  starting transfers between devices  96.5 us (15%)
  local copies, waits for them, and re-layouts  56.8 us (9%)
  other arithmetic  46.3 us (7%)
  between operations  7.55 us (1%)
    ppermute x103, waiting for transfers between devices, swap(): return lax.ppermute(values, 'fsdp', [(i, i ^ bits) for i in range(EVERY)])  169 us
    pallas_call x2, Pallas kernels, expert_pass(): pl.pallas_call(functools.partial(expert_kernel, k, prev is None, width, h...  103 us
    ppermute x12, waiting for transfers between devices, rep_swap(): return lax.ppermute(values, 'rep', [(i, i ^ bits) for i in range(4)])  98.6 us
    ppermute x103, starting transfers between devices, swap(): return lax.ppermute(values, 'fsdp', [(i, i ^ bits) for i in range(EVERY)])  78.9 us
    unnamed x179, local copies, waits for them, and re-layouts  19.7 us
    convert_element_type x16, other arithmetic, add_half(): (left.astype(jnp.float32) + right.astype(jnp.float32)).astype(jnp.bfloat16)  17.8 us
    pallas_call x1, Pallas kernels, project(): pl.pallas_call(functools.partial(project_kernel, rows, width, wide), in_s...  15.3 us
    pallas_call x1, Pallas kernels, attend_back(): pl.pallas_call(functools.partial(attend_back_kernel, rows, wide), in_spec...  15.1 us
  transfers between devices with their start and end apart: 116, of which 48 were waited for; matrix products, arithmetic and copies ran while one was open for 14% of the time, Pallas kernels for 11%

profile of v2, /device:TPU:0, one launch (start us, length us, event | category | flops | bytes accessed | tf_op | source)
XLA Modules:
  0.0 649.9 jit_solution(8199744824812334591)
XLA Ops:
  26.5 14.1 %collective-permute-done.12 = bf16[64,2048]{1,0:T(8,128)(2,1)S(1)} collective-permute-done((bf16[64,2048]{1,0:T(8,128)(2,1)S(1)}, bf16[64,2048]{1,0:T(8,128)(2,1)S(1)}, u32[]{:S(2)}, u32[]{:S(2)}) %collective-permute-start.12) | collective-permute-done | bytes 262176 | tf_op jit(solution)/shard_map/ppermute | solution.py:529
  43.6 9.1 %collective-permute-done.21.refs_15_.refs_7_ = bf16[3,256,256]{2,1,0:T(8,128)(2,1)S(1)} collective-permute-done((bf16[3,256,256]{2,1,0:T(8,128)(2,1)S(1)}, bf16[3,256,256]{2,1,0:T(8,128)(2,1)S(1)}, u32[]{:S(2)}, u32[]{:S(2)}) %collective-permute-start.21) | collective-permute-done | bytes 393248 | tf_op jit(solution)/shard_map/ppermute | solution.py:529
  59.7 20.6 %collective-permute-done.3 = bf16[128]{0:T(256)(128)(2,1)S(1)} collective-permute-done((bf16[128]{0:T(256)(128)(2,1)S(1)}, bf16[128]{0:T(256)(128)(2,1)S(1)}, u32[]{:S(2)}, u32[]{:S(2)}) %collective-permute-start.3) | collective-permute-done | bytes 288 | tf_op jit(solution)/shard_map/ppermute | solution.py:529
  99.3 4.8 collective-permute-done.16.refs_10_.refs_2_
  104.4 4.5 collective-permute-done.17.refs_11_.refs_3_
  118.9 9.6 %collective-permute-done.28 = bf16[128,640]{1,0:T(8,128)(2,1)S(1)} collective-permute-done((bf16[128,640]{1,0:T(8,128)(2,1)S(1)}, bf16[128,640]{1,0:T(8,128)(2,1)S(1)}, u32[]{:S(2)}, u32[]{:S(2)}) %collective-permute-start.28) | collective-permute-done | bytes 163872 | tf_op jit(solution)/shard_map/ppermute | solution.py:529
  136.3 15.3 %project.1 = (bf16[1024,256]{1,0:T(8,128)(2,1)}, bf16[1024,256]{1,0:T(8,128)(2,1)}, bf16[1024,256]{1,0:T(8,128)(2,1)}, bf16[1024,2048]{1,0:T(8,128)(2,1)}, bf16[1024,384]{1,0:T(8,128)(2,1)}) custom-call(s32[1]{0:T(128)} %bitcast.me_ref, f32[1,2048]{1,0:T(1,128)} %bitcast.186, f32[1024,128]{1,0:T(8,128)} %compare_convert_fusion.mask_ref, ...), custom_call_target="tpu_custom_call" | custom-call | flops 4831838208 | bytes 16777216 | tf_op jit(solution)/shard_map/project/pallas_call | solution.py:667
  153.3 7.0 %attend.1 = (f32[1024,256]{1,0:T(8,128)}, f32[8,1024]{1,0:T(8,128)}, bf16[128,256]{1,0:T(8,128)(2,1)}, bf16[128,256]{1,0:T(8,128)(2,1)}, bf16[128,256]{1,0:T(8,1...) custom-call(bf16[1024,256]{1,0:T(8,128)(2,1)} %get-tuple-element.56., ...), custom_call_target="tpu_custom_call" | custom-call | flops 1073741824 | bytes 4194304 | tf_op jit(solution)/shard_map/attend/pallas_call | solution.py:707
  162.3 4.0 collective-permute-done.31.refs_2_.refs_20_
  166.3 3.9 collective-permute-done.32.refs_3_.refs_21_
  174.7 4.4 collective-permute-done.34.refs_5_.refs_23_
  180.6 3.9 collective-permute-done.35.refs_6_.refs_24_
  184.6 4.7 collective-permute-done.36.refs_7_.refs_25_
  194.4 7.2 %mix.1 = (f32[128,2048]{1,0:T(8,128)}, bf16[128,2176]{1,0:T(8,128)(2,1)}, bf16[128,128]{1,0:T(8,128)(2,1)}, f32[128,128]{1,0:T(8,128)}) custom-call(s32[1]{0:T(128)} %bitcast.me_ref, bf16[128,2048]{1,0:T(8,128)(2,1)} %bitcast.172, f32[1,2048]{1,0:T(1,128)} %bitcast.184, f32[128,128]{1,0:T(8,128)} %slice.465.mask_ref, bf16[2048,128]{1,0:T(8,128)(2,1)} %pad.4.router_ref, ...), custom_call_target="tpu_custom_call" | custom-call | flops 1073741824 | bytes 10485760 | tf_op jit(solution)/shard_map/mix/pallas_call | solution.py:771
  206.8 11.2 %collective-permute-done.56.refs_12_ = bf16[128,2048]{1,0:T(8,128)(2,1)S(1)} collective-permute-done((bf16[128,2048]{1,0:T(8,128)(2,1)}, bf16[128,2048]{1,0:T(8,128)(2,1)S(1)}, u32[]{:S(2)}, u32[]{:S(2)}) %collective-permute-start.56) | collective-permute-done | bytes 524320 | tf_op jit(solution)/shard_map/ppermute | solution.py:529
  219.4 4.2 collective-permute-done.58
  225.9 9.7 %collective-permute-done.48.refs_4_ = bf16[128,2176]{1,0:T(8,128)(2,1)S(1)} collective-permute-done((bf16[128,2176]{1,0:T(8,128)(2,1)}, bf16[128,2176]{1,0:T(8,128)(2,1)S(1)}, u32[]{:S(2)}, u32[]{:S(2)}) %collective-permute-start.48) | collective-permute-done | bytes 557088 | tf_op jit(solution)/shard_map/ppermute | solution.py:529
  239.7 5.7 collective-permute-done.51
  249.9 50.4 %expert.2 = (bf16[512,2176]{1,0:T(8,128)(2,1)}, bf16[512,2176]{1,0:T(8,128)(2,1)}, bf16[512,2048]{1,0:T(8,128)(2,1)}, bf16[512,2048]{1,0:T(8,128)(2,1)}, bf16[576,2048]{1,0:T(8,128)(2,1)}) custom-call(f32[1024,128]{1,0:T(8,128)} %compare_convert_fusion.mask_ref, f32[8,128]{1,0:T(8,128)} %stack.145.pick_ref, bf16[128,2176]{1,0:T(8,128)(2,1)} %get-tuple-element.71.refs_0_, ...), custom_call_target="tpu_custom_call" | custom-call | flops 33017561088 | bytes 41943040 | tf_op jit(solution)/shard_map/expert/pallas_call | solution.py:948
  300.4 52.1 %expert.3 = (bf16[512,2176]{1,0:T(8,128)(2,1)}, bf16[512,2176]{1,0:T(8,128)(2,1)}, bf16[512,2048]{1,0:T(8,128)(2,1)}, bf16[512,2048]{1,0:T(8,128)(2,1)}, bf16[576,2048]{1,0:T(8,128)(2,1)}) custom-call(f32[1024,128]{1,0:T(8,128)} %compare_convert_fusion.mask_ref, f32[8,128]{1,0:T(8,128)} %stack.144.pick_ref, bf16[128,2176]{1,0:T(8,128)(2,1)} %get-tuple-element.71.refs_0_, ...), custom_call_target="tpu_custom_call" | custom-call | flops 33017561088 | bytes 41943040 | tf_op jit(solution)/shard_map/expert/pallas_call | solution.py:948
  357.8 26.4 %collective-permute-done.111 = bf16[288,2048]{1,0:T(8,128)(2,1)} collective-permute-done((bf16[288,2048]{1,0:T(8,128)(2,1)}, bf16[288,2048]{1,0:T(8,128)(2,1)}, u32[]{:S(2)}, u32[]{:S(2)}) %collective-permute-start.111) | collective-permute-done | bytes 1179680 | tf_op jit(solution)/shard_map/ppermute | solution.py:576
  389.0 32.3 %collective-permute-done.107 = bf16[288,2048]{1,0:T(8,128)(2,1)} collective-permute-done((bf16[288,2048]{1,0:T(8,128)(2,1)S(1)}, bf16[288,2048]{1,0:T(8,128)(2,1)}, u32[]{:S(2)}, u32[]{:S(2)}) %collective-permute-start.107) | collective-permute-done | bytes 1179680 | tf_op jit(solution)/shard_map/ppermute | solution.py:576
  430.9 8.5 %collective-permute-done.65 = bf16[64,2048]{1,0:T(8,128)(2,1)S(1)} collective-permute-done((bf16[64,2048]{1,0:T(8,128)(2,1)S(1)}, bf16[64,2048]{1,0:T(8,128)(2,1)S(1)}, u32[]{:S(2)}, u32[]{:S(2)}) %collective-permute-start.65) | collective-permute-done | bytes 262176 | tf_op jit(solution)/shard_map/ppermute | solution.py:529
  455.5 5.0 collective-permute-done.64.refs_3_
  465.9 11.9 %unmix.1 = (bf16[128,2048]{1,0:T(8,128)(2,1)}, f32[128,2048]{1,0:T(8,128)}, bf16[2048,256]{1,0:T(8,128)(2,1)}, bf16[128,256]{1,0:T(8,128)(2,1)}, bf16[128,256]{1...) custom-call(s32[1]{0:T(128)} %bitcast.me_ref, ...), custom_call_target="tpu_custom_call" | custom-call | flops 1073741824 | bytes 14680064 | tf_op jit(solution)/shard_map/unmix/pallas_call | solution.py:1041
  482.1 10.6 %collective-permute-done.113 = bf16[144,2048]{1,0:T(8,128)(2,1)S(1)} collective-permute-done((bf16[144,2048]{1,0:T(8,128)(2,1)S(1)}, bf16[144,2048]{1,0:T(8,128)(2,1)S(1)}, u32[]{:S(2)}, u32[]{:S(2)}) %collective-permute-start.113) | collective-permute-done | bytes 589856 | tf_op jit(solution)/shard_map/ppermute | solution.py:576
  494.9 9.4 %collective-permute-done.109 = bf16[144,2048]{1,0:T(8,128)(2,1)} collective-permute-done((bf16[144,2048]{1,0:T(8,128)(2,1)S(1)}, bf16[144,2048]{1,0:T(8,128)(2,1)}, u32[]{:S(2)}, u32[]{:S(2)}) %collective-permute-start.109) | collective-permute-done | bytes 589856 | tf_op jit(solution)/shard_map/ppermute | solution.py:576
  513.2 15.1 %attend_back.1 = (bf16[1024,768]{1,0:T(8,128)(2,1)}, bf16[1024,384]{1,0:T(8,128)(2,1)}, bf16[3072,256]{1,0:T(8,128)(2,1)}, bf16[384,256]{1,0:T(8,128)(2,1)}) custom-call(s32[1]{0:T(128)} %bitcast.me_ref, bf16[1024,256]{1,0:T(8,128)(2,1)} %get-tuple-element.56.q_ref, bf16[1024,256]{1,0:T(8,128)(2,1)} %get-tuple-element.57.k_ref, ...), custom_call_target="tpu_custom_call" | custom-call | flops 2684354560 | bytes 10485760 | tf_op jit(solution)/shard_map/attend_back/pallas_call | solution.py:1125
  532.0 12.4 %unproject.1 = (bf16[512,2048]{1,0:T(8,128)(2,1)}, bf16[512,2048]{1,0:T(8,128)(2,1)}) custom-call(s32[1]{0:T(128)} %bitcast.me_ref, bf16[1024,768]{1,0:T(8,128)(2,1)} %get-tuple-element.95.proj_ref, bf16[1024,384]{1,0:T(8,128)(2,1)} %get-tuple-element.96.low_ref, bf16[3,256,256]{2,1,0:T(8,128)(2,1)} %get-tuple-element.176.refs_8_.refs_0_, ...), custom_call_target="tpu_custom_call" | custom-call | flops 4831838208 | bytes 12582912 | tf_op jit(solution)/shard_map/unproject/pallas_call | solution.py:1190
  606.0 3.7 collective-permute-done.96
  610.6 12.8 %collective-permute-done.106 = bf16[640,256]{1,0:T(8,128)(2,1)S(1)} collective-permute-done((bf16[640,256]{1,0:T(8,128)(2,1)S(1)}, bf16[640,256]{1,0:T(8,128)(2,1)S(1)}, u32[]{:S(2)}, u32[]{:S(2)}) %collective-permute-start.106) | collective-permute-done | bytes 327712 | tf_op jit(solution)/shard_map/ppermute | solution.py:576
  645.9 3.6 finish.1
  (503 shorter events, 244.2 us)
Async XLA Ops:
  1.3 55.2 %collective-permute-start = (bf16[128]{0:T(256)(128)(2,1)S(1)}, bf16[128]{0:T(256)(128)(2,1)S(1)}, u32[]{:S(2)}, u32[]{:S(2)}) collective-permute-start(bf16[128]{0:T(256)(128)(2,1)S(1)} %convert_bitcast_fusion.5), channel_id=1, source_target_pairs={{0,1},{1,0},{2,3},{3,2},{4,5},{5,4},{6,7},{7,6},{8,9},{9,8},{10,11... | collective-permute-start | bytes 776 | tf_op jit(solution)/shard_map/ppermute | solution.py:529
  1.7 56.4 %collective-permute-start.1 = (bf16[128]{0:T(256)(128)(2,1)S(1)}, bf16[128]{0:T(256)(128)(2,1)S(1)}, u32[]{:S(2)}, u32[]{:S(2)}) collective-permute-start(bf16[128]{0:T(256)(128)(2,1)S(1)} %convert_bitcast_fusion.5), channel_id=1, source_target_pairs={{0,2},{1,3},{2,0},{3,1},{4,6},{5,7},{6,4},{7,5},{8,10},{9,11},{10,... | collective-permute-start | bytes 776 | tf_op jit(solution)/shard_map/ppermute | solution.py:529
  10.2 101.7 %all-to-all-start = ((bf16[8,2,2304]{2,1,0:T(2,128)(2,1)}), bf16[8,2,2304]{2,1,0:T(2,128)(2,1)S(1)}, u32[]{:S(2)}, u32[]{:S(2)}) async-start(bf16[8,2,2304]{2,1,0:T(2,128)(2,1)} %reshape.431), calls=%async_computation | async-start | bytes 147456 | tf_op jit(solution)/shard_map/all_to_all | solution.py:1268
  53.4 39.3 %collective-permute-start.38 = (bf16[256,2048]{1,0:T(8,128)(2,1)}, bf16[256,2048]{1,0:T(8,128)(2,1)S(1)}, u32[]{:S(2)}, u32[]{:S(2)}) collective-permute-start(bf16[256,2048]{1,0:T(8,128)(2,1)} %refs_26_.2), channel_id=1, source_target_pairs={{0,2},{1,3},{2,0},{3,1},{4,6},{5,7},{6,4},{7,5},{8,10},{9,11},{10,... | collective-permute-start | bytes 3145736 | tf_op jit(solution)/shard_map/ppermute | solution.py:529
  55.1 40.2 %collective-permute-start.40 = (bf16[256,2048]{1,0:T(8,128)(2,1)}, bf16[256,2048]{1,0:T(8,128)(2,1)S(1)}, u32[]{:S(2)}, u32[]{:S(2)}) collective-permute-start(bf16[256,2048]{1,0:T(8,128)(2,1)} %refs_26_.2), channel_id=1, source_target_pairs={{0,4},{1,5},{2,6},{3,7},{4,0},{5,1},{6,2},{7,3},{8,12},{9,13},{10,... | collective-permute-start | bytes 3145736 | tf_op jit(solution)/shard_map/ppermute | solution.py:529
  58.2 23.8 %collective-permute-start.5 = (bf16[128]{0:T(256)(128)(2,1)S(1)}, bf16[128]{0:T(256)(128)(2,1)S(1)}, u32[]{:S(2)}, u32[]{:S(2)}) collective-permute-start(bf16[128]{0:T(256)(128)(2,1)S(1)} %convert_bitcast_fusion.5), channel_id=1, source_target_pairs={{0,6},{1,7},{2,4},{3,5},{4,2},{5,3},{6,0},{7,1},{8,14},{9,15},{10,... | collective-permute-start | bytes 776 | tf_op jit(solution)/shard_map/ppermute | solution.py:529
  99.3 29.2 %collective-permute-start.7 = (bf16[128,2048]{1,0:T(8,128)(2,1)}, bf16[128,2048]{1,0:T(8,128)(2,1)}, u32[]{:S(2)}, u32[]{:S(2)}) collective-permute-start(bf16[128,2048]{1,0:T(8,128)(2,1)} %bitcast.170), channel_id=1, source_target_pairs={{0,1},{1,0},{2,3},{3,2},{4,5},{5,4},{6,7},{7,6},{8,9},{9,8},{10,11... | collective-permute-start | bytes 1572872 | tf_op jit(solution)/shard_map/ppermute | solution.py:529
  133.5 60.8 %collective-permute-start.37 = (bf16[256,2048]{1,0:T(8,128)(2,1)}, bf16[256,2048]{1,0:T(8,128)(2,1)}, u32[]{:S(2)}, u32[]{:S(2)}) collective-permute-start(bf16[256,2048]{1,0:T(8,128)(2,1)} %refs_26_.2), channel_id=1, source_target_pairs={{0,1},{1,0},{2,3},{3,2},{4,5},{5,4},{6,7},{7,6},{8,9},{9,8},{10,11... | collective-permute-start | bytes 3145736 | tf_op jit(solution)/shard_map/ppermute | solution.py:529
  134.0 60.3 %collective-permute-start.39 = (bf16[256,2048]{1,0:T(8,128)(2,1)S(1)}, bf16[256,2048]{1,0:T(8,128)(2,1)}, u32[]{:S(2)}, u32[]{:S(2)}) collective-permute-start(bf16[256,2048]{1,0:T(8,128)(2,1)S(1)} %collective-permute-done.38.refs_10_.refs_28_), channel_id=1, source_target_pairs={{0,1},{1,0},{2,3},{3,2},{4,5},{5,4},{6,7},{7,6},{8,9},{9,8},{10,11... | collective-permute-start | bytes 3145736 | tf_op jit(solution)/shard_map/ppermute | solution.py:529
  134.1 60.2 %collective-permute-start.41 = (bf16[256,2048]{1,0:T(8,128)(2,1)S(1)}, bf16[256,2048]{1,0:T(8,128)(2,1)}, u32[]{:S(2)}, u32[]{:S(2)}) collective-permute-start(bf16[256,2048]{1,0:T(8,128)(2,1)S(1)} %collective-permute-done.40.refs_12_.refs_30_), channel_id=1, source_target_pairs={{0,1},{1,0},{2,3},{3,2},{4,5},{5,4},{6,7},{7,6},{8,9},{9,8},{10,11... | collective-permute-start | bytes 3145736 | tf_op jit(solution)/shard_map/ppermute | solution.py:529
  134.7 59.6 %collective-permute-start.44 = (bf16[256,2048]{1,0:T(8,128)(2,1)}, bf16[256,2048]{1,0:T(8,128)(2,1)}, u32[]{:S(2)}, u32[]{:S(2)}) collective-permute-start(bf16[256,2048]{1,0:T(8,128)(2,1)} %constant_dynamic-update-slice_fusion.4.refs_14_.refs_32_), channel_id=1, source_target_pairs={{0,1},{1,0},{2,3},{3,2},{4,5},{5,4},{6,7},{7,6},{8,9},{9,8},{10,11... | collective-permute-start | bytes 3145736 | tf_op jit(solution)/shard_map/ppermute | solution.py:529
  206.0 29.6 %collective-permute-start.48 = (bf16[128,2176]{1,0:T(8,128)(2,1)}, bf16[128,2176]{1,0:T(8,128)(2,1)S(1)}, u32[]{:S(2)}, u32[]{:S(2)}) collective-permute-start(bf16[128,2176]{1,0:T(8,128)(2,1)} %get-tuple-element.71.refs_0_), channel_id=1, source_target_pairs={{0,4},{1,5},{2,6},{3,7},{4,0},{5,1},{6,2},{7,3},{8,12},{9,13},{10,... | collective-permute-start | bytes 1671176 | tf_op jit(solution)/shard_map/ppermute | solution.py:529
  218.9 26.6 %collective-permute-start.53 = (bf16[128,2048]{1,0:T(8,128)(2,1)}, bf16[128,2048]{1,0:T(8,128)(2,1)S(1)}, u32[]{:S(2)}, u32[]{:S(2)}) collective-permute-start(bf16[128,2048]{1,0:T(8,128)(2,1)} %bitcast.19.refs_8_.cot_ref), channel_id=1, source_target_pairs={{0,1},{1,0},{2,3},{3,2},{4,5},{5,4},{6,7},{7,6},{8,9},{9,8},{10,11... | collective-permute-start | bytes 1572872 | tf_op jit(solution)/shard_map/ppermute | solution.py:529
  218.9 27.2 %collective-permute-start.55 = (bf16[128,2048]{1,0:T(8,128)(2,1)}, bf16[128,2048]{1,0:T(8,128)(2,1)S(1)}, u32[]{:S(2)}, u32[]{:S(2)}) collective-permute-start(bf16[128,2048]{1,0:T(8,128)(2,1)} %collective-permute-done.54.refs_10_), channel_id=1, source_target_pairs={{0,1},{1,0},{2,3},{3,2},{4,5},{5,4},{6,7},{7,6},{8,9},{9,8},{10,11... | collective-permute-start | bytes 1572872 | tf_op jit(solution)/shard_map/ppermute | solution.py:529
  355.0 29.1 %collective-permute-start.111 = (bf16[288,2048]{1,0:T(8,128)(2,1)}, bf16[288,2048]{1,0:T(8,128)(2,1)}, u32[]{:S(2)}, u32[]{:S(2)}) collective-permute-start(bf16[288,2048]{1,0:T(8,128)(2,1)} %dynamic-slice_bitcast_fusion), channel_id=1, source_target_pairs={{0,8},{8,0},{16,24},{24,16},{1,9},{9,1},{17,25},{25,17},{2,10},{10... | collective-permute-start | bytes 3538952 | tf_op jit(solution)/shard_map/ppermute | solution.py:576
  356.7 64.5 %collective-permute-start.107 = (bf16[288,2048]{1,0:T(8,128)(2,1)S(1)}, bf16[288,2048]{1,0:T(8,128)(2,1)}, u32[]{:S(2)}, u32[]{:S(2)}) collective-permute-start(bf16[288,2048]{1,0:T(8,128)(2,1)S(1)} %dynamic-slice_bitcast_fusion.1), channel_id=1, source_target_pairs={{0,8},{8,0},{16,24},{24,16},{1,9},{9,1},{17,25},{25,17},{2,10},{10... | collective-permute-start | bytes 3538952 | tf_op jit(solution)/shard_map/ppermute | solution.py:576
  357.3 67.6 %collective-permute-start.61 = (bf16[512,2048]{1,0:T(8,128)(2,1)}, bf16[512,2048]{1,0:T(8,128)(2,1)}, u32[]{:S(2)}, u32[]{:S(2)}) collective-permute-start(bf16[512,2048]{1,0:T(8,128)(2,1)} %get-tuple-element.78), channel_id=1, source_target_pairs={{0,1},{1,0},{2,3},{3,2},{4,5},{5,4},{6,7},{7,6},{8,9},{9,8},{10,11... | collective-permute-start | bytes 6291464 | tf_op jit(solution)/shard_map/ppermute | solution.py:529
  357.3 72.1 %collective-permute-start.68 = (bf16[512,2176]{1,0:T(8,128)(2,1)}, bf16[512,2176]{1,0:T(8,128)(2,1)S(1)}, u32[]{:S(2)}, u32[]{:S(2)}) collective-permute-start(bf16[512,2176]{1,0:T(8,128)(2,1)} %get-tuple-element.80), channel_id=1, source_target_pairs={{0,1},{1,0},{2,3},{3,2},{4,5},{5,4},{6,7},{7,6},{8,9},{9,8},{10,11... | collective-permute-start | bytes 6684680 | tf_op jit(solution)/shard_map/ppermute | solution.py:529
  386.3 38.4 %collective-permute-start.112 = (bf16[144,2048]{1,0:T(8,128)(2,1)S(1)}, bf16[144,2048]{1,0:T(8,128)(2,1)S(1)}, u32[]{:S(2)}, u32[]{:S(2)}) collective-permute-start(bf16[144,2048]{1,0:T(8,128)(2,1)S(1)} %dynamic-slice_bitcast_fusion.2), channel_id=1, source_target_pairs={{0,16},{8,24},{16,0},{24,8},{1,17},{9,25},{17,1},{25,9},{2,18},{10... | collective-permute-start | bytes 1769480 | tf_op jit(solution)/shard_map/ppermute | solution.py:576
  423.1 28.1 %collective-permute-start.108 = (bf16[144,2048]{1,0:T(8,128)(2,1)S(1)}, bf16[144,2048]{1,0:T(8,128)(2,1)S(1)}, u32[]{:S(2)}, u32[]{:S(2)}) collective-permute-start(bf16[144,2048]{1,0:T(8,128)(2,1)S(1)} %dynamic-slice_bitcast_fusion.3), channel_id=1, source_target_pairs={{0,16},{8,24},{16,0},{24,8},{1,17},{9,25},{17,1},{25,9},{2,18},{10... | collective-permute-start | bytes 1769480 | tf_op jit(solution)/shard_map/ppermute | solution.py:576
  426.5 24.7 %collective-permute-start.62 = (bf16[64,2048]{1,0:T(8,128)(2,1)S(1)}, bf16[64,2048]{1,0:T(8,128)(2,1)S(1)}, u32[]{:S(2)}, u32[]{:S(2)}) collective-permute-start(bf16[64,2048]{1,0:T(8,128)(2,1)S(1)} %get-tuple-element.167), channel_id=1, source_target_pairs={{0,2},{1,3},{2,0},{3,1},{4,6},{5,7},{6,4},{7,5},{8,10},{9,11},{10,... | collective-permute-start | bytes 786440 | tf_op jit(solution)/shard_map/ppermute | solution.py:529
  451.2 41.4 %collective-permute-start.113 = (bf16[144,2048]{1,0:T(8,128)(2,1)S(1)}, bf16[144,2048]{1,0:T(8,128)(2,1)S(1)}, u32[]{:S(2)}, u32[]{:S(2)}) collective-permute-start(bf16[144,2048]{1,0:T(8,128)(2,1)S(1)} %fusion.2), channel_id=1, source_target_pairs={{0,16},{8,24},{16,0},{24,8},{1,17},{9,25},{17,1},{25,9},{2,18},{10... | collective-permute-start | bytes 1769480 | tf_op jit(solution)/shard_map/ppermute | solution.py:576
  460.5 43.8 %collective-permute-start.109 = (bf16[144,2048]{1,0:T(8,128)(2,1)S(1)}, bf16[144,2048]{1,0:T(8,128)(2,1)}, u32[]{:S(2)}, u32[]{:S(2)}) collective-permute-start(bf16[144,2048]{1,0:T(8,128)(2,1)S(1)} %fusion.3), channel_id=1, source_target_pairs={{0,16},{8,24},{16,0},{24,8},{1,17},{9,25},{17,1},{25,9},{2,18},{10... | collective-permute-start | bytes 1769480 | tf_op jit(solution)/shard_map/ppermute | solution.py:576
  477.7 27.3 %collective-permute-start.75 = (bf16[128,256]{1,0:T(8,128)(2,1)}, bf16[128,256]{1,0:T(8,128)(2,1)S(1)}, u32[]{:S(2)}, u32[]{:S(2)}) collective-permute-start(bf16[128,256]{1,0:T(8,128)(2,1)} %get-tuple-element.87), channel_id=1, source_target_pairs={{0,1},{1,0},{2,3},{3,2},{4,5},{5,4},{6,7},{7,6},{8,9},{9,8},{10,11... | collective-permute-start | bytes 196616 | tf_op jit(solution)/shard_map/ppermute | solution.py:529
  477.8 27.3 %collective-permute-start.76 = (bf16[128,256]{1,0:T(8,128)(2,1)}, bf16[128,256]{1,0:T(8,128)(2,1)S(1)}, u32[]{:S(2)}, u32[]{:S(2)}) collective-permute-start(bf16[128,256]{1,0:T(8,128)(2,1)} %get-tuple-element.88), channel_id=1, source_target_pairs={{0,2},{1,3},{2,0},{3,1},{4,6},{5,7},{6,4},{7,5},{8,10},{9,11},{10,... | collective-permute-start | bytes 196616 | tf_op jit(solution)/shard_map/ppermute | solution.py:529
  479.2 27.6 %collective-permute-start.77 = (bf16[128,256]{1,0:T(8,128)(2,1)}, bf16[128,256]{1,0:T(8,128)(2,1)S(1)}, u32[]{:S(2)}, u32[]{:S(2)}) collective-permute-start(bf16[128,256]{1,0:T(8,128)(2,1)} %get-tuple-element.89), channel_id=1, source_target_pairs={{0,3},{1,2},{2,1},{3,0},{4,7},{5,6},{6,5},{7,4},{8,11},{9,10},{10,... | collective-permute-start | bytes 196616 | tf_op jit(solution)/shard_map/ppermute | solution.py:529
  492.6 35.6 %collective-permute-start.98 = (bf16[1024,256]{1,0:T(8,128)(2,1)}, bf16[1024,256]{1,0:T(8,128)(2,1)}, u32[]{:S(2)}, u32[]{:S(2)}) collective-permute-start(bf16[1024,256]{1,0:T(8,128)(2,1)} %bitcast.32), channel_id=1, source_target_pairs={{0,1},{1,0},{2,3},{3,2},{4,5},{5,4},{6,7},{7,6},{8,9},{9,8},{10,11... | collective-permute-start | bytes 1572872 | tf_op jit(solution)/shard_map/ppermute | solution.py:529
  510.4 47.6 %collective-permute-start.114 = (bf16[288,2048]{1,0:T(8,128)(2,1)S(1)}, bf16[288,2048]{1,0:T(8,128)(2,1)}, u32[]{:S(2)}, u32[]{:S(2)}) collective-permute-start(bf16[288,2048]{1,0:T(8,128)(2,1)S(1)} %bitcast.152), channel_id=1, source_target_pairs={{0,8},{8,0},{16,24},{24,16},{1,9},{9,1},{17,25},{25,17},{2,10},{10... | collective-permute-start | bytes 3538952 | tf_op jit(solution)/shard_map/ppermute | solution.py:576
  510.5 54.3 %collective-permute-start.110 = (bf16[288,2048]{1,0:T(8,128)(2,1)S(1)}, bf16[288,2048]{1,0:T(8,128)(2,1)}, u32[]{:S(2)}, u32[]{:S(2)}) collective-permute-start(bf16[288,2048]{1,0:T(8,128)(2,1)S(1)} %bitcast.154), channel_id=1, source_target_pairs={{0,8},{8,0},{16,24},{24,16},{1,9},{9,1},{17,25},{25,17},{2,10},{10... | collective-permute-start | bytes 3538952 | tf_op jit(solution)/shard_map/ppermute | solution.py:576
  544.4 79.1 %collective-permute-start.82 = (bf16[512,2048]{1,0:T(8,128)(2,1)}, bf16[512,2048]{1,0:T(8,128)(2,1)}, u32[]{:S(2)}, u32[]{:S(2)}) collective-permute-start(bf16[512,2048]{1,0:T(8,128)(2,1)} %get-tuple-element.98), channel_id=1, source_target_pairs={{0,1},{1,0},{2,3},{3,2},{4,5},{5,4},{6,7},{7,6},{8,9},{9,8},{10,11... | collective-permute-start | bytes 6291464 | tf_op jit(solution)/shard_map/ppermute | solution.py:529
  554.6 31.4 %collective-permute-start.89 = (bf16[1536,256]{1,0:T(8,128)(2,1)}, bf16[1536,256]{1,0:T(8,128)(2,1)}, u32[]{:S(2)}, u32[]{:S(2)}) collective-permute-start(bf16[1536,256]{1,0:T(8,128)(2,1)} %bitcast.24), channel_id=1, source_target_pairs={{0,1},{1,0},{2,3},{3,2},{4,5},{5,4},{6,7},{7,6},{8,9},{9,8},{10,11... | collective-permute-start | bytes 2359304 | tf_op jit(solution)/shard_map/ppermute | solution.py:529
  557.2 45.7 %collective-permute-start.105 = (bf16[640,256]{1,0:T(8,128)(2,1)}, bf16[640,256]{1,0:T(8,128)(2,1)}, u32[]{:S(2)}, u32[]{:S(2)}) collective-permute-start(bf16[640,256]{1,0:T(8,128)(2,1)} %pad_maximum_fusion.8), channel_id=1, source_target_pairs={{0,8},{8,0},{16,24},{24,16},{1,9},{9,1},{17,25},{25,17},{2,10},{10... | collective-permute-start | bytes 983048 | tf_op jit(solution)/shard_map/ppermute | solution.py:576
  (162 other events, 1773.1 us)

commit v3 on v2

--- a/solution.py
+++ b/solution.py
@@ -529,159 +529,232 @@
     return lax.ppermute(values, "fsdp", [(i, i ^ bits) for i in range(EVERY)])
 
 
+def tie(*values):
+    return lax.optimization_barrier(values)
+
+
+def gather_first(values):
+    return [values, swap(values, 2), swap(values, 4)]
+
+
+def gather_second(values, side, over):
+    half = values.shape[0] // 2
+    far = [swap(side[:half], 4), swap(over[half:], 2)]
+    return far, swap(values, 1), swap(jnp.concatenate([side, over], axis=0), 1)
+
+
+def gather_third(first, far, own, pair):
+    far = jnp.concatenate(far, axis=0)
+    return [*first, far, own, pair, swap(far, 1)]
+
+
+GATHERED = 7
+
+
+def blocks_of(refs):
+    values, side, over, far, own, pair, last = refs
+    rows = values.shape[0]
+    return [values, own, side, pair.at[0:rows], over, pair.at[rows : 2 * rows], far, last]
+
+
 def gather_relative(values):
-    half = values.shape[0] // 2
-    side, over = swap(values, 2), swap(values, 4)
-    far = jnp.concatenate([swap(side[:half], 4), swap(over[half:], 2)], axis=0)
-    mine = [values, side, over, far]
-    other = [swap(block, 1) for block in mine]
-    return [mine[0], other[0], mine[1], other[1], mine[2], other[2], mine[3], other[3]]
+    first = gather_first(values)
+    return gather_third(first, *gather_second(*first))
 
 
 def add_half(left, right):
     return (left.astype(jnp.float32) + right.astype(jnp.float32)).astype(jnp.bfloat16)
 
 
-def scatter_relative(even, odd):
+def scatter_second(even, got):
     rows = even.shape[0] // 4
     half = rows // 2
+    far = 3 * rows
+    return [
+        swap(add_half(even[far : far + half], got[far : far + half]), 2),
+        swap(add_half(even[far + half :], got[far + half :]), 4),
+    ]
+
+
+def scatter_third(even, got, far_side, far_over):
+    rows = even.shape[0] // 4
+    half = rows // 2
+    f32 = jnp.float32
+    side = even[rows : 2 * rows].astype(f32) + got[rows : 2 * rows].astype(f32)
+    over = even[2 * rows : 3 * rows].astype(f32) + got[2 * rows : 3 * rows].astype(f32)
+    side = jnp.concatenate([side[:half], side[half:] + far_over.astype(f32)], axis=0)
+    over = jnp.concatenate([over[:half] + far_side.astype(f32), over[half:]], axis=0)
+    return even, got, swap(side.astype(jnp.bfloat16), 2), swap(over.astype(jnp.bfloat16), 4)
+
+
+def scatter_relative(even, odd):
     got = swap(odd, 1)
-
-    def pair(start):
-        return add_half(even[start : start + half], got[start : start + half])
-
-    far_side = swap(pair(3 * rows), 2)
-    far_over = swap(pair(3 * rows + half), 4)
-    side_top = swap(pair(rows), 2)
-    over_low = swap(pair(2 * rows + half), 4)
-    side_low = swap(add_half(pair(rows + half), far_over), 2)
-    over_top = swap(add_half(pair(2 * rows), far_side), 4)
-    return even, got, side_top, side_low, over_top, over_low
-
-
-def sum_pieces(even, got, side_top, side_low, over_top, over_low):
-    f32 = jnp.float32
-    top = side_top.astype(f32) + over_top.astype(f32)
-    low = side_low.astype(f32) + over_low.astype(f32)
-    return even.astype(f32) + got.astype(f32) + jnp.concatenate([top, low], axis=0)
+    return scatter_third(even, got, *scatter_second(even, got))
+
+
+def sum_pieces(*pieces):
+    return sum([piece.astype(jnp.float32) for piece in pieces[1:]], pieces[0].astype(jnp.float32))
+
+
+PIECES = 4
 
 
 def piece_specs(rows, columns, at=0):
-    return [pl.BlockSpec((rows, columns), lambda i: (0, at))] * 2 + [
-        pl.BlockSpec((rows // 2, columns), lambda i: (0, at))
-    ] * 4
+    return [pl.BlockSpec((rows, columns), lambda i: (0, at))] * PIECES
 
 
 def rep_swap(values, bits):
     return lax.ppermute(values, "rep", [(i, i ^ bits) for i in range(4)])
 
 
-def pick(pair, index):
-    return lax.dynamic_index_in_dim(pair, index, 0, keepdims=False)
-
-
-def joined(own, other, index):
-    return jnp.where(index == 0, jnp.stack([own, other]), jnp.stack([other, own]))
-
-
-def sum_rep(values):
-    where = lax.axis_index("rep")
-    low_bit, high_bit = where % 2, where // 2
-    rows, columns = values.shape
-    halves = values.reshape(2, rows // 2, columns)
-    half = add_half(pick(halves, low_bit), rep_swap(pick(halves, 1 - low_bit), 1))
-    parts = half.reshape(2, rows // 4, columns)
-    part = add_half(pick(parts, high_bit), rep_swap(pick(parts, 1 - high_bit), 2))
-    half = joined(part, rep_swap(part, 2), high_bit).reshape(rows // 2, columns)
-    return joined(half, rep_swap(half, 1), low_bit).reshape(rows, columns)
-
-
-def sum_rep_short(values):
-    values = add_half(values, rep_swap(values, 1))
-    return add_half(values, rep_swap(values, 2))
-
-
 def turn(values, cosine, signed_sine):
     return values * cosine + pltpu.roll(values, HD // 2, 1) * signed_sine
 
 
+SPOT = 16
+
+
+def relayout_kernel(wide, source_ref, out_ref):
+    for j in range(EVERY):
+        out_ref[j, 0] = source_ref[0, :, j * wide : (j + 1) * wide]
+
+
+def by_columns(values, wide):
+    count, rows, width = values.shape
+    half = rows // 2
+    return pl.pallas_call(
+        functools.partial(relayout_kernel, wide),
+        grid=(count, 2),
+        in_specs=[pl.BlockSpec((1, half, width), lambda i, j: (i, j, 0))],
+        out_specs=pl.BlockSpec((EVERY, 1, half, wide), lambda i, j: (0, i, j, 0)),
+        out_shape=shape_of((EVERY, count, rows, wide)),
+        cost_estimate=cost(1 << 20, 1 << 16),
+        name="by_columns",
+    )(values)
+
+
 def project_kernel(
     rows, width, wide,
-    me_ref, gain_ref, mask_ref, cos_ref, sin_ref, up_ref, *refs,
+    me_ref, sets_ref, cos_ref, sin_ref, up_ref, *refs,
 ):
     f32, bf16 = jnp.float32, jnp.bfloat16
-    hidden_hbm, w_hbm, small_hbm = refs[:EVERY], refs[EVERY : 2 * EVERY], refs[2 * EVERY : 3 * EVERY]
-    q_ref, k_ref, v_ref, normed_ref, low_ref, hidden, weight, down, sems = refs[3 * EVERY :]
-    me = me_ref[0]
+    hidden_hbm, given, w_hbm = blocks_of(refs[:GATHERED]), blocks_of(refs[GATHERED : 2 * GATHERED]), refs[2 * GATHERED]
+    refs = refs[2 * GATHERED + 1 :]
+    q_ref, k_ref, v_ref, normed_ref, low_ref, mask_ref, col_ref, row_ref, gains_ref, router_ref, *refs = refs
+    hidden, extra, weight, down, sems, w_sems = refs
+    me, step = me_ref[0], pl.program_id(0)
+    thin = 3 * SR
     copies = []
     for j in range(EVERY):
         at = pl.multiple_of((me ^ j) * wide, wide)
+        here = slice(j * rows, (j + 1) * rows)
         copies.append(
             [
-                pltpu.make_async_copy(hidden_hbm[j], hidden.at[j * rows : (j + 1) * rows], sems.at[j, 0]),
+                pltpu.make_async_copy(hidden_hbm[j], hidden.at[here], sems.at[j, 0]),
+                pltpu.make_async_copy(given[j].at[:, 2 * thin :], extra.at[here], sems.at[j, 1]),
                 pltpu.make_async_copy(
-                    small_hbm[j].at[:, 0 : 3 * SR], down.at[pl.ds(at, wide), :], sems.at[j, 1]
+                    given[j].at[:, 0:thin], down.at[pl.ds(at, rows), :], sems.at[j, 2]
+                ),
+                pltpu.make_async_copy(
+                    given[j].at[:, thin : 2 * thin], down.at[pl.ds(at + rows, rows), :], sems.at[j, 3]
                 ),
             ]
-            + [
-                pltpu.make_async_copy(
-                    w_hbm[j].at[i], weight.at[pl.ds(at, wide), i * wide : (i + 1) * wide], sems.at[j, 2 + i]
-                )
-                for i in range(3)
-            ]
         )
-    for group in copies:
-        for item in group:
+    w_copies = [
+        pltpu.make_async_copy(
+            w_hbm.at[j, i], weight.at[j * wide : (j + 1) * wide, i * wide : (i + 1) * wide], w_sems.at[j, i]
+        )
+        for i in range(3)
+        for j in range(EVERY)
+    ]
+
+    @pl.when(step == 0)
+    def _():
+        for which in (1, 0, 2, 3):
+            for group in copies:
+                group[which].start()
+        for item in w_copies:
             item.start()
-    for group in copies:
-        for item in group:
+        for group in copies:
+            group[1].wait()
+        for j in range(EVERY):
+            at = pl.multiple_of((me ^ j) * wide, wide)
+            for part in range(wide // rows):
+                spot = pl.multiple_of(at + part * rows, rows)
+                router_ref[pl.ds(spot, rows), :] = extra[j * rows : (j + 1) * rows, part * 128 : (part + 1) * 128]
+                for i in range(2):
+                    line = extra[j * rows : j * rows + 16, 256:384].astype(f32)
+                    gains_ref[i : i + 1, pl.ds(spot, rows)] = line[2 * i + part : 2 * i + part + 1, :]
+        for group in copies:
+            for which in (0, 2, 3):
+                group[which].wait()
+        for item in w_copies:
             item.wait()
-    gain = gain_ref[...]
-
-    def chunk(c, _):
-        at = pl.ds(pl.multiple_of(c * TILE, TILE), TILE)
-        values = hidden[at, :].astype(f32)
-        scale = lax.rsqrt(jnp.mean(values * values, axis=1, keepdims=True) + EPSILON)
-        normed = (values * scale * gain).astype(bf16)
-        normed_ref[at, :] = normed
-        mask = mask_ref[at, :]
-        low = (mm(normed, down[...]) * jnp.concatenate([mask] * 3, axis=1)).astype(bf16)
-        low_ref[at, :] = low
-        cosine, sine = cos_ref[at, :], sin_ref[at, :]
-        for i, ref in enumerate((q_ref, k_ref, v_ref)):
-            proj = mm(normed, weight[:, i * wide : (i + 1) * wide]) + mm_nt(
-                low[:, i * SR : (i + 1) * SR], up_ref[i]
-            )
-            for h in range(wide // HD):
-                part = proj[:, h * HD : (h + 1) * HD]
-                ref[at, h * HD : (h + 1) * HD] = (turn(part, cosine, sine) if i < 2 else part).astype(bf16)
-        return 0
-
-    lax.fori_loop(0, EVERY * rows // TILE, chunk, 0)
-
-
-def project(me, gain, mask, cosine, sine, up, hidden_blocks, w_blocks, small_blocks):
-    rows, width = hidden_blocks[0].shape
+
+    at = pl.ds(pl.multiple_of(step * TILE, TILE), TILE)
+    seg = jnp.broadcast_to(extra[at, 0:1].astype(f32), (TILE, 128))
+    col_ref[...] = seg
+    row_ref[...] = seg.T[0:8, :]
+    chosen = jnp.zeros_like(seg)
+    for i in range(SETS):
+        chosen = jnp.where(seg == float(i), sets_ref[0, i].astype(f32), chosen)
+    lane_set = (lax.broadcasted_iota(jnp.int32, (TILE, SR), 1) // R).astype(f32)
+    mask = (chosen == lane_set).astype(f32)
+    mask_ref[...] = mask
+    values = hidden[at, :].astype(f32)
+    scale = lax.rsqrt(jnp.mean(values * values, axis=1, keepdims=True) + EPSILON)
+    normed = (values * scale * gains_ref[0:1, :]).astype(bf16)
+    normed_ref[...] = normed
+    low = (mm(normed, down[...]) * jnp.concatenate([mask] * 3, axis=1)).astype(bf16)
+    low_ref[...] = low
+    cosine, sine = cos_ref[...], sin_ref[...]
+    for i, ref in enumerate((q_ref, k_ref, v_ref)):
+        proj = mm(normed, weight[:, i * wide : (i + 1) * wide]) + mm_nt(
+            low[:, i * SR : (i + 1) * SR], up_ref[i]
+        )
+        for h in range(wide // HD):
+            part = proj[:, h * HD : (h + 1) * HD]
+            ref[:, h * HD : (h + 1) * HD] = (turn(part, cosine, sine) if i < 2 else part).astype(bf16)
+
+
+def by_tile(rows, columns):
+    return pl.BlockSpec((rows, columns), lambda i: (i, 0))
+
+
+def project(me, sets, cosine, sine, up, hidden_given, given, w_got):
+    rows, width = hidden_given[0].shape
     wide = width // EVERY
     tokens = rows * EVERY
+    f32 = jnp.float32
     return pl.pallas_call(
         functools.partial(project_kernel, rows, width, wide),
-        in_specs=[scalars()] + [whole()] * 5 + [in_place()] * (3 * EVERY),
-        out_specs=[whole()] * 5,
-        out_shape=[shape_of((tokens, wide))] * 3 + [shape_of((tokens, width)), shape_of((tokens, 3 * SR))],
+        grid=(tokens // TILE,),
+        in_specs=[scalars(), scalars(), by_tile(TILE, 128), by_tile(TILE, 128), whole()] + [in_place()] * (2 * GATHERED + 1),
+        out_specs=[by_tile(TILE, wide)] * 3
+        + [by_tile(TILE, width), by_tile(TILE, 3 * SR), by_tile(TILE, SR), by_tile(TILE, 128)]
+        + [
+            pl.BlockSpec((8, TILE), lambda i: (0, i)),
+            pl.BlockSpec((8, width), lambda i: (0, 0)),
+            pl.BlockSpec((width, 128), lambda i: (0, 0)),
+        ],
+        out_shape=[shape_of((tokens, wide))] * 3
+        + [shape_of((tokens, width)), shape_of((tokens, 3 * SR)), shape_of((tokens, SR), f32)]
+        + [shape_of((tokens, 128), f32), shape_of((8, tokens), f32), shape_of((8, width), f32), shape_of((width, 128))],
         scratch_shapes=[
             pltpu.VMEM((tokens, width), jnp.bfloat16),
+            pltpu.VMEM((tokens, 384), jnp.bfloat16),
             pltpu.VMEM((width, 3 * wide), jnp.bfloat16),
             pltpu.VMEM((width, 3 * SR), jnp.bfloat16),
-            pltpu.SemaphoreType.DMA((EVERY, 5)),
+            pltpu.SemaphoreType.DMA((EVERY, 4)),
+            pltpu.SemaphoreType.DMA((EVERY, 3)),
         ],
         compiler_params=params(),
-        cost_estimate=cost(2 * tokens * width * 3 * (wide + SR), 16 << 20),
+        cost_estimate=cost(1 << 20, 1 << 16),
         name="project",
-    )(me, gain, mask, cosine, sine, up, *hidden_blocks, *w_blocks, *small_blocks)
-
-
-def attend_kernel(rows, q_ref, k_ref, v_ref, col_ref, row_ref, att_ref, lse_ref, *outs):
+    )(me, sets, cosine, sine, up, *hidden_given, *given, w_got)
+
+
+def attend_kernel(rows, me_ref, q_ref, k_ref, v_ref, col_ref, row_ref, att_ref, lse_ref, send_ref):
     f32, bf16 = jnp.float32, jnp.bfloat16
     scale = HD ** (-0.5)
     seg_row = row_ref[0:1, :]
@@ -699,62 +772,79 @@
             log_sum = jnp.broadcast_to(top + jnp.log(total), (TILE, HD))
             lse_ref[h : h + 1, at] = log_sum.T[0:1, :]
             for part in range(TILE // rows):
-                outs[c * (TILE // rows) + part][:, lanes] = att[part * rows : (part + 1) * rows].astype(bf16)
-
-
-def attend(rows, queries, keys, values, seg_col, seg_row):
+                j = c * (TILE // rows) + part
+                send_ref[me_ref[0] ^ j, :, lanes] = att[part * rows : (part + 1) * rows].astype(bf16)
+
+
+def attend(rows, me, queries, keys, values, seg_col, seg_row):
     tokens, wide = queries.shape
     return pl.pallas_call(
         functools.partial(attend_kernel, rows),
-        in_specs=[whole()] * 5,
-        out_specs=[whole()] * (2 + EVERY),
-        out_shape=[shape_of((tokens, wide), jnp.float32), shape_of((8, tokens), jnp.float32)]
-        + [shape_of((rows, wide))] * EVERY,
+        in_specs=[scalars()] + [whole()] * 5,
+        out_specs=[whole()] * 3,
+        out_shape=[
+            shape_of((tokens, wide), jnp.float32),
+            shape_of((8, tokens), jnp.float32),
+            shape_of((EVERY, rows, wide)),
+        ],
         compiler_params=params(),
-        cost_estimate=cost(4 * tokens * tokens * wide, 4 << 20),
+        cost_estimate=cost(1 << 20, 1 << 16),
         name="attend",
-    )(queries, keys, values, seg_col, seg_row)
-
-
-def mix_kernel(
-    wide,
-    me_ref, hidden_ref, gain_ref, mask_ref, router_ref, named_ref, *refs,
-):
-    f32, bf16 = jnp.float32, jnp.bfloat16
-    att_ref, w_hbm, small_hbm = refs[:EVERY], refs[EVERY : 2 * EVERY], refs[2 * EVERY : 3 * EVERY]
-    resid_ref, normed_ref, low_ref, gates_ref, weight, down, up, sems = refs[3 * EVERY :]
-    me = me_ref[0]
-    width = hidden_ref.shape[1]
+    )(me, queries, keys, values, seg_col, seg_row)
+
+
+def output_copies(me, wide, given, weight, down, up, sems):
+    width = weight.shape[1]
     copies = []
     for j in range(EVERY):
         at = pl.multiple_of((me ^ j) * wide, wide)
         here = slice(j * wide, (j + 1) * wide)
         copies.append(
             [
-                pltpu.make_async_copy(small_hbm[j].at[:, 3 * SR : 4 * SR], down.at[here, :], sems.at[j, 0]),
-                pltpu.make_async_copy(
-                    small_hbm[j].at[:, 4 * SR : 5 * SR], up.at[pl.ds(at, wide), :], sems.at[j, 1]
-                ),
-                pltpu.make_async_copy(w_hbm[j], weight.at[here, :], sems.at[j, 2]),
+                pltpu.make_async_copy(given[j].at[:, width : width + SR], down.at[here, :], sems.at[j, 0]),
+                pltpu.make_async_copy(given[j].at[:, width + SR :], up.at[pl.ds(at, wide), :], sems.at[j, 1]),
+                pltpu.make_async_copy(given[j].at[:, 0:width], weight.at[here, :], sems.at[j, 2]),
             ]
         )
+    return copies
+
+
+def output_scratch(width):
+    return [
+        pltpu.VMEM((width, width), jnp.bfloat16),
+        pltpu.VMEM((width, SR), jnp.bfloat16),
+        pltpu.VMEM((width, SR), jnp.bfloat16),
+        pltpu.SemaphoreType.DMA((EVERY, 3)),
+    ]
+
+
+def mix_kernel(
+    wide,
+    me_ref, hidden_ref, gains_ref, mask_ref, router_ref, named_ref, att_ref, *refs,
+):
+    f32, bf16 = jnp.float32, jnp.bfloat16
+    given = blocks_of(refs[:GATHERED])
+    resid_ref, normed_ref, low_ref, gates_ref, weight, down, up, sems = refs[GATHERED:]
+    me = me_ref[0]
+    width = hidden_ref.shape[1]
+    copies = output_copies(me, wide, given, weight, down, up, sems)
     for part in range(3):
         for group in copies:
             group[part].start()
     for part in range(2):
         for group in copies:
             group[part].wait()
-    att = jnp.concatenate([ref[...] for ref in att_ref], axis=1)
-    low = (mm(att, down[...]) * mask_ref[...]).astype(bf16)
+    blocks = [att_ref[me ^ j] for j in range(EVERY)]
+    low = (mm(jnp.concatenate(blocks, axis=1), down[...]) * mask_ref[...]).astype(bf16)
     low_ref[...] = low
     total = mm_nt(low, up[...])
     for j in range(EVERY):
         copies[j][2].wait()
-        total = total + mm(att_ref[j][...], weight[j * wide : (j + 1) * wide, :])
+        total = total + mm(blocks[j], weight[j * wide : (j + 1) * wide, :])
     resid = hidden_ref[...].astype(f32) + total
     resid_ref[...] = resid
     scale = lax.rsqrt(jnp.mean(resid * resid, axis=1, keepdims=True) + EPSILON)
-    normed = (resid * scale * gain_ref[...]).astype(bf16)
+    normed = (resid * scale * gains_ref[1:2, :]).astype(bf16)
     normed_ref[:, 0:width] = normed
     logits = jnp.where(named_ref[...] > 0.5, mm(normed, router_ref[...]), MASKED)
     share = jnp.exp(logits - jnp.max(logits, axis=1, keepdims=True)) * named_ref[...]
@@ -764,40 +854,38 @@
     normed_ref[:, width : width + 128] = (high + pltpu.roll(gates - high, 64, 1)).astype(bf16)
 
 
-def mix(me, hidden, gain, mask, router, named, att_blocks, w_blocks, small_blocks):
+def mix(me, hidden, gains, mask, router, named, att_got, given):
     rows, width = hidden.shape
     wide = width // EVERY
     f32 = jnp.float32
     return pl.pallas_call(
         functools.partial(mix_kernel, wide),
-        in_specs=[scalars()] + [whole()] * 5 + [whole()] * EVERY + [in_place()] * (2 * EVERY),
+        grid=(1,),
+        in_specs=[scalars(), whole(), whole(), pl.BlockSpec((rows, SR), lambda i: (0, 0))]
+        + [whole()] * 3
+        + [in_place()] * GATHERED,
         out_specs=[whole()] * 4,
         out_shape=[shape_of((rows, width), f32), shape_of((rows, width + 128)), shape_of((rows, SR)),
                    shape_of((rows, 128), f32)],
-        scratch_shapes=[
-            pltpu.VMEM((width, width), jnp.bfloat16),
-            pltpu.VMEM((width, SR), jnp.bfloat16),
-            pltpu.VMEM((width, SR), jnp.bfloat16),
-            pltpu.SemaphoreType.DMA((EVERY, 3)),
-        ],
+        scratch_shapes=output_scratch(width),
         compiler_params=params(),
-        cost_estimate=cost(2 * rows * width * width, 10 << 20),
+        cost_estimate=cost(1 << 20, 1 << 16),
         name="mix",
-    )(me, hidden, gain, mask, router, named, *att_blocks, *w_blocks, *small_blocks)
-
-
-def expert_kernel(k, first, width, hidden, blocks, mask_ref, pick_ref, *refs):
+    )(me, hidden, gains, mask, router, named, att_got, *given)
+
+
+def expert_kernel(k, first, width, hidden, blocks, where_ref, mask_ref, pick_ref, *refs):
     f32, bf16 = jnp.float32, jnp.bfloat16
-    rows_hbm, cot_hbm, refs = refs[:blocks], refs[blocks : 2 * blocks], refs[2 * blocks :]
+    rows_hbm, cot_hbm = blocks_of(refs[:GATHERED]), blocks_of(refs[GATHERED : 2 * GATHERED])
+    refs = refs[2 * GATHERED :]
     if not first:
-        prev_out, prev_row, refs = refs[:2], refs[2:4], refs[4:]
+        prev_out, refs = refs[:2], refs[2:]
     (
         w_gate_hbm, w_up_hbm, w_down_hbm, a_in_hbm, b_in_hbm, a_down_hbm, b_down_hbm,
-        out_even, out_odd, row_even, row_odd, grad_ref,
-        rows_s, cot_s, w_in, w_down, silu_s, slope_s,
-        g_a_in, g_b_down, g_b_in, g_a_down, sems, block_sems,
+        out_even, out_odd, d_all_ref, extra_ref, *refs,
     ) = refs
-    out_refs, row_refs = (out_even, out_odd), (row_even, row_odd)
+    *grad_refs, rows_s, cot_s, w_in, w_down, silu_s, slope_s, g_a_in, g_b_down, g_b_in, g_a_down, packed, sems, block_sems = refs
+    out_refs = (out_even, out_odd)
     step = pl.program_id(0)
     part = TILE // 2
     low_at, thin_at = 2 * hidden, width
@@ -881,12 +969,7 @@
             out_refs[i][:, at] = value.astype(bf16)
         d_gate = d_gate + jnp.sum(cot * out, axis=1, keepdims=True)
     high = d_gate.astype(bf16).astype(f32)
-    extra = high * pick_ref[1:2, :] + (d_gate - high) * pick_ref[2:3, :]
-    for i in range(2):
-        value = extra[i * part : (i + 1) * part]
-        if not first:
-            value = value + prev_out[i][:, width:].astype(f32)
-        out_refs[i][:, width:] = value.astype(bf16)
+    extra_ref[...] = high * pick_ref[1:2, :] + (d_gate - high) * pick_ref[2:3, :]
 
     mask_half = mask.astype(bf16)
     d_out = jnp.concatenate(d_out_parts, axis=1)
@@ -903,16 +986,12 @@
     d_low_gate = mm_nt(d_gate_h, w_in[width:, 0:hidden]).astype(bf16) * mask_half
     d_low_up = mm_nt(d_up_h, w_in[width:, hidden:low_at]).astype(bf16) * mask_half
     d_low_in = jnp.concatenate([d_low_gate, d_low_up], axis=1)
-    d_all = jnp.concatenate([d_gate_h, d_up_h, d_low_in], axis=1)
+    d_all_ref[:, 0:hidden] = d_gate_h
+    d_all_ref[:, hidden:low_at] = d_up_h
+    d_all_ref[:, low_at:] = d_low_in
     d_low_in_t, low_down_t, low_in_t, d_low_down_t = d_low_in.T, low_down.T, low_in.T, d_low_down.T
     for j in range(width // CUT):
         at = slice(j * CUT, (j + 1) * CUT)
-        d_row = mm_nt(d_all, w_in[at, :]).astype(bf16)
-        for i in range(2):
-            value = d_row[i * part : (i + 1) * part]
-            if not first:
-                value = (value.astype(f32) + prev_row[i][:, at].astype(f32)).astype(bf16)
-            row_refs[i][:, at] = value
         g_a_in[:, at] += mm(d_low_in_t, rows[:, at])
         g_b_down[:, at] += mm(low_down_t, d_out[:, at])
     for j in range(chunks):
@@ -923,38 +1002,44 @@
 
     @pl.when(step == pl.num_programs(0) - 1)
     def _():
-        grad_ref[0 : 2 * SR, :] = g_a_in[...].astype(bf16)
-        grad_ref[2 * SR : 3 * SR, :] = g_b_down[...].astype(bf16)
-        grad_ref[3 * SR : 4 * SR, 0:hidden] = g_b_in[0].astype(bf16)
-        grad_ref[3 * SR : 4 * SR, hidden:] = g_b_in[1].astype(bf16)
-        grad_ref[4 * SR : 4 * SR + SR // 2, 0:hidden] = g_a_down[: SR // 2].astype(bf16)
-        grad_ref[4 * SR : 4 * SR + SR // 2, hidden:] = g_a_down[SR // 2 :].astype(bf16)
-
-
-def expert_pass(k, rows, cot, mask, picks, prev, weights):
+        packed[0 : 2 * SR, :] = g_a_in[...].astype(bf16)
+        packed[2 * SR : 3 * SR, :] = g_b_down[...].astype(bf16)
+        packed[3 * SR : 4 * SR, 0:hidden] = g_b_in[0].astype(bf16)
+        packed[3 * SR : 4 * SR, hidden:] = g_b_in[1].astype(bf16)
+        packed[4 * SR :, 0:hidden] = g_a_down[: SR // 2].astype(bf16)
+        packed[4 * SR :, hidden:] = g_a_down[SR // 2 :].astype(bf16)
+        size = packed.shape[0] // 4
+        for spot, b in enumerate((0, 2, 1, 3)):
+            quarter = packed[pl.ds(pl.multiple_of((where_ref[0] ^ b) * size, 16), size), :]
+            per = 4 // len(grad_refs)
+            grad_refs[spot // per][(spot % per) * size : (spot % per + 1) * size, :] = quarter
+
+
+def expert_pass(k, where, rows, cot, mask, picks, prev, weights):
     f32, bf16 = jnp.float32, jnp.bfloat16
-    blocks = len(rows)
+    blocks = EVERY
     part, width = cot[0].shape
     hidden = weights[0].shape[2]
     tokens = blocks * part
-    by_tile = lambda size, columns: pl.BlockSpec((size, columns), lambda i: (i, 0))
-    in_specs = [by_tile(TILE, SR), pl.BlockSpec((8, 128), lambda i: (0, 0))] + [in_place()] * (2 * blocks)
-    operands = [mask, picks, *rows, *cot]
+    shares = 2
+    grad_shape = ((4 * SR + SR // 2) // shares, width)
+    in_specs = [scalars(), by_tile(TILE, SR), pl.BlockSpec((8, 128), lambda i: (0, 0))] + [in_place()] * (2 * GATHERED)
+    operands = [where, mask, picks, *rows, *cot]
     if prev is not None:
-        in_specs += [by_tile(part, width + 128)] * 2 + [by_tile(part, width)] * 2
+        in_specs += [by_tile(part, width)] * 2
         operands += list(prev)
     in_specs += [in_place()] * 7
-    flops = 2 * tokens * (6 * width * hidden + 9 * SR * (width + hidden))
+    flops = 2 * tokens * (4 * width * hidden + 7 * SR * (width + hidden))
     return pl.pallas_call(
         functools.partial(expert_kernel, k, prev is None, width, hidden, blocks),
         grid=(tokens // TILE,),
         in_specs=in_specs,
-        out_specs=[by_tile(part, width + 128)] * 2
-        + [by_tile(part, width)] * 2
-        + [pl.BlockSpec((4 * SR + SR // 2, width), lambda i: (0, 0))],
-        out_shape=[shape_of((tokens // 2, width + 128))] * 2
-        + [shape_of((tokens // 2, width))] * 2
-        + [shape_of((4 * SR + SR // 2, width))],
+        out_specs=[by_tile(part, width)] * 2
+        + [by_tile(TILE, 2 * hidden + 2 * SR), by_tile(TILE, 128)]
+        + [pl.BlockSpec(grad_shape, lambda i: (0, 0))] * shares,
+        out_shape=[shape_of((tokens // 2, width))] * 2
+        + [shape_of((tokens, 2 * hidden + 2 * SR)), shape_of((tokens, 128), f32)]
+        + [shape_of(grad_shape)] * shares,
         scratch_shapes=[
             pltpu.VMEM((tokens, width + 128), bf16),
             pltpu.VMEM((tokens, width), bf16),
@@ -966,6 +1051,7 @@
             pltpu.VMEM((SR, width), f32),
             pltpu.VMEM((2, SR, hidden), f32),
             pltpu.VMEM((SR, hidden), f32),
+            pltpu.VMEM((4 * SR + SR // 2, width), bf16),
             pltpu.SemaphoreType.DMA((7 + 2 * (hidden // CUT),)),
             pltpu.SemaphoreType.DMA((blocks, 2)),
         ],
@@ -975,6 +1061,73 @@
     )(*operands, *weights)
 
 
+def rows_kernel(part, width, hidden, local, *refs):
+    bf16 = jnp.bfloat16
+    d_all, extra, (w_gate_hbm, w_up_hbm, a_in_hbm) = refs[:local], refs[local : 2 * local], refs[2 * local : 2 * local + 3]
+    even_ref, odd_ref, weight, sems = refs[2 * local + 3 :]
+    step = pl.program_id(0)
+    span = 2 * hidden + 2 * SR
+    chunks = width // CUT
+    copies = []
+    for j in range(chunks):
+        at = slice(j * CUT, (j + 1) * CUT)
+        group = []
+        for k in range(local):
+            base = k * span
+            targets = [
+                (w_gate_hbm.at[k, at], base, hidden),
+                (w_up_hbm.at[k, at], base + hidden, hidden),
+                (a_in_hbm.at[k, 0, at], base + 2 * hidden, SR),
+                (a_in_hbm.at[k, 1, at], base + 2 * hidden + SR, SR),
+            ]
+            for i, (source, start, size) in enumerate(targets):
+                group.append(
+                    pltpu.make_async_copy(source, weight.at[at, start : start + size], sems.at[j, 4 * k + i])
+                )
+        copies.append(group)
+
+    @pl.when(step == 0)
+    def _():
+        for group in copies:
+            for item in group:
+                item.start()
+
+    both = jnp.concatenate([ref[...] for ref in d_all], axis=1)
+    for j in range(chunks):
+
+        @pl.when(step == 0)
+        def _():
+            for item in copies[j]:
+                item.wait()
+
+        at = slice(j * CUT, (j + 1) * CUT)
+        value = mm_nt(both, weight[at, :]).astype(bf16)
+        even_ref[:, at] = value[:part]
+        odd_ref[:, at] = value[part:]
+    total = sum([ref[...] for ref in extra[1:]], extra[0][...]).astype(bf16)
+    even_ref[:, width:] = total[:part]
+    odd_ref[:, width:] = total[part:]
+
+
+def rows_pass(part, d_all, extra, w_gate, w_up, a_in):
+    local, width, hidden = w_gate.shape
+    tokens, span = d_all[0].shape
+    return pl.pallas_call(
+        functools.partial(rows_kernel, part, width, hidden, local),
+        grid=(tokens // TILE,),
+        in_specs=[by_tile(TILE, span)] * local + [by_tile(TILE, 128)] * local + [in_place()] * 3,
+        out_specs=[by_tile(part, width + 128)] * 2,
+        out_shape=[shape_of((tokens // 2, width + 128))] * 2,
+        scratch_shapes=[
+            pltpu.VMEM((width, local * span), jnp.bfloat16),
+            pltpu.SemaphoreType.DMA((width // CUT, 4 * local)),
+        ],
+        compiler_params=params(),
+        cost_estimate=cost(2 * tokens * width * span * local, 40 << 20),
+        name="rows",
+    )(*d_all, *extra, w_gate, w_up, a_in)
+
+
 def norm_grad(values, gain_row, upstream_grad):
     scale = lax.rsqrt(jnp.mean(values * values, axis=1, keepdims=True) + EPSILON)
     inner = gain_row * upstream_grad
@@ -984,107 +1137,83 @@
 
 def unmix_kernel(
     wide,
-    me_ref, resid_ref, cot_ref, gain_ref, mask_ref, router_ref, gates_ref, low_ref, *refs,
+    me_ref, resid_ref, cot_ref, gains_ref, mask_ref, router_ref, gates_ref, low_ref, att_ref, *refs,
 ):
     f32, bf16 = jnp.float32, jnp.bfloat16
-    row_pieces, out_pieces, extra_pieces, refs = refs[:6], refs[6:12], refs[12:18], refs[18:]
-    att_ref, w_hbm, small_hbm = refs[:EVERY], refs[EVERY : 2 * EVERY], refs[2 * EVERY : 3 * EVERY]
-    layer_ref, resid_grad_ref, grad_ref, *refs = refs[3 * EVERY :]
-    att_grads, (weight, down, up, up_grad, sems) = refs[:EVERY], refs[EVERY:]
+    pieces, given, refs = refs[:PIECES], blocks_of(refs[PIECES : PIECES + GATHERED]), refs[PIECES + GATHERED :]
+    resid_grad_ref, grad_ref, send_ref, weight, down, up, up_grad, sems = refs
     me = me_ref[0]
     width = resid_ref.shape[1]
-    copies = []
-    for j in range(EVERY):
-        at = pl.multiple_of((me ^ j) * wide, wide)
-        here = slice(j * wide, (j + 1) * wide)
-        copies.append(
-            [
-                pltpu.make_async_copy(
-                    small_hbm[j].at[:, 4 * SR : 5 * SR], up.at[pl.ds(at, wide), :], sems.at[j, 1]
-                ),
-                pltpu.make_async_copy(small_hbm[j].at[:, 3 * SR : 4 * SR], down.at[here, :], sems.at[j, 0]),
-                pltpu.make_async_copy(w_hbm[j], weight.at[here, :], sems.at[j, 2]),
-            ]
-        )
-    for which in range(3):
+    copies = output_copies(me, wide, given, weight, down, up, sems)
+    for which in (1, 0, 2):
         for group in copies:
             group[which].start()
     resid = resid_ref[...]
-    layer_ref[...] = (resid + sum_pieces(*[ref[...] for ref in out_pieces])).astype(bf16)
-    extra = sum_pieces(*[ref[...] for ref in extra_pieces])
+    total = sum_pieces(*[ref[...] for ref in pieces])
+    extra = total[:, width:]
     gates = gates_ref[...]
     d_gates = extra + pltpu.roll(extra, 64, 1)
     d_chosen = gates * (d_gates - jnp.sum(gates * d_gates, axis=1, keepdims=True))
-    d_normed = sum_pieces(*[ref[...] for ref in row_pieces]) + mm_nt(d_chosen.astype(bf16), router_ref[...])
-    d_resid = cot_ref[...].astype(f32) + norm_grad(resid, gain_ref[...], d_normed)
+    d_normed = total[:, :width] + mm_nt(d_chosen.astype(bf16), router_ref[...])
+    d_resid = cot_ref[...].astype(f32) + norm_grad(resid, gains_ref[1:2, :], d_normed)
     resid_grad_ref[...] = d_resid
     branch = d_resid.astype(bf16)
     for group in copies:
-        group[0].wait()
+        group[1].wait()
     d_low = (mm(branch, up[...]).astype(bf16).astype(f32) * mask_ref[...]).astype(bf16)
     low_t, d_low_t = low_ref[...].T, d_low.T
     up_grad[...] = mm(low_t, branch).astype(bf16)
     for group in copies:
-        group[1].wait()
+        group[0].wait()
     for j in range(EVERY):
         here = slice(j * wide, (j + 1) * wide)
         copies[j][2].wait()
-        att_grads[j][...] = (mm_nt(branch, weight[here, :]) + mm_nt(d_low, down[here, :])).astype(bf16)
+        send_ref[me ^ j] = (mm_nt(branch, weight[here, :]) + mm_nt(d_low, down[here, :])).astype(bf16)
         at = pl.multiple_of((me ^ j) * wide, wide)
-        grad_ref[j * 2 * SR : j * 2 * SR + SR, :] = mm(d_low_t, att_ref[j][...]).astype(bf16)
-        grad_ref[j * 2 * SR + SR : (j + 1) * 2 * SR, :] = up_grad[:, pl.ds(at, wide)]
-
-
-def unmix(me, resid, cot, gain, mask, router, gates, low, row_pieces, out_pieces, att_blocks, w_blocks, small_blocks):
+        grad_ref[me ^ j, 0:SR, :] = mm(d_low_t, att_ref[me ^ j]).astype(bf16)
+        grad_ref[me ^ j, SR:, :] = up_grad[:, pl.ds(at, wide)]
+
+
+def unmix(me, resid, cot, gains, mask, router, gates, low, att_got, pieces, given):
     rows, width = resid.shape
     wide = width // EVERY
     return pl.pallas_call(
         functools.partial(unmix_kernel, wide),
         grid=(1,),
         in_specs=[scalars()]
-        + [whole()] * 7
-        + piece_specs(rows, width)
-        + piece_specs(rows, width)
-        + piece_specs(rows, 128, width // 128)
-        + [whole()] * EVERY
-        + [in_place()] * (2 * EVERY),
-        out_specs=[whole()] * (3 + EVERY),
+        + [whole()] * 3
+        + [pl.BlockSpec((rows, SR), lambda i: (0, 0))]
+        + [whole()] * 4
+        + piece_specs(rows, width + 128)
+        + [in_place()] * GATHERED,
+        out_specs=[whole()] * 3,
         out_shape=[
-            shape_of((rows, width)),
             shape_of((rows, width), jnp.float32),
-            shape_of((EVERY * 2 * SR, wide)),
-        ]
-        + [shape_of((rows, wide))] * EVERY,
-        scratch_shapes=[
-            pltpu.VMEM((width, width), jnp.bfloat16),
-            pltpu.VMEM((width, SR), jnp.bfloat16),
-            pltpu.VMEM((width, SR), jnp.bfloat16),
-            pltpu.VMEM((SR, width), jnp.bfloat16),
-            pltpu.SemaphoreType.DMA((EVERY, 3)),
+            shape_of((EVERY, 2 * SR, wide)),
+            shape_of((EVERY, rows, wide)),
         ],
+        scratch_shapes=output_scratch(width)[:3]
+        + [pltpu.VMEM((SR, width), jnp.bfloat16)]
+        + output_scratch(width)[3:],
         compiler_params=params(),
-        cost_estimate=cost(2 * rows * width * width, 14 << 20),
+        cost_estimate=cost(1 << 20, 1 << 16),
         name="unmix",
-    )(me, resid, cot, gain, mask, router, gates, low, *row_pieces, *out_pieces, *out_pieces,
-      *att_blocks, *w_blocks, *small_blocks)
+    )(me, resid, cot, gains, mask, router, gates, low, att_got, *pieces, *given)
 
 
 def attend_back_kernel(
     rows, wide,
     me_ref, q_ref, k_ref, v_ref, att_ref, lse_ref, col_ref, row_ref, cos_ref, sin_ref, low_ref, mask_ref, up_ref,
-    *refs,
+    got_ref, out_grad_ref, normed_hbm, d_proj_ref, d_low_ref, even_ref, odd_ref, up_grad_ref, d_att, normed, sems,
 ):
     f32, bf16 = jnp.float32, jnp.bfloat16
-    d_att_blocks, refs = refs[:EVERY], refs[EVERY:]
-    normed_hbm, small_hbm, refs = refs[0], refs[1 : 1 + EVERY], refs[1 + EVERY :]
-    d_proj_ref, d_low_ref, down_grad_ref, up_grad_ref, d_att, normed, down, sems = refs
     tokens = q_ref.shape[0]
     scale = HD ** (-0.5)
     me = me_ref[0]
     bring = pltpu.make_async_copy(normed_hbm, normed, sems.at[0])
     bring.start()
     for j in range(EVERY):
-        d_att[j * rows : (j + 1) * rows, :] = d_att_blocks[j][...]
+        d_att[j * rows : (j + 1) * rows, :] = got_ref[me ^ j]
     seg_row = row_ref[0:1, :]
     for h in range(wide // HD):
         lanes = slice(h * HD, (h + 1) * HD)
@@ -1094,9 +1223,8 @@
         d_query = jnp.zeros((tokens, HD), f32)
         for c in range(tokens // TILE):
             at = slice(c * TILE, (c + 1) * TILE)
-            scores = mm_nt(k_ref[at, lanes], q_ref[:, lanes]) * scale
-            same = col_ref[at, 0:1] == seg_row
-            probs = jnp.where(same, jnp.exp(jnp.where(same, scores - log_sum, 0.0)), 0.0)
+            scores = mm_nt(k_ref[at, lanes], q_ref[:, lanes]) * scale - log_sum
+            probs = jnp.exp(jnp.where(col_ref[at, 0:1] == seg_row, scores, MASKED))
             d_probs = mm_nt(v_ref[at, lanes], d_att[:, lanes])
             d_scores = (probs * (d_probs - delta)).astype(bf16)
             d_value = mm(probs.astype(bf16), d_att[:, lanes])
@@ -1116,100 +1244,107 @@
     bring.wait()
     for j in range(EVERY):
         at = pl.multiple_of((me ^ j) * wide, wide)
-        down_grad_ref[j * 3 * SR : (j + 1) * 3 * SR, :] = mm(d_low_t, normed[:, pl.ds(at, wide)]).astype(bf16)
-
-
-def attend_back(rows, me, q, k, v, att, lse, seg_col, seg_row, cosine, sine, low, mask, up, d_att_blocks, normed, small):
+        spot = (j // 2) * 5 * SR
+        ref = (even_ref, odd_ref)[j % 2]
+        ref[spot : spot + 2 * SR, :] = out_grad_ref[me ^ j]
+        ref[spot + 2 * SR : spot + 5 * SR, :] = mm(d_low_t, normed[:, pl.ds(at, wide)]).astype(bf16)
+
+
+def attend_back(rows, me, q, k, v, att, lse, seg_col, seg_row, cosine, sine, low, mask, up, got, out_grad, normed):
     tokens, wide = q.shape
     width = wide * EVERY
     return pl.pallas_call(
         functools.partial(attend_back_kernel, rows, wide),
-        in_specs=[scalars()] + [whole()] * 12 + [whole()] * EVERY + [in_place()] * (1 + EVERY),
-        out_specs=[whole()] * 4,
+        in_specs=[scalars()] + [whole()] * 14 + [in_place()],
+        out_specs=[whole()] * 5,
         out_shape=[
             shape_of((tokens, 3 * wide)),
             shape_of((tokens, 3 * SR)),
-            shape_of((EVERY * 3 * SR, wide)),
+            shape_of((4 * 5 * SR, wide)),
+            shape_of((4 * 5 * SR, wide)),
             shape_of((3 * SR, wide)),
         ],
         scratch_shapes=[
             pltpu.VMEM((tokens, wide), jnp.bfloat16),
             pltpu.VMEM((tokens, width), jnp.bfloat16),
-            pltpu.VMEM((16, 128), jnp.bfloat16),
-            pltpu.SemaphoreType.DMA((2,)),
+            pltpu.SemaphoreType.DMA((1,)),
         ],
         compiler_params=params(),
-        cost_estimate=cost(10 * tokens * tokens * wide, 10 << 20),
+        cost_estimate=cost(1 << 20, 1 << 16),
         name="attend_back",
-    )(me, q, k, v, att, lse, seg_col, seg_row, cosine, sine, low, mask, up, *d_att_blocks, normed, *small)
-
-
-def unproject_kernel(rows, wide, me_ref, proj_ref, low_ref, *refs):
+    )(me, q, k, v, att, lse, seg_col, seg_row, cosine, sine, low, mask, up, got, out_grad, normed)
+
+
+def unproject_kernel(rows, width, wide, me_ref, proj_ref, low_ref, *refs):
     bf16 = jnp.bfloat16
-    w_hbm, small_hbm, (even_ref, odd_ref, weight, sems) = refs[:EVERY], refs[EVERY : 2 * EVERY], refs[2 * EVERY :]
-    me = me_ref[0]
-    copies = []
-    for j in range(EVERY):
-        at = pl.multiple_of((me ^ j) * wide, wide)
-        for i in range(3):
-            copies.append(
-                pltpu.make_async_copy(
-                    w_hbm[j].at[i], weight.at[pl.ds(at, wide), i * wide : (i + 1) * wide], sems.at[j, i]
+    given, w_hbm = blocks_of(refs[:GATHERED]), refs[GATHERED]
+    even_ref, odd_ref, weight, sems, w_sems = refs[GATHERED + 1 :]
+    me, thin = me_ref[0], 3 * SR
+
+    @pl.when(pl.program_id(0) == 0)
+    def _():
+        copies = []
+        for j in range(EVERY):
+            at = pl.multiple_of((me ^ j) * wide, wide)
+            for i in range(3):
+                copies.append(
+                    pltpu.make_async_copy(
+                        w_hbm.at[j, i],
+                        weight.at[j * wide : (j + 1) * wide, i * wide : (i + 1) * wide],
+                        w_sems.at[j, i],
+                    )
                 )
-            )
-        copies.append(
-            pltpu.make_async_copy(
-                small_hbm[j].at[:, 0 : 3 * SR],
-                weight.at[pl.ds(at, wide), 3 * wide : 3 * wide + 3 * SR],
-                sems.at[j, 3],
-            )
-        )
-    for item in copies:
-        item.start()
-    for item in copies:
-        item.wait()
-
-    def chunk(c, _):
-        at = pl.ds(pl.multiple_of(c * TILE, TILE), TILE)
-        here = pl.ds(pl.multiple_of(c * rows, rows), rows)
-        both = jnp.concatenate([proj_ref[at, :], low_ref[at, :]], axis=1)
-        for j in range(EVERY * wide // CUT):
-            lanes = slice(j * CUT, (j + 1) * CUT)
-            value = mm_nt(both, weight[lanes, :]).astype(bf16)
-            even_ref[here, lanes] = value[:rows]
-            odd_ref[here, lanes] = value[rows:]
-        return 0
-
-    lax.fori_loop(0, EVERY * rows // TILE, chunk, 0)
-
-
-def unproject(rows, me, d_proj, d_low, w_blocks, small_blocks):
+            for part in range(2):
+                start = part * thin
+                copies.append(
+                    pltpu.make_async_copy(
+                        given[j].at[:, start : start + thin],
+                        weight.at[pl.ds(at + part * rows, rows), 3 * wide : 3 * wide + thin],
+                        sems.at[j, part],
+                    )
+                )
+        for item in copies:
+            item.start()
+        for item in copies:
+            item.wait()
+
+    both = jnp.concatenate([proj_ref[...], low_ref[...]], axis=1)
+    for j in range(width // CUT):
+        lanes = slice(j * CUT, (j + 1) * CUT)
+        value = mm_nt(both, weight[lanes, :]).astype(bf16)
+        even_ref[:, lanes] = value[:rows]
+        odd_ref[:, lanes] = value[rows:]
+
+
+def unproject(rows, me, d_proj, d_low, given, w_got):
     tokens = d_proj.shape[0]
     wide = d_proj.shape[1] // 3
     width = wide * EVERY
     return pl.pallas_call(
-        functools.partial(unproject_kernel, rows, wide),
-        in_specs=[scalars()] + [whole()] * 2 + [in_place()] * (2 * EVERY),
-        out_specs=[whole()] * 2,
+        functools.partial(unproject_kernel, rows, width, wide),
+        grid=(tokens // TILE,),
+        in_specs=[scalars(), by_tile(TILE, 3 * wide), by_tile(TILE, 3 * SR)] + [in_place()] * (GATHERED + 1),
+        out_specs=[by_tile(rows, width)] * 2,
         out_shape=[shape_of((tokens // 2, width))] * 2,
         scratch_shapes=[
             pltpu.VMEM((width, 3 * wide + 3 * SR), jnp.bfloat16),
-            pltpu.SemaphoreType.DMA((EVERY, 4)),
+            pltpu.SemaphoreType.DMA((EVERY, 2)),
+            pltpu.SemaphoreType.DMA((EVERY, 3)),
         ],
         compiler_params=params(),
-        cost_estimate=cost(2 * tokens * width * 3 * (wide + SR), 12 << 20),
+        cost_estimate=cost(1 << 20, 1 << 16),
         name="unproject",
-    )(me, d_proj, d_low, *w_blocks, *small_blocks)
-
-
-def finish_kernel(hidden_ref, gain_ref, resid_grad_ref, *refs):
-    pieces, out_ref = refs[:6], refs[6]
+    )(me, d_proj, d_low, *given, w_got)
+
+
+def finish_kernel(hidden_ref, gains_ref, resid_grad_ref, *refs):
+    pieces, out_ref = refs[:PIECES], refs[PIECES]
     d_normed = sum_pieces(*[ref[...] for ref in pieces])
-    back = norm_grad(hidden_ref[...].astype(jnp.float32), gain_ref[...], d_normed)
+    back = norm_grad(hidden_ref[...].astype(jnp.float32), gains_ref[0:1, :], d_normed)
     out_ref[...] = (resid_grad_ref[...] + back).astype(jnp.bfloat16)
 
 
-def finish(hidden, gain, resid_grad, pieces):
+def finish(hidden, gains, resid_grad, pieces):
     rows, width = hidden.shape
     return pl.pallas_call(
         finish_kernel,
@@ -1218,20 +1353,91 @@
         out_specs=whole(),
         out_shape=shape_of((rows, width)),
         compiler_params=params(),
-        cost_estimate=cost(20 * rows * width, 6 << 20),
+        cost_estimate=cost(1 << 20, 1 << 16),
         name="finish",
-    )(hidden, gain, resid_grad, *pieces)
-
-
-def set_masks(seg, doc_sets):
-    set_token = jnp.sum(
-        jnp.where(seg[:, None] == jnp.arange(SETS)[None, :], doc_sets[0][None, :], 0), axis=1
-    )
-    return (set_token[:, None] == (jnp.arange(SR) // R)[None, :]).astype(jnp.float32)
-
-
-def after(value, gate):
-    return lax.optimization_barrier((value, gate))[0]
+    )(hidden, gains, resid_grad, *pieces)
+
+
+def layer_kernel(resid_ref, *refs):
+    pieces, out_ref = refs[:PIECES], refs[PIECES]
+    out_ref[...] = (resid_ref[...] + sum_pieces(*[ref[...] for ref in pieces])).astype(jnp.bfloat16)
+
+
+def layer(resid, pieces):
+    rows, width = resid.shape
+    return pl.pallas_call(
+        layer_kernel,
+        grid=(1,),
+        in_specs=[whole()] + piece_specs(rows, width),
+        out_specs=whole(),
+        out_shape=shape_of((rows, width)),
+        compiler_params=params(),
+        cost_estimate=cost(1 << 20, 1 << 16),
+        name="layer",
+    )(resid, *pieces)
+
+
+def unpack_kernel(hidden, first, where_ref, *refs):
+    f32 = jnp.float32
+    parts, refs = refs[:8], refs[8:]
+    refs = refs if first else refs[4:]
+    a_in_ref, b_in_ref, a_down_ref, b_down_ref, packed = refs
+    size = packed.shape[0] // 4
+    for b in range(4):
+        for i in range(2):
+            spot = pl.multiple_of((where_ref[0] ^ b) * size + i * (size // 2), 8)
+            packed[pl.ds(spot, size // 2), :] = parts[2 * b + i][...].astype(f32)
+    for i in range(2):
+        a_in_ref[0, i] = packed[i * SR : (i + 1) * SR, :].T
+        b_in_ref[0, i] = packed[3 * SR : 4 * SR, i * hidden : (i + 1) * hidden]
+    b_down_ref[0] = packed[2 * SR : 3 * SR, :]
+    a_down_ref[0, :, 0 : SR // 2] = packed[4 * SR :, 0:hidden].T
+    a_down_ref[0, :, SR // 2 :] = packed[4 * SR :, hidden:].T
+
+
+def unpack(k, where, quarters, hidden, experts, before):
+    quarters = [part for quarter in quarters for part in quarter]
+    width = quarters[0].shape[1]
+    f32 = jnp.float32
+    first = before is None
+    shapes = [(experts, 2, width, SR), (experts, 2, SR, hidden), (experts, hidden, SR), (experts, SR, width)]
+    given = [] if first else list(before)
+    return pl.pallas_call(
+        functools.partial(unpack_kernel, hidden, first),
+        grid=(1,),
+        in_specs=[scalars()] + [whole()] * 8 + [in_place()] * len(given),
+        out_specs=[
+            pl.BlockSpec((1,) + shape[1:], lambda i, n=len(shape): (k,) + (0,) * (n - 1)) for shape in shapes
+        ],
+        out_shape=[shape_of(shape, f32) for shape in shapes],
+        input_output_aliases={} if first else {9 + i: i for i in range(4)},
+        scratch_shapes=[pltpu.VMEM((4 * SR + SR // 2, width), f32)],
+        compiler_params=params(),
+        cost_estimate=cost(1 << 20, 1 << 16),
+        name="unpack",
+    )(where, *quarters, *given)
+
+
+def thin_kernel(left_ref, right_ref, a_ref, b_ref):
+    total = left_ref[...].astype(jnp.float32) + right_ref[...].astype(jnp.float32)
+    for i in range(4):
+        at = (2 + i) * SR if i < 3 else 0
+        a_ref[i] = total[at : at + SR, :].T
+        at = (5 + i) * SR if i < 3 else SR
+        b_ref[i] = total[at : at + SR, :].T
+
+
+def thin_grads(left, right):
+    wide = left.shape[1]
+    return pl.pallas_call(
+        thin_kernel,
+        in_specs=[whole()] * 2,
+        out_specs=[whole()] * 2,
+        out_shape=[shape_of((4, wide, SR), jnp.float32)] * 2,
+        compiler_params=params(),
+        cost_estimate=cost(1 << 20, 1 << 16),
+        name="thin_grads",
+    )(left, right)
 
 
 def split_layer(
@@ -1258,106 +1464,150 @@
     bf16, f32 = jnp.bfloat16, jnp.float32
     index = lax.axis_index("fsdp")
     me = index.astype(jnp.int32).reshape(1)
+    where = lax.axis_index("rep").astype(jnp.int32).reshape(1)
     hidden, upstream = hidden_in[0], cotangent[0]
     rows, width = hidden.shape
     wide = width // EVERY
-    experts_all = w_gate.shape[0] * EVERY
+    local, _, inner = w_gate.shape
+    experts_all = local * EVERY
+
     order = index ^ jnp.arange(EVERY)
-
-    thin = jnp.concatenate([gain_attn, gain_moe, router.reshape(-1)])
-    thin = lax.all_to_all(
-        jnp.broadcast_to(thin[None], (EVERY, thin.shape[0])), "fsdp", split_axis=0, concat_axis=0, tiled=True
-    )
-    gain_one = thin[:, :wide].reshape(1, width).astype(f32)
-    gain_two = thin[:, wide : 2 * wide].reshape(1, width).astype(f32)
-    router_all = thin[:, 2 * wide :].reshape(width, experts_all)
-    router_all = jnp.pad(router_all, ((0, 0), (0, 128 - experts_all)))
-    seg_own = segments[0].astype(bf16)
-    seg_blocks = [seg_own] + [swap(seg_own, j) for j in range(1, EVERY)]
-    seg_all = jnp.concatenate(seg_blocks).astype(jnp.int32)
-    mask = set_masks(seg_all, doc_sets)
-    mask_own = mask[:rows]
-    seg_row = jnp.broadcast_to(seg_all.astype(f32)[None, :], (8, rows * EVERY))
-    seg_col = jnp.broadcast_to(seg_all.astype(f32)[:, None], (rows * EVERY, 128))
     positions = (order[:, None] * rows + jnp.arange(rows)[None, :]).reshape(-1)
     cosine, sine = rope_tables(positions, HD)
     cosine, sine = jnp.concatenate([cosine, cosine], axis=1), jnp.concatenate([-sine, sine], axis=1)
     lanes = jnp.arange(128)
-    named = jnp.any(routes[0][:, :, None] == lanes[None, None, :], axis=1).astype(f32)
-
-    hidden_blocks = gather_relative(hidden)
-    w_blocks = [
-        lax.dynamic_slice_in_dim(w_qkv, order[j] * wide, wide, axis=2) for j in range(EVERY)
-    ]
-    w_blocks = [w_blocks[0]] + [swap(w_blocks[j], j) for j in range(1, EVERY)]
-    small = jnp.concatenate([a_attn[0], a_attn[1], a_attn[2], a_attn[3], b_attn[3]], axis=1)
-    small_blocks = gather_relative(small)
-
-    queries, keys, values, normed_one, low_qkv = project(
-        me, gain_one, mask, cosine, sine, b_attn, hidden_blocks, w_blocks, small_blocks
-    )
-    out_blocks = gather_relative(after(w_out, (hidden_blocks[6], w_blocks[7], w_blocks[6])))
-    att, lse, *att_blocks = attend(rows, queries, keys, values, seg_col, seg_row)
-    att_blocks = [att_blocks[0]] + [swap(att_blocks[j], j) for j in range(1, EVERY)]
+    named = jnp.any(routes[0][:, :, None] + SPOT == lanes[None, None, :], axis=1).astype(f32)
+    out_own = jnp.concatenate([w_out, a_attn[3], b_attn[3]], axis=1)
+
+    def picks(k):
+        high = (lanes == SPOT + 2 * index + k).astype(f32)
+        low = (lanes == SPOT + 2 * index + k + 64).astype(f32)
+        return jnp.stack([high + low, high, low] + [jnp.zeros_like(high)] * 5)
+
+    hidden_first = gather_first(hidden)
+    narrow = jnp.concatenate([a_attn[0], a_attn[1], a_attn[2]], axis=1)
+    at_spot = ((0, 0), (SPOT, 128 - SPOT - experts_all))
+    meta = jnp.pad(router[:rows], at_spot) + jnp.pad(segments[0].astype(bf16)[:, None], ((0, 0), (0, 127)))
+    lines = jnp.concatenate([gain_attn.reshape(2, 128), gain_moe.reshape(2, 128)], axis=0)
+    lines = jnp.pad(lines, ((0, rows - 4), (0, 0)))
+    given = jnp.concatenate([narrow[:rows], narrow[rows:], meta, jnp.pad(router[rows:], at_spot), lines], axis=1)
+    given_first = gather_first(given)
+    w_got = lax.all_to_all(by_columns(w_qkv, wide), "fsdp", split_axis=0, concat_axis=0, tiled=True)
+    hidden_first, cosine, sine, out_own, named, pick_rows = tie(
+        hidden_first, cosine, sine, out_own, named, [picks(0), picks(1)]
+    )
+    hidden_given = gather_third(hidden_first, *gather_second(*hidden_first))
+    given = gather_third(given_first, *gather_second(*given_first))
+
+    hidden_given, given, w_got, out_own = tie(hidden_given, given, w_got, out_own)
+    out_first = gather_first(out_own)
+    queries, keys, values, normed_one, low_qkv, mask, seg_col, seg_row, gains, router_all = project(
+        me, doc_sets, cosine, sine, b_attn, hidden_given, given, w_got
+    )
+    att, lse, att_send = attend(rows, me, queries, keys, values, seg_col, seg_row)
+    att_send, out_first = tie(att_send, out_first)
+    att_got = lax.all_to_all(att_send, "fsdp", split_axis=0, concat_axis=0, tiled=True)
+    far, *others = gather_second(*out_first)
+    far, others, att_got, upstream_now = tie(far, others, att_got, upstream)
+    cot_first = gather_first(upstream_now)
+    out_given = gather_third(out_first, far, *others)
     resid_one, normed_own, low_out, gates_own = mix(
-        me, hidden, gain_two, mask_own, router_all, named, att_blocks, out_blocks, small_blocks
-    )
-    cot_blocks = gather_relative(after(upstream, out_blocks[6]))
-    normed_blocks = gather_relative(normed_own)
+        me, hidden, gains, mask, router_all, named, att_got, out_given
+    )
+    normed_own, cot_first = tie(normed_own, cot_first)
+    normed_given = gather_relative(normed_own)
+    cot_given = gather_third(cot_first, *gather_second(*cot_first))
 
     weights = (w_gate, w_up, w_down, exp_a_in, exp_b_in, exp_a_down, exp_b_down)
-    state, sums = None, []
-    for k in range(w_gate.shape[0]):
-        high = (lanes == 2 * index + k).astype(f32)
-        low = (lanes == 2 * index + k + 64).astype(f32)
-        picks = jnp.stack([high + low, high, low] + [jnp.zeros_like(high)] * 5)
-        *state, grads = expert_pass(k, normed_blocks, cot_blocks, mask, picks, state, weights)
-        sums.append(sum_rep(grads).astype(f32))
-    out_even, out_odd, row_even, row_odd = state
-    row_pieces = scatter_relative(row_even, row_odd)
-    out_pieces = scatter_relative(out_even, out_odd)
-    layer_out, d_resid, out_grads, *d_att_blocks = unmix(
-        me, resid_one, upstream, gain_two, mask_own, router_all, gates_own, low_out,
-        row_pieces, out_pieces, att_blocks, out_blocks, small_blocks,
-    )
-    d_att_blocks = [d_att_blocks[0]] + [swap(d_att_blocks[j], j) for j in range(1, EVERY)]
-    out_grads = out_grads.reshape(EVERY, 2 * SR, wide)
-    d_proj, d_low, down_grads, up_grads = attend_back(
+    *state, d_all_a, extra_a, kept_a, sent_a = expert_pass(
+        0, where, normed_given, cot_given, mask, pick_rows[0], None, weights
+    )
+    def in_two(values):
+        return [values[: values.shape[0] // 2], values[values.shape[0] // 2 :]]
+
+    def later(values, anchor):
+        return tie(values, anchor)[0]
+
+    def in_two(values):
+        return [values[: values.shape[0] // 2], values[values.shape[0] // 2 :]]
+
+    sent_a = rep_swap(sent_a, 1)
+    *state, d_all_b, extra_b, kept_b, sent_b = expert_pass(
+        1, where, normed_given, cot_given, mask, pick_rows[1], state, weights
+    )
+    d_all_b, kept_b, sent_b, sent_a, state = tie(d_all_b, kept_b, sent_b, sent_a, state)
+    out_even, out_odd = state
+    half_a = add_half(kept_a, sent_a)
+    size = half_a.shape[0] // 2
+    sent_b, kept_b = in_two(sent_b), in_two(kept_b)
+    sent_b[0] = rep_swap(sent_b[0], 1)
+    other_a = rep_swap(half_a[size:], 2)
+    out_got = swap(out_odd, 1)
+    row_even, row_odd = rows_pass(rows, [d_all_a, d_all_b], [extra_a, extra_b], w_gate, w_up, exp_a_in)
+    row_odd, other_a, sent_b[0], out_got = tie(row_odd, other_a, sent_b[0], out_got)
+    got = swap(row_odd, 1)
+    sent_b[1] = rep_swap(later(sent_b[1], row_odd), 1)
+    total_a = in_two(add_half(half_a[:size], other_a))
+    d_far = scatter_second(row_even, got)
+    d_far, sent_b[1] = tie(d_far, sent_b[1])
+    pieces = scatter_third(row_even, got, *d_far)
+    two_a = [rep_swap(later(total_a[0], d_far), 2)]
+    pieces, two_a[0] = tie(pieces, two_a[0])
+    early_a = later(total_a, pieces)
+    two_a.append(rep_swap(early_a[1], 2))
+    one_a = [None, rep_swap(early_a[1], 1)]
+    d_resid, thin_send, d_att_send = unmix(
+        me, resid_one, upstream, gains, mask, router_all, gates_own, low_out, att_got, pieces, out_given
+    )
+    d_att_send, two_a[1], one_a[1] = tie(d_att_send, two_a[1], one_a[1])
+    d_att_got = lax.all_to_all(d_att_send, "fsdp", split_axis=0, concat_axis=0, tiled=True)
+    mine_b = add_half(kept_b[0], sent_b[0])
+    half_b = later(in_two(add_half(kept_b[1], sent_b[1])), d_att_send)
+    one_a[0] = rep_swap(later(total_a[0], d_att_send), 1)
+    other_b = [rep_swap(half_b[0], 2)]
+    d_att_got, other_b[0], one_a[0] = tie(d_att_got, other_b[0], one_a[0])
+    total_b = [add_half(mine_b[: size // 2], other_b[0])]
+    other_b.append(rep_swap(later(half_b[1], d_att_got), 2))
+    three_a = [rep_swap(later(two_a[0], d_att_got), 1)]
+    d_proj, d_low, thin_even, thin_odd, up_grads = attend_back(
         rows, me, queries, keys, values, att, lse, seg_col, seg_row, cosine, sine, low_qkv, mask, b_attn,
-        d_att_blocks, normed_one, small_blocks,
-    )
-    even, odd = unproject(rows, me, d_proj, d_low, w_blocks, small_blocks)
-    pieces = scatter_relative(even, odd)
-    grad_in = finish(hidden, gain_one, d_resid, pieces)
-
-    def by_parity(values):
-        pairs = values.reshape(4, 2, values.shape[0] // EVERY, wide)
-        return pairs[:, 0].reshape(-1, wide), pairs[:, 1].reshape(-1, wide)
-
-    def own_sum(values):
-        size = values.shape[0] // EVERY
-        even, got, *rest = scatter_relative(*by_parity(values))
-        return sum_pieces(even[:size], got[:size], *rest).astype(bf16)
-
-    out_sum = own_sum(out_grads.reshape(-1, wide))
-    early = sum_rep_short(jnp.concatenate([out_sum, up_grads], axis=0))
-    late = sum_rep_short(own_sum(down_grads))
-    early, late = early.astype(f32).T, late.astype(f32).T
-    cut = lambda values, i: values[:, i * SR : (i + 1) * SR]
-    grad_a = jnp.stack([cut(late, 0), cut(late, 1), cut(late, 2), cut(early, 0)])
-    grad_b = jnp.stack([cut(early, 2), cut(early, 3), cut(early, 4), cut(early, 1)])
-    at = [2 * SR, 3 * SR, 4 * SR]
-    half = w_gate.shape[2]
-    return (
-        layer_out[None],
-        grad_in[None],
-        grad_a,
-        grad_b,
-        jnp.stack([g[: at[0]].reshape(2, SR, width).transpose(0, 2, 1) for g in sums]),
-        jnp.stack([jnp.stack([g[at[1] : at[2], :half], g[at[1] : at[2], half:]]) for g in sums]),
-        jnp.stack([jnp.concatenate([g[at[2] :, :half], g[at[2] :, half:]]).T for g in sums]),
-        jnp.stack([g[at[0] : at[1]] for g in sums]),
-    )
+        d_att_got, thin_send, normed_one,
+    )
+    d_proj, thin_odd, other_b[1], three_a[0] = tie(d_proj, thin_odd, other_b[1], three_a[0])
+    thin_got = swap(thin_odd, 1)
+    two_b = [rep_swap(later(total_b[0], d_proj), 2)]
+    three_a.append(rep_swap(later(two_a[1], d_proj), 1))
+    even, odd = unproject(rows, me, d_proj, d_low, given, w_got)
+    odd, thin_got, two_b[0], three_a[1] = tie(odd, thin_got, two_b[0], three_a[1])
+    total_b.append(later(add_half(mine_b[size // 2 :], other_b[1]), odd))
+    got = swap(odd, 1)
+    thin_far = scatter_second(thin_even, thin_got)
+    one_b = [rep_swap(later(total_b[0], odd), 1)]
+    got, thin_far, one_b[0] = tie(got, thin_far, one_b[0])
+    thin_pieces = scatter_third(thin_even, thin_got, *thin_far)
+    d_far = scatter_second(even, got)
+    two_b.append(rep_swap(later(total_b[1], got), 2))
+    d_far, thin_pieces, two_b[1] = tie(d_far, thin_pieces, two_b[1])
+    pieces = scatter_third(even, got, *d_far)
+    thin = jnp.concatenate(
+        [sum_pieces(*[piece[: 5 * SR] for piece in thin_pieces]).astype(bf16), up_grads], axis=0
+    )
+    thin_near = rep_swap(thin, 1)
+    out_far = scatter_second(*later((out_even, out_got), d_far))
+    grads = unpack(0, where, later([total_a, one_a, two_a, three_a], d_far), inner, local, None)
+    pieces, thin_near, out_far, grads = tie(pieces, thin_near, out_far, grads)
+    thin = add_half(thin, thin_near)
+    thin_last = rep_swap(thin, 2)
+    late_b = later([total_b[1], two_b], pieces)
+    one_b.append(rep_swap(late_b[0], 1))
+    three_b = [rep_swap(part, 1) for part in late_b[1]]
+    out_pieces = scatter_third(out_even, out_got, *out_far)
+    grad_in = finish(hidden, gains, d_resid, pieces)
+    layer_out = layer(resid_one, out_pieces)
+    one_b, three_b, thin_last, layer_out, grad_in = tie(one_b, three_b, thin_last, layer_out, grad_in)
+    grads = unpack(1, where, [total_b, one_b, two_b, three_b], inner, local, grads)
+    grad_a, grad_b = thin_grads(thin, thin_last)
+    return (layer_out[None], grad_in[None], grad_a, grad_b, *grads)
 
 
 def solution(mesh):

time: 659 us -> 516 us (0.78)
  waiting for transfers between devices: 268 us -> 154 us
  local copies, waits for them, and re-layouts: 56.8 us -> 21.6 us
  Pallas kernels: 175 us -> 206 us
  other arithmetic: 46.3 us -> 25.4 us
  blocking collectives: 0 us -> 19.5 us
  starting transfers between devices: 96.5 us -> 77.7 us
    ppermute x103 -> x55, waiting for transfers between devices: 169 us -> 97.4 us  [swap(): return lax.ppermute(values, 'fsdp', [(i, i ^ bits) for i in range(EVERY)])]
    pallas_call x4 -> x10, Pallas kernels: 42 us -> 90.4 us  [the longest x1 29 us: rows_pass(): pl.pallas_call(functools.partial(rows_kernel, part, width, hidden, local)...]
    ppermute x12 -> x20, waiting for transfers between devices: 98.6 us -> 56.6 us  [rep_swap(): return lax.ppermute(values, 'rep', [(i, i ^ bits) for i in range(4)])]
    ppermute x103 -> x55, starting transfers between devices: 78.9 us -> 43.4 us  [swap(): return lax.ppermute(values, 'fsdp', [(i, i ^ bits) for i in range(EVERY)])]
    all_to_all x0 -> x1, blocking collectives: none -> 19.5 us  [split_layer(): lax.all_to_all(att_send, 'fsdp', split_axis=0, concat_axis=0, tiled=True)]
    pallas_call x2, Pallas kernels: 103 us -> 84.9 us  [expert_pass(): pl.pallas_call(functools.partial(expert_kernel, k, prev is None, width, h...]
    ppermute x12 -> x20, starting transfers between devices: 14.3 us -> 25.9 us  [rep_swap(): return lax.ppermute(values, 'rep', [(i, i ^ bits) for i in range(4)])]
    convert_element_type x16 -> x9, other arithmetic: 17.8 us -> 8.09 us  [add_half(): (left.astype(jnp.float32) + right.astype(jnp.float32)).astype(jnp.bfloat16)]
  transfers between devices with their start and end apart: 116 -> 77, of which waited for: 48 -> 32; matrix products, arithmetic and copies ran while one was open for 14% -> 5% of each run, Pallas kernels for 11% -> 31%
where the time goes in v3:
time: 516 us; the launch traced here: 506 us
  Pallas kernels  206 us (40%)
  waiting for transfers between devices  154 us (30%)
  starting transfers between devices  77.7 us (15%)
  other arithmetic  25.4 us (5%)
  local copies, waits for them, and re-layouts  21.6 us (4%)
  blocking collectives  19.5 us (4%)
    ppermute x55, waiting for transfers between devices, swap(): return lax.ppermute(values, 'fsdp', [(i, i ^ bits) for i in range(EVERY)])  97.4 us
    pallas_call x2, Pallas kernels, expert_pass(): pl.pallas_call(functools.partial(expert_kernel, k, prev is None, width, h...  84.9 us
    ppermute x20, waiting for transfers between devices, rep_swap(): return lax.ppermute(values, 'rep', [(i, i ^ bits) for i in range(4)])  56.6 us
    ppermute x55, starting transfers between devices, swap(): return lax.ppermute(values, 'fsdp', [(i, i ^ bits) for i in range(EVERY)])  43.4 us
    pallas_call x1, Pallas kernels, rows_pass(): pl.pallas_call(functools.partial(rows_kernel, part, width, hidden, local)...  29 us
    ppermute x20, starting transfers between devices, rep_swap(): return lax.ppermute(values, 'rep', [(i, i ^ bits) for i in range(4)])  25.9 us
    all_to_all x1, blocking collectives, split_layer(): lax.all_to_all(att_send, 'fsdp', split_axis=0, concat_axis=0, tiled=True)  19.5 us
    pallas_call x1, Pallas kernels, project(): pl.pallas_call(functools.partial(project_kernel, rows, width, wide), grid...  15.7 us
  transfers between devices with their start and end apart: 77, of which 32 were waited for; matrix products, arithmetic and copies ran while one was open for 5% of the time, Pallas kernels for 31%

profile of v3, /device:TPU:0, one launch (start us, length us, event | category | flops | bytes accessed | tf_op | source)
XLA Modules:
  0.0 506.0 jit_solution(5762884732773180809)
XLA Ops:
  11.9 5.3 %by_columns.1 = bf16[8,3,256,256]{3,2,1,0:T(8,128)(2,1)} custom-call(bf16[3,256,2048]{2,1,0:T(8,128)(2,1)} %source_ref.1), custom_call_target="tpu_custom_call" | custom-call | flops 1048576 | bytes 65536 | tf_op jit(solution)/shard_map/by_columns/pallas_call | solution.py:625
  17.2 4.6 all-to-all-start
  34.6 31.4 %collective-permute-done.9 = bf16[64,1152]{1,0:T(8,128)(2,1)S(1)} collective-permute-done((bf16[64,1152]{1,0:T(8,128)(2,1)S(1)}, bf16[64,1152]{1,0:T(8,128)(2,1)S(1)}, u32[]{:S(2)}, u32[]{:S(2)}) %collective-permute-start.9) | collective-permute-done | bytes 147488 | tf_op jit(solution)/shard_map/ppermute | solution.py:529
  66.0 5.4 %collective-permute-done.2 = bf16[64,2048]{1,0:T(8,128)(2,1)S(1)} collective-permute-done((bf16[64,2048]{1,0:T(8,128)(2,1)S(1)}, bf16[64,2048]{1,0:T(8,128)(2,1)S(1)}, u32[]{:S(2)}, u32[]{:S(2)}) %collective-permute-start.2) | collective-permute-done | bytes 262176 | tf_op jit(solution)/shard_map/ppermute | solution.py:529
  80.4 15.7 %project.1 = (bf16[1024,256]{1,0:T(8,128)(2,1)}, bf16[1024,256]{1,0:T(8,128)(2,1)}, bf16[1024,256]{1,0:T(8,128)(2,1)}, bf16[1024,2048]{1,0:T(8,128)(2,1)}, bf16[...) custom-call(s32[1]{0:T(128)} %bitcast.me_ref, ...), custom_call_target="tpu_custom_call" | custom-call | flops 1048576 | bytes 65536 | tf_op jit(solution)/shard_map/project/pallas_call | solution.py:729
  96.0 7.2 %attend.1 = (f32[1024,256]{1,0:T(8,128)}, f32[8,1024]{1,0:T(8,128)}, bf16[8,128,256]{2,1,0:T(8,128)(2,1)}) custom-call(s32[1]{0:T(128)} %bitcast.me_ref, bf16[1024,256]{1,0:T(8,128)(2,1)} %get-tuple-element.206.q_ref, bf16[1024,256]{1,0:T(8,128)(2,1)} %get-tuple-element.207.k_ref, bf16[1024,256]{1,0:T(8,128)(2,1)} %get-tuple-element.208.v_ref, ...), custom_call_target="tpu_custom_call" | custom-call | flops 1048576 | bytes 65536 | tf_op jit(solution)/shard_map/attend/pallas_call | solution.py:781
  103.2 2.8 collective-permute-done.15.refs_2_.refs_6_
  110.5 19.5 %all_to_all.15.att_ref = bf16[8,128,256]{2,1,0:T(8,128)(2,1)} all-to-all(bf16[8,128,256]{2,1,0:T(8,128)(2,1)S(1)} %copy-done.44), channel_id=1, replica_groups=mesh['rep'=4,'fsdp'=8] {'fsdp'}, dimensions={0} | all-to-all | bytes 1048576 | tf_op jit(solution)/shard_map/all_to_all | solution.py:1509
  134.0 7.2 %mix.1 = (f32[128,2048]{1,0:T(8,128)}, bf16[128,2176]{1,0:T(8,128)(2,1)}, bf16[128,128]{1,0:T(8,128)(2,1)}, f32[128,128]{1,0:T(8,128)}) custom-call(s32[1]{0:T(128)} %bitcast.me_ref, bf16[128,2048]{1,0:T(8,128)(2,1)} %bitcast.25, f32[8,2048]{1,0:T(8,128)} %get-tuple-element.215.gains_ref, f32[1024,128]{1,0:T(8,128)} %get-tuple-element.214.mask_ref, ...), custom_call_target="tpu_custom_call" | custom-call | flops 1048576 | bytes 65536 | tf_op jit(solution)/shard_map/mix/pallas_call | solution.py:861
  141.3 3.5 collective-permute-done.22.refs_9_
  152.8 12.4 %collective-permute-done.30 = bf16[64,2048]{1,0:T(8,128)(2,1)S(1)} collective-permute-done((bf16[64,2048]{1,0:T(8,128)(2,1)S(1)}, bf16[64,2048]{1,0:T(8,128)(2,1)S(1)}, u32[]{:S(2)}, u32[]{:S(2)}) %collective-permute-start.30) | collective-permute-done | bytes 262176 | tf_op jit(solution)/shard_map/ppermute | solution.py:529
  167.8 7.7 %collective-permute-done.25 = bf16[64,2176]{1,0:T(8,128)(2,1)S(1)} collective-permute-done((bf16[64,2176]{1,0:T(8,128)(2,1)S(1)}, bf16[64,2176]{1,0:T(8,128)(2,1)S(1)}, u32[]{:S(2)}, u32[]{:S(2)}) %collective-permute-start.25) | collective-permute-done | bytes 278560 | tf_op jit(solution)/shard_map/ppermute | solution.py:529
  177.4 4.2 collective-permute-done.34.refs_13_
  182.7 41.9 %expert.2 = (bf16[512,2048]{1,0:T(8,128)(2,1)}, bf16[512,2048]{1,0:T(8,128)(2,1)}, bf16[1024,2304]{1,0:T(8,128)(2,1)}, f32[1024,128]{1,0:T(8,128)}, bf16[288,204...) custom-call(s32[1]{0:T(128)} %bitcast.13.where_ref, f32[1024,128]{1,0:T(8,128)} %get-tuple-element.214.mask_ref, ...), custom_call_target="tpu_custom_call" | custom-call | flops 22817013760 | bytes 41943040 | tf_op jit(solution)/shard_map/expert/pallas_call | solution.py:1033
  226.2 43.0 %expert.3 = (bf16[512,2048]{1,0:T(8,128)(2,1)}, bf16[512,2048]{1,0:T(8,128)(2,1)}, bf16[1024,2304]{1,0:T(8,128)(2,1)}, f32[1024,128]{1,0:T(8,128)}, bf16[288,204...) custom-call(s32[1]{0:T(128)} %bitcast.13.where_ref, f32[1024,128]{1,0:T(8,128)} %get-tuple-element.214.mask_ref, ...), custom_call_target="tpu_custom_call" | custom-call | flops 22817013760 | bytes 41943040 | tf_op jit(solution)/shard_map/expert/pallas_call | solution.py:1033
  274.7 29.0 %rows.1 = (bf16[512,2176]{1,0:T(8,128)(2,1)}, bf16[512,2176]{1,0:T(8,128)(2,1)}) custom-call(bf16[1024,2304]{1,0:T(8,128)(2,1)} %get-tuple-element.239.refs_0_, bf16[1024,2304]{1,0:T(8,128)(2,1)} %get-tuple-element.249.refs_1_, f32[1024,128]{1,0:T(8,128)} %get-tuple-element.250.refs_2_, f32[1024,128]{1,0:T(8,128)} %get-tuple-element.251.refs_3_, ...), custom_call_target="tpu_custom_call" | custom-call | flops 19327352832 | bytes 41943040 | tf_op jit(solution)/shard_map/rows/pallas_call | solution.py:1115
  312.9 7.9 %collective-permute-done.42 = bf16[144,2048]{1,0:T(8,128)(2,1)S(1)} collective-permute-done((bf16[144,2048]{1,0:T(8,128)(2,1)}, bf16[144,2048]{1,0:T(8,128)(2,1)S(1)}, u32[]{:S(2)}, u32[]{:S(2)}) %collective-permute-start.42) | collective-permute-done | bytes 589856 | tf_op jit(solution)/shard_map/ppermute | solution.py:607
  324.2 14.6 %collective-permute-done.45.refs_4_ = bf16[72,2048]{1,0:T(8,128)(2,1)S(1)} collective-permute-done((bf16[72,2048]{1,0:T(8,128)(2,1)S(1)}, bf16[72,2048]{1,0:T(8,128)(2,1)S(1)}, u32[]{:S(2)}, u32[]{:S(2)}) %collective-permute-start.45) | collective-permute-done | bytes 294944 | tf_op jit(solution)/shard_map/ppermute | solution.py:607
  341.1 11.4 %unmix.1 = (f32[128,2048]{1,0:T(8,128)}, bf16[8,256,256]{2,1,0:T(8,128)(2,1)}, bf16[8,128,256]{2,1,0:T(8,128)(2,1)}) custom-call(s32[1]{0:T(128)} %bitcast.me_ref, f32[128,2048]{1,0:T(8,128)} %get-tuple-element.229.resid_ref, bf16[128,2048]{1,0:T(8,128)(2,1)} %bitcast.12.refs_7_.cot_ref, f32[8,2048]{1,0:T(8,128)} %get-tuple-element.215.gains_ref, ...), custom_call_target="tpu_custom_call" | custom-call | flops 1048576 | bytes 65536 | tf_op jit(solution)/shard_map/unmix/pallas_call | solution.py:1180
  354.2 3.7 all-to-all-start.2
  360.8 13.5 %collective-permute-done.48 = bf16[72,2048]{1,0:T(8,128)(2,1)S(1)} collective-permute-done((bf16[72,2048]{1,0:T(8,128)(2,1)S(1)}, bf16[72,2048]{1,0:T(8,128)(2,1)S(1)}, u32[]{:S(2)}, u32[]{:S(2)}) %collective-permute-start.48) | collective-permute-done | bytes 294944 | tf_op jit(solution)/shard_map/ppermute | solution.py:607
  377.1 15.3 %attend_back.1 = (bf16[1024,768]{1,0:T(8,128)(2,1)}, bf16[1024,384]{1,0:T(8,128)(2,1)}, bf16[2560,256]{1,0:T(8,128)(2,1)}, bf16[2560,256]{1,0:T(8,128)(2,1)}, bf16[384,256]{1,0:T(8,128)(2,1)}) custom-call(s32[1]{0:T(128)} %bitcast.me_ref, bf16[1024,256]{1,0:T(8,128)(2,1)} %get-tuple-element.206.q_ref, bf16[1024,256]{1,0:T(8,128)(2,1)} %get-tuple-element.207.k_ref, ...), custom_call_target="tpu_custom_call" | custom-call | flops 1048576 | bytes 65536 | tf_op jit(solution)/shard_map/attend_back/pallas_call | solution.py:1256
  397.9 11.3 %unproject.1 = (bf16[512,2048]{1,0:T(8,128)(2,1)}, bf16[512,2048]{1,0:T(8,128)(2,1)}) custom-call(s32[1]{0:T(128)} %bitcast.me_ref, bf16[1024,768]{1,0:T(8,128)(2,1)} %get-tuple-element.284.proj_ref, bf16[1024,384]{1,0:T(8,128)(2,1)} %get-tuple-element.285.low_ref, bf16[128,1152]{1,0:T(8,128)(2,1)} %fusion.13.refs_7_.refs_0_, bf16[128,1152]{1,0:T(8,128)(2,1)} %copy-done.15, ...), custom_call_target="tpu_custom_call" | custom-call | flops 1048576 | bytes 65536 | tf_op jit(solution)/shard_map/unproject/pallas_call | solution.py:1323
  416.0 2.9 collective-permute-done.57
  428.6 11.5 %collective-permute-done.60 = bf16[64,2048]{1,0:T(8,128)(2,1)S(1)} collective-permute-done((bf16[64,2048]{1,0:T(8,128)(2,1)S(1)}, bf16[64,2048]{1,0:T(8,128)(2,1)S(1)}, u32[]{:S(2)}, u32[]{:S(2)}) %collective-permute-start.60) | collective-permute-done | bytes 262176 | tf_op jit(solution)/shard_map/ppermute | solution.py:529
  452.3 4.7 unpack.2
  470.4 4.3 collective-permute-done.73.refs_2_
  477.7 3.7 finish.1
  481.4 2.9 layer.1
  487.1 7.3 %collective-permute-done.70.refs_6_ = bf16[72,2048]{1,0:T(8,128)(2,1)S(1)} collective-permute-done((bf16[72,2048]{1,0:T(8,128)(2,1)}, bf16[72,2048]{1,0:T(8,128)(2,1)S(1)}, u32[]{:S(2)}, u32[]{:S(2)}) %collective-permute-start.70) | collective-permute-done | bytes 294944 | tf_op jit(solution)/shard_map/ppermute | solution.py:607
  494.4 3.3 collective-permute-done.71.refs_7_
  500.9 4.7 unpack.3
  (355 shorter events, 140.3 us)
Async XLA Ops:
  6.9 66.8 %collective-permute-start.11 = (bf16[128,1152]{1,0:T(8,128)(2,1)}, bf16[128,1152]{1,0:T(8,128)(2,1)}, u32[]{:S(2)}, u32[]{:S(2)}) collective-permute-start(bf16[128,1152]{1,0:T(8,128)(2,1)} %fusion.13.refs_7_.refs_0_), channel_id=1, source_target_pairs={{0,1},{1,0},{2,3},{3,2},{4,5},{5,4},{6,7},{7,6},{8,9},{9,8},{10,11... | collective-permute-start | bytes 884744 | tf_op jit(solution)/shard_map/ppermute | solution.py:529
  7.3 22.0 %collective-permute-start.8 = (bf16[128,1152]{1,0:T(8,128)(2,1)}, bf16[128,1152]{1,0:T(8,128)(2,1)S(1)}, u32[]{:S(2)}, u32[]{:S(2)}) collective-permute-start(bf16[128,1152]{1,0:T(8,128)(2,1)} %fusion.13.refs_7_.refs_0_), channel_id=1, source_target_pairs={{0,4},{1,5},{2,6},{3,7},{4,0},{5,1},{6,2},{7,3},{8,12},{9,13},{10,... | collective-permute-start | bytes 884744 | tf_op jit(solution)/shard_map/ppermute | solution.py:529
  9.8 21.5 %collective-permute-start.7 = (bf16[128,1152]{1,0:T(8,128)(2,1)}, bf16[128,1152]{1,0:T(8,128)(2,1)S(1)}, u32[]{:S(2)}, u32[]{:S(2)}) collective-permute-start(bf16[128,1152]{1,0:T(8,128)(2,1)} %fusion.13.refs_7_.refs_0_), channel_id=1, source_target_pairs={{0,2},{1,3},{2,0},{3,1},{4,6},{5,7},{6,4},{7,5},{8,10},{9,11},{10,... | collective-permute-start | bytes 884744 | tf_op jit(solution)/shard_map/ppermute | solution.py:529
  11.3 21.7 %collective-permute-start.1 = (bf16[128,2048]{1,0:T(8,128)(2,1)S(1)}, bf16[128,2048]{1,0:T(8,128)(2,1)S(1)}, u32[]{:S(2)}, u32[]{:S(2)}) collective-permute-start(bf16[128,2048]{1,0:T(8,128)(2,1)S(1)} %bitcast.27), channel_id=1, source_target_pairs={{0,4},{1,5},{2,6},{3,7},{4,0},{5,1},{6,2},{7,3},{8,12},{9,13},{10,... | collective-permute-start | bytes 1572872 | tf_op jit(solution)/shard_map/ppermute | solution.py:529
  11.8 21.2 %collective-permute-start = (bf16[128,2048]{1,0:T(8,128)(2,1)S(1)}, bf16[128,2048]{1,0:T(8,128)(2,1)S(1)}, u32[]{:S(2)}, u32[]{:S(2)}) collective-permute-start(bf16[128,2048]{1,0:T(8,128)(2,1)S(1)} %bitcast.28), channel_id=1, source_target_pairs={{0,2},{1,3},{2,0},{3,1},{4,6},{5,7},{6,4},{7,5},{8,10},{9,11},{10,... | collective-permute-start | bytes 1572872 | tf_op jit(solution)/shard_map/ppermute | solution.py:529
  17.2 60.6 %all-to-all-start = ((bf16[8,3,256,256]{3,2,1,0:T(8,128)(2,1)}), bf16[8,3,256,256]{3,2,1,0:T(8,128)(2,1)}, u32[]{:S(2)}, u32[]{:S(2)}) async-start(bf16[8,3,256,256]{3,2,1,0:T(8,128)(2,1)} %by_columns.1), calls=%async_computation | async-start | bytes 6291456 | tf_op jit(solution)/shard_map/all_to_all | solution.py:1495
  29.4 43.7 %collective-permute-start.10 = (bf16[64,1152]{1,0:T(8,128)(2,1)S(1)}, bf16[64,1152]{1,0:T(8,128)(2,1)S(1)}, u32[]{:S(2)}, u32[]{:S(2)}) collective-permute-start(bf16[64,1152]{1,0:T(8,128)(2,1)S(1)} %slice.335), channel_id=1, source_target_pairs={{0,2},{1,3},{2,0},{3,1},{4,6},{5,7},{6,4},{7,5},{8,10},{9,11},{10,... | collective-permute-start | bytes 442376 | tf_op jit(solution)/shard_map/ppermute | solution.py:529
  31.4 34.6 %collective-permute-start.9 = (bf16[64,1152]{1,0:T(8,128)(2,1)S(1)}, bf16[64,1152]{1,0:T(8,128)(2,1)S(1)}, u32[]{:S(2)}, u32[]{:S(2)}) collective-permute-start(bf16[64,1152]{1,0:T(8,128)(2,1)S(1)} %slice.334), channel_id=1, source_target_pairs={{0,4},{1,5},{2,6},{3,7},{4,0},{5,1},{6,2},{7,3},{8,12},{9,13},{10,... | collective-permute-start | bytes 442376 | tf_op jit(solution)/shard_map/ppermute | solution.py:529
  33.1 38.4 %collective-permute-start.2 = (bf16[64,2048]{1,0:T(8,128)(2,1)S(1)}, bf16[64,2048]{1,0:T(8,128)(2,1)S(1)}, u32[]{:S(2)}, u32[]{:S(2)}) collective-permute-start(bf16[64,2048]{1,0:T(8,128)(2,1)S(1)} %slice.253), channel_id=1, source_target_pairs={{0,4},{1,5},{2,6},{3,7},{4,0},{5,1},{6,2},{7,3},{8,12},{9,13},{10,... | collective-permute-start | bytes 786440 | tf_op jit(solution)/shard_map/ppermute | solution.py:529
  34.0 39.0 %collective-permute-start.3 = (bf16[64,2048]{1,0:T(8,128)(2,1)S(1)}, bf16[64,2048]{1,0:T(8,128)(2,1)S(1)}, u32[]{:S(2)}, u32[]{:S(2)}) collective-permute-start(bf16[64,2048]{1,0:T(8,128)(2,1)S(1)} %slice.254), channel_id=1, source_target_pairs={{0,2},{1,3},{2,0},{3,1},{4,6},{5,7},{6,4},{7,5},{8,10},{9,11},{10,... | collective-permute-start | bytes 786440 | tf_op jit(solution)/shard_map/ppermute | solution.py:529
  77.8 28.3 %collective-permute-start.15 = (bf16[256,2304]{1,0:T(8,128)(2,1)}, bf16[256,2304]{1,0:T(8,128)(2,1)S(1)}, u32[]{:S(2)}, u32[]{:S(2)}) collective-permute-start(bf16[256,2304]{1,0:T(8,128)(2,1)} %pad_maximum_fusion.1.refs_0_.refs_4_), channel_id=1, source_target_pairs={{0,4},{1,5},{2,6},{3,7},{4,0},{5,1},{6,2},{7,3},{8,12},{9,13},{10,... | collective-permute-start | bytes 3538952 | tf_op jit(solution)/shard_map/ppermute | solution.py:529
  78.9 27.9 %collective-permute-start.14 = (bf16[256,2304]{1,0:T(8,128)(2,1)}, bf16[256,2304]{1,0:T(8,128)(2,1)S(1)}, u32[]{:S(2)}, u32[]{:S(2)}) collective-permute-start(bf16[256,2304]{1,0:T(8,128)(2,1)} %pad_maximum_fusion.1.refs_0_.refs_4_), channel_id=1, source_target_pairs={{0,2},{1,3},{2,0},{3,1},{4,6},{5,7},{6,4},{7,5},{8,10},{9,11},{10,... | collective-permute-start | bytes 3538952 | tf_op jit(solution)/shard_map/ppermute | solution.py:529
  107.0 23.0 %collective-permute-start.19 = (bf16[512,2304]{1,0:T(8,128)(2,1)S(1)}, bf16[512,2304]{1,0:T(8,128)(2,1)}, u32[]{:S(2)}, u32[]{:S(2)}) collective-permute-start(bf16[512,2304]{1,0:T(8,128)(2,1)S(1)} %pad_maximum_fusion), channel_id=1, source_target_pairs={{0,1},{1,0},{2,3},{3,2},{4,5},{5,4},{6,7},{7,6},{8,9},{9,8},{10,11... | collective-permute-start | bytes 7077896 | tf_op jit(solution)/shard_map/ppermute | solution.py:529
  107.0 22.9 %collective-permute-start.18 = (bf16[256,2304]{1,0:T(8,128)(2,1)}, bf16[256,2304]{1,0:T(8,128)(2,1)S(1)}, u32[]{:S(2)}, u32[]{:S(2)}) collective-permute-start(bf16[256,2304]{1,0:T(8,128)(2,1)} %pad_maximum_fusion.1.refs_0_.refs_4_), channel_id=1, source_target_pairs={{0,1},{1,0},{2,3},{3,2},{4,5},{5,4},{6,7},{7,6},{8,9},{9,8},{10,11... | collective-permute-start | bytes 3538952 | tf_op jit(solution)/shard_map/ppermute | solution.py:529
  107.9 22.0 %collective-permute-start.17 = (bf16[128,2304]{1,0:T(8,128)(2,1)S(1)}, bf16[128,2304]{1,0:T(8,128)(2,1)S(1)}, u32[]{:S(2)}, u32[]{:S(2)}) collective-permute-start(bf16[128,2304]{1,0:T(8,128)(2,1)S(1)} %slice.265), channel_id=1, source_target_pairs={{0,2},{1,3},{2,0},{3,1},{4,6},{5,7},{6,4},{7,5},{8,10},{9,11},{10,... | collective-permute-start | bytes 1769480 | tf_op jit(solution)/shard_map/ppermute | solution.py:529
  109.5 20.5 %collective-permute-start.16 = (bf16[128,2304]{1,0:T(8,128)(2,1)S(1)}, bf16[128,2304]{1,0:T(8,128)(2,1)S(1)}, u32[]{:S(2)}, u32[]{:S(2)}) collective-permute-start(bf16[128,2304]{1,0:T(8,128)(2,1)S(1)} %slice.264), channel_id=1, source_target_pairs={{0,4},{1,5},{2,6},{3,7},{4,0},{5,1},{6,2},{7,3},{8,12},{9,13},{10,... | collective-permute-start | bytes 1769480 | tf_op jit(solution)/shard_map/ppermute | solution.py:529
  145.5 20.4 %collective-permute-start.24 = (bf16[128,2176]{1,0:T(8,128)(2,1)}, bf16[128,2176]{1,0:T(8,128)(2,1)S(1)}, u32[]{:S(2)}, u32[]{:S(2)}) collective-permute-start(bf16[128,2176]{1,0:T(8,128)(2,1)} %get-tuple-element.235.refs_0_), channel_id=1, source_target_pairs={{0,4},{1,5},{2,6},{3,7},{4,0},{5,1},{6,2},{7,3},{8,12},{9,13},{10,... | collective-permute-start | bytes 1671176 | tf_op jit(solution)/shard_map/ppermute | solution.py:529
  146.6 20.0 %collective-permute-start.23 = (bf16[128,2176]{1,0:T(8,128)(2,1)}, bf16[128,2176]{1,0:T(8,128)(2,1)S(1)}, u32[]{:S(2)}, u32[]{:S(2)}) collective-permute-start(bf16[128,2176]{1,0:T(8,128)(2,1)} %get-tuple-element.235.refs_0_), channel_id=1, source_target_pairs={{0,2},{1,3},{2,0},{3,1},{4,6},{5,7},{6,4},{7,5},{8,10},{9,11},{10,... | collective-permute-start | bytes 1671176 | tf_op jit(solution)/shard_map/ppermute | solution.py:529
  149.1 28.3 %collective-permute-start.27 = (bf16[128,2176]{1,0:T(8,128)(2,1)}, bf16[128,2176]{1,0:T(8,128)(2,1)}, u32[]{:S(2)}, u32[]{:S(2)}) collective-permute-start(bf16[128,2176]{1,0:T(8,128)(2,1)} %get-tuple-element.235.refs_0_), channel_id=1, source_target_pairs={{0,1},{1,0},{2,3},{3,2},{4,5},{5,4},{6,7},{7,6},{8,9},{9,8},{10,11... | collective-permute-start | bytes 1671176 | tf_op jit(solution)/shard_map/ppermute | solution.py:529
  149.2 27.0 %collective-permute-start.31 = (bf16[64,2048]{1,0:T(8,128)(2,1)S(1)}, bf16[64,2048]{1,0:T(8,128)(2,1)S(1)}, u32[]{:S(2)}, u32[]{:S(2)}) collective-permute-start(bf16[64,2048]{1,0:T(8,128)(2,1)S(1)} %slice.269), channel_id=1, source_target_pairs={{0,2},{1,3},{2,0},{3,1},{4,6},{5,7},{6,4},{7,5},{8,10},{9,11},{10,... | collective-permute-start | bytes 786440 | tf_op jit(solution)/shard_map/ppermute | solution.py:529
  224.6 44.7 %collective-permute-start.35 = (bf16[288,2048]{1,0:T(8,128)(2,1)}, bf16[288,2048]{1,0:T(8,128)(2,1)S(1)}, u32[]{:S(2)}, u32[]{:S(2)}) collective-permute-start(bf16[288,2048]{1,0:T(8,128)(2,1)} %get-tuple-element.246), channel_id=1, source_target_pairs={{0,8},{8,0},{16,24},{24,16},{1,9},{9,1},{17,25},{25,17},{2,10},{10... | collective-permute-start | bytes 3538952 | tf_op jit(solution)/shard_map/ppermute | solution.py:607
  270.6 33.1 %collective-permute-start.36 = (bf16[144,2048]{1,0:T(8,128)(2,1)}, bf16[144,2048]{1,0:T(8,128)(2,1)}, u32[]{:S(2)}, u32[]{:S(2)}) collective-permute-start(bf16[144,2048]{1,0:T(8,128)(2,1)} %slice.338), channel_id=1, source_target_pairs={{0,16},{8,24},{16,0},{24,8},{1,17},{9,25},{17,1},{25,9},{2,18},{10... | collective-permute-start | bytes 1769480 | tf_op jit(solution)/shard_map/ppermute | solution.py:607
  273.2 30.5 %collective-permute-start.38 = (bf16[512,2048]{1,0:T(8,128)(2,1)}, bf16[512,2048]{1,0:T(8,128)(2,1)S(1)}, u32[]{:S(2)}, u32[]{:S(2)}) collective-permute-start(bf16[512,2048]{1,0:T(8,128)(2,1)} %get-tuple-element.257), channel_id=1, source_target_pairs={{0,1},{1,0},{2,3},{3,2},{4,5},{5,4},{6,7},{7,6},{8,9},{9,8},{10,11... | collective-permute-start | bytes 6291464 | tf_op jit(solution)/shard_map/ppermute | solution.py:529
  274.3 29.4 %collective-permute-start.37 = (bf16[144,2048]{1,0:T(8,128)(2,1)}, bf16[144,2048]{1,0:T(8,128)(2,1)S(1)}, u32[]{:S(2)}, u32[]{:S(2)}) collective-permute-start(bf16[144,2048]{1,0:T(8,128)(2,1)} %get-tuple-element.381), channel_id=1, source_target_pairs={{0,8},{8,0},{16,24},{24,16},{1,9},{9,1},{17,25},{25,17},{2,10},{10... | collective-permute-start | bytes 1769480 | tf_op jit(solution)/shard_map/ppermute | solution.py:607
  321.0 17.8 %collective-permute-start.43 = (bf16[128,2176]{1,0:T(8,128)(2,1)S(1)}, bf16[128,2176]{1,0:T(8,128)(2,1)S(1)}, u32[]{:S(2)}, u32[]{:S(2)}) collective-permute-start(bf16[128,2176]{1,0:T(8,128)(2,1)S(1)} %pad_maximum_fusion.6), channel_id=1, source_target_pairs={{0,2},{1,3},{2,0},{3,1},{4,6},{5,7},{6,4},{7,5},{8,10},{9,11},{10,... | collective-permute-start | bytes 1671176 | tf_op jit(solution)/shard_map/ppermute | solution.py:529
  354.2 20.3 %all-to-all-start.2 = ((bf16[8,128,256]{2,1,0:T(8,128)(2,1)}), bf16[8,128,256]{2,1,0:T(8,128)(2,1)S(1)}, u32[]{:S(2)}, u32[]{:S(2)}) async-start(bf16[8,128,256]{2,1,0:T(8,128)(2,1)} %get-tuple-element.270), calls=%async_computation.2 | async-start | bytes 1048576 | tf_op jit(solution)/shard_map/all_to_all | solution.py:1563
  393.2 18.9 %collective-permute-start.52 = (bf16[2560,256]{1,0:T(8,128)(2,1)}, bf16[2560,256]{1,0:T(8,128)(2,1)S(1)}, u32[]{:S(2)}, u32[]{:S(2)}) collective-permute-start(bf16[2560,256]{1,0:T(8,128)(2,1)} %get-tuple-element.287), channel_id=1, source_target_pairs={{0,1},{1,0},{2,3},{3,2},{4,5},{5,4},{6,7},{7,6},{8,9},{9,8},{10,11... | collective-permute-start | bytes 3932168 | tf_op jit(solution)/shard_map/ppermute | solution.py:529
  422.6 17.6 %collective-permute-start.63 = (bf16[72,2048]{1,0:T(8,128)(2,1)S(1)}, bf16[72,2048]{1,0:T(8,128)(2,1)}, u32[]{:S(2)}, u32[]{:S(2)}) collective-permute-start(bf16[72,2048]{1,0:T(8,128)(2,1)S(1)} %get-tuple-element.338.refs_1_), channel_id=1, source_target_pairs={{0,16},{8,24},{16,0},{24,8},{1,17},{9,25},{17,1},{25,9},{2,18},{10... | collective-permute-start | bytes 884744 | tf_op jit(solution)/shard_map/ppermute | solution.py:607
  466.1 31.5 %collective-permute-start.72 = (bf16[1024,256]{1,0:T(8,128)(2,1)S(1)}, bf16[1024,256]{1,0:T(8,128)(2,1)S(1)}, u32[]{:S(2)}, u32[]{:S(2)}) collective-permute-start(bf16[1024,256]{1,0:T(8,128)(2,1)S(1)} %add_convert_fusion.4.left_ref), channel_id=1, source_target_pairs={{0,16},{8,24},{16,0},{24,8},{1,17},{9,25},{17,1},{25,9},{2,18},{10... | collective-permute-start | bytes 1572872 | tf_op jit(solution)/shard_map/ppermute | solution.py:607
  468.4 18.7 %collective-permute-start.69 = (bf16[72,2048]{1,0:T(8,128)(2,1)S(1)}, bf16[72,2048]{1,0:T(8,128)(2,1)S(1)}, u32[]{:S(2)}, u32[]{:S(2)}) collective-permute-start(bf16[72,2048]{1,0:T(8,128)(2,1)S(1)} %get-tuple-element.338.refs_1_), channel_id=1, source_target_pairs={{0,8},{8,0},{16,24},{24,16},{1,9},{9,1},{17,25},{25,17},{2,10},{10... | collective-permute-start | bytes 884744 | tf_op jit(solution)/shard_map/ppermute | solution.py:607
  469.2 25.2 %collective-permute-start.70 = (bf16[72,2048]{1,0:T(8,128)(2,1)}, bf16[72,2048]{1,0:T(8,128)(2,1)S(1)}, u32[]{:S(2)}, u32[]{:S(2)}) collective-permute-start(bf16[72,2048]{1,0:T(8,128)(2,1)} %collective-permute-done.53.refs_4_), channel_id=1, source_target_pairs={{0,8},{8,0},{16,24},{24,16},{1,9},{9,1},{17,25},{25,17},{2,10},{10... | collective-permute-start | bytes 884744 | tf_op jit(solution)/shard_map/ppermute | solution.py:607
  475.5 22.1 %collective-permute-start.71 = (bf16[72,2048]{1,0:T(8,128)(2,1)}, bf16[72,2048]{1,0:T(8,128)(2,1)}, u32[]{:S(2)}, u32[]{:S(2)}) collective-permute-start(bf16[72,2048]{1,0:T(8,128)(2,1)} %collective-permute-done.63.refs_5_), channel_id=1, source_target_pairs={{0,8},{8,0},{16,24},{24,16},{1,9},{9,1},{17,25},{25,17},{2,10},{10... | collective-permute-start | bytes 884744 | tf_op jit(solution)/shard_map/ppermute | solution.py:607
  (104 other events, 983.3 us)

commit v4 on v3

--- a/solution.py
+++ b/solution.py
@@ -490,6 +490,8 @@
 EVERY = 8
 TILE = 256
 CUT = 512
+ROWS_TILE = 256
+ROWS_CUT = 512
 VMEM_BYTES = 64000000
 
 
@@ -670,11 +672,13 @@
 
     @pl.when(step == 0)
     def _():
-        for which in (1, 0, 2, 3):
+        for which in (1, 2, 3):
             for group in copies:
                 group[which].start()
         for item in w_copies:
             item.start()
+        for group in copies:
+            group[0].start()
         for group in copies:
             group[1].wait()
         for j in range(EVERY):
@@ -686,10 +690,17 @@
                     line = extra[j * rows : j * rows + 16, 256:384].astype(f32)
                     gains_ref[i : i + 1, pl.ds(spot, rows)] = line[2 * i + part : 2 * i + part + 1, :]
         for group in copies:
-            for which in (0, 2, 3):
+            for which in (2, 3):
                 group[which].wait()
         for item in w_copies:
             item.wait()
+
+    for i in range(EVERY // 2):
+
+        @pl.when(step == i)
+        def _():
+            copies[2 * i][0].wait()
+            copies[2 * i + 1][0].wait()
 
     at = pl.ds(pl.multiple_of(step * TILE, TILE), TILE)
     seg = jnp.broadcast_to(extra[at, 0:1].astype(f32), (TILE, 128))
@@ -705,13 +716,12 @@
     scale = lax.rsqrt(jnp.mean(values * values, axis=1, keepdims=True) + EPSILON)
     normed = (values * scale * gains_ref[0:1, :]).astype(bf16)
     normed_ref[...] = normed
+    wide_all = mm(normed, weight[...])
     low = (mm(normed, down[...]) * jnp.concatenate([mask] * 3, axis=1)).astype(bf16)
     low_ref[...] = low
     cosine, sine = cos_ref[...], sin_ref[...]
     for i, ref in enumerate((q_ref, k_ref, v_ref)):
-        proj = mm(normed, weight[:, i * wide : (i + 1) * wide]) + mm_nt(
-            low[:, i * SR : (i + 1) * SR], up_ref[i]
-        )
+        proj = wide_all[:, i * wide : (i + 1) * wide] + mm_nt(low[:, i * SR : (i + 1) * SR], up_ref[i])
         for h in range(wide // HD):
             part = proj[:, h * HD : (h + 1) * HD]
             ref[:, h * HD : (h + 1) * HD] = (turn(part, cosine, sine) if i < 2 else part).astype(bf16)
@@ -911,24 +921,26 @@
         given.append(pltpu.make_async_copy(rows_hbm[j], rows_s.at[at, :], block_sems.at[j, 0]))
         given.append(pltpu.make_async_copy(cot_hbm[j], cot_s.at[at, :], block_sems.at[j, 1]))
 
-    def wait_for(group, when=0):
+    def wait_for(group, then=(), when=0):
         @pl.when(step == when)
         def _():
             for item in group:
                 item.wait()
+            for item in then:
+                item.start()
 
     @pl.when(step == 0)
     def _():
-        for item in given[0:4] + early + late + given[4:]:
+        for item in given[0:4] + early[:6]:
             item.start()
         g_a_in[...] = jnp.zeros_like(g_a_in)
         g_b_down[...] = jnp.zeros_like(g_b_down)
         g_b_in[...] = jnp.zeros_like(g_b_in)
         g_a_down[...] = jnp.zeros_like(g_a_down)
 
-    for i in range(blocks // 2):
-        wait_for(given[4 * i : 4 * i + 4], i)
-    wait_for(early[:2])
+    for i in range(1, blocks // 2):
+        wait_for(given[4 * i : 4 * i + 4], when=i)
+    wait_for([given[0], given[2]] + early[:2], early[6:])
     at_rows = pl.ds(pl.multiple_of(step * TILE, TILE), TILE)
     mask = mask_ref[...]
     mask_two = jnp.concatenate([mask, mask], axis=1)
@@ -940,7 +952,7 @@
     wait_for(early[2:4])
     act_parts = []
     for j in range(chunks):
-        wait_for(early[4 + 2 * j : 6 + 2 * j])
+        wait_for(early[4 + 2 * j : 6 + 2 * j], late if j == 0 else given[4:] if j == 1 else ())
         at = slice(j * CUT, (j + 1) * CUT)
         gate_h = mm(rows_gate, w_in[:, at])
         up_h = mm(rows_up, w_in[:, hidden + j * CUT : hidden + (j + 1) * CUT])
@@ -950,7 +962,7 @@
         slope_s[:, at] = up_h * (share * (1.0 + gate_h * (1.0 - share)))
         act_parts.append((silu * up_h).astype(bf16))
     act = jnp.concatenate(act_parts, axis=1)
-    wait_for(late)
+    wait_for([given[1], given[3]] + late)
 
     low_down = (mm(act, w_down[0:hidden, thin_at:]) * mask).astype(bf16)
     act_low = jnp.concatenate([act, low_down], axis=1)
@@ -1021,7 +1033,7 @@
     part, width = cot[0].shape
     hidden = weights[0].shape[2]
     tokens = blocks * part
-    shares = 2
+    shares = 2 if prev is None else 4
     grad_shape = ((4 * SR + SR // 2) // shares, width)
     in_specs = [scalars(), by_tile(TILE, SR), pl.BlockSpec((8, 128), lambda i: (0, 0))] + [in_place()] * (2 * GATHERED)
     operands = [where, mask, picks, *rows, *cot]
@@ -1067,10 +1079,10 @@
     even_ref, odd_ref, weight, sems = refs[2 * local + 3 :]
     step = pl.program_id(0)
     span = 2 * hidden + 2 * SR
-    chunks = width // CUT
+    chunks = width // ROWS_CUT
     copies = []
     for j in range(chunks):
-        at = slice(j * CUT, (j + 1) * CUT)
+        at = slice(j * ROWS_CUT, (j + 1) * ROWS_CUT)
         group = []
         for k in range(local):
             base = k * span
@@ -1100,13 +1112,13 @@
             for item in copies[j]:
                 item.wait()
 
-        at = slice(j * CUT, (j + 1) * CUT)
+        at = slice(j * ROWS_CUT, (j + 1) * ROWS_CUT)
         value = mm_nt(both, weight[at, :]).astype(bf16)
-        even_ref[:, at] = value[:part]
-        odd_ref[:, at] = value[part:]
+        for b in range(ROWS_TILE // part):
+            (even_ref, odd_ref)[b % 2][b // 2 * part : (b // 2 + 1) * part, at] = value[b * part : (b + 1) * part]
     total = sum([ref[...] for ref in extra[1:]], extra[0][...]).astype(bf16)
-    even_ref[:, width:] = total[:part]
-    odd_ref[:, width:] = total[part:]
+    for b in range(ROWS_TILE // part):
+        (even_ref, odd_ref)[b % 2][b // 2 * part : (b // 2 + 1) * part, width:] = total[b * part : (b + 1) * part]
 
 
 def rows_pass(part, d_all, extra, w_gate, w_up, a_in):
@@ -1114,13 +1126,13 @@
     tokens, span = d_all[0].shape
     return pl.pallas_call(
         functools.partial(rows_kernel, part, width, hidden, local),
-        grid=(tokens // TILE,),
-        in_specs=[by_tile(TILE, span)] * local + [by_tile(TILE, 128)] * local + [in_place()] * 3,
-        out_specs=[by_tile(part, width + 128)] * 2,
+        grid=(tokens // ROWS_TILE,),
+        in_specs=[by_tile(ROWS_TILE, span)] * local + [by_tile(ROWS_TILE, 128)] * local + [in_place()] * 3,
+        out_specs=[by_tile(ROWS_TILE // 2, width + 128)] * 2,
         out_shape=[shape_of((tokens // 2, width + 128))] * 2,
         scratch_shapes=[
             pltpu.VMEM((width, local * span), jnp.bfloat16),
-            pltpu.SemaphoreType.DMA((width // CUT, 4 * local)),
+            pltpu.SemaphoreType.DMA((width // ROWS_CUT, 4 * local)),
         ],
         compiler_params=params(),
         cost_estimate=cost(2 * tokens * width * span * local, 40 << 20),
@@ -1204,7 +1216,7 @@
 def attend_back_kernel(
     rows, wide,
     me_ref, q_ref, k_ref, v_ref, att_ref, lse_ref, col_ref, row_ref, cos_ref, sin_ref, low_ref, mask_ref, up_ref,
-    got_ref, out_grad_ref, normed_hbm, d_proj_ref, d_low_ref, even_ref, odd_ref, up_grad_ref, d_att, normed, sems,
+    got_ref, normed_hbm, d_proj_ref, d_low_ref, down_grad_ref, up_grad_ref, d_att, normed, sems,
 ):
     f32, bf16 = jnp.float32, jnp.bfloat16
     tokens = q_ref.shape[0]
@@ -1243,25 +1255,20 @@
     d_low_t = d_low_ref[...].T
     bring.wait()
     for j in range(EVERY):
-        at = pl.multiple_of((me ^ j) * wide, wide)
-        spot = (j // 2) * 5 * SR
-        ref = (even_ref, odd_ref)[j % 2]
-        ref[spot : spot + 2 * SR, :] = out_grad_ref[me ^ j]
-        ref[spot + 2 * SR : spot + 5 * SR, :] = mm(d_low_t, normed[:, pl.ds(at, wide)]).astype(bf16)
-
-
-def attend_back(rows, me, q, k, v, att, lse, seg_col, seg_row, cosine, sine, low, mask, up, got, out_grad, normed):
+        down_grad_ref[j] = mm(d_low_t, normed[:, j * wide : (j + 1) * wide]).astype(bf16)
+
+
+def attend_back(rows, me, q, k, v, att, lse, seg_col, seg_row, cosine, sine, low, mask, up, got, normed):
     tokens, wide = q.shape
     width = wide * EVERY
     return pl.pallas_call(
         functools.partial(attend_back_kernel, rows, wide),
-        in_specs=[scalars()] + [whole()] * 14 + [in_place()],
-        out_specs=[whole()] * 5,
+        in_specs=[scalars()] + [whole()] * 13 + [in_place()],
+        out_specs=[whole()] * 4,
         out_shape=[
             shape_of((tokens, 3 * wide)),
             shape_of((tokens, 3 * SR)),
-            shape_of((4 * 5 * SR, wide)),
-            shape_of((4 * 5 * SR, wide)),
+            shape_of((EVERY, 3 * SR, wide)),
             shape_of((3 * SR, wide)),
         ],
         scratch_shapes=[
@@ -1272,7 +1279,7 @@
         compiler_params=params(),
         cost_estimate=cost(1 << 20, 1 << 16),
         name="attend_back",
-    )(me, q, k, v, att, lse, seg_col, seg_row, cosine, sine, low, mask, up, got, out_grad, normed)
+    )(me, q, k, v, att, lse, seg_col, seg_row, cosine, sine, low, mask, up, got, normed)
 
 
 def unproject_kernel(rows, width, wide, me_ref, proj_ref, low_ref, *refs):
@@ -1377,22 +1384,31 @@
     )(resid, *pieces)
 
 
-def unpack_kernel(hidden, first, where_ref, *refs):
+UNPACK_STEPS = 4
+
+
+def unpack_kernel(hidden, where_ref, *refs):
     f32 = jnp.float32
-    parts, refs = refs[:8], refs[8:]
-    refs = refs if first else refs[4:]
+    parts, refs = refs[:8], refs[-5:]
     a_in_ref, b_in_ref, a_down_ref, b_down_ref, packed = refs
     size = packed.shape[0] // 4
-    for b in range(4):
-        for i in range(2):
-            spot = pl.multiple_of((where_ref[0] ^ b) * size + i * (size // 2), 8)
-            packed[pl.ds(spot, size // 2), :] = parts[2 * b + i][...].astype(f32)
+    step = pl.program_id(0)
+    wide, thin = packed.shape[1] // UNPACK_STEPS, hidden // UNPACK_STEPS
+
+    @pl.when(step == 0)
+    def _():
+        for b in range(4):
+            for i in range(2):
+                spot = pl.multiple_of((where_ref[0] ^ b) * size + i * (size // 2), 8)
+                packed[pl.ds(spot, size // 2), :] = parts[2 * b + i][...].astype(f32)
+
+    at = pl.ds(pl.multiple_of(step * wide, 128), wide)
+    halves = [pl.ds(pl.multiple_of(i * hidden + step * thin, 128), thin) for i in range(2)]
     for i in range(2):
-        a_in_ref[0, i] = packed[i * SR : (i + 1) * SR, :].T
-        b_in_ref[0, i] = packed[3 * SR : 4 * SR, i * hidden : (i + 1) * hidden]
-    b_down_ref[0] = packed[2 * SR : 3 * SR, :]
-    a_down_ref[0, :, 0 : SR // 2] = packed[4 * SR :, 0:hidden].T
-    a_down_ref[0, :, SR // 2 :] = packed[4 * SR :, hidden:].T
+        a_in_ref[0, i] = packed[i * SR : (i + 1) * SR, at].T
+        b_in_ref[0, i] = packed[3 * SR : 4 * SR, halves[i]]
+        a_down_ref[0, :, i * (SR // 2) : (i + 1) * (SR // 2)] = packed[4 * SR :, halves[i]].T
+    b_down_ref[0] = packed[2 * SR : 3 * SR, at]
 
 
 def unpack(k, where, quarters, hidden, experts, before):
@@ -1402,12 +1418,16 @@
     first = before is None
     shapes = [(experts, 2, width, SR), (experts, 2, SR, hidden), (experts, hidden, SR), (experts, SR, width)]
     given = [] if first else list(before)
+    wide, thin = width // UNPACK_STEPS, hidden // UNPACK_STEPS
     return pl.pallas_call(
-        functools.partial(unpack_kernel, hidden, first),
-        grid=(1,),
+        functools.partial(unpack_kernel, hidden),
+        grid=(UNPACK_STEPS,),
         in_specs=[scalars()] + [whole()] * 8 + [in_place()] * len(given),
         out_specs=[
-            pl.BlockSpec((1,) + shape[1:], lambda i, n=len(shape): (k,) + (0,) * (n - 1)) for shape in shapes
+            pl.BlockSpec((1, 2, wide, SR), lambda i: (k, 0, i, 0)),
+            pl.BlockSpec((1, 2, SR, thin), lambda i: (k, 0, 0, i)),
+            pl.BlockSpec((1, thin, SR), lambda i: (k, i, 0)),
+            pl.BlockSpec((1, SR, wide), lambda i: (k, 0, i)),
         ],
         out_shape=[shape_of(shape, f32) for shape in shapes],
         input_output_aliases={} if first else {9 + i: i for i in range(4)},
@@ -1418,26 +1438,27 @@
     )(where, *quarters, *given)
 
 
-def thin_kernel(left_ref, right_ref, a_ref, b_ref):
-    total = left_ref[...].astype(jnp.float32) + right_ref[...].astype(jnp.float32)
+def thin_kernel(late_left, late_right, early_left, early_right, a_ref, b_ref):
+    f32 = jnp.float32
+    late = late_left[...].astype(f32) + late_right[...].astype(f32)
+    early = early_left[...].astype(f32) + early_right[...].astype(f32)
     for i in range(4):
         at = (2 + i) * SR if i < 3 else 0
-        a_ref[i] = total[at : at + SR, :].T
-        at = (5 + i) * SR if i < 3 else SR
-        b_ref[i] = total[at : at + SR, :].T
-
-
-def thin_grads(left, right):
-    wide = left.shape[1]
+        a_ref[i] = late[at : at + SR, :].T
+        b_ref[i] = (early[i * SR : (i + 1) * SR, :] if i < 3 else late[SR : 2 * SR, :]).T
+
+
+def thin_grads(late, early):
+    wide = late[0].shape[1]
     return pl.pallas_call(
         thin_kernel,
-        in_specs=[whole()] * 2,
+        in_specs=[whole()] * 4,
         out_specs=[whole()] * 2,
         out_shape=[shape_of((4, wide, SR), jnp.float32)] * 2,
         compiler_params=params(),
         cost_estimate=cost(1 << 20, 1 << 16),
         name="thin_grads",
-    )(left, right)
+    )(*late, *early)
 
 
 def split_layer(
@@ -1508,15 +1529,16 @@
     att_send, out_first = tie(att_send, out_first)
     att_got = lax.all_to_all(att_send, "fsdp", split_axis=0, concat_axis=0, tiled=True)
     far, *others = gather_second(*out_first)
-    far, others, att_got, upstream_now = tie(far, others, att_got, upstream)
-    cot_first = gather_first(upstream_now)
+    cot_first = gather_first(tie(upstream, att_send)[0])
+    far, others, att_got, cot_first = tie(far, others, att_got, cot_first)
     out_given = gather_third(out_first, far, *others)
+    cot_second = gather_second(*cot_first)
     resid_one, normed_own, low_out, gates_own = mix(
         me, hidden, gains, mask, router_all, named, att_got, out_given
     )
-    normed_own, cot_first = tie(normed_own, cot_first)
+    normed_own, cot_second = tie(normed_own, cot_second)
     normed_given = gather_relative(normed_own)
-    cot_given = gather_third(cot_first, *gather_second(*cot_first))
+    cot_given = gather_third(cot_first, *cot_second)
 
     weights = (w_gate, w_up, w_down, exp_a_in, exp_b_in, exp_a_down, exp_b_down)
     *state, d_all_a, extra_a, kept_a, sent_a = expert_pass(
@@ -1532,14 +1554,14 @@
         return [values[: values.shape[0] // 2], values[values.shape[0] // 2 :]]
 
     sent_a = rep_swap(sent_a, 1)
-    *state, d_all_b, extra_b, kept_b, sent_b = expert_pass(
+    *state, d_all_b, extra_b, kept_0, kept_1, sent_0, sent_1 = expert_pass(
         1, where, normed_given, cot_given, mask, pick_rows[1], state, weights
     )
+    kept_b, sent_b = [kept_0, kept_1], [sent_0, sent_1]
     d_all_b, kept_b, sent_b, sent_a, state = tie(d_all_b, kept_b, sent_b, sent_a, state)
     out_even, out_odd = state
     half_a = add_half(kept_a, sent_a)
     size = half_a.shape[0] // 2
-    sent_b, kept_b = in_two(sent_b), in_two(kept_b)
     sent_b[0] = rep_swap(sent_b[0], 1)
     other_a = rep_swap(half_a[size:], 2)
     out_got = swap(out_odd, 1)
@@ -1565,48 +1587,50 @@
     half_b = later(in_two(add_half(kept_b[1], sent_b[1])), d_att_send)
     one_a[0] = rep_swap(later(total_a[0], d_att_send), 1)
     other_b = [rep_swap(half_b[0], 2)]
-    d_att_got, other_b[0], one_a[0] = tie(d_att_got, other_b[0], one_a[0])
+    out_far = scatter_second(*later((out_even, out_got), d_att_send))
+    d_att_got, other_b[0], one_a[0], out_far = tie(d_att_got, other_b[0], one_a[0], out_far)
     total_b = [add_half(mine_b[: size // 2], other_b[0])]
     other_b.append(rep_swap(later(half_b[1], d_att_got), 2))
     three_a = [rep_swap(later(two_a[0], d_att_got), 1)]
-    d_proj, d_low, thin_even, thin_odd, up_grads = attend_back(
+
+    def exchange(values):
+        return lax.all_to_all(values, "fsdp", split_axis=0, concat_axis=0, tiled=True)
+
+    out_grads = exchange(later(thin_send, d_att_got))
+    d_proj, d_low, down_send, up_grads = attend_back(
         rows, me, queries, keys, values, att, lse, seg_col, seg_row, cosine, sine, low_qkv, mask, b_attn,
-        d_att_got, thin_send, normed_one,
-    )
-    d_proj, thin_odd, other_b[1], three_a[0] = tie(d_proj, thin_odd, other_b[1], three_a[0])
-    thin_got = swap(thin_odd, 1)
+        d_att_got, normed_one,
+    )
+    d_proj, down_send, other_b[1], three_a[0], out_grads = tie(d_proj, down_send, other_b[1], three_a[0], out_grads)
+    down_grads = exchange(down_send)
     two_b = [rep_swap(later(total_b[0], d_proj), 2)]
     three_a.append(rep_swap(later(two_a[1], d_proj), 1))
     even, odd = unproject(rows, me, d_proj, d_low, given, w_got)
-    odd, thin_got, two_b[0], three_a[1] = tie(odd, thin_got, two_b[0], three_a[1])
+    odd, down_grads, two_b[0], three_a[1] = tie(odd, down_grads, two_b[0], three_a[1])
+    got = swap(odd, 1)
+    thin = [jnp.sum(part.astype(f32), axis=0).astype(bf16) for part in (out_grads, down_grads)]
+    thin = jnp.concatenate(thin, axis=0)
+    thin_near = rep_swap(thin, 1)
     total_b.append(later(add_half(mine_b[size // 2 :], other_b[1]), odd))
-    got = swap(odd, 1)
-    thin_far = scatter_second(thin_even, thin_got)
-    one_b = [rep_swap(later(total_b[0], odd), 1)]
-    got, thin_far, one_b[0] = tie(got, thin_far, one_b[0])
-    thin_pieces = scatter_third(thin_even, thin_got, *thin_far)
+    two_b.append(rep_swap(total_b[1], 2))
+    up_near = rep_swap(later(up_grads, odd), 1)
     d_far = scatter_second(even, got)
-    two_b.append(rep_swap(later(total_b[1], got), 2))
-    d_far, thin_pieces, two_b[1] = tie(d_far, thin_pieces, two_b[1])
+    d_far, thin_near, two_b[1], up_near = tie(d_far, thin_near, two_b[1], up_near)
     pieces = scatter_third(even, got, *d_far)
-    thin = jnp.concatenate(
-        [sum_pieces(*[piece[: 5 * SR] for piece in thin_pieces]).astype(bf16), up_grads], axis=0
-    )
-    thin_near = rep_swap(thin, 1)
-    out_far = scatter_second(*later((out_even, out_got), d_far))
+    thin, up_grads = add_half(thin, thin_near), add_half(up_grads, up_near)
+    thin_last, up_far = rep_swap(thin, 2), rep_swap(up_grads, 2)
+    one_b = [rep_swap(later(total_b[0], d_far), 1)]
     grads = unpack(0, where, later([total_a, one_a, two_a, three_a], d_far), inner, local, None)
-    pieces, thin_near, out_far, grads = tie(pieces, thin_near, out_far, grads)
-    thin = add_half(thin, thin_near)
-    thin_last = rep_swap(thin, 2)
-    late_b = later([total_b[1], two_b], pieces)
-    one_b.append(rep_swap(late_b[0], 1))
-    three_b = [rep_swap(part, 1) for part in late_b[1]]
-    out_pieces = scatter_third(out_even, out_got, *out_far)
+    pieces, grads = tie(pieces, grads)
+    one_b.append(rep_swap(later(total_b[1], pieces), 1))
+    three_b = [rep_swap(part, 1) for part in later(two_b, pieces)]
     grad_in = finish(hidden, gains, d_resid, pieces)
+    grad_in, thin_last, up_far, one_b[0] = tie(grad_in, thin_last, up_far, one_b[0])
+    grad_a, grad_b = thin_grads([thin, thin_last], [up_grads, up_far])
+    out_pieces = scatter_third(*later((out_even, out_got), pieces), *out_far)
     layer_out = layer(resid_one, out_pieces)
-    one_b, three_b, thin_last, layer_out, grad_in = tie(one_b, three_b, thin_last, layer_out, grad_in)
+    one_b, three_b, layer_out, grad_in, grad_a, grad_b = tie(one_b, three_b, layer_out, grad_in, grad_a, grad_b)
     grads = unpack(1, where, [total_b, one_b, two_b, three_b], inner, local, grads)
-    grad_a, grad_b = thin_grads(thin, thin_last)
     return (layer_out[None], grad_in[None], grad_a, grad_b, *grads)
 
 

time: 516 us -> 510 us (0.988)
    all_to_all x0 -> x2, starting transfers between devices: none -> 8.8 us  [exchange(): lax.all_to_all(values, 'fsdp', split_axis=0, concat_axis=0, tiled=True)]
    ppermute x55 -> x50, waiting for transfers between devices: 97.4 us -> 91.5 us  [swap(): return lax.ppermute(values, 'fsdp', [(i, i ^ bits) for i in range(EVERY)])]
    ppermute x55 -> x50, starting transfers between devices: 43.4 us -> 38.3 us  [swap(): return lax.ppermute(values, 'fsdp', [(i, i ^ bits) for i in range(EVERY)])]
    ppermute x20 -> x22, waiting for transfers between devices: 56.6 us -> 57.9 us  [rep_swap(): return lax.ppermute(values, 'rep', [(i, i ^ bits) for i in range(4)])]
    unnamed x128 -> x124, local copies, waits for them, and re-layouts: 12 us -> 12.3 us
    ppermute x20 -> x22, starting transfers between devices: 25.9 us -> 26.1 us  [rep_swap(): return lax.ppermute(values, 'rep', [(i, i ^ bits) for i in range(4)])]
  transfers between devices with their start and end apart: 77 -> 76, of which waited for: 32 -> 27; matrix products, arithmetic and copies ran while one was open for 5% -> 6% of each run, Pallas kernels for 31% -> 31%
where the time goes in v4:
time: 510 us; the launch traced here: 500 us
  Pallas kernels  201 us (39%)
  waiting for transfers between devices  152 us (30%)
  starting transfers between devices  81.2 us (16%)
  other arithmetic  25.7 us (5%)
  local copies, waits for them, and re-layouts  20.5 us (4%)
  blocking collectives  17.1 us (3%)
    ppermute x50, waiting for transfers between devices, swap(): return lax.ppermute(values, 'fsdp', [(i, i ^ bits) for i in range(EVERY)])  91.5 us
    pallas_call x2, Pallas kernels, expert_pass(): pl.pallas_call(functools.partial(expert_kernel, k, prev is None, width, h...  82 us
    ppermute x22, waiting for transfers between devices, rep_swap(): return lax.ppermute(values, 'rep', [(i, i ^ bits) for i in range(4)])  57.9 us
    ppermute x50, starting transfers between devices, swap(): return lax.ppermute(values, 'fsdp', [(i, i ^ bits) for i in range(EVERY)])  38.3 us
    pallas_call x1, Pallas kernels, rows_pass(): pl.pallas_call(functools.partial(rows_kernel, part, width, hidden, local)...  29 us
    ppermute x22, starting transfers between devices, rep_swap(): return lax.ppermute(values, 'rep', [(i, i ^ bits) for i in range(4)])  26.1 us
    all_to_all x1, blocking collectives, split_layer(): lax.all_to_all(att_send, 'fsdp', split_axis=0, concat_axis=0, tiled=True)  17.1 us
    pallas_call x1, Pallas kernels, project(): pl.pallas_call(functools.partial(project_kernel, rows, width, wide), grid...  14.5 us
  transfers between devices with their start and end apart: 76, of which 27 were waited for; matrix products, arithmetic and copies ran while one was open for 6% of the time, Pallas kernels for 31%

profile of v4, /device:TPU:0, one launch (start us, length us, event | category | flops | bytes accessed | tf_op | source)
XLA Modules:
  0.0 500.2 jit_solution(7773214128846692003)
XLA Ops:
  12.4 5.3 %by_columns.1 = bf16[8,3,256,256]{3,2,1,0:T(8,128)(2,1)} custom-call(bf16[3,256,2048]{2,1,0:T(8,128)(2,1)} %source_ref.1), custom_call_target="tpu_custom_call" | custom-call | flops 1048576 | bytes 65536 | tf_op jit(solution)/shard_map/by_columns/pallas_call | solution.py:627
  17.7 4.6 all-to-all-start
  34.5 32.1 %collective-permute-done.9 = bf16[64,1152]{1,0:T(8,128)(2,1)S(1)} collective-permute-done((bf16[64,1152]{1,0:T(8,128)(2,1)S(1)}, bf16[64,1152]{1,0:T(8,128)(2,1)S(1)}, u32[]{:S(2)}, u32[]{:S(2)}) %collective-permute-start.9) | collective-permute-done | bytes 147488 | tf_op jit(solution)/shard_map/ppermute | solution.py:531
  66.6 5.4 %collective-permute-done.2 = bf16[64,2048]{1,0:T(8,128)(2,1)S(1)} collective-permute-done((bf16[64,2048]{1,0:T(8,128)(2,1)S(1)}, bf16[64,2048]{1,0:T(8,128)(2,1)S(1)}, u32[]{:S(2)}, u32[]{:S(2)}) %collective-permute-start.2) | collective-permute-done | bytes 262176 | tf_op jit(solution)/shard_map/ppermute | solution.py:531
  80.9 14.5 %project.1 = (bf16[1024,256]{1,0:T(8,128)(2,1)}, bf16[1024,256]{1,0:T(8,128)(2,1)}, bf16[1024,256]{1,0:T(8,128)(2,1)}, bf16[1024,2048]{1,0:T(8,128)(2,1)}, bf16[...) custom-call(s32[1]{0:T(128)} %bitcast.1.me_ref, ...), custom_call_target="tpu_custom_call" | custom-call | flops 1048576 | bytes 65536 | tf_op jit(solution)/shard_map/project/pallas_call | solution.py:739
  95.4 7.2 %attend.1 = (f32[1024,256]{1,0:T(8,128)}, f32[8,1024]{1,0:T(8,128)}, bf16[8,128,256]{2,1,0:T(8,128)(2,1)}) custom-call(s32[1]{0:T(128)} %bitcast.1.me_ref, bf16[1024,256]{1,0:T(8,128)(2,1)} %get-tuple-element.219.q_ref, bf16[1024,256]{1,0:T(8,128)(2,1)} %get-tuple-element.220.k_ref, bf16[1024,256]{1,0:T(8,128)(2,1)} %get-tuple-element.221.v_ref, ...), custom_call_target="tpu_custom_call" | custom-call | flops 1048576 | bytes 65536 | tf_op jit(solution)/shard_map/attend/pallas_call | solution.py:791
  102.6 4.0 collective-permute-done.15.refs_2_.refs_6_
  111.8 11.3 %collective-permute-done.21.refs_9_ = bf16[128,2048]{1,0:T(8,128)(2,1)S(1)} collective-permute-done((bf16[128,2048]{1,0:T(8,128)(2,1)}, bf16[128,2048]{1,0:T(8,128)(2,1)S(1)}, u32[]{:S(2)}, u32[]{:S(2)}) %collective-permute-start.21) | collective-permute-done | bytes 524320 | tf_op jit(solution)/shard_map/ppermute | solution.py:531
  124.6 17.1 %all_to_all.25.att_ref = bf16[8,128,256]{2,1,0:T(8,128)(2,1)} all-to-all(bf16[8,128,256]{2,1,0:T(8,128)(2,1)S(1)} %copy-done.39), channel_id=1, replica_groups=mesh['rep'=4,'fsdp'=8] {'fsdp'}, dimensions={0} | all-to-all | bytes 1048576 | tf_op jit(solution)/shard_map/all_to_all | solution.py:1530
  149.2 7.3 %mix.1 = (f32[128,2048]{1,0:T(8,128)}, bf16[128,2176]{1,0:T(8,128)(2,1)}, bf16[128,128]{1,0:T(8,128)(2,1)}, f32[128,128]{1,0:T(8,128)}) custom-call(s32[1]{0:T(128)} %bitcast.1.me_ref, bf16[128,2048]{1,0:T(8,128)(2,1)} %bitcast.27, f32[8,2048]{1,0:T(8,128)} %get-tuple-element.215.gains_ref, f32[1024,128]{1,0:T(8,128)} %get-tuple-element.216.mask_ref, ...), custom_call_target="tpu_custom_call" | custom-call | flops 1048576 | bytes 65536 | tf_op jit(solution)/shard_map/mix/pallas_call | solution.py:871
  159.3 11.9 %collective-permute-done.28.refs_2_ = bf16[128,2176]{1,0:T(8,128)(2,1)S(1)} collective-permute-done((bf16[128,2176]{1,0:T(8,128)(2,1)}, bf16[128,2176]{1,0:T(8,128)(2,1)S(1)}, u32[]{:S(2)}, u32[]{:S(2)}) %collective-permute-start.28) | collective-permute-done | bytes 557088 | tf_op jit(solution)/shard_map/ppermute | solution.py:531
  173.4 6.0 %collective-permute-done.29 = bf16[64,2176]{1,0:T(8,128)(2,1)S(1)} collective-permute-done((bf16[64,2176]{1,0:T(8,128)(2,1)S(1)}, bf16[64,2176]{1,0:T(8,128)(2,1)S(1)}, u32[]{:S(2)}, u32[]{:S(2)}) %collective-permute-start.29) | collective-permute-done | bytes 278560 | tf_op jit(solution)/shard_map/ppermute | solution.py:531
  184.7 40.5 %expert.2 = (bf16[512,2048]{1,0:T(8,128)(2,1)}, bf16[512,2048]{1,0:T(8,128)(2,1)}, bf16[1024,2304]{1,0:T(8,128)(2,1)}, f32[1024,128]{1,0:T(8,128)}, bf16[288,204...) custom-call(s32[1]{0:T(128)} %bitcast.13.where_ref, f32[1024,128]{1,0:T(8,128)} %get-tuple-element.216.mask_ref, ...), custom_call_target="tpu_custom_call" | custom-call | flops 22817013760 | bytes 41943040 | tf_op jit(solution)/shard_map/expert/pallas_call | solution.py:1045
  226.9 41.5 %expert.3 = (bf16[512,2048]{1,0:T(8,128)(2,1)}, bf16[512,2048]{1,0:T(8,128)(2,1)}, bf16[1024,2304]{1,0:T(8,128)(2,1)}, f32[1024,128]{1,0:T(8,128)}, bf16[144,204...) custom-call(s32[1]{0:T(128)} %bitcast.13.where_ref, ...), custom_call_target="tpu_custom_call" | custom-call | flops 22817013760 | bytes 41943040 | tf_op jit(solution)/shard_map/expert/pallas_call | solution.py:1045
  273.4 29.0 %rows.1 = (bf16[512,2176]{1,0:T(8,128)(2,1)}, bf16[512,2176]{1,0:T(8,128)(2,1)}) custom-call(bf16[1024,2304]{1,0:T(8,128)(2,1)} %get-tuple-element.249.refs_0_, bf16[1024,2304]{1,0:T(8,128)(2,1)} %get-tuple-element.261.refs_1_, f32[1024,128]{1,0:T(8,128)} %get-tuple-element.262.refs_2_, f32[1024,128]{1,0:T(8,128)} %get-tuple-element.263.refs_3_, ...), custom_call_target="tpu_custom_call" | custom-call | flops 19327352832 | bytes 41943040 | tf_op jit(solution)/shard_map/rows/pallas_call | solution.py:1127
  311.2 7.3 %collective-permute-done.42 = bf16[144,2048]{1,0:T(8,128)(2,1)S(1)} collective-permute-done((bf16[144,2048]{1,0:T(8,128)(2,1)}, bf16[144,2048]{1,0:T(8,128)(2,1)S(1)}, u32[]{:S(2)}, u32[]{:S(2)}) %collective-permute-start.42) | collective-permute-done | bytes 589856 | tf_op jit(solution)/shard_map/ppermute | solution.py:609
  321.7 14.7 %collective-permute-done.45.refs_4_ = bf16[72,2048]{1,0:T(8,128)(2,1)S(1)} collective-permute-done((bf16[72,2048]{1,0:T(8,128)(2,1)S(1)}, bf16[72,2048]{1,0:T(8,128)(2,1)S(1)}, u32[]{:S(2)}, u32[]{:S(2)}) %collective-permute-start.45) | collective-permute-done | bytes 294944 | tf_op jit(solution)/shard_map/ppermute | solution.py:609
  339.1 11.4 %unmix.1 = (f32[128,2048]{1,0:T(8,128)}, bf16[8,256,256]{2,1,0:T(8,128)(2,1)}, bf16[8,128,256]{2,1,0:T(8,128)(2,1)}) custom-call(s32[1]{0:T(128)} %bitcast.1.me_ref, f32[128,2048]{1,0:T(8,128)} %get-tuple-element.236.resid_ref, bf16[128,2048]{1,0:T(8,128)(2,1)} %bitcast.12.refs_7_.cot_ref, f32[8,2048]{1,0:T(8,128)} %get-tuple-element.215.gains_ref, ...), custom_call_target="tpu_custom_call" | custom-call | flops 1048576 | bytes 65536 | tf_op jit(solution)/shard_map/unmix/pallas_call | solution.py:1192
  363.0 6.7 %collective-permute-done.51 = bf16[64,2048]{1,0:T(8,128)(2,1)S(1)} collective-permute-done((bf16[64,2048]{1,0:T(8,128)(2,1)S(1)}, bf16[64,2048]{1,0:T(8,128)(2,1)S(1)}, u32[]{:S(2)}, u32[]{:S(2)}) %collective-permute-start.51) | collective-permute-done | bytes 262176 | tf_op jit(solution)/shard_map/ppermute | solution.py:531
  372.5 4.1 all-to-all-start.3
  378.8 14.5 %attend_back.1 = (bf16[1024,768]{1,0:T(8,128)(2,1)}, bf16[1024,384]{1,0:T(8,128)(2,1)}, bf16[8,384,256]{2,1,0:T(8,128)(2,1)}, bf16[384,256]{1,0:T(8,128)(2,1)}) custom-call(s32[1]{0:T(128)} %bitcast.1.me_ref, bf16[1024,256]{1,0:T(8,128)(2,1)} %get-tuple-element.219.q_ref, bf16[1024,256]{1,0:T(8,128)(2,1)} %get-tuple-element.220.k_ref, ...), custom_call_target="tpu_custom_call" | custom-call | flops 1048576 | bytes 65536 | tf_op jit(solution)/shard_map/attend_back/pallas_call | solution.py:1264
  393.4 4.7 all-to-all-start.4
  402.0 11.0 %unproject.1 = (bf16[512,2048]{1,0:T(8,128)(2,1)}, bf16[512,2048]{1,0:T(8,128)(2,1)}) custom-call(s32[1]{0:T(128)} %bitcast.1.me_ref, bf16[1024,768]{1,0:T(8,128)(2,1)} %get-tuple-element.306.proj_ref, bf16[1024,384]{1,0:T(8,128)(2,1)} %get-tuple-element.307.low_ref, bf16[128,1152]{1,0:T(8,128)(2,1)} %fusion.11.refs_7_.refs_0_, ...), custom_call_target="tpu_custom_call" | custom-call | flops 1048576 | bytes 65536 | tf_op jit(solution)/shard_map/unproject/pallas_call | solution.py:1330
  429.6 3.9 collective-permute-done.61
  433.5 5.2 %collective-permute-done.60.refs_5_ = bf16[72,2048]{1,0:T(8,128)(2,1)} collective-permute-done((bf16[72,2048]{1,0:T(8,128)(2,1)S(1)}, bf16[72,2048]{1,0:T(8,128)(2,1)}, u32[]{:S(2)}, u32[]{:S(2)}) %collective-permute-start.60) | collective-permute-done | bytes 294944 | tf_op jit(solution)/shard_map/ppermute | solution.py:609
  438.7 3.8 collective-permute-done.59
  448.5 5.0 %unpack.2 = (f32[2,2,2048,128]{3,2,1,0:T(8,128)}, f32[2,2,128,1024]{3,2,1,0:T(8,128)}, f32[2,1024,128]{2,1,0:T(8,128)}, f32[2,128,2048]{2,1,0:T(8,128)}) custom-call(s32[1]{0:T(128)} %bitcast.13.where_ref, bf16[72,2048]{1,0:T(8,128)(2,1)} %copy-done.24, bf16[72,2048]{1,0:T(8,128)(2,1)} %copy-done.23, bf16[72,2048]{1,0:T(8,128)(2,1)} %copy-done.44, ...), custom_call_target="tpu_custom_call" | custom-call | flops 1048576 | bytes 65536 | tf_op jit(solution)/shard_map/unpack/pallas_call | solution.py:1422
  453.6 3.8 collective-permute-done.62.refs_2_
  464.8 8.5 %collective-permute-done.65.early_right = bf16[384,256]{1,0:T(8,128)(2,1)S(1)} collective-permute-done((bf16[384,256]{1,0:T(8,128)(2,1)S(1)}, bf16[384,256]{1,0:T(8,128)(2,1)S(1)}, u32[]{:S(2)}, u32[]{:S(2)}) %collective-permute-start.65) | collective-permute-done | bytes 196640 | tf_op jit(solution)/shard_map/ppermute | solution.py:609
  475.4 3.7 finish.1
  489.7 4.3 collective-permute-done.69.refs_7_
  494.7 5.0 %unpack.3 = (f32[2,2,2048,128]{3,2,1,0:T(8,128)}, f32[2,2,128,1024]{3,2,1,0:T(8,128)}, f32[2,1024,128]{2,1,0:T(8,128)}, f32[2,128,2048]{2,1,0:T(8,128)}) custom-call(s32[1]{0:T(128)} %bitcast.13.where_ref, bf16[72,2048]{1,0:T(8,128)(2,1)} %get-tuple-element.348.refs_0_, ...), custom_call_target="tpu_custom_call", output_to_operand_aliasing={{0}: (9, {}), {1}: (10, {}), {2}: (11, {}), {3}: (12, {})} | custom-call | flops 1048576 | bytes 65536 | tf_op jit(solution)/shard_map/unpack/pallas_call | solution.py:1422
  (343 shorter events, 142.8 us)
Async XLA Ops:
  7.4 66.8 %collective-permute-start.11 = (bf16[128,1152]{1,0:T(8,128)(2,1)}, bf16[128,1152]{1,0:T(8,128)(2,1)}, u32[]{:S(2)}, u32[]{:S(2)}) collective-permute-start(bf16[128,1152]{1,0:T(8,128)(2,1)} %fusion.11.refs_7_.refs_0_), channel_id=1, source_target_pairs={{0,1},{1,0},{2,3},{3,2},{4,5},{5,4},{6,7},{7,6},{8,9},{9,8},{10,11... | collective-permute-start | bytes 884744 | tf_op jit(solution)/shard_map/ppermute | solution.py:531
  7.9 22.0 %collective-permute-start.8 = (bf16[128,1152]{1,0:T(8,128)(2,1)}, bf16[128,1152]{1,0:T(8,128)(2,1)S(1)}, u32[]{:S(2)}, u32[]{:S(2)}) collective-permute-start(bf16[128,1152]{1,0:T(8,128)(2,1)} %fusion.11.refs_7_.refs_0_), channel_id=1, source_target_pairs={{0,4},{1,5},{2,6},{3,7},{4,0},{5,1},{6,2},{7,3},{8,12},{9,13},{10,... | collective-permute-start | bytes 884744 | tf_op jit(solution)/shard_map/ppermute | solution.py:531
  10.4 21.5 %collective-permute-start.7 = (bf16[128,1152]{1,0:T(8,128)(2,1)}, bf16[128,1152]{1,0:T(8,128)(2,1)S(1)}, u32[]{:S(2)}, u32[]{:S(2)}) collective-permute-start(bf16[128,1152]{1,0:T(8,128)(2,1)} %fusion.11.refs_7_.refs_0_), channel_id=1, source_target_pairs={{0,2},{1,3},{2,0},{3,1},{4,6},{5,7},{6,4},{7,5},{8,10},{9,11},{10,... | collective-permute-start | bytes 884744 | tf_op jit(solution)/shard_map/ppermute | solution.py:531
  11.9 21.7 %collective-permute-start.1 = (bf16[128,2048]{1,0:T(8,128)(2,1)}, bf16[128,2048]{1,0:T(8,128)(2,1)S(1)}, u32[]{:S(2)}, u32[]{:S(2)}) collective-permute-start(bf16[128,2048]{1,0:T(8,128)(2,1)} %bitcast.24), channel_id=1, source_target_pairs={{0,4},{1,5},{2,6},{3,7},{4,0},{5,1},{6,2},{7,3},{8,12},{9,13},{10,... | collective-permute-start | bytes 1572872 | tf_op jit(solution)/shard_map/ppermute | solution.py:531
  12.4 21.2 %collective-permute-start = (bf16[128,2048]{1,0:T(8,128)(2,1)}, bf16[128,2048]{1,0:T(8,128)(2,1)S(1)}, u32[]{:S(2)}, u32[]{:S(2)}) collective-permute-start(bf16[128,2048]{1,0:T(8,128)(2,1)} %bitcast.25), channel_id=1, source_target_pairs={{0,2},{1,3},{2,0},{3,1},{4,6},{5,7},{6,4},{7,5},{8,10},{9,11},{10,... | collective-permute-start | bytes 1572872 | tf_op jit(solution)/shard_map/ppermute | solution.py:531
  17.7 60.6 %all-to-all-start = ((bf16[8,3,256,256]{3,2,1,0:T(8,128)(2,1)}), bf16[8,3,256,256]{3,2,1,0:T(8,128)(2,1)}, u32[]{:S(2)}, u32[]{:S(2)}) async-start(bf16[8,3,256,256]{3,2,1,0:T(8,128)(2,1)} %by_columns.1), calls=%async_computation | async-start | bytes 6291456 | tf_op jit(solution)/shard_map/all_to_all | solution.py:1516
  29.9 43.7 %collective-permute-start.10 = (bf16[64,1152]{1,0:T(8,128)(2,1)S(1)}, bf16[64,1152]{1,0:T(8,128)(2,1)S(1)}, u32[]{:S(2)}, u32[]{:S(2)}) collective-permute-start(bf16[64,1152]{1,0:T(8,128)(2,1)S(1)} %slice.261), channel_id=1, source_target_pairs={{0,2},{1,3},{2,0},{3,1},{4,6},{5,7},{6,4},{7,5},{8,10},{9,11},{10,... | collective-permute-start | bytes 442376 | tf_op jit(solution)/shard_map/ppermute | solution.py:531
  32.0 34.6 %collective-permute-start.9 = (bf16[64,1152]{1,0:T(8,128)(2,1)S(1)}, bf16[64,1152]{1,0:T(8,128)(2,1)S(1)}, u32[]{:S(2)}, u32[]{:S(2)}) collective-permute-start(bf16[64,1152]{1,0:T(8,128)(2,1)S(1)} %slice.260), channel_id=1, source_target_pairs={{0,4},{1,5},{2,6},{3,7},{4,0},{5,1},{6,2},{7,3},{8,12},{9,13},{10,... | collective-permute-start | bytes 442376 | tf_op jit(solution)/shard_map/ppermute | solution.py:531
  33.6 38.4 %collective-permute-start.2 = (bf16[64,2048]{1,0:T(8,128)(2,1)S(1)}, bf16[64,2048]{1,0:T(8,128)(2,1)S(1)}, u32[]{:S(2)}, u32[]{:S(2)}) collective-permute-start(bf16[64,2048]{1,0:T(8,128)(2,1)S(1)} %slice.197), channel_id=1, source_target_pairs={{0,4},{1,5},{2,6},{3,7},{4,0},{5,1},{6,2},{7,3},{8,12},{9,13},{10,... | collective-permute-start | bytes 786440 | tf_op jit(solution)/shard_map/ppermute | solution.py:531
  34.4 39.2 %collective-permute-start.3 = (bf16[64,2048]{1,0:T(8,128)(2,1)S(1)}, bf16[64,2048]{1,0:T(8,128)(2,1)S(1)}, u32[]{:S(2)}, u32[]{:S(2)}) collective-permute-start(bf16[64,2048]{1,0:T(8,128)(2,1)S(1)} %slice.198), channel_id=1, source_target_pairs={{0,2},{1,3},{2,0},{3,1},{4,6},{5,7},{6,4},{7,5},{8,10},{9,11},{10,... | collective-permute-start | bytes 786440 | tf_op jit(solution)/shard_map/ppermute | solution.py:531
  78.3 28.3 %collective-permute-start.15 = (bf16[256,2304]{1,0:T(8,128)(2,1)}, bf16[256,2304]{1,0:T(8,128)(2,1)S(1)}, u32[]{:S(2)}, u32[]{:S(2)}) collective-permute-start(bf16[256,2304]{1,0:T(8,128)(2,1)} %pad_maximum_fusion.1.refs_0_.refs_4_), channel_id=1, source_target_pairs={{0,4},{1,5},{2,6},{3,7},{4,0},{5,1},{6,2},{7,3},{8,12},{9,13},{10,... | collective-permute-start | bytes 3538952 | tf_op jit(solution)/shard_map/ppermute | solution.py:531
  79.4 27.9 %collective-permute-start.14 = (bf16[256,2304]{1,0:T(8,128)(2,1)}, bf16[256,2304]{1,0:T(8,128)(2,1)S(1)}, u32[]{:S(2)}, u32[]{:S(2)}) collective-permute-start(bf16[256,2304]{1,0:T(8,128)(2,1)} %pad_maximum_fusion.1.refs_0_.refs_4_), channel_id=1, source_target_pairs={{0,2},{1,3},{2,0},{3,1},{4,6},{5,7},{6,4},{7,5},{8,10},{9,11},{10,... | collective-permute-start | bytes 3538952 | tf_op jit(solution)/shard_map/ppermute | solution.py:531
  107.5 34.2 %collective-permute-start.19 = (bf16[512,2304]{1,0:T(8,128)(2,1)S(1)}, bf16[512,2304]{1,0:T(8,128)(2,1)}, u32[]{:S(2)}, u32[]{:S(2)}) collective-permute-start(bf16[512,2304]{1,0:T(8,128)(2,1)S(1)} %pad_maximum_fusion), channel_id=1, source_target_pairs={{0,1},{1,0},{2,3},{3,2},{4,5},{5,4},{6,7},{7,6},{8,9},{9,8},{10,11... | collective-permute-start | bytes 7077896 | tf_op jit(solution)/shard_map/ppermute | solution.py:531
  107.6 34.1 %collective-permute-start.18 = (bf16[256,2304]{1,0:T(8,128)(2,1)}, bf16[256,2304]{1,0:T(8,128)(2,1)S(1)}, u32[]{:S(2)}, u32[]{:S(2)}) collective-permute-start(bf16[256,2304]{1,0:T(8,128)(2,1)} %pad_maximum_fusion.1.refs_0_.refs_4_), channel_id=1, source_target_pairs={{0,1},{1,0},{2,3},{3,2},{4,5},{5,4},{6,7},{7,6},{8,9},{9,8},{10,11... | collective-permute-start | bytes 3538952 | tf_op jit(solution)/shard_map/ppermute | solution.py:531
  109.2 32.5 %collective-permute-start.17 = (bf16[128,2304]{1,0:T(8,128)(2,1)S(1)}, bf16[128,2304]{1,0:T(8,128)(2,1)S(1)}, u32[]{:S(2)}, u32[]{:S(2)}) collective-permute-start(bf16[128,2304]{1,0:T(8,128)(2,1)S(1)} %slice.209), channel_id=1, source_target_pairs={{0,2},{1,3},{2,0},{3,1},{4,6},{5,7},{6,4},{7,5},{8,10},{9,11},{10,... | collective-permute-start | bytes 1769480 | tf_op jit(solution)/shard_map/ppermute | solution.py:531
  110.8 31.0 %collective-permute-start.16 = (bf16[128,2304]{1,0:T(8,128)(2,1)S(1)}, bf16[128,2304]{1,0:T(8,128)(2,1)S(1)}, u32[]{:S(2)}, u32[]{:S(2)}) collective-permute-start(bf16[128,2304]{1,0:T(8,128)(2,1)S(1)} %slice.208), channel_id=1, source_target_pairs={{0,4},{1,5},{2,6},{3,7},{4,0},{5,1},{6,2},{7,3},{8,12},{9,13},{10,... | collective-permute-start | bytes 1769480 | tf_op jit(solution)/shard_map/ppermute | solution.py:531
  123.1 18.6 %collective-permute-start.20 = (bf16[128,2048]{1,0:T(8,128)(2,1)}, bf16[128,2048]{1,0:T(8,128)(2,1)S(1)}, u32[]{:S(2)}, u32[]{:S(2)}) collective-permute-start(bf16[128,2048]{1,0:T(8,128)(2,1)} %bitcast.12.refs_7_.cot_ref), channel_id=1, source_target_pairs={{0,2},{1,3},{2,0},{3,1},{4,6},{5,7},{6,4},{7,5},{8,10},{9,11},{10,... | collective-permute-start | bytes 1572872 | tf_op jit(solution)/shard_map/ppermute | solution.py:531
  158.5 25.4 %collective-permute-start.31 = (bf16[128,2176]{1,0:T(8,128)(2,1)}, bf16[128,2176]{1,0:T(8,128)(2,1)}, u32[]{:S(2)}, u32[]{:S(2)}) collective-permute-start(bf16[128,2176]{1,0:T(8,128)(2,1)} %get-tuple-element.244.refs_0_), channel_id=1, source_target_pairs={{0,1},{1,0},{2,3},{3,2},{4,5},{5,4},{6,7},{7,6},{8,9},{9,8},{10,11... | collective-permute-start | bytes 1671176 | tf_op jit(solution)/shard_map/ppermute | solution.py:531
  225.2 43.2 %collective-permute-start.35 = (bf16[288,2048]{1,0:T(8,128)(2,1)}, bf16[288,2048]{1,0:T(8,128)(2,1)}, u32[]{:S(2)}, u32[]{:S(2)}) collective-permute-start(bf16[288,2048]{1,0:T(8,128)(2,1)} %get-tuple-element.258), channel_id=1, source_target_pairs={{0,8},{8,0},{16,24},{24,16},{1,9},{9,1},{17,25},{25,17},{2,10},{10... | collective-permute-start | bytes 3538952 | tf_op jit(solution)/shard_map/ppermute | solution.py:609
  268.4 34.1 %collective-permute-start.38 = (bf16[512,2048]{1,0:T(8,128)(2,1)}, bf16[512,2048]{1,0:T(8,128)(2,1)}, u32[]{:S(2)}, u32[]{:S(2)}) collective-permute-start(bf16[512,2048]{1,0:T(8,128)(2,1)} %get-tuple-element.269), channel_id=1, source_target_pairs={{0,1},{1,0},{2,3},{3,2},{4,5},{5,4},{6,7},{7,6},{8,9},{9,8},{10,11... | collective-permute-start | bytes 6291464 | tf_op jit(solution)/shard_map/ppermute | solution.py:531
  270.3 32.1 %collective-permute-start.36 = (bf16[144,2048]{1,0:T(8,128)(2,1)S(1)}, bf16[144,2048]{1,0:T(8,128)(2,1)S(1)}, u32[]{:S(2)}, u32[]{:S(2)}) collective-permute-start(bf16[144,2048]{1,0:T(8,128)(2,1)S(1)} %slice.264), channel_id=1, source_target_pairs={{0,16},{8,24},{16,0},{24,8},{1,17},{9,25},{17,1},{25,9},{2,18},{10... | collective-permute-start | bytes 1769480 | tf_op jit(solution)/shard_map/ppermute | solution.py:609
  273.0 29.4 %collective-permute-start.37 = (bf16[144,2048]{1,0:T(8,128)(2,1)}, bf16[144,2048]{1,0:T(8,128)(2,1)S(1)}, u32[]{:S(2)}, u32[]{:S(2)}) collective-permute-start(bf16[144,2048]{1,0:T(8,128)(2,1)} %get-tuple-element.268), channel_id=1, source_target_pairs={{0,8},{8,0},{16,24},{24,16},{1,9},{9,1},{17,25},{25,17},{2,10},{10... | collective-permute-start | bytes 1769480 | tf_op jit(solution)/shard_map/ppermute | solution.py:609
  318.7 17.7 %collective-permute-start.43 = (bf16[128,2176]{1,0:T(8,128)(2,1)S(1)}, bf16[128,2176]{1,0:T(8,128)(2,1)S(1)}, u32[]{:S(2)}, u32[]{:S(2)}) collective-permute-start(bf16[128,2176]{1,0:T(8,128)(2,1)S(1)} %pad_maximum_fusion.6), channel_id=1, source_target_pairs={{0,2},{1,3},{2,0},{3,1},{4,6},{5,7},{6,4},{7,5},{8,10},{9,11},{10,... | collective-permute-start | bytes 1671176 | tf_op jit(solution)/shard_map/ppermute | solution.py:531
  351.8 20.0 %all-to-all-start.2 = ((bf16[8,128,256]{2,1,0:T(8,128)(2,1)}), bf16[8,128,256]{2,1,0:T(8,128)(2,1)S(1)}, u32[]{:S(2)}, u32[]{:S(2)}) async-start(bf16[8,128,256]{2,1,0:T(8,128)(2,1)} %get-tuple-element.287), calls=%async_computation.2 | async-start | bytes 1048576 | tf_op jit(solution)/shard_map/all_to_all | solution.py:1585
  372.5 20.8 %all-to-all-start.3 = ((bf16[8,256,256]{2,1,0:T(8,128)(2,1)}), bf16[8,256,256]{2,1,0:T(8,128)(2,1)S(1)}, u32[]{:S(2)}, u32[]{:S(2)}) async-start(bf16[8,256,256]{2,1,0:T(8,128)(2,1)} %get-tuple-element.305), calls=%async_computation.3 | async-start | bytes 2097152 | tf_op jit(solution)/shard_map/all_to_all | solution.py:1597
  393.4 25.7 %all-to-all-start.4 = ((bf16[8,384,256]{2,1,0:T(8,128)(2,1)}), bf16[8,384,256]{2,1,0:T(8,128)(2,1)}, u32[]{:S(2)}, u32[]{:S(2)}) async-start(bf16[8,384,256]{2,1,0:T(8,128)(2,1)} %get-tuple-element.310), calls=%async_computation.4 | async-start | bytes 3145728 | tf_op jit(solution)/shard_map/all_to_all | solution.py:1597
  425.4 17.1 %collective-permute-start.59 = (bf16[640,256]{1,0:T(8,128)(2,1)S(1)}, bf16[640,256]{1,0:T(8,128)(2,1)S(1)}, u32[]{:S(2)}, u32[]{:S(2)}) collective-permute-start(bf16[640,256]{1,0:T(8,128)(2,1)S(1)} %pad_maximum_fusion.14), channel_id=1, source_target_pairs={{0,8},{8,0},{16,24},{24,16},{1,9},{9,1},{17,25},{25,17},{2,10},{10... | collective-permute-start | bytes 983048 | tf_op jit(solution)/shard_map/ppermute | solution.py:609
  445.5 27.8 %collective-permute-start.66 = (bf16[72,2048]{1,0:T(8,128)(2,1)}, bf16[72,2048]{1,0:T(8,128)(2,1)}, u32[]{:S(2)}, u32[]{:S(2)}) collective-permute-start(bf16[72,2048]{1,0:T(8,128)(2,1)} %get-tuple-element.348.refs_0_), channel_id=1, source_target_pairs={{0,8},{8,0},{16,24},{24,16},{1,9},{9,1},{17,25},{25,17},{2,10},{10... | collective-permute-start | bytes 884744 | tf_op jit(solution)/shard_map/ppermute | solution.py:609
  446.1 29.2 %collective-permute-start.64 = (bf16[640,256]{1,0:T(8,128)(2,1)S(1)}, bf16[640,256]{1,0:T(8,128)(2,1)}, u32[]{:S(2)}, u32[]{:S(2)}) collective-permute-start(bf16[640,256]{1,0:T(8,128)(2,1)S(1)} %add_convert_fusion.4.late_left), channel_id=1, source_target_pairs={{0,16},{8,24},{16,0},{24,8},{1,17},{9,25},{17,1},{25,9},{2,18},{10... | collective-permute-start | bytes 983048 | tf_op jit(solution)/shard_map/ppermute | solution.py:609
  461.1 20.5 %collective-permute-start.70 = (bf16[128,2048]{1,0:T(8,128)(2,1)S(1)}, bf16[128,2048]{1,0:T(8,128)(2,1)S(1)}, u32[]{:S(2)}, u32[]{:S(2)}) collective-permute-start(bf16[128,2048]{1,0:T(8,128)(2,1)S(1)} %pad_maximum_fusion.12), channel_id=1, source_target_pairs={{0,2},{1,3},{2,0},{3,1},{4,6},{5,7},{6,4},{7,5},{8,10},{9,11},{10,... | collective-permute-start | bytes 1572872 | tf_op jit(solution)/shard_map/ppermute | solution.py:531
  462.7 18.8 %collective-permute-start.71 = (bf16[128,2048]{1,0:T(8,128)(2,1)S(1)}, bf16[128,2048]{1,0:T(8,128)(2,1)S(1)}, u32[]{:S(2)}, u32[]{:S(2)}) collective-permute-start(bf16[128,2048]{1,0:T(8,128)(2,1)S(1)} %pad_maximum_fusion.13), channel_id=1, source_target_pairs={{0,4},{1,5},{2,6},{3,7},{4,0},{5,1},{6,2},{7,3},{8,12},{9,13},{10,... | collective-permute-start | bytes 1572872 | tf_op jit(solution)/shard_map/ppermute | solution.py:531
  475.4 18.6 %collective-permute-start.69 = (bf16[72,2048]{1,0:T(8,128)(2,1)}, bf16[72,2048]{1,0:T(8,128)(2,1)S(1)}, u32[]{:S(2)}, u32[]{:S(2)}) collective-permute-start(bf16[72,2048]{1,0:T(8,128)(2,1)} %collective-permute-done.60.refs_5_), channel_id=1, source_target_pairs={{0,8},{8,0},{16,24},{24,16},{1,9},{9,1},{17,25},{25,17},{2,10},{10... | collective-permute-start | bytes 884744 | tf_op jit(solution)/shard_map/ppermute | solution.py:609
  (101 other events, 1122.5 us)

commit v5 on v4

--- a/solution.py
+++ b/solution.py
@@ -1384,31 +1384,22 @@
     )(resid, *pieces)
 
 
-UNPACK_STEPS = 4
-
-
-def unpack_kernel(hidden, where_ref, *refs):
+def unpack_kernel(hidden, first, where_ref, *refs):
     f32 = jnp.float32
-    parts, refs = refs[:8], refs[-5:]
+    parts, refs = refs[:8], refs[8:]
+    refs = refs if first else refs[4:]
     a_in_ref, b_in_ref, a_down_ref, b_down_ref, packed = refs
     size = packed.shape[0] // 4
-    step = pl.program_id(0)
-    wide, thin = packed.shape[1] // UNPACK_STEPS, hidden // UNPACK_STEPS
-
-    @pl.when(step == 0)
-    def _():
-        for b in range(4):
-            for i in range(2):
-                spot = pl.multiple_of((where_ref[0] ^ b) * size + i * (size // 2), 8)
-                packed[pl.ds(spot, size // 2), :] = parts[2 * b + i][...].astype(f32)
-
-    at = pl.ds(pl.multiple_of(step * wide, 128), wide)
-    halves = [pl.ds(pl.multiple_of(i * hidden + step * thin, 128), thin) for i in range(2)]
+    for b in range(4):
+        for i in range(2):
+            spot = pl.multiple_of((where_ref[0] ^ b) * size + i * (size // 2), 8)
+            packed[pl.ds(spot, size // 2), :] = parts[2 * b + i][...].astype(f32)
     for i in range(2):
-        a_in_ref[0, i] = packed[i * SR : (i + 1) * SR, at].T
-        b_in_ref[0, i] = packed[3 * SR : 4 * SR, halves[i]]
-        a_down_ref[0, :, i * (SR // 2) : (i + 1) * (SR // 2)] = packed[4 * SR :, halves[i]].T
-    b_down_ref[0] = packed[2 * SR : 3 * SR, at]
+        a_in_ref[0, i] = packed[i * SR : (i + 1) * SR, :].T
+        b_in_ref[0, i] = packed[3 * SR : 4 * SR, i * hidden : (i + 1) * hidden]
+    b_down_ref[0] = packed[2 * SR : 3 * SR, :]
+    a_down_ref[0, :, 0 : SR // 2] = packed[4 * SR :, 0:hidden].T
+    a_down_ref[0, :, SR // 2 :] = packed[4 * SR :, hidden:].T
 
 
 def unpack(k, where, quarters, hidden, experts, before):
@@ -1418,16 +1409,12 @@
     first = before is None
     shapes = [(experts, 2, width, SR), (experts, 2, SR, hidden), (experts, hidden, SR), (experts, SR, width)]
     given = [] if first else list(before)
-    wide, thin = width // UNPACK_STEPS, hidden // UNPACK_STEPS
     return pl.pallas_call(
-        functools.partial(unpack_kernel, hidden),
-        grid=(UNPACK_STEPS,),
+        functools.partial(unpack_kernel, hidden, first),
+        grid=(1,),
         in_specs=[scalars()] + [whole()] * 8 + [in_place()] * len(given),
         out_specs=[
-            pl.BlockSpec((1, 2, wide, SR), lambda i: (k, 0, i, 0)),
-            pl.BlockSpec((1, 2, SR, thin), lambda i: (k, 0, 0, i)),
-            pl.BlockSpec((1, thin, SR), lambda i: (k, i, 0)),
-            pl.BlockSpec((1, SR, wide), lambda i: (k, 0, i)),
+            pl.BlockSpec((1,) + shape[1:], lambda i, n=len(shape): (k,) + (0,) * (n - 1)) for shape in shapes
         ],
         out_shape=[shape_of(shape, f32) for shape in shapes],
         input_output_aliases={} if first else {9 + i: i for i in range(4)},
@@ -1529,7 +1516,7 @@
     att_send, out_first = tie(att_send, out_first)
     att_got = lax.all_to_all(att_send, "fsdp", split_axis=0, concat_axis=0, tiled=True)
     far, *others = gather_second(*out_first)
-    cot_first = gather_first(tie(upstream, att_send)[0])
+    cot_first = gather_first(tie(upstream, others)[0])
     far, others, att_got, cot_first = tie(far, others, att_got, cot_first)
     out_given = gather_third(out_first, far, *others)
     cot_second = gather_second(*cot_first)

time: 510 us -> 508 us (level)
  blocking collectives: 17.1 us -> 25.3 us
  waiting for transfers between devices: 152 us -> 144 us
    ppermute x50, waiting for transfers between devices: 91.5 us -> 82.5 us  [swap(): return lax.ppermute(values, 'fsdp', [(i, i ^ bits) for i in range(EVERY)])]
    all_to_all x1, blocking collectives: 17.1 us -> 25.3 us  [split_layer(): lax.all_to_all(att_send, 'fsdp', split_axis=0, concat_axis=0, tiled=True)]
  transfers between devices with their start and end apart: 76 -> 76, of which waited for: 27 -> 28; matrix products, arithmetic and copies ran while one was open for 6% -> 6% of each run, Pallas kernels for 31% -> 31%
where the time goes in v5:
time: 508 us; the launch traced here: 498 us
  Pallas kernels  200 us (39%)
  waiting for transfers between devices  144 us (28%)
  starting transfers between devices  80.8 us (16%)
  other arithmetic  25.8 us (5%)
  blocking collectives  25.3 us (5%)
  local copies, waits for them, and re-layouts  19.9 us (4%)
    ppermute x50, waiting for transfers between devices, swap(): return lax.ppermute(values, 'fsdp', [(i, i ^ bits) for i in range(EVERY)])  82.5 us
    pallas_call x2, Pallas kernels, expert_pass(): pl.pallas_call(functools.partial(expert_kernel, k, prev is None, width, h...  82 us
    ppermute x22, waiting for transfers between devices, rep_swap(): return lax.ppermute(values, 'rep', [(i, i ^ bits) for i in range(4)])  58.5 us
    ppermute x50, starting transfers between devices, swap(): return lax.ppermute(values, 'fsdp', [(i, i ^ bits) for i in range(EVERY)])  37.8 us
    pallas_call x1, Pallas kernels, rows_pass(): pl.pallas_call(functools.partial(rows_kernel, part, width, hidden, local)...  29 us
    ppermute x22, starting transfers between devices, rep_swap(): return lax.ppermute(values, 'rep', [(i, i ^ bits) for i in range(4)])  26.1 us
    all_to_all x1, blocking collectives, split_layer(): lax.all_to_all(att_send, 'fsdp', split_axis=0, concat_axis=0, tiled=True)  25.3 us
    pallas_call x1, Pallas kernels, project(): pl.pallas_call(functools.partial(project_kernel, rows, width, wide), grid...  14.5 us
  transfers between devices with their start and end apart: 76, of which 28 were waited for; matrix products, arithmetic and copies ran while one was open for 6% of the time, Pallas kernels for 31%

profile of v5, /device:TPU:0, one launch (start us, length us, event | category | flops | bytes accessed | tf_op | source)
XLA Modules:
  0.0 498.2 jit_solution(765799559266291961)
XLA Ops:
  12.4 5.3 %by_columns.1 = bf16[8,3,256,256]{3,2,1,0:T(8,128)(2,1)} custom-call(bf16[3,256,2048]{2,1,0:T(8,128)(2,1)} %source_ref.1), custom_call_target="tpu_custom_call" | custom-call | flops 1048576 | bytes 65536 | tf_op jit(solution)/shard_map/by_columns/pallas_call | solution.py:627
  17.7 4.6 all-to-all-start
  34.5 32.1 %collective-permute-done.9 = bf16[64,1152]{1,0:T(8,128)(2,1)S(1)} collective-permute-done((bf16[64,1152]{1,0:T(8,128)(2,1)S(1)}, bf16[64,1152]{1,0:T(8,128)(2,1)S(1)}, u32[]{:S(2)}, u32[]{:S(2)}) %collective-permute-start.9) | collective-permute-done | bytes 147488 | tf_op jit(solution)/shard_map/ppermute | solution.py:531
  66.6 5.4 %collective-permute-done.2 = bf16[64,2048]{1,0:T(8,128)(2,1)S(1)} collective-permute-done((bf16[64,2048]{1,0:T(8,128)(2,1)S(1)}, bf16[64,2048]{1,0:T(8,128)(2,1)S(1)}, u32[]{:S(2)}, u32[]{:S(2)}) %collective-permute-start.2) | collective-permute-done | bytes 262176 | tf_op jit(solution)/shard_map/ppermute | solution.py:531
  80.9 14.5 %project.1 = (bf16[1024,256]{1,0:T(8,128)(2,1)}, bf16[1024,256]{1,0:T(8,128)(2,1)}, bf16[1024,256]{1,0:T(8,128)(2,1)}, bf16[1024,2048]{1,0:T(8,128)(2,1)}, bf16[...) custom-call(s32[1]{0:T(128)} %bitcast.1.me_ref, ...), custom_call_target="tpu_custom_call" | custom-call | flops 1048576 | bytes 65536 | tf_op jit(solution)/shard_map/project/pallas_call | solution.py:739
  95.4 7.2 %attend.1 = (f32[1024,256]{1,0:T(8,128)}, f32[8,1024]{1,0:T(8,128)}, bf16[8,128,256]{2,1,0:T(8,128)(2,1)}) custom-call(s32[1]{0:T(128)} %bitcast.1.me_ref, bf16[1024,256]{1,0:T(8,128)(2,1)} %get-tuple-element.219.q_ref, bf16[1024,256]{1,0:T(8,128)(2,1)} %get-tuple-element.220.k_ref, bf16[1024,256]{1,0:T(8,128)(2,1)} %get-tuple-element.221.v_ref, ...), custom_call_target="tpu_custom_call" | custom-call | flops 1048576 | bytes 65536 | tf_op jit(solution)/shard_map/attend/pallas_call | solution.py:791
  102.6 4.0 collective-permute-done.15.refs_2_.refs_6_
  116.5 25.3 %all_to_all.25.att_ref = bf16[8,128,256]{2,1,0:T(8,128)(2,1)} all-to-all(bf16[8,128,256]{2,1,0:T(8,128)(2,1)S(1)} %copy-done.39), channel_id=1, replica_groups=mesh['rep'=4,'fsdp'=8] {'fsdp'}, dimensions={0} | all-to-all | bytes 1048576 | tf_op jit(solution)/shard_map/all_to_all | solution.py:1517
  147.9 7.3 %mix.1 = (f32[128,2048]{1,0:T(8,128)}, bf16[128,2176]{1,0:T(8,128)(2,1)}, bf16[128,128]{1,0:T(8,128)(2,1)}, f32[128,128]{1,0:T(8,128)}) custom-call(s32[1]{0:T(128)} %bitcast.1.me_ref, bf16[128,2048]{1,0:T(8,128)(2,1)} %bitcast.27, f32[8,2048]{1,0:T(8,128)} %get-tuple-element.215.gains_ref, f32[1024,128]{1,0:T(8,128)} %get-tuple-element.216.mask_ref, ...), custom_call_target="tpu_custom_call" | custom-call | flops 1048576 | bytes 65536 | tf_op jit(solution)/shard_map/mix/pallas_call | solution.py:871
  158.5 11.2 %collective-permute-done.28.refs_2_ = bf16[128,2176]{1,0:T(8,128)(2,1)S(1)} collective-permute-done((bf16[128,2176]{1,0:T(8,128)(2,1)}, bf16[128,2176]{1,0:T(8,128)(2,1)S(1)}, u32[]{:S(2)}, u32[]{:S(2)}) %collective-permute-start.28) | collective-permute-done | bytes 557088 | tf_op jit(solution)/shard_map/ppermute | solution.py:531
  172.5 5.9 %collective-permute-done.29 = bf16[64,2176]{1,0:T(8,128)(2,1)S(1)} collective-permute-done((bf16[64,2176]{1,0:T(8,128)(2,1)S(1)}, bf16[64,2176]{1,0:T(8,128)(2,1)S(1)}, u32[]{:S(2)}, u32[]{:S(2)}) %collective-permute-start.29) | collective-permute-done | bytes 278560 | tf_op jit(solution)/shard_map/ppermute | solution.py:531
  183.7 40.5 %expert.2 = (bf16[512,2048]{1,0:T(8,128)(2,1)}, bf16[512,2048]{1,0:T(8,128)(2,1)}, bf16[1024,2304]{1,0:T(8,128)(2,1)}, f32[1024,128]{1,0:T(8,128)}, bf16[288,204...) custom-call(s32[1]{0:T(128)} %bitcast.13.where_ref, f32[1024,128]{1,0:T(8,128)} %get-tuple-element.216.mask_ref, ...), custom_call_target="tpu_custom_call" | custom-call | flops 22817013760 | bytes 41943040 | tf_op jit(solution)/shard_map/expert/pallas_call | solution.py:1045
  225.9 41.5 %expert.3 = (bf16[512,2048]{1,0:T(8,128)(2,1)}, bf16[512,2048]{1,0:T(8,128)(2,1)}, bf16[1024,2304]{1,0:T(8,128)(2,1)}, f32[1024,128]{1,0:T(8,128)}, bf16[144,204...) custom-call(s32[1]{0:T(128)} %bitcast.13.where_ref, ...), custom_call_target="tpu_custom_call" | custom-call | flops 22817013760 | bytes 41943040 | tf_op jit(solution)/shard_map/expert/pallas_call | solution.py:1045
  272.4 29.0 %rows.1 = (bf16[512,2176]{1,0:T(8,128)(2,1)}, bf16[512,2176]{1,0:T(8,128)(2,1)}) custom-call(bf16[1024,2304]{1,0:T(8,128)(2,1)} %get-tuple-element.249.refs_0_, bf16[1024,2304]{1,0:T(8,128)(2,1)} %get-tuple-element.261.refs_1_, f32[1024,128]{1,0:T(8,128)} %get-tuple-element.262.refs_2_, f32[1024,128]{1,0:T(8,128)} %get-tuple-element.263.refs_3_, ...), custom_call_target="tpu_custom_call" | custom-call | flops 19327352832 | bytes 41943040 | tf_op jit(solution)/shard_map/rows/pallas_call | solution.py:1127
  309.6 7.8 %collective-permute-done.42 = bf16[144,2048]{1,0:T(8,128)(2,1)S(1)} collective-permute-done((bf16[144,2048]{1,0:T(8,128)(2,1)}, bf16[144,2048]{1,0:T(8,128)(2,1)S(1)}, u32[]{:S(2)}, u32[]{:S(2)}) %collective-permute-start.42) | collective-permute-done | bytes 589856 | tf_op jit(solution)/shard_map/ppermute | solution.py:609
  320.1 14.7 %collective-permute-done.45.refs_4_ = bf16[72,2048]{1,0:T(8,128)(2,1)S(1)} collective-permute-done((bf16[72,2048]{1,0:T(8,128)(2,1)S(1)}, bf16[72,2048]{1,0:T(8,128)(2,1)S(1)}, u32[]{:S(2)}, u32[]{:S(2)}) %collective-permute-start.45) | collective-permute-done | bytes 294944 | tf_op jit(solution)/shard_map/ppermute | solution.py:609
  337.6 11.4 %unmix.1 = (f32[128,2048]{1,0:T(8,128)}, bf16[8,256,256]{2,1,0:T(8,128)(2,1)}, bf16[8,128,256]{2,1,0:T(8,128)(2,1)}) custom-call(s32[1]{0:T(128)} %bitcast.1.me_ref, f32[128,2048]{1,0:T(8,128)} %get-tuple-element.236.resid_ref, bf16[128,2048]{1,0:T(8,128)(2,1)} %bitcast.12.refs_7_.cot_ref, f32[8,2048]{1,0:T(8,128)} %get-tuple-element.215.gains_ref, ...), custom_call_target="tpu_custom_call" | custom-call | flops 1048576 | bytes 65536 | tf_op jit(solution)/shard_map/unmix/pallas_call | solution.py:1192
  361.4 6.7 %collective-permute-done.51 = bf16[64,2048]{1,0:T(8,128)(2,1)S(1)} collective-permute-done((bf16[64,2048]{1,0:T(8,128)(2,1)S(1)}, bf16[64,2048]{1,0:T(8,128)(2,1)S(1)}, u32[]{:S(2)}, u32[]{:S(2)}) %collective-permute-start.51) | collective-permute-done | bytes 262176 | tf_op jit(solution)/shard_map/ppermute | solution.py:531
  370.9 4.1 all-to-all-start.3
  377.2 14.5 %attend_back.1 = (bf16[1024,768]{1,0:T(8,128)(2,1)}, bf16[1024,384]{1,0:T(8,128)(2,1)}, bf16[8,384,256]{2,1,0:T(8,128)(2,1)}, bf16[384,256]{1,0:T(8,128)(2,1)}) custom-call(s32[1]{0:T(128)} %bitcast.1.me_ref, bf16[1024,256]{1,0:T(8,128)(2,1)} %get-tuple-element.219.q_ref, bf16[1024,256]{1,0:T(8,128)(2,1)} %get-tuple-element.220.k_ref, ...), custom_call_target="tpu_custom_call" | custom-call | flops 1048576 | bytes 65536 | tf_op jit(solution)/shard_map/attend_back/pallas_call | solution.py:1264
  391.8 4.7 all-to-all-start.4
  400.4 11.0 %unproject.1 = (bf16[512,2048]{1,0:T(8,128)(2,1)}, bf16[512,2048]{1,0:T(8,128)(2,1)}) custom-call(s32[1]{0:T(128)} %bitcast.1.me_ref, bf16[1024,768]{1,0:T(8,128)(2,1)} %get-tuple-element.306.proj_ref, bf16[1024,384]{1,0:T(8,128)(2,1)} %get-tuple-element.307.low_ref, bf16[128,1152]{1,0:T(8,128)(2,1)} %fusion.11.refs_7_.refs_0_, ...), custom_call_target="tpu_custom_call" | custom-call | flops 1048576 | bytes 65536 | tf_op jit(solution)/shard_map/unproject/pallas_call | solution.py:1330
  428.0 3.9 collective-permute-done.61
  431.9 5.2 %collective-permute-done.60.refs_5_ = bf16[72,2048]{1,0:T(8,128)(2,1)} collective-permute-done((bf16[72,2048]{1,0:T(8,128)(2,1)S(1)}, bf16[72,2048]{1,0:T(8,128)(2,1)}, u32[]{:S(2)}, u32[]{:S(2)}) %collective-permute-start.60) | collective-permute-done | bytes 294944 | tf_op jit(solution)/shard_map/ppermute | solution.py:609
  437.2 3.8 collective-permute-done.59
  446.9 4.7 unpack.2
  451.6 4.2 collective-permute-done.62.refs_2_
  463.3 8.5 %collective-permute-done.65.early_right = bf16[384,256]{1,0:T(8,128)(2,1)S(1)} collective-permute-done((bf16[384,256]{1,0:T(8,128)(2,1)S(1)}, bf16[384,256]{1,0:T(8,128)(2,1)S(1)}, u32[]{:S(2)}, u32[]{:S(2)}) %collective-permute-start.65) | collective-permute-done | bytes 196640 | tf_op jit(solution)/shard_map/ppermute | solution.py:609
  473.8 3.7 finish.1
  484.5 3.6 collective-permute-done.68.refs_6_
  488.1 4.3 collective-permute-done.69.refs_7_
  493.1 4.7 unpack.3
  (343 shorter events, 141.0 us)
Async XLA Ops:
  7.4 66.8 %collective-permute-start.11 = (bf16[128,1152]{1,0:T(8,128)(2,1)}, bf16[128,1152]{1,0:T(8,128)(2,1)}, u32[]{:S(2)}, u32[]{:S(2)}) collective-permute-start(bf16[128,1152]{1,0:T(8,128)(2,1)} %fusion.11.refs_7_.refs_0_), channel_id=1, source_target_pairs={{0,1},{1,0},{2,3},{3,2},{4,5},{5,4},{6,7},{7,6},{8,9},{9,8},{10,11... | collective-permute-start | bytes 884744 | tf_op jit(solution)/shard_map/ppermute | solution.py:531
  7.9 22.0 %collective-permute-start.8 = (bf16[128,1152]{1,0:T(8,128)(2,1)}, bf16[128,1152]{1,0:T(8,128)(2,1)S(1)}, u32[]{:S(2)}, u32[]{:S(2)}) collective-permute-start(bf16[128,1152]{1,0:T(8,128)(2,1)} %fusion.11.refs_7_.refs_0_), channel_id=1, source_target_pairs={{0,4},{1,5},{2,6},{3,7},{4,0},{5,1},{6,2},{7,3},{8,12},{9,13},{10,... | collective-permute-start | bytes 884744 | tf_op jit(solution)/shard_map/ppermute | solution.py:531
  10.4 21.5 %collective-permute-start.7 = (bf16[128,1152]{1,0:T(8,128)(2,1)}, bf16[128,1152]{1,0:T(8,128)(2,1)S(1)}, u32[]{:S(2)}, u32[]{:S(2)}) collective-permute-start(bf16[128,1152]{1,0:T(8,128)(2,1)} %fusion.11.refs_7_.refs_0_), channel_id=1, source_target_pairs={{0,2},{1,3},{2,0},{3,1},{4,6},{5,7},{6,4},{7,5},{8,10},{9,11},{10,... | collective-permute-start | bytes 884744 | tf_op jit(solution)/shard_map/ppermute | solution.py:531
  11.9 21.7 %collective-permute-start.1 = (bf16[128,2048]{1,0:T(8,128)(2,1)}, bf16[128,2048]{1,0:T(8,128)(2,1)S(1)}, u32[]{:S(2)}, u32[]{:S(2)}) collective-permute-start(bf16[128,2048]{1,0:T(8,128)(2,1)} %bitcast.24), channel_id=1, source_target_pairs={{0,4},{1,5},{2,6},{3,7},{4,0},{5,1},{6,2},{7,3},{8,12},{9,13},{10,... | collective-permute-start | bytes 1572872 | tf_op jit(solution)/shard_map/ppermute | solution.py:531
  12.4 21.2 %collective-permute-start = (bf16[128,2048]{1,0:T(8,128)(2,1)}, bf16[128,2048]{1,0:T(8,128)(2,1)S(1)}, u32[]{:S(2)}, u32[]{:S(2)}) collective-permute-start(bf16[128,2048]{1,0:T(8,128)(2,1)} %bitcast.25), channel_id=1, source_target_pairs={{0,2},{1,3},{2,0},{3,1},{4,6},{5,7},{6,4},{7,5},{8,10},{9,11},{10,... | collective-permute-start | bytes 1572872 | tf_op jit(solution)/shard_map/ppermute | solution.py:531
  17.7 60.6 %all-to-all-start = ((bf16[8,3,256,256]{3,2,1,0:T(8,128)(2,1)}), bf16[8,3,256,256]{3,2,1,0:T(8,128)(2,1)}, u32[]{:S(2)}, u32[]{:S(2)}) async-start(bf16[8,3,256,256]{3,2,1,0:T(8,128)(2,1)} %by_columns.1), calls=%async_computation | async-start | bytes 6291456 | tf_op jit(solution)/shard_map/all_to_all | solution.py:1503
  29.9 43.7 %collective-permute-start.10 = (bf16[64,1152]{1,0:T(8,128)(2,1)S(1)}, bf16[64,1152]{1,0:T(8,128)(2,1)S(1)}, u32[]{:S(2)}, u32[]{:S(2)}) collective-permute-start(bf16[64,1152]{1,0:T(8,128)(2,1)S(1)} %slice.261), channel_id=1, source_target_pairs={{0,2},{1,3},{2,0},{3,1},{4,6},{5,7},{6,4},{7,5},{8,10},{9,11},{10,... | collective-permute-start | bytes 442376 | tf_op jit(solution)/shard_map/ppermute | solution.py:531
  32.0 34.6 %collective-permute-start.9 = (bf16[64,1152]{1,0:T(8,128)(2,1)S(1)}, bf16[64,1152]{1,0:T(8,128)(2,1)S(1)}, u32[]{:S(2)}, u32[]{:S(2)}) collective-permute-start(bf16[64,1152]{1,0:T(8,128)(2,1)S(1)} %slice.260), channel_id=1, source_target_pairs={{0,4},{1,5},{2,6},{3,7},{4,0},{5,1},{6,2},{7,3},{8,12},{9,13},{10,... | collective-permute-start | bytes 442376 | tf_op jit(solution)/shard_map/ppermute | solution.py:531
  33.6 38.4 %collective-permute-start.2 = (bf16[64,2048]{1,0:T(8,128)(2,1)S(1)}, bf16[64,2048]{1,0:T(8,128)(2,1)S(1)}, u32[]{:S(2)}, u32[]{:S(2)}) collective-permute-start(bf16[64,2048]{1,0:T(8,128)(2,1)S(1)} %slice.197), channel_id=1, source_target_pairs={{0,4},{1,5},{2,6},{3,7},{4,0},{5,1},{6,2},{7,3},{8,12},{9,13},{10,... | collective-permute-start | bytes 786440 | tf_op jit(solution)/shard_map/ppermute | solution.py:531
  34.4 39.2 %collective-permute-start.3 = (bf16[64,2048]{1,0:T(8,128)(2,1)S(1)}, bf16[64,2048]{1,0:T(8,128)(2,1)S(1)}, u32[]{:S(2)}, u32[]{:S(2)}) collective-permute-start(bf16[64,2048]{1,0:T(8,128)(2,1)S(1)} %slice.198), channel_id=1, source_target_pairs={{0,2},{1,3},{2,0},{3,1},{4,6},{5,7},{6,4},{7,5},{8,10},{9,11},{10,... | collective-permute-start | bytes 786440 | tf_op jit(solution)/shard_map/ppermute | solution.py:531
  78.3 28.3 %collective-permute-start.15 = (bf16[256,2304]{1,0:T(8,128)(2,1)}, bf16[256,2304]{1,0:T(8,128)(2,1)S(1)}, u32[]{:S(2)}, u32[]{:S(2)}) collective-permute-start(bf16[256,2304]{1,0:T(8,128)(2,1)} %pad_maximum_fusion.1.refs_0_.refs_4_), channel_id=1, source_target_pairs={{0,4},{1,5},{2,6},{3,7},{4,0},{5,1},{6,2},{7,3},{8,12},{9,13},{10,... | collective-permute-start | bytes 3538952 | tf_op jit(solution)/shard_map/ppermute | solution.py:531
  79.4 27.9 %collective-permute-start.14 = (bf16[256,2304]{1,0:T(8,128)(2,1)}, bf16[256,2304]{1,0:T(8,128)(2,1)S(1)}, u32[]{:S(2)}, u32[]{:S(2)}) collective-permute-start(bf16[256,2304]{1,0:T(8,128)(2,1)} %pad_maximum_fusion.1.refs_0_.refs_4_), channel_id=1, source_target_pairs={{0,2},{1,3},{2,0},{3,1},{4,6},{5,7},{6,4},{7,5},{8,10},{9,11},{10,... | collective-permute-start | bytes 3538952 | tf_op jit(solution)/shard_map/ppermute | solution.py:531
  108.6 33.2 %collective-permute-start.17 = (bf16[128,2304]{1,0:T(8,128)(2,1)S(1)}, bf16[128,2304]{1,0:T(8,128)(2,1)S(1)}, u32[]{:S(2)}, u32[]{:S(2)}) collective-permute-start(bf16[128,2304]{1,0:T(8,128)(2,1)S(1)} %slice.209), channel_id=1, source_target_pairs={{0,2},{1,3},{2,0},{3,1},{4,6},{5,7},{6,4},{7,5},{8,10},{9,11},{10,... | collective-permute-start | bytes 1769480 | tf_op jit(solution)/shard_map/ppermute | solution.py:531
  110.1 31.7 %collective-permute-start.16 = (bf16[128,2304]{1,0:T(8,128)(2,1)S(1)}, bf16[128,2304]{1,0:T(8,128)(2,1)S(1)}, u32[]{:S(2)}, u32[]{:S(2)}) collective-permute-start(bf16[128,2304]{1,0:T(8,128)(2,1)S(1)} %slice.208), channel_id=1, source_target_pairs={{0,4},{1,5},{2,6},{3,7},{4,0},{5,1},{6,2},{7,3},{8,12},{9,13},{10,... | collective-permute-start | bytes 1769480 | tf_op jit(solution)/shard_map/ppermute | solution.py:531
  114.0 27.8 %collective-permute-start.21 = (bf16[128,2048]{1,0:T(8,128)(2,1)}, bf16[128,2048]{1,0:T(8,128)(2,1)S(1)}, u32[]{:S(2)}, u32[]{:S(2)}) collective-permute-start(bf16[128,2048]{1,0:T(8,128)(2,1)} %bitcast.12.refs_7_.cot_ref), channel_id=1, source_target_pairs={{0,4},{1,5},{2,6},{3,7},{4,0},{5,1},{6,2},{7,3},{8,12},{9,13},{10,... | collective-permute-start | bytes 1572872 | tf_op jit(solution)/shard_map/ppermute | solution.py:531
  115.0 26.8 %collective-permute-start.20 = (bf16[128,2048]{1,0:T(8,128)(2,1)}, bf16[128,2048]{1,0:T(8,128)(2,1)S(1)}, u32[]{:S(2)}, u32[]{:S(2)}) collective-permute-start(bf16[128,2048]{1,0:T(8,128)(2,1)} %bitcast.12.refs_7_.cot_ref), channel_id=1, source_target_pairs={{0,2},{1,3},{2,0},{3,1},{4,6},{5,7},{6,4},{7,5},{8,10},{9,11},{10,... | collective-permute-start | bytes 1572872 | tf_op jit(solution)/shard_map/ppermute | solution.py:531
  157.8 25.1 %collective-permute-start.31 = (bf16[128,2176]{1,0:T(8,128)(2,1)}, bf16[128,2176]{1,0:T(8,128)(2,1)}, u32[]{:S(2)}, u32[]{:S(2)}) collective-permute-start(bf16[128,2176]{1,0:T(8,128)(2,1)} %get-tuple-element.244.refs_0_), channel_id=1, source_target_pairs={{0,1},{1,0},{2,3},{3,2},{4,5},{5,4},{6,7},{7,6},{8,9},{9,8},{10,11... | collective-permute-start | bytes 1671176 | tf_op jit(solution)/shard_map/ppermute | solution.py:531
  224.2 43.2 %collective-permute-start.35 = (bf16[288,2048]{1,0:T(8,128)(2,1)}, bf16[288,2048]{1,0:T(8,128)(2,1)}, u32[]{:S(2)}, u32[]{:S(2)}) collective-permute-start(bf16[288,2048]{1,0:T(8,128)(2,1)} %get-tuple-element.258), channel_id=1, source_target_pairs={{0,8},{8,0},{16,24},{24,16},{1,9},{9,1},{17,25},{25,17},{2,10},{10... | collective-permute-start | bytes 3538952 | tf_op jit(solution)/shard_map/ppermute | solution.py:609
  267.4 34.0 %collective-permute-start.38 = (bf16[512,2048]{1,0:T(8,128)(2,1)}, bf16[512,2048]{1,0:T(8,128)(2,1)}, u32[]{:S(2)}, u32[]{:S(2)}) collective-permute-start(bf16[512,2048]{1,0:T(8,128)(2,1)} %get-tuple-element.269), channel_id=1, source_target_pairs={{0,1},{1,0},{2,3},{3,2},{4,5},{5,4},{6,7},{7,6},{8,9},{9,8},{10,11... | collective-permute-start | bytes 6291464 | tf_op jit(solution)/shard_map/ppermute | solution.py:531
  269.3 32.1 %collective-permute-start.36 = (bf16[144,2048]{1,0:T(8,128)(2,1)S(1)}, bf16[144,2048]{1,0:T(8,128)(2,1)S(1)}, u32[]{:S(2)}, u32[]{:S(2)}) collective-permute-start(bf16[144,2048]{1,0:T(8,128)(2,1)S(1)} %slice.264), channel_id=1, source_target_pairs={{0,16},{8,24},{16,0},{24,8},{1,17},{9,25},{17,1},{25,9},{2,18},{10... | collective-permute-start | bytes 1769480 | tf_op jit(solution)/shard_map/ppermute | solution.py:609
  272.0 29.4 %collective-permute-start.37 = (bf16[144,2048]{1,0:T(8,128)(2,1)}, bf16[144,2048]{1,0:T(8,128)(2,1)S(1)}, u32[]{:S(2)}, u32[]{:S(2)}) collective-permute-start(bf16[144,2048]{1,0:T(8,128)(2,1)} %get-tuple-element.268), channel_id=1, source_target_pairs={{0,8},{8,0},{16,24},{24,16},{1,9},{9,1},{17,25},{25,17},{2,10},{10... | collective-permute-start | bytes 1769480 | tf_op jit(solution)/shard_map/ppermute | solution.py:609
  317.7 17.2 %collective-permute-start.43 = (bf16[128,2176]{1,0:T(8,128)(2,1)S(1)}, bf16[128,2176]{1,0:T(8,128)(2,1)S(1)}, u32[]{:S(2)}, u32[]{:S(2)}) collective-permute-start(bf16[128,2176]{1,0:T(8,128)(2,1)S(1)} %pad_maximum_fusion.6), channel_id=1, source_target_pairs={{0,2},{1,3},{2,0},{3,1},{4,6},{5,7},{6,4},{7,5},{8,10},{9,11},{10,... | collective-permute-start | bytes 1671176 | tf_op jit(solution)/shard_map/ppermute | solution.py:531
  350.2 20.0 %all-to-all-start.2 = ((bf16[8,128,256]{2,1,0:T(8,128)(2,1)}), bf16[8,128,256]{2,1,0:T(8,128)(2,1)S(1)}, u32[]{:S(2)}, u32[]{:S(2)}) async-start(bf16[8,128,256]{2,1,0:T(8,128)(2,1)} %get-tuple-element.287), calls=%async_computation.2 | async-start | bytes 1048576 | tf_op jit(solution)/shard_map/all_to_all | solution.py:1572
  370.9 20.8 %all-to-all-start.3 = ((bf16[8,256,256]{2,1,0:T(8,128)(2,1)}), bf16[8,256,256]{2,1,0:T(8,128)(2,1)S(1)}, u32[]{:S(2)}, u32[]{:S(2)}) async-start(bf16[8,256,256]{2,1,0:T(8,128)(2,1)} %get-tuple-element.305), calls=%async_computation.3 | async-start | bytes 2097152 | tf_op jit(solution)/shard_map/all_to_all | solution.py:1584
  375.1 16.7 %collective-permute-start.52 = (bf16[72,2048]{1,0:T(8,128)(2,1)}, bf16[72,2048]{1,0:T(8,128)(2,1)S(1)}, u32[]{:S(2)}, u32[]{:S(2)}) collective-permute-start(bf16[72,2048]{1,0:T(8,128)(2,1)} %get-tuple-element.301), channel_id=1, source_target_pairs={{0,16},{8,24},{16,0},{24,8},{1,17},{9,25},{17,1},{25,9},{2,18},{10... | collective-permute-start | bytes 884744 | tf_op jit(solution)/shard_map/ppermute | solution.py:609
  391.8 25.7 %all-to-all-start.4 = ((bf16[8,384,256]{2,1,0:T(8,128)(2,1)}), bf16[8,384,256]{2,1,0:T(8,128)(2,1)}, u32[]{:S(2)}, u32[]{:S(2)}) async-start(bf16[8,384,256]{2,1,0:T(8,128)(2,1)} %get-tuple-element.310), calls=%async_computation.4 | async-start | bytes 3145728 | tf_op jit(solution)/shard_map/all_to_all | solution.py:1584
  423.9 17.1 %collective-permute-start.59 = (bf16[640,256]{1,0:T(8,128)(2,1)S(1)}, bf16[640,256]{1,0:T(8,128)(2,1)S(1)}, u32[]{:S(2)}, u32[]{:S(2)}) collective-permute-start(bf16[640,256]{1,0:T(8,128)(2,1)S(1)} %pad_maximum_fusion.14), channel_id=1, source_target_pairs={{0,8},{8,0},{16,24},{24,16},{1,9},{9,1},{17,25},{25,17},{2,10},{10... | collective-permute-start | bytes 983048 | tf_op jit(solution)/shard_map/ppermute | solution.py:609
  443.9 27.8 %collective-permute-start.66 = (bf16[72,2048]{1,0:T(8,128)(2,1)}, bf16[72,2048]{1,0:T(8,128)(2,1)}, u32[]{:S(2)}, u32[]{:S(2)}) collective-permute-start(bf16[72,2048]{1,0:T(8,128)(2,1)} %get-tuple-element.348.refs_0_), channel_id=1, source_target_pairs={{0,8},{8,0},{16,24},{24,16},{1,9},{9,1},{17,25},{25,17},{2,10},{10... | collective-permute-start | bytes 884744 | tf_op jit(solution)/shard_map/ppermute | solution.py:609
  444.5 29.2 %collective-permute-start.64 = (bf16[640,256]{1,0:T(8,128)(2,1)S(1)}, bf16[640,256]{1,0:T(8,128)(2,1)}, u32[]{:S(2)}, u32[]{:S(2)}) collective-permute-start(bf16[640,256]{1,0:T(8,128)(2,1)S(1)} %add_convert_fusion.4.late_left), channel_id=1, source_target_pairs={{0,16},{8,24},{16,0},{24,8},{1,17},{9,25},{17,1},{25,9},{2,18},{10... | collective-permute-start | bytes 983048 | tf_op jit(solution)/shard_map/ppermute | solution.py:609
  459.5 20.5 %collective-permute-start.70 = (bf16[128,2048]{1,0:T(8,128)(2,1)S(1)}, bf16[128,2048]{1,0:T(8,128)(2,1)S(1)}, u32[]{:S(2)}, u32[]{:S(2)}) collective-permute-start(bf16[128,2048]{1,0:T(8,128)(2,1)S(1)} %pad_maximum_fusion.12), channel_id=1, source_target_pairs={{0,2},{1,3},{2,0},{3,1},{4,6},{5,7},{6,4},{7,5},{8,10},{9,11},{10,... | collective-permute-start | bytes 1572872 | tf_op jit(solution)/shard_map/ppermute | solution.py:531
  461.2 18.8 %collective-permute-start.71 = (bf16[128,2048]{1,0:T(8,128)(2,1)S(1)}, bf16[128,2048]{1,0:T(8,128)(2,1)S(1)}, u32[]{:S(2)}, u32[]{:S(2)}) collective-permute-start(bf16[128,2048]{1,0:T(8,128)(2,1)S(1)} %pad_maximum_fusion.13), channel_id=1, source_target_pairs={{0,4},{1,5},{2,6},{3,7},{4,0},{5,1},{6,2},{7,3},{8,12},{9,13},{10,... | collective-permute-start | bytes 1572872 | tf_op jit(solution)/shard_map/ppermute | solution.py:531
  473.8 18.6 %collective-permute-start.69 = (bf16[72,2048]{1,0:T(8,128)(2,1)}, bf16[72,2048]{1,0:T(8,128)(2,1)S(1)}, u32[]{:S(2)}, u32[]{:S(2)}) collective-permute-start(bf16[72,2048]{1,0:T(8,128)(2,1)} %collective-permute-done.60.refs_5_), channel_id=1, source_target_pairs={{0,8},{8,0},{16,24},{24,16},{1,9},{9,1},{17,25},{25,17},{2,10},{10... | collective-permute-start | bytes 884744 | tf_op jit(solution)/shard_map/ppermute | solution.py:609
  (101 other events, 1096.7 us)

commit v6 on v5

--- a/solution.py
+++ b/solution.py
@@ -635,6 +635,27 @@
     )(values)
 
 
+def pack_kernel(rows, maps_ref, extra_ref, out_ref):
+    for part in range(2):
+        for i in range(3):
+            at = (3 * part + i) * SR
+            out_ref[:, at : at + SR] = maps_ref[i, part * rows : (part + 1) * rows, :]
+    out_ref[:, 6 * SR :] = extra_ref[...]
+
+
+def pack(maps, extra):
+    rows, lanes = extra.shape
+    return pl.pallas_call(
+        functools.partial(pack_kernel, rows),
+        in_specs=[whole()] * 2,
+        out_specs=whole(),
+        out_shape=shape_of((rows, 6 * SR + lanes)),
+        compiler_params=params(),
+        cost_estimate=cost(1 << 20, 1 << 16),
+        name="pack",
+    )(maps, extra)
+
+
 def project_kernel(
     rows, width, wide,
     me_ref, sets_ref, cos_ref, sin_ref, up_ref, *refs,
@@ -1493,12 +1514,11 @@
         return jnp.stack([high + low, high, low] + [jnp.zeros_like(high)] * 5)
 
     hidden_first = gather_first(hidden)
-    narrow = jnp.concatenate([a_attn[0], a_attn[1], a_attn[2]], axis=1)
     at_spot = ((0, 0), (SPOT, 128 - SPOT - experts_all))
     meta = jnp.pad(router[:rows], at_spot) + jnp.pad(segments[0].astype(bf16)[:, None], ((0, 0), (0, 127)))
     lines = jnp.concatenate([gain_attn.reshape(2, 128), gain_moe.reshape(2, 128)], axis=0)
     lines = jnp.pad(lines, ((0, rows - 4), (0, 0)))
-    given = jnp.concatenate([narrow[:rows], narrow[rows:], meta, jnp.pad(router[rows:], at_spot), lines], axis=1)
+    given = pack(a_attn, jnp.concatenate([meta, jnp.pad(router[rows:], at_spot), lines], axis=1))
     given_first = gather_first(given)
     w_got = lax.all_to_all(by_columns(w_qkv, wide), "fsdp", split_axis=0, concat_axis=0, tiled=True)
     hidden_first, cosine, sine, out_own, named, pick_rows = tie(

time: 508 us -> 507 us (level)
    unnamed x124 -> x123, local copies, waits for them, and re-layouts: 11.6 us -> 10.4 us
where the time goes in v6:
time: 507 us; the launch traced here: 497 us
  Pallas kernels  202 us (40%)
  waiting for transfers between devices  143 us (28%)
  starting transfers between devices  80.8 us (16%)
  blocking collectives  25.3 us (5%)
  other arithmetic  25.2 us (5%)
  local copies, waits for them, and re-layouts  18.6 us (4%)
    pallas_call x2, Pallas kernels, expert_pass(): pl.pallas_call(functools.partial(expert_kernel, k, prev is None, width, h...  82 us
    ppermute x50, waiting for transfers between devices, swap(): return lax.ppermute(values, 'fsdp', [(i, i ^ bits) for i in range(EVERY)])  81.6 us
    ppermute x22, waiting for transfers between devices, rep_swap(): return lax.ppermute(values, 'rep', [(i, i ^ bits) for i in range(4)])  58.4 us
    ppermute x50, starting transfers between devices, swap(): return lax.ppermute(values, 'fsdp', [(i, i ^ bits) for i in range(EVERY)])  37.8 us
    pallas_call x1, Pallas kernels, rows_pass(): pl.pallas_call(functools.partial(rows_kernel, part, width, hidden, local)...  29 us
    ppermute x22, starting transfers between devices, rep_swap(): return lax.ppermute(values, 'rep', [(i, i ^ bits) for i in range(4)])  26.1 us
    all_to_all x1, blocking collectives, split_layer(): lax.all_to_all(att_send, 'fsdp', split_axis=0, concat_axis=0, tiled=True)  25.3 us
    pallas_call x1, Pallas kernels, project(): pl.pallas_call(functools.partial(project_kernel, rows, width, wide), grid...  14.5 us
  transfers between devices with their start and end apart: 76, of which 28 were waited for; matrix products, arithmetic and copies ran while one was open for 6% of the time, Pallas kernels for 31%

profile of v6, /device:TPU:0, one launch (start us, length us, event | category | flops | bytes accessed | tf_op | source)
XLA Modules:
  0.0 497.4 jit_solution(8552440315717594269)
XLA Ops:
  10.6 5.3 %by_columns.1 = bf16[8,3,256,256]{3,2,1,0:T(8,128)(2,1)} custom-call(bf16[3,256,2048]{2,1,0:T(8,128)(2,1)} %source_ref.1), custom_call_target="tpu_custom_call" | custom-call | flops 1048576 | bytes 65536 | tf_op jit(solution)/shard_map/by_columns/pallas_call | solution.py:627
  15.9 4.6 all-to-all-start
  33.5 31.2 %collective-permute-done.9 = bf16[64,1152]{1,0:T(8,128)(2,1)S(1)} collective-permute-done((bf16[64,1152]{1,0:T(8,128)(2,1)S(1)}, bf16[64,1152]{1,0:T(8,128)(2,1)S(1)}, u32[]{:S(2)}, u32[]{:S(2)}) %collective-permute-start.9) | collective-permute-done | bytes 147488 | tf_op jit(solution)/shard_map/ppermute | solution.py:531
  64.8 5.4 %collective-permute-done.2 = bf16[64,2048]{1,0:T(8,128)(2,1)S(1)} collective-permute-done((bf16[64,2048]{1,0:T(8,128)(2,1)S(1)}, bf16[64,2048]{1,0:T(8,128)(2,1)S(1)}, u32[]{:S(2)}, u32[]{:S(2)}) %collective-permute-start.2) | collective-permute-done | bytes 262176 | tf_op jit(solution)/shard_map/ppermute | solution.py:531
  79.1 14.5 %project.1 = (bf16[1024,256]{1,0:T(8,128)(2,1)}, bf16[1024,256]{1,0:T(8,128)(2,1)}, bf16[1024,256]{1,0:T(8,128)(2,1)}, bf16[1024,2048]{1,0:T(8,128)(2,1)}, bf16[...) custom-call(s32[1]{0:T(128)} %bitcast.1.me_ref, ...), custom_call_target="tpu_custom_call" | custom-call | flops 1048576 | bytes 65536 | tf_op jit(solution)/shard_map/project/pallas_call | solution.py:760
  93.6 7.2 %attend.1 = (f32[1024,256]{1,0:T(8,128)}, f32[8,1024]{1,0:T(8,128)}, bf16[8,128,256]{2,1,0:T(8,128)(2,1)}) custom-call(s32[1]{0:T(128)} %bitcast.1.me_ref, bf16[1024,256]{1,0:T(8,128)(2,1)} %get-tuple-element.219.q_ref, bf16[1024,256]{1,0:T(8,128)(2,1)} %get-tuple-element.220.k_ref, bf16[1024,256]{1,0:T(8,128)(2,1)} %get-tuple-element.221.v_ref, ...), custom_call_target="tpu_custom_call" | custom-call | flops 1048576 | bytes 65536 | tf_op jit(solution)/shard_map/attend/pallas_call | solution.py:812
  100.8 4.0 collective-permute-done.15.refs_2_.refs_6_
  114.6 25.3 %all_to_all.25.att_ref = bf16[8,128,256]{2,1,0:T(8,128)(2,1)} all-to-all(bf16[8,128,256]{2,1,0:T(8,128)(2,1)S(1)} %copy-done.40), channel_id=1, replica_groups=mesh['rep'=4,'fsdp'=8] {'fsdp'}, dimensions={0} | all-to-all | bytes 1048576 | tf_op jit(solution)/shard_map/all_to_all | solution.py:1537
  146.0 7.3 %mix.1 = (f32[128,2048]{1,0:T(8,128)}, bf16[128,2176]{1,0:T(8,128)(2,1)}, bf16[128,128]{1,0:T(8,128)(2,1)}, f32[128,128]{1,0:T(8,128)}) custom-call(s32[1]{0:T(128)} %bitcast.1.me_ref, bf16[128,2048]{1,0:T(8,128)(2,1)} %bitcast.21, f32[8,2048]{1,0:T(8,128)} %get-tuple-element.215.gains_ref, f32[1024,128]{1,0:T(8,128)} %get-tuple-element.216.mask_ref, ...), custom_call_target="tpu_custom_call" | custom-call | flops 1048576 | bytes 65536 | tf_op jit(solution)/shard_map/mix/pallas_call | solution.py:892
  156.7 11.2 %collective-permute-done.28.refs_2_ = bf16[128,2176]{1,0:T(8,128)(2,1)S(1)} collective-permute-done((bf16[128,2176]{1,0:T(8,128)(2,1)}, bf16[128,2176]{1,0:T(8,128)(2,1)S(1)}, u32[]{:S(2)}, u32[]{:S(2)}) %collective-permute-start.28) | collective-permute-done | bytes 557088 | tf_op jit(solution)/shard_map/ppermute | solution.py:531
  170.7 5.9 %collective-permute-done.29 = bf16[64,2176]{1,0:T(8,128)(2,1)S(1)} collective-permute-done((bf16[64,2176]{1,0:T(8,128)(2,1)S(1)}, bf16[64,2176]{1,0:T(8,128)(2,1)S(1)}, u32[]{:S(2)}, u32[]{:S(2)}) %collective-permute-start.29) | collective-permute-done | bytes 278560 | tf_op jit(solution)/shard_map/ppermute | solution.py:531
  181.8 40.5 %expert.2 = (bf16[512,2048]{1,0:T(8,128)(2,1)}, bf16[512,2048]{1,0:T(8,128)(2,1)}, bf16[1024,2304]{1,0:T(8,128)(2,1)}, f32[1024,128]{1,0:T(8,128)}, bf16[288,204...) custom-call(s32[1]{0:T(128)} %bitcast.10.where_ref, f32[1024,128]{1,0:T(8,128)} %get-tuple-element.216.mask_ref, ...), custom_call_target="tpu_custom_call" | custom-call | flops 22817013760 | bytes 41943040 | tf_op jit(solution)/shard_map/expert/pallas_call | solution.py:1066
  224.0 41.5 %expert.3 = (bf16[512,2048]{1,0:T(8,128)(2,1)}, bf16[512,2048]{1,0:T(8,128)(2,1)}, bf16[1024,2304]{1,0:T(8,128)(2,1)}, f32[1024,128]{1,0:T(8,128)}, bf16[144,204...) custom-call(s32[1]{0:T(128)} %bitcast.10.where_ref, ...), custom_call_target="tpu_custom_call" | custom-call | flops 22817013760 | bytes 41943040 | tf_op jit(solution)/shard_map/expert/pallas_call | solution.py:1066
  271.5 29.0 %rows.1 = (bf16[512,2176]{1,0:T(8,128)(2,1)}, bf16[512,2176]{1,0:T(8,128)(2,1)}) custom-call(bf16[1024,2304]{1,0:T(8,128)(2,1)} %get-tuple-element.249.refs_0_, bf16[1024,2304]{1,0:T(8,128)(2,1)} %get-tuple-element.261.refs_1_, f32[1024,128]{1,0:T(8,128)} %get-tuple-element.262.refs_2_, f32[1024,128]{1,0:T(8,128)} %get-tuple-element.263.refs_3_, ...), custom_call_target="tpu_custom_call" | custom-call | flops 19327352832 | bytes 41943040 | tf_op jit(solution)/shard_map/rows/pallas_call | solution.py:1148
  308.7 7.8 %collective-permute-done.42 = bf16[144,2048]{1,0:T(8,128)(2,1)S(1)} collective-permute-done((bf16[144,2048]{1,0:T(8,128)(2,1)}, bf16[144,2048]{1,0:T(8,128)(2,1)S(1)}, u32[]{:S(2)}, u32[]{:S(2)}) %collective-permute-start.42) | collective-permute-done | bytes 589856 | tf_op jit(solution)/shard_map/ppermute | solution.py:609
  319.2 14.7 %collective-permute-done.45.refs_4_ = bf16[72,2048]{1,0:T(8,128)(2,1)S(1)} collective-permute-done((bf16[72,2048]{1,0:T(8,128)(2,1)S(1)}, bf16[72,2048]{1,0:T(8,128)(2,1)S(1)}, u32[]{:S(2)}, u32[]{:S(2)}) %collective-permute-start.45) | collective-permute-done | bytes 294944 | tf_op jit(solution)/shard_map/ppermute | solution.py:609
  336.7 11.4 %unmix.1 = (f32[128,2048]{1,0:T(8,128)}, bf16[8,256,256]{2,1,0:T(8,128)(2,1)}, bf16[8,128,256]{2,1,0:T(8,128)(2,1)}) custom-call(s32[1]{0:T(128)} %bitcast.1.me_ref, f32[128,2048]{1,0:T(8,128)} %get-tuple-element.236.resid_ref, bf16[128,2048]{1,0:T(8,128)(2,1)} %bitcast.9.refs_7_.cot_ref, f32[8,2048]{1,0:T(8,128)} %get-tuple-element.215.gains_ref, ...), custom_call_target="tpu_custom_call" | custom-call | flops 1048576 | bytes 65536 | tf_op jit(solution)/shard_map/unmix/pallas_call | solution.py:1213
  360.5 6.7 %collective-permute-done.51 = bf16[64,2048]{1,0:T(8,128)(2,1)S(1)} collective-permute-done((bf16[64,2048]{1,0:T(8,128)(2,1)S(1)}, bf16[64,2048]{1,0:T(8,128)(2,1)S(1)}, u32[]{:S(2)}, u32[]{:S(2)}) %collective-permute-start.51) | collective-permute-done | bytes 262176 | tf_op jit(solution)/shard_map/ppermute | solution.py:531
  370.1 4.1 all-to-all-start.3
  376.3 14.5 %attend_back.1 = (bf16[1024,768]{1,0:T(8,128)(2,1)}, bf16[1024,384]{1,0:T(8,128)(2,1)}, bf16[8,384,256]{2,1,0:T(8,128)(2,1)}, bf16[384,256]{1,0:T(8,128)(2,1)}) custom-call(s32[1]{0:T(128)} %bitcast.1.me_ref, bf16[1024,256]{1,0:T(8,128)(2,1)} %get-tuple-element.219.q_ref, bf16[1024,256]{1,0:T(8,128)(2,1)} %get-tuple-element.220.k_ref, ...), custom_call_target="tpu_custom_call" | custom-call | flops 1048576 | bytes 65536 | tf_op jit(solution)/shard_map/attend_back/pallas_call | solution.py:1285
  390.9 4.7 all-to-all-start.4
  399.5 11.0 %unproject.1 = (bf16[512,2048]{1,0:T(8,128)(2,1)}, bf16[512,2048]{1,0:T(8,128)(2,1)}) custom-call(s32[1]{0:T(128)} %bitcast.1.me_ref, bf16[1024,768]{1,0:T(8,128)(2,1)} %get-tuple-element.306.proj_ref, bf16[1024,384]{1,0:T(8,128)(2,1)} %get-tuple-element.307.low_ref, bf16[128,1152]{1,0:T(8,128)(2,1)} %pack.1.refs_7_.refs_0_, bf16[128,1152]{1,0:T(8,128)(2,1)} %copy-done.11, ...), custom_call_target="tpu_custom_call" | custom-call | flops 1048576 | bytes 65536 | tf_op jit(solution)/shard_map/unproject/pallas_call | solution.py:1351
  427.2 3.9 collective-permute-done.61
  431.0 5.2 %collective-permute-done.60.refs_5_ = bf16[72,2048]{1,0:T(8,128)(2,1)} collective-permute-done((bf16[72,2048]{1,0:T(8,128)(2,1)S(1)}, bf16[72,2048]{1,0:T(8,128)(2,1)}, u32[]{:S(2)}, u32[]{:S(2)}) %collective-permute-start.60) | collective-permute-done | bytes 294944 | tf_op jit(solution)/shard_map/ppermute | solution.py:609
  436.3 3.8 collective-permute-done.59
  446.1 4.7 unpack.2
  450.7 4.2 collective-permute-done.62.refs_2_
  462.4 8.5 %collective-permute-done.65.early_right = bf16[384,256]{1,0:T(8,128)(2,1)S(1)} collective-permute-done((bf16[384,256]{1,0:T(8,128)(2,1)S(1)}, bf16[384,256]{1,0:T(8,128)(2,1)S(1)}, u32[]{:S(2)}, u32[]{:S(2)}) %collective-permute-start.65) | collective-permute-done | bytes 196640 | tf_op jit(solution)/shard_map/ppermute | solution.py:609
  473.0 3.7 finish.1
  483.6 3.6 collective-permute-done.68.refs_6_
  487.2 4.3 collective-permute-done.69.refs_7_
  492.2 4.7 unpack.3
  (342 shorter events, 140.9 us)
Async XLA Ops:
  5.6 66.8 %collective-permute-start.11 = (bf16[128,1152]{1,0:T(8,128)(2,1)}, bf16[128,1152]{1,0:T(8,128)(2,1)}, u32[]{:S(2)}, u32[]{:S(2)}) collective-permute-start(bf16[128,1152]{1,0:T(8,128)(2,1)} %pack.1.refs_7_.refs_0_), channel_id=1, source_target_pairs={{0,1},{1,0},{2,3},{3,2},{4,5},{5,4},{6,7},{7,6},{8,9},{9,8},{10,11... | collective-permute-start | bytes 884744 | tf_op jit(solution)/shard_map/ppermute | solution.py:531
  6.1 22.8 %collective-permute-start.8 = (bf16[128,1152]{1,0:T(8,128)(2,1)}, bf16[128,1152]{1,0:T(8,128)(2,1)S(1)}, u32[]{:S(2)}, u32[]{:S(2)}) collective-permute-start(bf16[128,1152]{1,0:T(8,128)(2,1)} %pack.1.refs_7_.refs_0_), channel_id=1, source_target_pairs={{0,4},{1,5},{2,6},{3,7},{4,0},{5,1},{6,2},{7,3},{8,12},{9,13},{10,... | collective-permute-start | bytes 884744 | tf_op jit(solution)/shard_map/ppermute | solution.py:531
  8.6 22.4 %collective-permute-start.7 = (bf16[128,1152]{1,0:T(8,128)(2,1)}, bf16[128,1152]{1,0:T(8,128)(2,1)S(1)}, u32[]{:S(2)}, u32[]{:S(2)}) collective-permute-start(bf16[128,1152]{1,0:T(8,128)(2,1)} %pack.1.refs_7_.refs_0_), channel_id=1, source_target_pairs={{0,2},{1,3},{2,0},{3,1},{4,6},{5,7},{6,4},{7,5},{8,10},{9,11},{10,... | collective-permute-start | bytes 884744 | tf_op jit(solution)/shard_map/ppermute | solution.py:531
  10.1 22.5 %collective-permute-start.1 = (bf16[128,2048]{1,0:T(8,128)(2,1)}, bf16[128,2048]{1,0:T(8,128)(2,1)S(1)}, u32[]{:S(2)}, u32[]{:S(2)}) collective-permute-start(bf16[128,2048]{1,0:T(8,128)(2,1)} %bitcast.18), channel_id=1, source_target_pairs={{0,4},{1,5},{2,6},{3,7},{4,0},{5,1},{6,2},{7,3},{8,12},{9,13},{10,... | collective-permute-start | bytes 1572872 | tf_op jit(solution)/shard_map/ppermute | solution.py:531
  10.6 22.0 %collective-permute-start = (bf16[128,2048]{1,0:T(8,128)(2,1)}, bf16[128,2048]{1,0:T(8,128)(2,1)S(1)}, u32[]{:S(2)}, u32[]{:S(2)}) collective-permute-start(bf16[128,2048]{1,0:T(8,128)(2,1)} %bitcast.19), channel_id=1, source_target_pairs={{0,2},{1,3},{2,0},{3,1},{4,6},{5,7},{6,4},{7,5},{8,10},{9,11},{10,... | collective-permute-start | bytes 1572872 | tf_op jit(solution)/shard_map/ppermute | solution.py:531
  15.9 60.6 %all-to-all-start = ((bf16[8,3,256,256]{3,2,1,0:T(8,128)(2,1)}), bf16[8,3,256,256]{3,2,1,0:T(8,128)(2,1)}, u32[]{:S(2)}, u32[]{:S(2)}) async-start(bf16[8,3,256,256]{3,2,1,0:T(8,128)(2,1)} %by_columns.1), calls=%async_computation | async-start | bytes 6291456 | tf_op jit(solution)/shard_map/all_to_all | solution.py:1523
  28.9 42.9 %collective-permute-start.10 = (bf16[64,1152]{1,0:T(8,128)(2,1)S(1)}, bf16[64,1152]{1,0:T(8,128)(2,1)S(1)}, u32[]{:S(2)}, u32[]{:S(2)}) collective-permute-start(bf16[64,1152]{1,0:T(8,128)(2,1)S(1)} %slice.239), channel_id=1, source_target_pairs={{0,2},{1,3},{2,0},{3,1},{4,6},{5,7},{6,4},{7,5},{8,10},{9,11},{10,... | collective-permute-start | bytes 442376 | tf_op jit(solution)/shard_map/ppermute | solution.py:531
  31.0 33.8 %collective-permute-start.9 = (bf16[64,1152]{1,0:T(8,128)(2,1)S(1)}, bf16[64,1152]{1,0:T(8,128)(2,1)S(1)}, u32[]{:S(2)}, u32[]{:S(2)}) collective-permute-start(bf16[64,1152]{1,0:T(8,128)(2,1)S(1)} %slice.238), channel_id=1, source_target_pairs={{0,4},{1,5},{2,6},{3,7},{4,0},{5,1},{6,2},{7,3},{8,12},{9,13},{10,... | collective-permute-start | bytes 442376 | tf_op jit(solution)/shard_map/ppermute | solution.py:531
  32.7 37.5 %collective-permute-start.2 = (bf16[64,2048]{1,0:T(8,128)(2,1)S(1)}, bf16[64,2048]{1,0:T(8,128)(2,1)S(1)}, u32[]{:S(2)}, u32[]{:S(2)}) collective-permute-start(bf16[64,2048]{1,0:T(8,128)(2,1)S(1)} %slice.182), channel_id=1, source_target_pairs={{0,4},{1,5},{2,6},{3,7},{4,0},{5,1},{6,2},{7,3},{8,12},{9,13},{10,... | collective-permute-start | bytes 786440 | tf_op jit(solution)/shard_map/ppermute | solution.py:531
  33.4 38.4 %collective-permute-start.3 = (bf16[64,2048]{1,0:T(8,128)(2,1)S(1)}, bf16[64,2048]{1,0:T(8,128)(2,1)S(1)}, u32[]{:S(2)}, u32[]{:S(2)}) collective-permute-start(bf16[64,2048]{1,0:T(8,128)(2,1)S(1)} %slice.183), channel_id=1, source_target_pairs={{0,2},{1,3},{2,0},{3,1},{4,6},{5,7},{6,4},{7,5},{8,10},{9,11},{10,... | collective-permute-start | bytes 786440 | tf_op jit(solution)/shard_map/ppermute | solution.py:531
  76.5 28.3 %collective-permute-start.15 = (bf16[256,2304]{1,0:T(8,128)(2,1)}, bf16[256,2304]{1,0:T(8,128)(2,1)S(1)}, u32[]{:S(2)}, u32[]{:S(2)}) collective-permute-start(bf16[256,2304]{1,0:T(8,128)(2,1)} %pad_maximum_fusion.1.refs_0_.refs_4_), channel_id=1, source_target_pairs={{0,4},{1,5},{2,6},{3,7},{4,0},{5,1},{6,2},{7,3},{8,12},{9,13},{10,... | collective-permute-start | bytes 3538952 | tf_op jit(solution)/shard_map/ppermute | solution.py:531
  77.6 27.9 %collective-permute-start.14 = (bf16[256,2304]{1,0:T(8,128)(2,1)}, bf16[256,2304]{1,0:T(8,128)(2,1)S(1)}, u32[]{:S(2)}, u32[]{:S(2)}) collective-permute-start(bf16[256,2304]{1,0:T(8,128)(2,1)} %pad_maximum_fusion.1.refs_0_.refs_4_), channel_id=1, source_target_pairs={{0,2},{1,3},{2,0},{3,1},{4,6},{5,7},{6,4},{7,5},{8,10},{9,11},{10,... | collective-permute-start | bytes 3538952 | tf_op jit(solution)/shard_map/ppermute | solution.py:531
  106.7 33.2 %collective-permute-start.17 = (bf16[128,2304]{1,0:T(8,128)(2,1)S(1)}, bf16[128,2304]{1,0:T(8,128)(2,1)S(1)}, u32[]{:S(2)}, u32[]{:S(2)}) collective-permute-start(bf16[128,2304]{1,0:T(8,128)(2,1)S(1)} %slice.189), channel_id=1, source_target_pairs={{0,2},{1,3},{2,0},{3,1},{4,6},{5,7},{6,4},{7,5},{8,10},{9,11},{10,... | collective-permute-start | bytes 1769480 | tf_op jit(solution)/shard_map/ppermute | solution.py:531
  108.3 31.6 %collective-permute-start.16 = (bf16[128,2304]{1,0:T(8,128)(2,1)S(1)}, bf16[128,2304]{1,0:T(8,128)(2,1)S(1)}, u32[]{:S(2)}, u32[]{:S(2)}) collective-permute-start(bf16[128,2304]{1,0:T(8,128)(2,1)S(1)} %slice.188), channel_id=1, source_target_pairs={{0,4},{1,5},{2,6},{3,7},{4,0},{5,1},{6,2},{7,3},{8,12},{9,13},{10,... | collective-permute-start | bytes 1769480 | tf_op jit(solution)/shard_map/ppermute | solution.py:531
  112.1 27.8 %collective-permute-start.21 = (bf16[128,2048]{1,0:T(8,128)(2,1)}, bf16[128,2048]{1,0:T(8,128)(2,1)S(1)}, u32[]{:S(2)}, u32[]{:S(2)}) collective-permute-start(bf16[128,2048]{1,0:T(8,128)(2,1)} %bitcast.9.refs_7_.cot_ref), channel_id=1, source_target_pairs={{0,4},{1,5},{2,6},{3,7},{4,0},{5,1},{6,2},{7,3},{8,12},{9,13},{10,... | collective-permute-start | bytes 1572872 | tf_op jit(solution)/shard_map/ppermute | solution.py:531
  113.1 26.8 %collective-permute-start.20 = (bf16[128,2048]{1,0:T(8,128)(2,1)}, bf16[128,2048]{1,0:T(8,128)(2,1)S(1)}, u32[]{:S(2)}, u32[]{:S(2)}) collective-permute-start(bf16[128,2048]{1,0:T(8,128)(2,1)} %bitcast.9.refs_7_.cot_ref), channel_id=1, source_target_pairs={{0,2},{1,3},{2,0},{3,1},{4,6},{5,7},{6,4},{7,5},{8,10},{9,11},{10,... | collective-permute-start | bytes 1572872 | tf_op jit(solution)/shard_map/ppermute | solution.py:531
  155.9 25.1 %collective-permute-start.31 = (bf16[128,2176]{1,0:T(8,128)(2,1)}, bf16[128,2176]{1,0:T(8,128)(2,1)}, u32[]{:S(2)}, u32[]{:S(2)}) collective-permute-start(bf16[128,2176]{1,0:T(8,128)(2,1)} %get-tuple-element.244.refs_0_), channel_id=1, source_target_pairs={{0,1},{1,0},{2,3},{3,2},{4,5},{5,4},{6,7},{7,6},{8,9},{9,8},{10,11... | collective-permute-start | bytes 1671176 | tf_op jit(solution)/shard_map/ppermute | solution.py:531
  222.3 43.2 %collective-permute-start.35 = (bf16[288,2048]{1,0:T(8,128)(2,1)}, bf16[288,2048]{1,0:T(8,128)(2,1)S(1)}, u32[]{:S(2)}, u32[]{:S(2)}) collective-permute-start(bf16[288,2048]{1,0:T(8,128)(2,1)} %get-tuple-element.258), channel_id=1, source_target_pairs={{0,8},{8,0},{16,24},{24,16},{1,9},{9,1},{17,25},{25,17},{2,10},{10... | collective-permute-start | bytes 3538952 | tf_op jit(solution)/shard_map/ppermute | solution.py:609
  265.6 35.0 %collective-permute-start.38 = (bf16[512,2048]{1,0:T(8,128)(2,1)}, bf16[512,2048]{1,0:T(8,128)(2,1)}, u32[]{:S(2)}, u32[]{:S(2)}) collective-permute-start(bf16[512,2048]{1,0:T(8,128)(2,1)} %get-tuple-element.269), channel_id=1, source_target_pairs={{0,1},{1,0},{2,3},{3,2},{4,5},{5,4},{6,7},{7,6},{8,9},{9,8},{10,11... | collective-permute-start | bytes 6291464 | tf_op jit(solution)/shard_map/ppermute | solution.py:531
  268.4 32.1 %collective-permute-start.36 = (bf16[144,2048]{1,0:T(8,128)(2,1)S(1)}, bf16[144,2048]{1,0:T(8,128)(2,1)S(1)}, u32[]{:S(2)}, u32[]{:S(2)}) collective-permute-start(bf16[144,2048]{1,0:T(8,128)(2,1)S(1)} %slice.242), channel_id=1, source_target_pairs={{0,16},{8,24},{16,0},{24,8},{1,17},{9,25},{17,1},{25,9},{2,18},{10... | collective-permute-start | bytes 1769480 | tf_op jit(solution)/shard_map/ppermute | solution.py:609
  271.1 29.5 %collective-permute-start.37 = (bf16[144,2048]{1,0:T(8,128)(2,1)}, bf16[144,2048]{1,0:T(8,128)(2,1)S(1)}, u32[]{:S(2)}, u32[]{:S(2)}) collective-permute-start(bf16[144,2048]{1,0:T(8,128)(2,1)} %get-tuple-element.268), channel_id=1, source_target_pairs={{0,8},{8,0},{16,24},{24,16},{1,9},{9,1},{17,25},{25,17},{2,10},{10... | collective-permute-start | bytes 1769480 | tf_op jit(solution)/shard_map/ppermute | solution.py:609
  316.8 17.2 %collective-permute-start.43 = (bf16[128,2176]{1,0:T(8,128)(2,1)S(1)}, bf16[128,2176]{1,0:T(8,128)(2,1)S(1)}, u32[]{:S(2)}, u32[]{:S(2)}) collective-permute-start(bf16[128,2176]{1,0:T(8,128)(2,1)S(1)} %pad_maximum_fusion.6), channel_id=1, source_target_pairs={{0,2},{1,3},{2,0},{3,1},{4,6},{5,7},{6,4},{7,5},{8,10},{9,11},{10,... | collective-permute-start | bytes 1671176 | tf_op jit(solution)/shard_map/ppermute | solution.py:531
  349.3 20.0 %all-to-all-start.2 = ((bf16[8,128,256]{2,1,0:T(8,128)(2,1)}), bf16[8,128,256]{2,1,0:T(8,128)(2,1)S(1)}, u32[]{:S(2)}, u32[]{:S(2)}) async-start(bf16[8,128,256]{2,1,0:T(8,128)(2,1)} %get-tuple-element.287), calls=%async_computation.2 | async-start | bytes 1048576 | tf_op jit(solution)/shard_map/all_to_all | solution.py:1592
  370.1 20.8 %all-to-all-start.3 = ((bf16[8,256,256]{2,1,0:T(8,128)(2,1)}), bf16[8,256,256]{2,1,0:T(8,128)(2,1)S(1)}, u32[]{:S(2)}, u32[]{:S(2)}) async-start(bf16[8,256,256]{2,1,0:T(8,128)(2,1)} %get-tuple-element.305), calls=%async_computation.3 | async-start | bytes 2097152 | tf_op jit(solution)/shard_map/all_to_all | solution.py:1604
  374.2 16.7 %collective-permute-start.52 = (bf16[72,2048]{1,0:T(8,128)(2,1)}, bf16[72,2048]{1,0:T(8,128)(2,1)S(1)}, u32[]{:S(2)}, u32[]{:S(2)}) collective-permute-start(bf16[72,2048]{1,0:T(8,128)(2,1)} %get-tuple-element.301), channel_id=1, source_target_pairs={{0,16},{8,24},{16,0},{24,8},{1,17},{9,25},{17,1},{25,9},{2,18},{10... | collective-permute-start | bytes 884744 | tf_op jit(solution)/shard_map/ppermute | solution.py:609
  390.9 25.7 %all-to-all-start.4 = ((bf16[8,384,256]{2,1,0:T(8,128)(2,1)}), bf16[8,384,256]{2,1,0:T(8,128)(2,1)}, u32[]{:S(2)}, u32[]{:S(2)}) async-start(bf16[8,384,256]{2,1,0:T(8,128)(2,1)} %get-tuple-element.310), calls=%async_computation.4 | async-start | bytes 3145728 | tf_op jit(solution)/shard_map/all_to_all | solution.py:1604
  423.0 17.1 %collective-permute-start.59 = (bf16[640,256]{1,0:T(8,128)(2,1)S(1)}, bf16[640,256]{1,0:T(8,128)(2,1)S(1)}, u32[]{:S(2)}, u32[]{:S(2)}) collective-permute-start(bf16[640,256]{1,0:T(8,128)(2,1)S(1)} %pad_maximum_fusion.14), channel_id=1, source_target_pairs={{0,8},{8,0},{16,24},{24,16},{1,9},{9,1},{17,25},{25,17},{2,10},{10... | collective-permute-start | bytes 983048 | tf_op jit(solution)/shard_map/ppermute | solution.py:609
  443.0 27.8 %collective-permute-start.66 = (bf16[72,2048]{1,0:T(8,128)(2,1)}, bf16[72,2048]{1,0:T(8,128)(2,1)}, u32[]{:S(2)}, u32[]{:S(2)}) collective-permute-start(bf16[72,2048]{1,0:T(8,128)(2,1)} %get-tuple-element.348.refs_0_), channel_id=1, source_target_pairs={{0,8},{8,0},{16,24},{24,16},{1,9},{9,1},{17,25},{25,17},{2,10},{10... | collective-permute-start | bytes 884744 | tf_op jit(solution)/shard_map/ppermute | solution.py:609
  443.6 29.2 %collective-permute-start.64 = (bf16[640,256]{1,0:T(8,128)(2,1)S(1)}, bf16[640,256]{1,0:T(8,128)(2,1)}, u32[]{:S(2)}, u32[]{:S(2)}) collective-permute-start(bf16[640,256]{1,0:T(8,128)(2,1)S(1)} %add_convert_fusion.4.late_left), channel_id=1, source_target_pairs={{0,16},{8,24},{16,0},{24,8},{1,17},{9,25},{17,1},{25,9},{2,18},{10... | collective-permute-start | bytes 983048 | tf_op jit(solution)/shard_map/ppermute | solution.py:609
  458.6 20.5 %collective-permute-start.70 = (bf16[128,2048]{1,0:T(8,128)(2,1)S(1)}, bf16[128,2048]{1,0:T(8,128)(2,1)S(1)}, u32[]{:S(2)}, u32[]{:S(2)}) collective-permute-start(bf16[128,2048]{1,0:T(8,128)(2,1)S(1)} %pad_maximum_fusion.12), channel_id=1, source_target_pairs={{0,2},{1,3},{2,0},{3,1},{4,6},{5,7},{6,4},{7,5},{8,10},{9,11},{10,... | collective-permute-start | bytes 1572872 | tf_op jit(solution)/shard_map/ppermute | solution.py:531
  460.3 18.8 %collective-permute-start.71 = (bf16[128,2048]{1,0:T(8,128)(2,1)S(1)}, bf16[128,2048]{1,0:T(8,128)(2,1)S(1)}, u32[]{:S(2)}, u32[]{:S(2)}) collective-permute-start(bf16[128,2048]{1,0:T(8,128)(2,1)S(1)} %pad_maximum_fusion.13), channel_id=1, source_target_pairs={{0,4},{1,5},{2,6},{3,7},{4,0},{5,1},{6,2},{7,3},{8,12},{9,13},{10,... | collective-permute-start | bytes 1572872 | tf_op jit(solution)/shard_map/ppermute | solution.py:531
  472.9 18.6 %collective-permute-start.69 = (bf16[72,2048]{1,0:T(8,128)(2,1)}, bf16[72,2048]{1,0:T(8,128)(2,1)S(1)}, u32[]{:S(2)}, u32[]{:S(2)}) collective-permute-start(bf16[72,2048]{1,0:T(8,128)(2,1)} %collective-permute-done.60.refs_5_), channel_id=1, source_target_pairs={{0,8},{8,0},{16,24},{24,16},{1,9},{9,1},{17,25},{25,17},{2,10},{10... | collective-permute-start | bytes 884744 | tf_op jit(solution)/shard_map/ppermute | solution.py:609
  (102 other events, 1095.2 us)
